TPU v7x, 256 devices: a whole 4x4x8 slice. The times are simulated.
256 devices in a mesh: row: 4 (over y), col: 64 (over z, x, core).
Axes of the slice: x: 4, y: 4, z: 8, core: 2. Of those that a mesh axis runs over, the one named last changes fastest.
Arguments:
- queries: bfloat16 [1024, 4096], P(('row', 'col')), may hold values from -1.25 to 1.25
- passages: bfloat16 [32768, 4096], P(('col', 'row')), may hold values from -0.375 to 0.375
- positives: int32 [1024], P('row'), may hold values from 0 to 32767, as said below
- hard_negatives: int32 [1024, 7], P('row'), may hold values from 0 to 32767, as said below
- thresholds: float32 [1024], P('row'), may hold values from 0.1 to 2
Outputs:
- row_losses: float32 [1024], P(('row', 'col'))
- grad_queries: float32 [1024, 4096], P(('row', 'col'))
- grad_passages: float32 [32768, 4096], P(('col', 'row'))
Inputs may be any that keep to these rules, and one draw needn't show every extreme that they name: `positives`: each query's positive passage. `hard_negatives`: passages mined for each query; ids may repeat or equal the query's positive.
All inputs are finite; a program needn't handle non-finite values.
Results may differ from a plain program's by a relative error of at most 0.0023.
Values may be sent and summed in bfloat16 or wider, within the bound.
No kernel may reach another device: no remote copies, remote signals or barrier semaphores. Data moves between devices by JAX's collectives and lax.ppermute only.
A program may use at most 64 MiB of HBM per device.

v0:
```python
import jax
import jax.numpy as jnp
from jax import lax
from jax.sharding import Mesh
from jax.sharding import PartitionSpec as P

COL = ("col_0", "col_1", "col_2")
ROW_COL = ("row", "col_0", "col_1", "col_2")
COL_ROW = ("col_0", "col_1", "col_2", "row")


inv_temp = 50.0
sharpness = 4.0


def copy_for_each(shard, axis):
    copies = jnp.broadcast_to(shard, (lax.axis_size(axis), *shard.shape))
    return lax.all_to_all(copies, axis, split_axis=0, concat_axis=0, tiled=True)


def joined_along(tiles, dim):
    tiles = jnp.moveaxis(tiles, 0, dim)
    lengths = tiles.shape
    return tiles.reshape(*lengths[:dim], lengths[dim] * lengths[dim + 1], *lengths[dim + 2 :])


def whole_of(shard, axes, dim):
    far, near = axes
    leading = copy_for_each(shard, far)
    tiles = jnp.swapaxes(copy_for_each(leading, near), 0, 1)
    return joined_along(tiles.reshape(-1, *shard.shape), dim)


def over_copies(shard, axis):
    return copy_for_each(shard, axis).sum(axis=0)


def all_in_one(shard, axis):
    leaves = jax.tree.leaves(shard)
    order = sorted(range(len(leaves)), key=lambda k: -leaves[k].size)
    width = (1, *leaves[order[0]].shape)[-1]
    lines = [
        jnp.pad(leaves[k].reshape(-1), (0, -leaves[k].size % width)).reshape(-1, width)
        for k in order
    ]
    both, at, found = (copy_for_each(jnp.concatenate(lines), axis), 0, {})
    for k, line in zip(order, lines):
        piece = both[:, at : at + len(line)].reshape(len(both), -1)
        found[k] = piece[:, : leaves[k].size].reshape(-1, *leaves[k].shape)
        at += len(line)
    numbers = iter(range(len(leaves)))
    return jax.tree.map(lambda _: found[next(numbers)], shard)


def joined_by_halves(pieces, combine):
    while len(jax.tree.leaves(pieces)[0]) > 1:
        pieces = jax.vmap(combine)(
            *(jax.tree.map(lambda part: part[side::2], pieces) for side in (0, 1))
        )
    return jax.tree.map(lambda part: part[0], pieces)


def combined_all(shard, axis, combine):
    pieces = all_in_one(shard, axis)
    return joined_by_halves(pieces, combine)


def cut_along(shard, dim, count):
    before, after = (shard.shape[:dim], shard.shape[dim + 1 :])
    return jnp.moveaxis(shard.reshape(*before, count, -1, *after), dim, 0)


def sum_at_owner(shard, axis, dim):
    count = lax.axis_size(axis)
    tiles = lax.all_to_all(cut_along(shard, dim, count), axis, 0, 0, tiled=True)
    return jnp.sum(tiles, axis=0)


def sum_in_two_steps(shard, axes, dim):
    far, near = axes
    tiles = cut_along(shard, dim, lax.axis_size(far))
    nearer = sum_at_owner(tiles, near, dim + 1)
    arrived = lax.all_to_all(nearer, far, split_axis=0, concat_axis=0, tiled=True)
    return arrived.sum(axis=0)


def pair_merge(left_pair, right_pair):
    left_top, left_total = left_pair
    right_top, right_total = right_pair
    joined = jnp.maximum(left_top, right_top)
    return (
        joined,
        left_total * jnp.exp(left_top - joined) + right_total * jnp.exp(right_top - joined),
    )


def on_device(queries, passages, positives, hard_negatives, thresholds):
    query_block = whole_of(queries, (("col_0", "col_1"), "col_2"), 0)
    passage_block = lax.all_gather(passages, "row", axis=0, tiled=True)
    block_width = passage_block.shape[0]
    query_rows = queries.shape[0]
    scores = jnp.dot(query_block, passage_block.T, preferred_element_type=jnp.float32) * inv_temp
    columns = lax.axis_index(COL) * block_width + lax.iota(jnp.int32, block_width)
    positive_mask = positives[:, None] == columns[None, :]
    kept_mask = positive_mask
    for mined_slot in range(hard_negatives.shape[1]):
        kept_mask = kept_mask | (hard_negatives[:, mined_slot : mined_slot + 1] == columns[None, :])
    picked = over_copies(jnp.sum(jnp.where(positive_mask, scores, 0.0), axis=1), COL)
    penalty = jax.nn.softplus(sharpness * (scores - picked[:, None] - thresholds[:, None]))
    logits = jnp.where(kept_mask, scores, scores - penalty)
    local_top = jnp.max(logits, axis=1)
    local_exp = jnp.exp(logits - local_top[:, None])
    row_top, denominator = combined_all((local_top, jnp.sum(local_exp, axis=1)), COL, pair_merge)
    shifted = local_exp * jnp.exp(local_top - row_top)[:, None]
    losses = row_top + jnp.log(denominator) - picked
    row_losses = lax.dynamic_slice_in_dim(losses, lax.axis_index(COL) * query_rows, query_rows, 0)
    grad_scores = (
        (shifted / denominator[:, None] - positive_mask.astype(jnp.float32)) * inv_temp
    ).astype(jnp.bfloat16)
    query_full = jnp.dot(grad_scores, passage_block, preferred_element_type=jnp.float32)
    grad_queries = sum_in_two_steps(query_full, (("col_0", "col_1"), "col_2"), 0)
    passage_full = lax.dot_general(
        grad_scores, query_block, (((0,), (0,)), ((), ())), preferred_element_type=jnp.float32
    )
    grad_passages = lax.psum_scatter(passage_full, "row", scatter_dimension=0, tiled=True)
    return (row_losses, grad_queries, grad_passages)


def solution(mesh):
    torus = Mesh(
        mesh.devices.reshape(mesh.shape["row"], 8, 4, 2), ("row", "col_0", "col_1", "col_2")
    )
    in_specs = (P(ROW_COL, None), P(COL_ROW, None), P("row"), P("row", None), P("row"))
    out_specs = (P(ROW_COL), P(ROW_COL, None), P(COL_ROW, None))
    return jax.shard_map(
        on_device, mesh=torus, in_specs=in_specs, out_specs=out_specs, check_vma=False
    )
```

profile of v0, /device:TPU:1, one launch (start us, length us, event | category | flops | bytes accessed | tf_op | source)
XLA Modules:
  0.0 199.7 jit_solution(1825640955636901026)
XLA Ops:
  7.2 0.0 all-gather.2.cloned.1.call-start
  7.2 0.7 all-gather.2.cloned.1.call-update
  7.9 2.2 %broadcast_in_dim.11 = bf16[32,4,4096]{2,1,0:T(4,128)(2,1)} broadcast(bf16[4,4096]{1,0:T(4,128)(2,1)} %param.5), dimensions={1,2} | broadcast | bytes 1081344 | tf_op jit(solution)/shard_map/broadcast_in_dim | solution.py:17
  10.1 11.9 %all-to-all-start = ((bf16[32,4,4096]{2,1,0:T(4,128)(2,1)}), bf16[32,4,4096]{2,1,0:T(4,128)(2,1)S(1)}, u32[]{:S(2)}, u32[]{:S(2)}) async-start(bf16[32,4,4096]{2,1,0:T(4,128)(2,1)} %broadcast_in_dim.11), calls=%async_computation | async-start | bytes 2097152 | tf_op jit(solution)/shard_map/all_to_all | solution.py:18
  22.0 26.2 %all-to-all-done = bf16[32,4,4096]{2,1,0:T(4,128)(2,1)S(1)} async-done(((bf16[32,4,4096]{2,1,0:T(4,128)(2,1)}), bf16[32,4,4096]{2,1,0:T(4,128)(2,1)S(1)}, u32[]{:S(2)}, u32[]{:S(2)}) %all-to-all-start) | async-done | bytes 1048608 | tf_op jit(solution)/shard_map/all_to_all | solution.py:18
  48.2 1.3 broadcast_in_dim.13
  49.4 7.9 %all_to_all.31 = bf16[2,32,4,4096]{3,2,1,0:T(4,128)(2,1)S(1)} all-to-all(bf16[2,32,4,4096]{3,2,1,0:T(4,128)(2,1)S(1)} %broadcast_in_dim.13), channel_id=1, replica_groups=mesh['row'=4,'col_0'=8,'col_1'=4,'col_2'=2] {'col_2'}, dimensions={0} | all-to-all | bytes 4194304 | tf_op jit(solution)/shard_map/all_to_all | solution.py:18
  57.3 1.6 copy.16
  58.9 2.0 %reshape_reshape.6 = bf16[256,4096]{1,0:T(8,128)(2,1)} reshape(bf16[32,2,4,4096]{3,2,1,0:T(4,128)(2,1)S(1)} %copy.16) | data formatting | bytes 4194304 | tf_op jit(solution)/shard_map/reshape;reshape | solution.py:24
  60.9 3.6 %all-gather.2.cloned.1.call-done = bf16[512,4096]{1,0:T(8,128)(2,1)} async-done(((bf16[128,4096]{1,0:T(8,128)(2,1)}), bf16[512,4096]{1,0:T(8,128)(2,1)}) %all-gather.2.cloned.1.call-update) | async-done | bytes 4194320 | tf_op jit(solution)/shard_map/all_gather | solution.py:99
  64.5 0.0 copy-done.1
  64.5 4.2 %fusion = (f32[256]{0:T(256)S(1)}, f32[256,512]{1,0:T(8,128)S(1)}) fusion(s32[512]{0:T(512)S(1)} %iota_add_fusion, s32[256]{0:T(256)S(1)} %copy-done.1, bf16[256,4096]{1,0:T(8,128)(2,1)} %reshape_reshape.6, bf16[512,4096]{1,0:T(8,128)(2,1)} %all-gather.2.cloned.1.call-done), kind=kOutput, calls=%fused_computation.7 | convolution fusion | flops 1074265856 | bytes 6819840 | tf_op jit(solution)/shard_map/dot_general | solution.py:102
  68.7 0.7 broadcast_in_dim.15
  69.4 10.7 %all-to-all-start.2 = ((f32[64,1,256]{2,1,0:T(1,128)}), f32[64,1,256]{2,1,0:T(1,128)S(1)}, u32[]{:S(2)}, u32[]{:S(2)}) async-start(f32[64,1,256]{2,1,0:T(1,128)} %broadcast_in_dim.15), calls=%async_computation.2 | async-start | bytes 131072 | tf_op jit(solution)/shard_map/all_to_all | solution.py:18
  80.0 0.0 reduce-scatter.2.cloned.1.call-start
  80.1 10.0 %all-to-all-done.2 = f32[64,1,256]{2,1,0:T(1,128)S(1)} async-done(((f32[64,1,256]{2,1,0:T(1,128)}), f32[64,1,256]{2,1,0:T(1,128)S(1)}, u32[]{:S(2)}, u32[]{:S(2)}) %all-to-all-start.2) | async-done | bytes 65568 | tf_op jit(solution)/shard_map/all_to_all | solution.py:18
  90.1 0.1 reduce_sum.46
  90.2 1.1 fusion.15
  91.3 0.2 fusion.9
  91.6 15.0 %all_to_all.32 = f32[64,2,256]{2,1,0:T(2,128)S(1)} all-to-all(f32[64,2,256]{2,1,0:T(2,128)S(1)} %broadcast_in_dim.16), channel_id=1, replica_groups=mesh['row'=4,'col_0'=8,'col_1'=4,'col_2'=2] {'col_0','col_1','col_2'}, dimensions={0} | all-to-all | bytes 262144 | tf_op jit(solution)/shard_map/all_to_all | solution.py:18
  106.5 0.1 fusion.16
  107.2 4.7 %fusion.11 = f32[512,4096]{1,0:T(8,128)} fusion(bf16[256,4096]{1,0:T(8,128)(2,1)S(1)} %copy-done, f32[256,512]{1,0:T(8,128)S(1)} %get-tuple-element.16, f32[256]{0:T(256)S(1)} %bitcast.27, f32[256]{0:T(256)S(1)} %get-tuple-element.26, f32[256]{0:T(256)S(1)} %get-tuple-element.15, s32[512]{0:T(512)S(1)} %iota_add_fusion, s32[256]{0:T(256)S(1)} %copy-done.1), kind=kOutput, calls=%fused_computation.33 | convolution fusion | flops 1074790400 | bytes 11016192 | tf_op jit(solution)/shard_map/dot_general | solution.py:122
  112.0 0.0 reduce-scatter.2.cloned.1.call-update
  112.0 5.7 %fusion.13 = f32[256,4096]{1,0:T(8,128)} fusion(bf16[512,4096]{1,0:T(8,128)(2,1)} %all-gather.2.cloned.1.call-done, f32[256,512]{1,0:T(8,128)S(1)} %get-tuple-element.16, f32[256]{0:T(256)S(1)} %bitcast.28, f32[256]{0:T(256)S(1)} %get-tuple-element.26, f32[256]{0:T(256)S(1)} %get-tuple-element.15, s32[512]{0:T(512)S(1)} %iota_add_fusion, s32[256]{0:T(256)S(1)} %copy-done.1), kind=kOutput, calls=%fused_computation.34 | convolution fusion | flops 1074790400 | bytes 8919040 | tf_op jit(solution)/shard_map/dot_general | solution.py:120
  117.7 5.3 %reshape_reshape.7 = f32[32,2,4,4096]{3,2,1,0:T(4,128)} reshape(f32[256,4096]{1,0:T(8,128)} %fusion.13) | data formatting | bytes 8388608 | tf_op jit(solution)/shard_map/reshape;reshape | solution.py:70
  122.9 2.5 %copy.28 = f32[32,2,4,4096]{3,2,0,1:T(4,128)S(1)} copy(f32[32,2,4,4096]{3,2,1,0:T(4,128)} %reshape_reshape.7) | data formatting | bytes 8388608 | tf_op jit(solution)/shard_map/reshape;reshape | solution.py:70
  125.5 8.2 %all_to_all.33 = f32[2,32,4,4096]{3,2,1,0:T(4,128)} all-to-all(f32[2,32,4,4096]{3,2,1,0:T(4,128)S(1)} %bitcast.23), channel_id=1, replica_groups=mesh['row'=4,'col_0'=8,'col_1'=4,'col_2'=2] {'col_2'}, dimensions={0} | all-to-all | bytes 8388608 | tf_op jit(solution)/shard_map/all_to_all | solution.py:75
  133.7 5.5 %reduce_sum.48 = f32[32,4,4096]{2,1,0:T(4,128)} reduce(f32[2,32,4,4096]{3,2,1,0:T(4,128)} %all_to_all.33, f32[]{:T(128)} %constant.11.clone.1), dimensions={0}, to_apply=%region_4.5 | reduce | flops 524288 | bytes 6291460 | tf_op jit(solution)/shard_map/reduce_sum | solution.py:76
  139.2 4.0 %all-to-all-start.5 = ((f32[32,4,4096]{2,1,0:T(4,128)}), f32[32,4,4096]{2,1,0:T(4,128)S(1)}, u32[]{:S(2)}, u32[]{:S(2)}) async-start(f32[32,4,4096]{2,1,0:T(4,128)} %reduce_sum.48), calls=%async_computation.5 | async-start | bytes 4194304 | tf_op jit(solution)/shard_map/all_to_all | solution.py:83
  143.2 0.6 dynamic_slice.3
  143.8 48.0 %all-to-all-done.5 = f32[32,4,4096]{2,1,0:T(4,128)S(1)} async-done(((f32[32,4,4096]{2,1,0:T(4,128)}), f32[32,4,4096]{2,1,0:T(4,128)S(1)}, u32[]{:S(2)}, u32[]{:S(2)}) %all-to-all-start.5) | async-done | bytes 2097184 | tf_op jit(solution)/shard_map/all_to_all | solution.py:83
  191.9 1.0 reduce_sum.49
  (40 shorter events, 0.6 us)
Async XLA Ops:
  7.2 57.3 %all-gather.2.cloned.1.call-start = ((), (), s32[]{:S(2)}) async-start(), calls=%async_computation.7 | async-start | bytes 5242880 | tf_op jit(solution)/shard_map/all_gather | solution.py:99
  10.1 38.1 %all-to-all-start = ((bf16[32,4,4096]{2,1,0:T(4,128)(2,1)}), bf16[32,4,4096]{2,1,0:T(4,128)(2,1)S(1)}, u32[]{:S(2)}, u32[]{:S(2)}) async-start(bf16[32,4,4096]{2,1,0:T(4,128)(2,1)} %broadcast_in_dim.11), calls=%async_computation | async-start | bytes 2097152 | tf_op jit(solution)/shard_map/all_to_all | solution.py:18
  57.3 7.2 %copy-start.1 = (s32[256]{0:T(256)S(1)}, s32[256]{0:T(256)}, u32[]{:S(2)}) copy-start(s32[256]{0:T(256)} %param.7) | copy-start | bytes 3076
  60.9 19.2 %copy-start.2 = (s32[256,7]{0,1:T(8,128)S(1)}, s32[256,7]{0,1:T(8,128)}, u32[]{:S(2)}) copy-start(s32[256,7]{0,1:T(8,128)} %param.8) | copy-start | bytes 21508
  60.9 29.3 %copy-start.3 = (f32[256]{0:T(256)S(1)}, f32[256]{0:T(256)}, u32[]{:S(2)}) copy-start(f32[256]{0:T(256)} %param.9) | copy-start | bytes 3076
  60.9 46.3 %copy-start = (bf16[256,4096]{1,0:T(8,128)(2,1)S(1)}, bf16[256,4096]{1,0:T(8,128)(2,1)}, u32[]{:S(2)}) copy-start(bf16[256,4096]{1,0:T(8,128)(2,1)} %reshape_reshape.6) | copy-start | bytes 6291460
  69.4 20.8 %all-to-all-start.2 = ((f32[64,1,256]{2,1,0:T(1,128)}), f32[64,1,256]{2,1,0:T(1,128)S(1)}, u32[]{:S(2)}, u32[]{:S(2)}) async-start(f32[64,1,256]{2,1,0:T(1,128)} %broadcast_in_dim.15), calls=%async_computation.2 | async-start | bytes 131072 | tf_op jit(solution)/shard_map/all_to_all | solution.py:18
  80.0 112.8 %reduce-scatter.2.cloned.1.call-start = ((), (), s32[]{:S(2)}) async-start(), calls=%async_computation.8 | async-start | bytes 10485760 | tf_op jit(solution)/shard_map/reduce_scatter | solution.py:125
  139.2 52.7 %all-to-all-start.5 = ((f32[32,4,4096]{2,1,0:T(4,128)}), f32[32,4,4096]{2,1,0:T(4,128)S(1)}, u32[]{:S(2)}, u32[]{:S(2)}) async-start(f32[32,4,4096]{2,1,0:T(4,128)} %reduce_sum.48), calls=%async_computation.5 | async-start | bytes 4194304 | tf_op jit(solution)/shard_map/all_to_all | solution.py:83
Sparse Core Ops, SparseCore 0:
  9.8 54.6 all-gather.1
  112.1 76.6 reduce-scatter.1
where the time goes:
time: 202 us; the launch traced here: 200 us
  waiting for transfers between devices  88.5 us (44%)
  blocking collectives  31.1 us (15%)
  starting transfers between devices  26.6 us (13%)
  local copies, waits for them, and re-layouts  16.7 us (8%)
  matrix products  14.6 us (7%)
  between operations  14.2 us (7%)
  other arithmetic  7.97 us (4%)
    all_to_all x1, waiting for transfers between devices, sum_in_two_steps(): lax.all_to_all(nearer, far, split_axis=0, concat_axis=0, tiled=True)  48 us
    all_to_all x2, waiting for transfers between devices, copy_for_each(): return lax.all_to_all(copies, axis, split_axis=0, concat_axis=0, tiled=True)  36.2 us
    all_to_all x2, blocking collectives, copy_for_each(): return lax.all_to_all(copies, axis, split_axis=0, concat_axis=0, tiled=True)  22.8 us
    all_to_all x2, starting transfers between devices, copy_for_each(): return lax.all_to_all(copies, axis, split_axis=0, concat_axis=0, tiled=True)  22.5 us
    all_to_all x1, blocking collectives, sum_at_owner(): tiles = lax.all_to_all(cut_along(shard, dim, count), axis, 0, 0, tiled=True)  8.23 us
    another operation x2, local copies, waits for them, and re-layouts, cut_along(): return jnp.moveaxis(shard.reshape(*before, count, -1, *after), dim, 0)  7.83 us
    dot_general x1, matrix products, on_device(): jnp.dot(grad_scores, passage_block, preferred_element_type=jnp.float32)  5.67 us
    reduce_sum x1, other arithmetic, sum_at_owner(): return jnp.sum(tiles, axis=0)  5.5 us
  transfers between devices with their start and end apart: 5, of which 4 were waited for; matrix products, arithmetic and copies ran while one was open for 14% of the time, Pallas kernels for 0%

commit v1 on v0

v1 whole, which is shorter than its diff:
```python
import functools

import jax
import jax.numpy as jnp
from jax import lax
from jax.experimental import pallas as pl
from jax.experimental.pallas import tpu as pltpu
from jax.sharding import Mesh
from jax.sharding import PartitionSpec as P

Y, Z, X, CORE = "row", "col_0", "col_1", "col_2"
COL = (Z, X, CORE)
ROW_COL = (Y, Z, X, CORE)
COL_ROW = (Z, X, CORE, Y)

inv_temp = 50.0
sharpness = 4.0
LOWEST = -3.0e38
F32, BF16 = jnp.float32, jnp.bfloat16
TILE = 512


def shifted(value, axis, step):
    n = lax.axis_size(axis)
    return lax.ppermute(value, axis, [(i, (i + step) % n) for i in range(n)])


def copies(value, axis):
    n = lax.axis_size(axis)
    return lax.all_to_all(jnp.broadcast_to(value, (n, *value.shape)), axis, 0, 0, tiled=True)


def shape(dims, dtype):
    return jax.ShapeDtypeStruct(dims, dtype)


def call(body, outs, args, flops=0, scalars=0):
    size = sum(a.size * a.dtype.itemsize for a in (*args, *outs))
    spaces = [pltpu.SMEM] * scalars + [pltpu.VMEM] * (len(args) - scalars)
    return pl.pallas_call(
        body,
        out_shape=outs,
        in_specs=[pl.BlockSpec(memory_space=s) for s in spaces],
        out_specs=[pl.BlockSpec(memory_space=pltpu.VMEM)] * len(outs),
        cost_estimate=pl.CostEstimate(flops=flops, bytes_accessed=size, transcendentals=0),
        compiler_params=pltpu.CompilerParams(vmem_limit_bytes=48 << 20),
    )(*args)


def eye():
    rows = lax.broadcasted_iota(jnp.int32, (128, 128), 0)
    return rows == lax.broadcasted_iota(jnp.int32, (128, 128), 1)


def as_row(column, diagonal):
    return jnp.sum(jnp.where(diagonal, column, 0.0), axis=0, keepdims=True)


def as_column(row, diagonal):
    return jnp.sum(jnp.where(diagonal, row, 0.0), axis=1, keepdims=True)


def in_place(core, own, other):
    return jnp.where(core == 0, own, other), jnp.where(core == 0, other, own)


def mask_body(meta_ref, columns_ref, code_ref):
    columns = columns_ref[0:1, :]
    for block in range(2):
        rows = slice(128 * block, 128 * block + 128)
        meta = meta_ref[rows, :]
        kept = meta[:, 1:2] == columns
        for slot in range(2, 8):
            kept = kept | (meta[:, slot : slot + 1] == columns)
        code_ref[rows, :] = jnp.where(meta[:, 0:1] == columns, 2.0, jnp.where(kept, 1.0, 0.0))


def tiles(width, body):
    def step(k, _):
        body(pl.ds(pl.multiple_of(k * TILE, TILE), TILE))
        return 0

    lax.fori_loop(0, width // TILE, step, 0)


def score_body(*refs):
    own, other = refs[0:2]
    pool, scores = refs[2:-1], refs[-1]
    scores[...] = jnp.zeros_like(scores)
    contract = (((1,), (1,)), ((), ()))

    def step(at):
        block = jnp.concatenate([p[:, at] for p in pool], axis=0)
        for k, q in ((0, own), (1, other)):
            scores[128 * k : 128 * k + 128, :] += lax.dot_general(
                q[:, at], block, contract, preferred_element_type=F32
            )

    tiles(own.shape[1], step)


def stat_body(core_ref, first, last, code, table):
    diagonal = eye()
    found = []
    for k in range(2):
        rows = slice(128 * k, 128 * k + 128)
        block = jnp.concatenate([first[rows, :], last[rows, :]], axis=1) * inv_temp
        flags = code[rows, :]
        positive = jnp.max(jnp.where(flags == 2.0, block, LOWEST), axis=1, keepdims=True)
        kept = jnp.max(jnp.where(flags > 0.0, block, LOWEST), axis=1, keepdims=True)
        found.append((as_row(positive, diagonal), as_row(kept, diagonal)))
    core = core_ref[0]
    lines = [*in_place(core, found[0][0], found[1][0]), *in_place(core, found[0][1], found[1][1])]
    table[...] = jnp.broadcast_to(jnp.concatenate(lines, axis=0)[None], table.shape)


def soft_body(core_ref, table, meta_ref, code, first, last, weights, totals, stats):
    core = core_ref[0]
    merged = jnp.max(table[...], axis=0)
    lines = [
        *in_place(core, merged[0:1], merged[1:2]),
        *in_place(core, merged[2:3], merged[3:4]),
    ]
    diagonal = eye()
    sums, tops = [], []
    for k in range(2):
        rows = slice(128 * k, 128 * k + 128)
        picked = as_column(lines[k], diagonal)
        kept = as_column(lines[2 + k], diagonal)
        margin = meta_ref[rows, 8:9]
        ceiling = jnp.maximum(kept, picked + margin)
        block = jnp.concatenate([first[rows, :], last[rows, :]], axis=1) * inv_temp
        over = sharpness * (block - picked - margin)
        penalty = jnp.maximum(over, 0.0) + jnp.log(1.0 + jnp.exp(-jnp.abs(over)))
        logits = jnp.where(code[rows, :] > 0.0, block, block - penalty)
        weight = jnp.exp(logits - ceiling)
        weights[rows, :] = weight
        sums.append(as_row(jnp.sum(weight, axis=1, keepdims=True), diagonal))
        tops.append(as_row(ceiling, diagonal) - lines[k])
    lines = in_place(core, *sums)
    totals[...] = jnp.broadcast_to(jnp.concatenate(lines, axis=0)[None], totals.shape)
    stats[...] = jnp.broadcast_to(tops[0], stats.shape)


def grad_body(core_ref, table, stats, code, weights, own, other, grads, losses, low, high):
    merged = jnp.sum(table[...], axis=0)
    lines = in_place(core_ref[0], merged[0:1], merged[1:2])
    losses[...] = stats[...] + jnp.log(lines[0])
    diagonal = eye()
    for k in range(2):
        rows = slice(128 * k, 128 * k + 128)
        total = as_column(lines[k], diagonal)
        positive = jnp.where(code[rows, :] == 2.0, 1.0, 0.0)
        grads[rows, :] = ((weights[rows, :] / total - positive) * inv_temp).astype(BF16)
    block = grads[:, 384:512].T

    def step(at):
        pool = jnp.concatenate([own[:, at], other[:, at]], axis=0)
        out = jnp.dot(block, pool, preferred_element_type=F32).astype(BF16)
        low[:, at] = out[:64]
        high[:, at] = out[64:]

    tiles(own.shape[1], step)


def passage_body(grads, own, other, here, back, ahead):
    block = grads[:, 0:384].T

    def step(at):
        pool = jnp.concatenate([own[:, at], other[:, at]], axis=0)
        out = jnp.dot(block, pool, preferred_element_type=F32)
        here[:, at] = out[0:128]
        back[:, at] = out[128:256]
        ahead[:, at] = out[256:384]

    tiles(own.shape[1], step)


def query_body(grads, here, back, ahead, low, high, own, other):
    block = grads[...]

    def step(at):
        pool = jnp.concatenate([p[:, at] for p in (here, back, ahead, low, high)], axis=0)
        out = jnp.dot(block, pool, preferred_element_type=F32)
        own[:, at] = out[:128]
        other[:, at] = out[128:]

    tiles(here.shape[1], step)


def on_device(queries, passages, positives, hard_negatives, thresholds):
    rows, width = queries.shape
    count = passages.shape[0]
    depth, breadth, ring = lax.axis_size(Z), lax.axis_size(X), lax.axis_size(Y)
    core, far, across, along = (lax.axis_index(a) for a in (CORE, Z, X, Y))
    flag = core.reshape(1)
    half = count // 2

    back, ahead = shifted(passages, Y, 1), shifted(passages, Y, -1)
    line = copies(queries, Z).reshape(depth * rows, width)
    own = copies(line, X).reshape(-1, width)
    low, high = shifted(back[:half], Y, 1), shifted(ahead[half:], Y, -1)
    other = shifted(own, CORE, 1)
    plane = own.shape[0]
    total, pool = 2 * plane, ring * count

    meta = jnp.concatenate(
        [positives[None, :].astype(F32), hard_negatives.T.astype(F32), thresholds[None, :]], axis=0
    )
    meta = meta.reshape(9, depth, breadth, 2, rows)
    meta = jnp.transpose(meta, (3, 2, 1, 4, 0)).reshape(2, plane, 9)
    meta = jnp.where(core == 0, meta, jnp.flip(meta, 0)).reshape(total, 9)
    meta = jnp.pad(meta, ((0, 0), (0, 7)))
    steps = jnp.array([0, 1, 3, 2], jnp.int32)
    base = ((far * breadth + across) * 2 + core) * ring + (along - steps) % ring
    columns = (base[:, None] * count + lax.iota(jnp.int32, count)[None, :]).astype(F32)
    columns = jnp.broadcast_to(columns.reshape(1, pool), (8, pool))
    code = call(mask_body, [shape((total, pool), F32)], [meta, columns])[0]

    first = call(
        score_body,
        [shape((total, 3 * count), F32)],
        [own, other, passages, back, ahead],
        flops=2 * total * 3 * count * width,
    )[0]
    last = call(
        score_body,
        [shape((total, count), F32)],
        [own, other, low, high],
        flops=2 * total * count * width,
    )[0]
    members = depth * breadth * 2
    table = call(stat_body, [shape((members, 4, plane), F32)], [flag, first, last, code], scalars=1)[0]
    table = lax.all_to_all(table, COL, 0, 0, tiled=True)
    weights, table, stats = call(
        soft_body,
        [shape((total, pool), F32), shape((members, 2, plane), F32), shape((8, plane), F32)],
        [flag, table, meta, code, first, last],
        scalars=1,
    )
    table = lax.all_to_all(table, COL, 0, 0, tiled=True)
    grads, losses, low_sum, high_sum = call(
        grad_body,
        [shape((total, pool), BF16), shape((8, plane), F32)] + [shape((half, width), BF16)] * 2,
        [flag, table, stats, code, weights, own, other],
        flops=2 * total * count * width,
        scalars=1,
    )
    low_sum, high_sum = shifted(low_sum, Y, -1), shifted(high_sum, Y, 1)

    own_sum, other_sum = call(
        query_body,
        [shape((plane, width), F32)] * 2,
        [grads, passages, back, ahead, low, high],
        flops=2 * total * pool * width,
    )
    own_sum = own_sum + shifted(other_sum, CORE, 1)
    own_sum = lax.psum_scatter(own_sum, X, scatter_dimension=0, tiled=True)
    grad_queries = lax.psum_scatter(own_sum, Z, scatter_dimension=0, tiled=True)

    here, back_sum, ahead_sum = call(
        passage_body,
        [shape((count, width), F32)] * 3,
        [grads, own, other],
        flops=2 * total * 3 * count * width,
    )
    back_sum = jnp.concatenate([back_sum[:half] + low_sum.astype(F32), back_sum[half:]], axis=0)
    ahead_sum = jnp.concatenate([ahead_sum[:half], ahead_sum[half:] + high_sum.astype(F32)], axis=0)
    back_sum, ahead_sum = shifted(back_sum.astype(BF16), Y, -1), shifted(ahead_sum.astype(BF16), Y, 1)
    grad_passages = here + back_sum.astype(F32) + ahead_sum.astype(F32)

    at = (across * depth + far) * rows
    row_losses = lax.dynamic_slice_in_dim(losses[0], at, rows, 0)
    return row_losses, grad_queries, grad_passages


def solution(mesh):
    torus = Mesh(mesh.devices.reshape(mesh.shape[Y], 8, 4, 2), ROW_COL)
    in_specs = (P(ROW_COL, None), P(COL_ROW, None), P(Y), P(Y, None), P(Y))
    out_specs = (P(ROW_COL), P(ROW_COL, None), P(COL_ROW, None))
    return jax.shard_map(
        on_device, mesh=torus, in_specs=in_specs, out_specs=out_specs, check_vma=False
    )
```

time: 202 us -> 238 us (1.18)
  blocking collectives: 31.1 us -> 56 us
  Pallas kernels: 0 us -> 22.4 us
  matrix products: 14.6 us -> 0 us
  waiting for transfers between devices: 88.5 us -> 93.4 us
  starting transfers between devices: 26.6 us -> 22 us
  other arithmetic: 7.97 us -> 10.6 us
    all_to_all x3 -> x1, waiting for transfers between devices: 84.2 us -> 9.27 us  [copies(): lax.all_to_all(jnp.broadcast_to(value, (n, *value.shape)), axis, 0, 0, ti...]
    unnamed x2 -> x3, waiting for transfers between devices: 0.7 us -> 46.9 us
    ppermute x0 -> x10, waiting for transfers between devices: none -> 37.3 us  [shifted(): return lax.ppermute(value, axis, [(i, (i + step) % n) for i in range(n)])]
    all_to_all x3, blocking collectives: 31.1 us -> 56 us  [the longest x2 36.8 us: on_device(): table = lax.all_to_all(table, COL, 0, 0, tiled=True)]
    all_to_all x3 -> x1, starting transfers between devices: 26.5 us -> 4.01 us  [copies(): lax.all_to_all(jnp.broadcast_to(value, (n, *value.shape)), axis, 0, 0, ti...]
    pallas_call x0 -> x8, Pallas kernels: none -> 22.4 us  [call(): pl.pallas_call(body, out_shape=outs, in_specs=[pl.BlockSpec(memory_space=...]
    ppermute x0 -> x10, starting transfers between devices: none -> 17.9 us  [shifted(): return lax.ppermute(value, axis, [(i, (i + step) % n) for i in range(n)])]
    dot_general x3 -> x0, matrix products: 14.6 us -> none  [the longest x1 5.67 us: on_device(): jnp.dot(grad_scores, passage_block, preferred_element_type=jnp.float32)]
  transfers between devices with their start and end apart: 5 -> 13, of which waited for: 4 -> 9; matrix products, arithmetic and copies ran while one was open for 14% -> 9% of each run, Pallas kernels for 0% -> 4%
where the time goes in v1:
time: 238 us; the launch traced here: 234 us
  waiting for transfers between devices  93.4 us (39%)
  blocking collectives  56 us (24%)
  Pallas kernels  22.4 us (9%)
  starting transfers between devices  22 us (9%)
  between operations  14.9 us (6%)
  local copies, waits for them, and re-layouts  14.5 us (6%)
  other arithmetic  10.6 us (4%)
    unnamed x3, waiting for transfers between devices  46.9 us
    ppermute x10, waiting for transfers between devices, shifted(): return lax.ppermute(value, axis, [(i, (i + step) % n) for i in range(n)])  37.3 us
    all_to_all x2, blocking collectives, on_device(): table = lax.all_to_all(table, COL, 0, 0, tiled=True)  36.8 us
    pallas_call x8, Pallas kernels, call(): pl.pallas_call(body, out_shape=outs, in_specs=[pl.BlockSpec(memory_space=...  22.4 us
    all_to_all x1, blocking collectives, copies(): lax.all_to_all(jnp.broadcast_to(value, (n, *value.shape)), axis, 0, 0, ti...  19.2 us
    ppermute x10, starting transfers between devices, shifted(): return lax.ppermute(value, axis, [(i, (i + step) % n) for i in range(n)])  17.9 us
    all_to_all x1, waiting for transfers between devices, copies(): lax.all_to_all(jnp.broadcast_to(value, (n, *value.shape)), axis, 0, 0, ti...  9.27 us
  transfers between devices with their start and end apart: 13, of which 9 were waited for; matrix products, arithmetic and copies ran while one was open for 9% of the time, Pallas kernels for 4%

profile of v1, /device:TPU:1, one launch (start us, length us, event | category | flops | bytes accessed | tf_op | source)
XLA Modules:
  0.0 233.8 jit_solution(971097913656212462)
XLA Ops:
  8.0 19.2 %all_to_all.20 = bf16[8,4,4096]{2,1,0:T(4,128)(2,1)S(1)} all-to-all(bf16[8,4,4096]{2,1,0:T(4,128)(2,1)S(1)} %broadcast_in_dim.6), channel_id=1, replica_groups=mesh['row'=4,'col_0'=8,'col_1'=4,'col_2'=2] {'col_0'}, dimensions={0} | all-to-all | bytes 524288 | tf_op jit(solution)/shard_map/all_to_all | solution.py:30
  27.3 1.1 broadcast_in_dim.7
  28.3 4.0 %all-to-all-start.1 = ((bf16[4,32,4096]{2,1,0:T(8,128)(2,1)}), bf16[4,32,4096]{2,1,0:T(8,128)(2,1)S(1)}, u32[]{:S(2)}, u32[]{:S(2)}) async-start(bf16[4,32,4096]{2,1,0:T(8,128)(2,1)} %broadcast_in_dim.7), calls=%async_computation.1 | async-start | bytes 2097152 | tf_op jit(solution)/shard_map/all_to_all | solution.py:30
  32.4 1.3 collective-permute-start.1
  33.7 1.5 collective-permute-start.2
  35.2 9.3 %all-to-all-done.1 = bf16[4,32,4096]{2,1,0:T(8,128)(2,1)S(1)} async-done(((bf16[4,32,4096]{2,1,0:T(8,128)(2,1)}), bf16[4,32,4096]{2,1,0:T(8,128)(2,1)S(1)}, u32[]{:S(2)}, u32[]{:S(2)}) %all-to-all-start.1) | async-done | bytes 1048608 | tf_op jit(solution)/shard_map/all_to_all | solution.py:30
  44.4 4.0 %collective-permute-start = (bf16[128,4096]{1,0:T(8,128)(2,1)S(1)}, bf16[128,4096]{1,0:T(8,128)(2,1)S(1)}, u32[]{:S(2)}, u32[]{:S(2)}) collective-permute-start(bf16[128,4096]{1,0:T(8,128)(2,1)S(1)} %bitcast.13), channel_id=1, source_target_pairs={{0,1},{1,0},{2,3},{3,2},{4,5},{5,4},{6,7},{7,6},{8,9},{9,8},{10,11... | collective-permute-start | bytes 3145736 | tf_op jit(solution)/shard_map/ppermute | solution.py:25
  49.4 1.2 copy.12
  52.4 3.4 %collective-permute-done.1.refs_3_.back = bf16[128,4096]{1,0:T(8,128)(2,1)S(1)} collective-permute-done((bf16[128,4096]{1,0:T(8,128)(2,1)}, bf16[128,4096]{1,0:T(8,128)(2,1)S(1)}, u32[]{:S(2)}, u32[]{:S(2)}) %collective-permute-start.1) | collective-permute-done | bytes 1048608 | tf_op jit(solution)/shard_map/ppermute | solution.py:25
  56.7 1.9 slice.31
  58.6 2.6 %collective-permute-start.4 = (bf16[64,4096]{1,0:T(8,128)(2,1)}, bf16[64,4096]{1,0:T(8,128)(2,1)}, u32[]{:S(2)}, u32[]{:S(2)}) collective-permute-start(bf16[64,4096]{1,0:T(8,128)(2,1)} %slice.31), channel_id=1, source_target_pairs={{0,192},{64,0},{128,64},{192,128},{1,193},{65,1},{129,65},{193,129... | collective-permute-start | bytes 1572872 | tf_op jit(solution)/shard_map/ppermute | solution.py:25
  62.0 4.6 %shard_map.85.first = f32[256,384]{1,0:T(8,128)S(1)} custom-call(bf16[128,4096]{1,0:T(8,128)(2,1)S(1)} %bitcast.14, bf16[128,4096]{1,0:T(8,128)(2,1)S(1)} %collective-permute-done.refs_1_.other, bf16[128,4096]{1,0:T(8,128)(2,1)} %here.1, bf16[128,4096]{1,0:T(8,128)(2,1)S(1)} %collective-permute-done.1.refs_3_.back, ...), custom_call_target="tpu_custom_call" | custom-call | flops 805306368 | bytes 5636096 | tf_op jit(solution)/shard_map/pallas_call | solution.py:40
  66.6 1.3 collective-permute-done.3.refs_2_.low
  68.9 3.1 %shard_map.86.last = f32[256,128]{1,0:T(8,128)S(1)} custom-call(bf16[128,4096]{1,0:T(8,128)(2,1)S(1)} %bitcast.15, bf16[128,4096]{1,0:T(8,128)(2,1)S(1)} %collective-permute-done.refs_1_.other, bf16[64,4096]{1,0:T(8,128)(2,1)} %collective-permute-done.3.refs_2_.low, bf16[64,4096]{1,0:T(8,128)(2,1)} %collective-permute-done.4.refs_3_.high), custom_call_target="tpu_custom_call" | custom-call | flops 268435456 | bytes 3276800 | tf_op jit(solution)/shard_map/pallas_call | solution.py:40
  72.2 22.9 %all_to_all.21.table = f32[64,4,128]{2,1,0:T(4,128)S(1)} all-to-all(f32[64,4,128]{2,1,0:T(4,128)S(1)} %shard_map.88), channel_id=1, replica_groups=mesh['row'=4,'col_0'=8,'col_1'=4,'col_2'=2] {'col_0','col_1','col_2'}, dimensions={0} | all-to-all | bytes 262144 | tf_op jit(solution)/shard_map/all_to_all | solution.py:234
  95.8 13.9 %all_to_all.22.table = f32[64,2,128]{2,1,0:T(2,128)S(1)} all-to-all(f32[64,2,128]{2,1,0:T(2,128)S(1)} %get-tuple-element.15), channel_id=1, replica_groups=mesh['row'=4,'col_0'=8,'col_1'=4,'col_2'=2] {'col_0','col_1','col_2'}, dimensions={0} | all-to-all | bytes 131072 | tf_op jit(solution)/shard_map/all_to_all | solution.py:241
  109.7 2.6 %shard_map.90 = (bf16[256,512]{1,0:T(8,128)(2,1)S(1)}, f32[8,128]{1,0:T(8,128)S(1)}, bf16[64,4096]{1,0:T(8,128)(2,1)S(1)}, bf16[64,4096]{1,0:T(8,128)(2,1)}) custom-call(s32[1]{0:T(128)} %bitcast.core_ref, f32[64,2,128]{2,1,0:T(2,128)S(1)} %all_to_all.22.table, f32[8,128]{1,0:T(8,128)S(1)} %get-tuple-element.16.stats, f32[256,512]{1,0:T(8,128)S(1)} %shard_map.87.code, ...), custom_call_target="tpu_custom_call" | custom-call | flops 268435456 | bytes 4530180 | tf_op jit(solution)/shard_map/pallas_call | solution.py:40
  113.1 6.3 %shard_map.91 = (f32[128,4096]{1,0:T(8,128)}, f32[128,4096]{1,0:T(8,128)}) custom-call(bf16[256,512]{1,0:T(8,128)(2,1)S(1)} %get-tuple-element.19.grads, bf16[128,4096]{1,0:T(8,128)(2,1)} %here.1, bf16[128,4096]{1,0:T(8,128)(2,1)S(1)} %collective-permute-done.1.refs_3_.back, bf16[128,4096]{1,0:T(8,128)(2,1)} %collective-permute-done.2.refs_4_.ahead, ...), custom_call_target="tpu_custom_call" | custom-call | flops 1073741824 | bytes 8650752 | tf_op jit(solution)/shard_map/pallas_call | solution.py:40
  120.6 3.1 %collective-permute-done.5 = f32[128,4096]{1,0:T(8,128)S(1)} collective-permute-done((f32[128,4096]{1,0:T(8,128)}, f32[128,4096]{1,0:T(8,128)S(1)}, u32[]{:S(2)}, u32[]{:S(2)}) %collective-permute-start.5) | collective-permute-done | bytes 2097184 | tf_op jit(solution)/shard_map/ppermute | solution.py:25
  123.8 3.2 %add.73 = f32[128,4096]{1,0:T(8,128)} add(f32[128,4096]{1,0:T(8,128)} %get-tuple-element.20, f32[128,4096]{1,0:T(8,128)S(1)} %collective-permute-done.5) | non-fusion elementwise | flops 524288 | bytes 6291456 | tf_op jit(solution)/shard_map/add | solution.py:257
  127.0 4.2 %shard_map.92 = (f32[128,4096]{1,0:T(8,128)S(1)}, f32[128,4096]{1,0:T(8,128)}, f32[128,4096]{1,0:T(8,128)}) custom-call(bf16[256,512]{1,0:T(8,128)(2,1)S(1)} %get-tuple-element.19.grads, bf16[128,4096]{1,0:T(8,128)(2,1)S(1)} %bitcast.17, bf16[128,4096]{1,0:T(8,128)(2,1)S(1)} %collective-permute-done.refs_1_.other), custom_call_target="tpu_custom_call" | custom-call | flops 805306368 | bytes 8650752 | tf_op jit(solution)/shard_map/pallas_call | solution.py:40
  131.2 2.1 slice.38
  133.3 1.3 slice.39
  134.7 3.7 %collective-permute-start.6 = (bf16[64,4096]{1,0:T(8,128)(2,1)S(1)}, bf16[64,4096]{1,0:T(8,128)(2,1)S(1)}, u32[]{:S(2)}, u32[]{:S(2)}) collective-permute-start(bf16[64,4096]{1,0:T(8,128)(2,1)S(1)} %copy-done.3), channel_id=1, source_target_pairs={{0,192},{64,0},{128,64},{192,128},{1,193},{65,1},{129,65},{193,129... | collective-permute-start | bytes 1572872 | tf_op jit(solution)/shard_map/ppermute | solution.py:25
  138.4 1.1 add_convert_fusion
  140.6 8.7 %collective-permute-done.6 = bf16[64,4096]{1,0:T(8,128)(2,1)S(1)} collective-permute-done((bf16[64,4096]{1,0:T(8,128)(2,1)S(1)}, bf16[64,4096]{1,0:T(8,128)(2,1)S(1)}, u32[]{:S(2)}, u32[]{:S(2)}) %collective-permute-start.6) | collective-permute-done | bytes 524320 | tf_op jit(solution)/shard_map/ppermute | solution.py:25
  150.5 3.5 %collective-permute-start.7 = (bf16[128,4096]{1,0:T(8,128)(2,1)}, bf16[128,4096]{1,0:T(8,128)(2,1)S(1)}, u32[]{:S(2)}, u32[]{:S(2)}) collective-permute-start(bf16[128,4096]{1,0:T(8,128)(2,1)} %pad_maximum_fusion), channel_id=1, source_target_pairs={{0,192},{64,0},{128,64},{192,128},{1,193},{65,1},{129,65},{193,129... | collective-permute-start | bytes 3145736 | tf_op jit(solution)/shard_map/ppermute | solution.py:25
  155.9 10.3 %collective-permute-done.9 = bf16[128,4096]{1,0:T(8,128)(2,1)} collective-permute-done((bf16[128,4096]{1,0:T(8,128)(2,1)}, bf16[128,4096]{1,0:T(8,128)(2,1)}, u32[]{:S(2)}, u32[]{:S(2)}) %collective-permute-start.9) | collective-permute-done | bytes 1048608 | tf_op jit(solution)/shard_map/ppermute | solution.py:25
  166.2 9.5 %collective-permute-done.7 = bf16[128,4096]{1,0:T(8,128)(2,1)S(1)} collective-permute-done((bf16[128,4096]{1,0:T(8,128)(2,1)}, bf16[128,4096]{1,0:T(8,128)(2,1)S(1)}, u32[]{:S(2)}, u32[]{:S(2)}) %collective-permute-start.7) | collective-permute-done | bytes 1048608 | tf_op jit(solution)/shard_map/ppermute | solution.py:25
  175.7 2.9 %convert_add_fusion = f32[128,4096]{1,0:T(8,128)} fusion(bf16[128,4096]{1,0:T(8,128)(2,1)} %collective-permute-done.9, f32[128,4096]{1,0:T(8,128)S(1)} %copy-done.1, bf16[128,4096]{1,0:T(8,128)(2,1)S(1)} %collective-permute-done.7), kind=kLoop, calls=%fused_computation | loop fusion | flops 2097152 | bytes 6291456 | tf_op jit(solution)/shard_map/add | solution.py:270
  178.5 46.9 %all-reduce.4.cloned.1.call-done = f32[32,4096]{1,0:T(8,128)} async-done(((f32[32,4096]{1,0:T(8,128)}), f32[32,4096]{1,0:T(8,128)}) %all-reduce.4.cloned.1.call-update) | async-done | bytes 524304
  225.4 1.5 constant_dynamic-slice_fusion
  (61 shorter events, 12.6 us)
Async XLA Ops:
  27.2 21.2 %copy-start.7 = (f32[256]{0:T(256)S(1)}, f32[256]{0:T(256)}, u32[]{:S(2)}) copy-start(f32[256]{0:T(256)} %param.10) | copy-start | bytes 3076
  27.2 21.8 %copy-start.6 = (s32[256,7]{0,1:T(8,128)S(1)}, s32[256,7]{0,1:T(8,128)}, u32[]{:S(2)}) copy-start(s32[256,7]{0,1:T(8,128)} %param.9) | copy-start | bytes 21508
  27.3 23.4 %copy-start.8 = (s32[256]{0:T(256)S(1)}, s32[256]{0:T(256)}, u32[]{:S(2)}) copy-start(s32[256]{0:T(256)} %param.8) | copy-start | bytes 3076
  28.3 16.1 %all-to-all-start.1 = ((bf16[4,32,4096]{2,1,0:T(8,128)(2,1)}), bf16[4,32,4096]{2,1,0:T(8,128)(2,1)S(1)}, u32[]{:S(2)}, u32[]{:S(2)}) async-start(bf16[4,32,4096]{2,1,0:T(8,128)(2,1)} %broadcast_in_dim.7), calls=%async_computation.1 | async-start | bytes 2097152 | tf_op jit(solution)/shard_map/all_to_all | solution.py:30
  32.4 123.5 %reduce-scatter.2.cloned.1.call-start = ((), (), s32[]{:S(2)}) async-start(), calls=%async_computation.5 | async-start | bytes 2621440 | tf_op jit(solution)/shard_map/reduce_scatter | solution.py:258
  32.4 23.5 %collective-permute-start.1 = (bf16[128,4096]{1,0:T(8,128)(2,1)}, bf16[128,4096]{1,0:T(8,128)(2,1)S(1)}, u32[]{:S(2)}, u32[]{:S(2)}) collective-permute-start(bf16[128,4096]{1,0:T(8,128)(2,1)} %here.1), channel_id=1, source_target_pairs={{0,64},{64,128},{128,192},{192,0},{1,65},{65,129},{129,193},{193,1... | collective-permute-start | bytes 3145736 | tf_op jit(solution)/shard_map/ppermute | solution.py:25
  33.7 23.1 %collective-permute-start.2 = (bf16[128,4096]{1,0:T(8,128)(2,1)}, bf16[128,4096]{1,0:T(8,128)(2,1)}, u32[]{:S(2)}, u32[]{:S(2)}) collective-permute-start(bf16[128,4096]{1,0:T(8,128)(2,1)} %here.1), channel_id=1, source_target_pairs={{0,192},{64,0},{128,64},{192,128},{1,193},{65,1},{129,65},{193,129... | collective-permute-start | bytes 3145736 | tf_op jit(solution)/shard_map/ppermute | solution.py:25
  44.4 17.5 %collective-permute-start = (bf16[128,4096]{1,0:T(8,128)(2,1)S(1)}, bf16[128,4096]{1,0:T(8,128)(2,1)S(1)}, u32[]{:S(2)}, u32[]{:S(2)}) collective-permute-start(bf16[128,4096]{1,0:T(8,128)(2,1)S(1)} %bitcast.13), channel_id=1, source_target_pairs={{0,1},{1,0},{2,3},{3,2},{4,5},{5,4},{6,7},{7,6},{8,9},{9,8},{10,11... | collective-permute-start | bytes 3145736 | tf_op jit(solution)/shard_map/ppermute | solution.py:25
  49.0 12.2 %copy-start.9 = (s32[4]{0:T(128)S(1)}, s32[4]{0:T(128)}, u32[]{:S(2)}) copy-start(s32[4]{0:T(128)} %constant.49) | copy-start | bytes 52
  56.6 11.3 %collective-permute-start.3 = (bf16[64,4096]{1,0:T(8,128)(2,1)}, bf16[64,4096]{1,0:T(8,128)(2,1)}, u32[]{:S(2)}, u32[]{:S(2)}) collective-permute-start(bf16[64,4096]{1,0:T(8,128)(2,1)} %slice.30), channel_id=1, source_target_pairs={{0,64},{64,128},{128,192},{192,0},{1,65},{65,129},{129,193},{193,1... | collective-permute-start | bytes 1572872 | tf_op jit(solution)/shard_map/ppermute | solution.py:25
  58.6 10.3 %collective-permute-start.4 = (bf16[64,4096]{1,0:T(8,128)(2,1)}, bf16[64,4096]{1,0:T(8,128)(2,1)}, u32[]{:S(2)}, u32[]{:S(2)}) collective-permute-start(bf16[64,4096]{1,0:T(8,128)(2,1)} %slice.31), channel_id=1, source_target_pairs={{0,192},{64,0},{128,64},{192,128},{1,193},{65,1},{129,65},{193,129... | collective-permute-start | bytes 1572872 | tf_op jit(solution)/shard_map/ppermute | solution.py:25
  112.3 0.8 copy-start.2
  119.3 4.4 %collective-permute-start.5 = (f32[128,4096]{1,0:T(8,128)}, f32[128,4096]{1,0:T(8,128)S(1)}, u32[]{:S(2)}, u32[]{:S(2)}) collective-permute-start(f32[128,4096]{1,0:T(8,128)} %get-tuple-element.21), channel_id=1, source_target_pairs={{0,1},{1,0},{2,3},{3,2},{4,5},{5,4},{6,7},{7,6},{8,9},{9,8},{10,11... | collective-permute-start | bytes 6291464 | tf_op jit(solution)/shard_map/ppermute | solution.py:25
  119.8 18.6 %collective-permute-start.8 = (bf16[64,4096]{1,0:T(8,128)(2,1)}, bf16[64,4096]{1,0:T(8,128)(2,1)}, u32[]{:S(2)}, u32[]{:S(2)}) collective-permute-start(bf16[64,4096]{1,0:T(8,128)(2,1)} %get-tuple-element.26), channel_id=1, source_target_pairs={{0,64},{64,128},{128,192},{192,0},{1,65},{65,129},{129,193},{193,1... | collective-permute-start | bytes 1572872 | tf_op jit(solution)/shard_map/ppermute | solution.py:25
  127.0 7.7 %copy-start.3 = (bf16[64,4096]{1,0:T(8,128)(2,1)S(1)}, bf16[64,4096]{1,0:T(8,128)(2,1)}, u32[]{:S(2)}) copy-start(bf16[64,4096]{1,0:T(8,128)(2,1)} %copy-done.2) | copy-start | bytes 1572868
  127.0 98.4 %all-reduce.4.cloned.1.call-start = ((), (), s32[]{:S(2)}) async-start(), calls=%async_computation.6 | async-start | bytes 1048576
  131.2 8.3 %copy-start = (f32[128,4096]{1,0:T(8,128)}, f32[128,4096]{1,0:T(8,128)S(1)}, u32[]{:S(2)}) copy-start(f32[128,4096]{1,0:T(8,128)S(1)} %get-tuple-element.22) | copy-start | bytes 6291460
  131.2 7.2 %copy-start.5 = (f32[128,4096]{1,0:T(8,128)S(1)}, f32[128,4096]{1,0:T(8,128)}, u32[]{:S(2)}) copy-start(f32[128,4096]{1,0:T(8,128)} %get-tuple-element.25) | copy-start | bytes 6291460
  134.7 14.6 %copy-start.4 = (f32[128,4096]{1,0:T(8,128)S(1)}, f32[128,4096]{1,0:T(8,128)}, u32[]{:S(2)}) copy-start(f32[128,4096]{1,0:T(8,128)} %get-tuple-element.23) | copy-start | bytes 6291460
  134.7 14.6 %collective-permute-start.6 = (bf16[64,4096]{1,0:T(8,128)(2,1)S(1)}, bf16[64,4096]{1,0:T(8,128)(2,1)S(1)}, u32[]{:S(2)}, u32[]{:S(2)}) collective-permute-start(bf16[64,4096]{1,0:T(8,128)(2,1)S(1)} %copy-done.3), channel_id=1, source_target_pairs={{0,192},{64,0},{128,64},{192,128},{1,193},{65,1},{129,65},{193,129... | collective-permute-start | bytes 1572872 | tf_op jit(solution)/shard_map/ppermute | solution.py:25
  140.6 13.4 %copy-start.10 = (u32[256]{0:T(256)S(1)}, u32[256]{0:T(256)}, u32[]{:S(2)}) copy-start(u32[256]{0:T(256)} %constant.52) | copy-start | bytes 3076
  140.6 35.0 %copy-start.1 = (f32[128,4096]{1,0:T(8,128)S(1)}, f32[128,4096]{1,0:T(8,128)}, u32[]{:S(2)}) copy-start(f32[128,4096]{1,0:T(8,128)} %copy-done) | copy-start | bytes 6291460
  140.6 25.6 %collective-permute-start.9 = (bf16[128,4096]{1,0:T(8,128)(2,1)}, bf16[128,4096]{1,0:T(8,128)(2,1)}, u32[]{:S(2)}, u32[]{:S(2)}) collective-permute-start(bf16[128,4096]{1,0:T(8,128)(2,1)} %pad_maximum_fusion.1), channel_id=1, source_target_pairs={{0,64},{64,128},{128,192},{192,0},{1,65},{65,129},{129,193},{193,1... | collective-permute-start | bytes 3145736 | tf_op jit(solution)/shard_map/ppermute | solution.py:25
  150.5 25.2 %collective-permute-start.7 = (bf16[128,4096]{1,0:T(8,128)(2,1)}, bf16[128,4096]{1,0:T(8,128)(2,1)S(1)}, u32[]{:S(2)}, u32[]{:S(2)}) collective-permute-start(bf16[128,4096]{1,0:T(8,128)(2,1)} %pad_maximum_fusion), channel_id=1, source_target_pairs={{0,192},{64,0},{128,64},{192,128},{1,193},{65,1},{129,65},{193,129... | collective-permute-start | bytes 3145736 | tf_op jit(solution)/shard_map/ppermute | solution.py:25
Sparse Core Ops, SparseCore 0:
  127.1 27.1 reduce-scatter.1
  156.7 68.6 all-reduce.3

commit v2 on v1

v2 whole, which is shorter than its diff:
```python
import functools

import jax
import jax.numpy as jnp
from jax import lax
from jax.experimental import pallas as pl
from jax.experimental.pallas import tpu as pltpu
from jax.sharding import Mesh
from jax.sharding import PartitionSpec as P

Y, Z, X, CORE = "row", "col_0", "col_1", "col_2"
COL = (Z, X, CORE)
ROW_COL = (Y, Z, X, CORE)
COL_ROW = (Z, X, CORE, Y)

inv_temp = 50.0
sharpness = 4.0
LOWEST = -3.0e38
F32, BF16 = jnp.float32, jnp.bfloat16
TILE = 512


def shifted(value, axis, step):
    n = lax.axis_size(axis)
    return lax.ppermute(value, axis, [(i, (i + step) % n) for i in range(n)])


def copies(value, axis):
    n = lax.axis_size(axis)
    return lax.all_to_all(jnp.broadcast_to(value, (n, *value.shape)), axis, 0, 0, tiled=True)


def shape(dims, dtype):
    return jax.ShapeDtypeStruct(dims, dtype)


def call(body, outs, args, flops=0, scalars=0, tiled=(), scratch=()):
    size = sum(a.size * a.dtype.itemsize for a in (*args, *outs))
    specs = []
    for k, a in enumerate((*args, *outs)):
        if k < scalars:
            specs.append(pl.BlockSpec(memory_space=pltpu.SMEM))
        elif k in tiled:
            specs.append(pl.BlockSpec((a.shape[0], TILE), lambda i: (0, i)))
        else:
            specs.append(pl.BlockSpec(a.shape, lambda i, n=len(a.shape): (0,) * n))
    steps = (*args, *outs)[tiled[0]].shape[1] // TILE if tiled else 1
    return pl.pallas_call(
        body,
        grid=(steps,),
        out_shape=outs,
        in_specs=specs[: len(args)],
        out_specs=specs[len(args) :],
        scratch_shapes=scratch,
        cost_estimate=pl.CostEstimate(flops=flops, bytes_accessed=size, transcendentals=0),
        compiler_params=pltpu.CompilerParams(vmem_limit_bytes=24 << 20),
    )(*args)


def swapped(core, row):
    half = row.shape[1] // 2
    return jnp.where(core == 0, row, jnp.concatenate([row[:, half:], row[:, :half]], axis=1))


def on_step(k):
    return pl.when(pl.program_id(0) == k)


def products(own, other, pool, scores):
    @on_step(0)
    def _():
        scores[...] = jnp.zeros_like(scores)

    rows = jnp.concatenate([p[...] for p in pool], axis=0)
    columns = jnp.concatenate([own[...], other[...]], axis=0)
    scores[...] += lax.dot_general(
        rows, columns, (((1,), (1,)), ((), ())), preferred_element_type=F32
    )


def score_body(own, other, here, back, ahead, scores):
    products(own, other, (here, back, ahead), scores)


def stat_body(place, own, other, low, high, first, ids, last, code, table):
    products(own, other, (low, high), last)

    @pl.when(pl.program_id(0) == pl.num_programs(0) - 1)
    def _():
        positive, kept = [], []
        for k in range(4):
            rows = slice(128 * k, 128 * k + 128)
            block = (last[...] if k == 3 else first[rows, :]) * inv_temp
            column = place[1 + k] + lax.broadcasted_iota(jnp.int32, block.shape, 0)
            is_positive = column == ids[0:1, :]
            is_kept = is_positive
            for slot in range(1, 8):
                is_kept = is_kept | (column == ids[slot : slot + 1, :])
            code[rows, :] = jnp.where(is_positive, 2.0, jnp.where(is_kept, 1.0, 0.0))
            positive.append(jnp.max(jnp.where(is_positive, block, LOWEST), axis=0, keepdims=True))
            kept.append(jnp.max(jnp.where(is_kept, block, LOWEST), axis=0, keepdims=True))
        lines = [swapped(place[0], functools.reduce(jnp.maximum, v)) for v in (positive, kept)]
        table[...] = jnp.broadcast_to(jnp.concatenate(lines, axis=0)[None], table.shape)


def soft_body(place, table, margin_ref, code, first, last, weights, totals, stats):
    merged = swapped(place[0], jnp.max(table[...], axis=0))
    picked, kept = merged[0:1], merged[1:2]
    margin = margin_ref[0:1, :]
    ceiling = jnp.maximum(kept, picked + margin)
    sums = []
    for k in range(4):
        rows = slice(128 * k, 128 * k + 128)
        block = (last[...] if k == 3 else first[rows, :]) * inv_temp
        over = sharpness * (block - picked - margin)
        penalty = jnp.maximum(over, 0.0) + jnp.log(1.0 + jnp.exp(-jnp.abs(over)))
        logits = jnp.where(code[rows, :] > 0.0, block, block - penalty)
        weight = jnp.exp(logits - ceiling)
        weights[rows, :] = weight
        sums.append(jnp.sum(weight, axis=0, keepdims=True))
    total = swapped(place[0], functools.reduce(jnp.add, sums))
    totals[...] = jnp.broadcast_to(total[None], totals.shape)
    stats[...] = jnp.broadcast_to(ceiling - picked, stats.shape)


def grad_body(place, table, stats, code, weights, own, other, grads, losses, low, high):
    @on_step(0)
    def _():
        total = swapped(place[0], jnp.sum(table[...], axis=0))
        losses[...] = stats[...] + jnp.log(total)
        for k in range(4):
            rows = slice(128 * k, 128 * k + 128)
            positive = jnp.where(code[rows, :] == 2.0, 1.0, 0.0)
            grads[rows, :] = ((weights[rows, :] / total - positive) * inv_temp).astype(BF16)

    columns = jnp.concatenate([own[...], other[...]], axis=0)
    out = jnp.dot(grads[384:512, :], columns, preferred_element_type=F32).astype(BF16)
    low[...] = out[:64]
    high[...] = out[64:]


def passage_body(grads, own, other, low, high, here, back, ahead):
    columns = jnp.concatenate([own[...], other[...]], axis=0)
    out = jnp.dot(grads[0:384, :], columns, preferred_element_type=F32)
    here[...] = out[0:128]
    back[0:64, :] = (out[128:192] + low[...].astype(F32)).astype(BF16)
    back[64:128, :] = out[192:256].astype(BF16)
    ahead[0:64, :] = out[256:320].astype(BF16)
    ahead[64:128, :] = (out[320:384] + high[...].astype(F32)).astype(BF16)


def query_body(grads, here, back, ahead, low, high, own, other, turned):
    @on_step(0)
    def _():
        turned[...] = grads[...].T

    rows = jnp.concatenate([p[...] for p in (here, back, ahead, low, high)], axis=0)
    out = jnp.dot(turned[...], rows, preferred_element_type=F32)
    own[...] = out[:128]
    other[...] = out[128:]


def join_body(own, arrived, exact, sent):
    total = own[...] + arrived[...]
    exact[...] = total
    sent[...] = total.astype(BF16)


def spread_sum(sent, exact, axis):
    n = lax.axis_size(axis)
    mine = lax.axis_index(axis)
    parts = lax.all_to_all(sent.reshape(n, -1, sent.shape[-1]), axis, 0, 0, tiled=True)
    rest = jnp.where((lax.iota(jnp.int32, n) == mine)[:, None, None], 0.0, parts.astype(F32))
    own = lax.dynamic_index_in_dim(exact.reshape(parts.shape), mine, 0, keepdims=False)
    return jnp.sum(rest, axis=0) + own


def on_device(queries, passages, positives, hard_negatives, thresholds):
    rows, width = queries.shape
    count = passages.shape[0]
    depth, breadth, ring = lax.axis_size(Z), lax.axis_size(X), lax.axis_size(Y)
    core, far, across, along = (lax.axis_index(a) for a in (CORE, Z, X, Y))
    half = count // 2

    back, ahead = shifted(passages, Y, 1), shifted(passages, Y, -1)
    line = copies(queries, Z)
    line, back, ahead = lax.optimization_barrier((line, back, ahead))
    low, high = shifted(back[:half], Y, 1), shifted(ahead[half:], Y, -1)
    own = copies(line.reshape(depth * rows, width), X)
    own, low, high = lax.optimization_barrier((own, low, high))
    own = own.reshape(-1, width)
    other = shifted(own, CORE, 1)
    plane = own.shape[0]
    total, pool = 2 * plane, ring * count

    def ordered(table):
        table = table.reshape(-1, depth, breadth, 2, rows)
        table = jnp.transpose(table, (0, 3, 2, 1, 4)).reshape(-1, 2, plane)
        return jnp.where(core == 0, table, jnp.flip(table, 1)).reshape(-1, total)

    ids = ordered(jnp.concatenate([positives[None, :], hard_negatives.T], axis=0))
    margin = ordered(jnp.broadcast_to(thresholds, (8, total)))
    steps = jnp.array([0, 1, 3, 2], jnp.int32)
    base = (((far * breadth + across) * 2 + core) * ring + (along - steps) % ring) * count
    place = jnp.concatenate([core.reshape(1), base]).astype(jnp.int32)

    members = depth * breadth * 2
    first = call(
        score_body,
        [shape((3 * count, total), F32)],
        [own, other, passages, back, ahead],
        flops=2 * total * 3 * count * width,
        tiled=(0, 1, 2, 3, 4),
    )[0]
    last, code, table = call(
        stat_body,
        [shape((count, total), F32), shape((pool, total), F32), shape((members, 2, total), F32)],
        [place, own, other, low, high, first, ids],
        flops=2 * total * count * width,
        scalars=1,
        tiled=(1, 2, 3, 4),
    )
    table = lax.all_to_all(table, COL, 0, 0, tiled=True)
    weights, table, stats = call(
        soft_body,
        [shape((pool, total), F32), shape((members, 1, total), F32), shape((8, total), F32)],
        [place, table, margin, code, first, last],
        scalars=1,
    )
    table = lax.all_to_all(table, COL, 0, 0, tiled=True)
    grads, losses, low_sum, high_sum = call(
        grad_body,
        [shape((pool, total), BF16), shape((8, total), F32)] + [shape((half, width), BF16)] * 2,
        [place, table, stats, code, weights, own, other],
        flops=2 * total * count * width,
        scalars=1,
        tiled=(5, 6, 9, 10),
    )
    low_sum, high_sum = shifted(low_sum, Y, -1), shifted(high_sum, Y, 1)

    own_sum, other_sum = call(
        query_body,
        [shape((plane, width), F32)] * 2,
        [grads, passages, back, ahead, low, high],
        flops=2 * total * pool * width,
        tiled=(1, 2, 3, 4, 5, 6, 7),
        scratch=[pltpu.VMEM((total, pool), BF16)],
    )
    exact, sent = call(
        join_body,
        [shape((plane, width), F32), shape((plane, width), BF16)],
        [own_sum, shifted(other_sum, CORE, 1)],
        tiled=(0, 1, 2, 3),
    )
    exact = spread_sum(sent, exact, X)
    grad_queries = spread_sum(exact.astype(BF16), exact, Z)

    here, back_sum, ahead_sum = call(
        passage_body,
        [shape((count, width), F32)] + [shape((count, width), BF16)] * 2,
        [grads, own, other, low_sum, high_sum],
        flops=2 * total * 3 * count * width,
        tiled=(1, 2, 3, 4, 5, 6, 7),
    )
    back_sum, ahead_sum = shifted(back_sum, Y, -1), shifted(ahead_sum, Y, 1)
    grad_passages = here + back_sum.astype(F32) + ahead_sum.astype(F32)

    at = (across * depth + far) * rows
    row_losses = lax.dynamic_slice_in_dim(losses[0], at, rows, 0)
    return row_losses, grad_queries, grad_passages


def solution(mesh):
    torus = Mesh(mesh.devices.reshape(mesh.shape[Y], 8, 4, 2), ROW_COL)
    in_specs = (P(ROW_COL, None), P(COL_ROW, None), P(Y), P(Y, None), P(Y))
    out_specs = (P(ROW_COL), P(ROW_COL, None), P(COL_ROW, None))
    return jax.shard_map(
        on_device, mesh=torus, in_specs=in_specs, out_specs=out_specs, check_vma=False
    )
```

time: 238 us -> 166 us (0.70); the launches traced: 234 us -> 165 us
  waiting for transfers between devices: 93.4 us -> 39.2 us
  blocking collectives: 56 us -> 32 us
  starting transfers between devices: 22 us -> 38.9 us
  between operations: 14.9 us -> 0.87 us
  local copies, waits for them, and re-layouts: 14.5 us -> 20.5 us
    unnamed x3 -> x0, waiting for transfers between devices: 46.9 us -> none
    all_to_all x2 -> x1, blocking collectives: 36.8 us -> 13.9 us  [on_device(): table = lax.all_to_all(table, COL, 0, 0, tiled=True)]
    all_to_all x0 -> x3, starting transfers between devices: none -> 19.7 us  [the longest x1 12 us: on_device(): table = lax.all_to_all(table, COL, 0, 0, tiled=True)]
    all_to_all x1, waiting for transfers between devices: 9.27 us -> 0.01 us  [copies(): lax.all_to_all(jnp.broadcast_to(value, (n, *value.shape)), axis, 0, 0, ti...]
    all_to_all x0 -> x3, waiting for transfers between devices: none -> 8.73 us  [the longest x1 7.76 us: on_device(): table = lax.all_to_all(table, COL, 0, 0, tiled=True)]
    unnamed x24 -> x46, local copies, waits for them, and re-layouts: 2.97 us -> 10.8 us
    ppermute x10, waiting for transfers between devices: 37.3 us -> 30.4 us  [shifted(): return lax.ppermute(value, axis, [(i, (i + step) % n) for i in range(n)])]
    ppermute x10, starting transfers between devices: 17.9 us -> 14.4 us  [shifted(): return lax.ppermute(value, axis, [(i, (i + step) % n) for i in range(n)])]
  transfers between devices with their start and end apart: 13 -> 14, of which waited for: 9 -> 9; matrix products, arithmetic and copies ran while one was open for 9% -> 10% of each run, Pallas kernels for 4% -> 5%
where the time goes in v2:
time: 166 us; the launch traced here: 165 us
  waiting for transfers between devices  39.2 us (24%)
  starting transfers between devices  38.9 us (23%)
  blocking collectives  32 us (19%)
  Pallas kernels  23.1 us (14%)
  local copies, waits for them, and re-layouts  20.5 us (12%)
  other arithmetic  10.2 us (6%)
    ppermute x10, waiting for transfers between devices, shifted(): return lax.ppermute(value, axis, [(i, (i + step) % n) for i in range(n)])  30.4 us
    pallas_call x7, Pallas kernels, call(): pl.pallas_call(body, grid=(steps,), out_shape=outs, in_specs=specs[:len(a...  23.1 us
    all_to_all x1, blocking collectives, copies(): lax.all_to_all(jnp.broadcast_to(value, (n, *value.shape)), axis, 0, 0, ti...  18.1 us
    ppermute x10, starting transfers between devices, shifted(): return lax.ppermute(value, axis, [(i, (i + step) % n) for i in range(n)])  14.4 us
    all_to_all x1, blocking collectives, on_device(): table = lax.all_to_all(table, COL, 0, 0, tiled=True)  13.9 us
    all_to_all x1, starting transfers between devices, on_device(): table = lax.all_to_all(table, COL, 0, 0, tiled=True)  12 us
    unnamed x46, local copies, waits for them, and re-layouts  10.8 us
    all_to_all x1, waiting for transfers between devices, on_device(): table = lax.all_to_all(table, COL, 0, 0, tiled=True)  7.76 us
  transfers between devices with their start and end apart: 14, of which 9 were waited for; matrix products, arithmetic and copies ran while one was open for 10% of the time, Pallas kernels for 5%

profile of v2, /device:TPU:1, one launch (start us, length us, event | category | flops | bytes accessed | tf_op | source)
XLA Modules:
  0.0 164.7 jit_solution(3387763050544058898)
XLA Ops:
  0.6 2.2 %collective-permute-start = (bf16[128,4096]{1,0:T(8,128)(2,1)}, bf16[128,4096]{1,0:T(8,128)(2,1)S(1)}, u32[]{:S(2)}, u32[]{:S(2)}) collective-permute-start(bf16[128,4096]{1,0:T(8,128)(2,1)} %here.3), channel_id=1, source_target_pairs={{0,64},{64,128},{128,192},{192,0},{1,65},{65,129},{129,193},{193,1... | collective-permute-start | bytes 3145736 | tf_op jit(solution)/shard_map/ppermute | solution.py:25
  2.8 1.5 collective-permute-start.1
  5.2 18.1 %all_to_all.30 = bf16[8,4,4096]{2,1,0:T(4,128)(2,1)S(1)} all-to-all(bf16[8,4,4096]{2,1,0:T(4,128)(2,1)S(1)} %broadcast_in_dim.38), channel_id=1, replica_groups=mesh['row'=4,'col_0'=8,'col_1'=4,'col_2'=2] {'col_0'}, dimensions={0} | all-to-all | bytes 524288 | tf_op jit(solution)/shard_map/all_to_all | solution.py:30
  23.3 2.1 %collective-permute-done.back = bf16[128,4096]{1,0:T(8,128)(2,1)S(1)} collective-permute-done((bf16[128,4096]{1,0:T(8,128)(2,1)}, bf16[128,4096]{1,0:T(8,128)(2,1)S(1)}, u32[]{:S(2)}, u32[]{:S(2)}) %collective-permute-start) | collective-permute-done | bytes 1048608 | tf_op jit(solution)/shard_map/ppermute | solution.py:25
  26.6 1.2 broadcast_in_dim.39
  27.8 4.8 %all-to-all-start.1 = ((bf16[4,32,4096]{2,1,0:T(8,128)(2,1)}), bf16[4,32,4096]{2,1,0:T(8,128)(2,1)S(1)}, u32[]{:S(2)}, u32[]{:S(2)}) async-start(bf16[4,32,4096]{2,1,0:T(8,128)(2,1)} %broadcast_in_dim.39), calls=%async_computation.1 | async-start | bytes 2097152 | tf_op jit(solution)/shard_map/all_to_all | solution.py:30
  33.7 1.8 %collective-permute-start.3 = (bf16[64,4096]{1,0:T(8,128)(2,1)S(1)}, bf16[64,4096]{1,0:T(8,128)(2,1)S(1)}, u32[]{:S(2)}, u32[]{:S(2)}) collective-permute-start(bf16[64,4096]{1,0:T(8,128)(2,1)S(1)} %slice.10), channel_id=1, source_target_pairs={{0,192},{64,0},{128,64},{192,128},{1,193},{65,1},{129,65},{193,129... | collective-permute-start | bytes 1572872 | tf_op jit(solution)/shard_map/ppermute | solution.py:25
  35.5 10.1 %collective-permute-done.2.low = bf16[64,4096]{1,0:T(8,128)(2,1)S(1)} collective-permute-done((bf16[64,4096]{1,0:T(8,128)(2,1)S(1)}, bf16[64,4096]{1,0:T(8,128)(2,1)S(1)}, u32[]{:S(2)}, u32[]{:S(2)}) %collective-permute-start.2) | collective-permute-done | bytes 524320 | tf_op jit(solution)/shard_map/ppermute | solution.py:25
  47.2 2.7 %collective-permute-start.4 = (bf16[128,4096]{1,0:T(8,128)(2,1)S(1)}, bf16[128,4096]{1,0:T(8,128)(2,1)S(1)}, u32[]{:S(2)}, u32[]{:S(2)}) collective-permute-start(bf16[128,4096]{1,0:T(8,128)(2,1)S(1)} %bitcast.17), channel_id=1, source_target_pairs={{0,1},{1,0},{2,3},{3,2},{4,5},{5,4},{6,7},{7,6},{8,9},{9,8},{10,11... | collective-permute-start | bytes 3145736 | tf_op jit(solution)/shard_map/ppermute | solution.py:25
  55.3 2.9 %shard_map.85.first = f32[384,256]{1,0:T(8,128)S(1)} custom-call(bf16[128,4096]{1,0:T(8,128)(2,1)S(1)} %bitcast.18, bf16[128,4096]{1,0:T(8,128)(2,1)S(1)} %collective-permute-done.4.other, bf16[128,4096]{1,0:T(8,128)(2,1)S(1)} %copy-done.3, bf16[128,4096]{1,0:T(8,128)(2,1)S(1)} %collective-permute-done.back, bf16[128,4096]{1,0:T(8,128)(2,1)S(1)} %copy-done.1), custom_call_target="tpu_custom_call" | custom-call | flops 805306368 | bytes 5636096 | tf_op jit(solution)/shard_map/pallas_call | solution.py:48
  58.3 3.3 %shard_map.86 = (f32[128,256]{1,0:T(8,128)S(1)}, f32[512,256]{1,0:T(8,128)S(1)}, f32[64,2,256]{2,1,0:T(2,128)S(1)}) custom-call(s32[5]{0:T(128)S(1)} %pad_add_fusion.place, bf16[128,4096]{1,0:T(8,128)(2,1)S(1)} %bitcast.19, bf16[128,4096]{1,0:T(8,128)(2,1)S(1)} %collective-permute-done.4.other, bf16[64,4096]{1,0:T(8,128)(2,1)S(1)} %copy-done.10, ...), custom_call_target="tpu_custom_call" | custom-call | flops 268435456 | bytes 4333588 | tf_op jit(solution)/shard_map/pallas_call | solution.py:48
  63.7 12.0 %all-to-all-start.2 = ((f32[64,2,256]{2,1,0:T(2,128)}), f32[64,2,256]{2,1,0:T(2,128)}, u32[]{:S(2)}, u32[]{:S(2)}) async-start(f32[64,2,256]{2,1,0:T(2,128)} %copy-done.17), calls=%async_computation.2 | async-start | bytes 262144 | tf_op jit(solution)/shard_map/all_to_all | solution.py:223
  79.0 7.8 %all-to-all-done.2.table = f32[64,2,256]{2,1,0:T(2,128)} async-done(((f32[64,2,256]{2,1,0:T(2,128)}), f32[64,2,256]{2,1,0:T(2,128)}, u32[]{:S(2)}, u32[]{:S(2)}) %all-to-all-start.2) | async-done | bytes 131104 | tf_op jit(solution)/shard_map/all_to_all | solution.py:223
  88.7 1.5 shard_map.87
  90.2 13.9 %all_to_all.31.table = f32[64,1,256]{2,1,0:T(1,128)S(1)} all-to-all(f32[64,1,256]{2,1,0:T(1,128)S(1)} %get-tuple-element.35), channel_id=1, replica_groups=mesh['row'=4,'col_0'=8,'col_1'=4,'col_2'=2] {'col_0','col_1','col_2'}, dimensions={0} | all-to-all | bytes 131072 | tf_op jit(solution)/shard_map/all_to_all | solution.py:230
  104.1 4.5 %shard_map.88 = (bf16[512,256]{1,0:T(8,128)(2,1)S(1)}, f32[8,256]{1,0:T(8,128)S(1)}, bf16[64,4096]{1,0:T(8,128)(2,1)}, bf16[64,4096]{1,0:T(8,128)(2,1)}) custom-call(s32[5]{0:T(128)S(1)} %pad_add_fusion.place, f32[64,1,256]{2,1,0:T(1,128)S(1)} %all_to_all.31.table, f32[8,256]{1,0:T(8,128)S(1)} %get-tuple-element.36.stats, f32[512,256]{1,0:T(8,128)S(1)} %copy-done.8, ...), custom_call_target="tpu_custom_call" | custom-call | flops 268435456 | bytes 4538388 | tf_op jit(solution)/shard_map/pallas_call | solution.py:48
  108.6 3.2 %shard_map.89 = (f32[128,4096]{1,0:T(8,128)S(1)}, f32[128,4096]{1,0:T(8,128)S(1)}) custom-call(bf16[512,256]{1,0:T(8,128)(2,1)S(1)} %get-tuple-element.39.grads, bf16[128,4096]{1,0:T(8,128)(2,1)S(1)} %copy-done.4, bf16[128,4096]{1,0:T(8,128)(2,1)S(1)} %collective-permute-done.back, bf16[128,4096]{1,0:T(8,128)(2,1)S(1)} %copy-done.2, ...), custom_call_target="tpu_custom_call" | custom-call | flops 1073741824 | bytes 8650752 | tf_op jit(solution)/shard_map/pallas_call | solution.py:48
  112.3 2.0 %collective-permute-start.6 = (bf16[64,4096]{1,0:T(8,128)(2,1)}, bf16[64,4096]{1,0:T(8,128)(2,1)S(1)}, u32[]{:S(2)}, u32[]{:S(2)}) collective-permute-start(bf16[64,4096]{1,0:T(8,128)(2,1)} %get-tuple-element.44), channel_id=1, source_target_pairs={{0,192},{64,0},{128,64},{192,128},{1,193},{65,1},{129,65},{193,129... | collective-permute-start | bytes 1572872 | tf_op jit(solution)/shard_map/ppermute | solution.py:25
  114.3 1.8 %collective-permute-done.5.arrived = f32[128,4096]{1,0:T(8,128)S(1)} collective-permute-done((f32[128,4096]{1,0:T(8,128)S(1)}, f32[128,4096]{1,0:T(8,128)S(1)}, u32[]{:S(2)}, u32[]{:S(2)}) %collective-permute-start.5) | collective-permute-done | bytes 2097184 | tf_op jit(solution)/shard_map/ppermute | solution.py:25
  116.1 3.2 %shard_map.90 = (f32[128,4096]{1,0:T(8,128)S(1)}, bf16[128,4096]{1,0:T(8,128)(2,1)}) custom-call(f32[128,4096]{1,0:T(8,128)S(1)} %get-tuple-element.40.own, f32[128,4096]{1,0:T(8,128)S(1)} %collective-permute-done.5.arrived), custom_call_target="tpu_custom_call" | custom-call | bytes 7340032 | tf_op jit(solution)/shard_map/pallas_call | solution.py:48
  119.2 1.3 copy-done.18
  120.6 4.2 %all-to-all-start.4 = ((bf16[4,32,4096]{2,1,0:T(8,128)(2,1)}), bf16[4,32,4096]{2,1,0:T(8,128)(2,1)}, u32[]{:S(2)}, u32[]{:S(2)}) async-start(bf16[4,32,4096]{2,1,0:T(8,128)(2,1)} %bitcast.11), calls=%async_computation.4 | async-start | bytes 2097152 | tf_op jit(solution)/shard_map/all_to_all | solution.py:172
  126.0 2.9 %collective-permute-done.7.high = bf16[64,4096]{1,0:T(8,128)(2,1)S(1)} collective-permute-done((bf16[64,4096]{1,0:T(8,128)(2,1)}, bf16[64,4096]{1,0:T(8,128)(2,1)S(1)}, u32[]{:S(2)}, u32[]{:S(2)}) %collective-permute-start.7) | collective-permute-done | bytes 524320 | tf_op jit(solution)/shard_map/ppermute | solution.py:25
  128.9 4.6 %shard_map.91 = (f32[128,4096]{1,0:T(8,128)S(1)}, bf16[128,4096]{1,0:T(8,128)(2,1)}, bf16[128,4096]{1,0:T(8,128)(2,1)}) custom-call(bf16[512,256]{1,0:T(8,128)(2,1)S(1)} %get-tuple-element.39.grads, bf16[128,4096]{1,0:T(8,128)(2,1)S(1)} %bitcast.21, bf16[128,4096]{1,0:T(8,128)(2,1)S(1)} %collective-permute-done.4.other, ...), custom_call_target="tpu_custom_call" | custom-call | flops 805306368 | bytes 7602176 | tf_op jit(solution)/shard_map/pallas_call | solution.py:48
  133.5 1.4 copy-done.5
  134.8 2.7 %collective-permute-start.8 = (bf16[128,4096]{1,0:T(8,128)(2,1)}, bf16[128,4096]{1,0:T(8,128)(2,1)}, u32[]{:S(2)}, u32[]{:S(2)}) collective-permute-start(bf16[128,4096]{1,0:T(8,128)(2,1)} %get-tuple-element.47), channel_id=1, source_target_pairs={{0,192},{64,0},{128,64},{192,128},{1,193},{65,1},{129,65},{193,129... | collective-permute-start | bytes 3145736 | tf_op jit(solution)/shard_map/ppermute | solution.py:25
  139.7 2.3 %select_reduce_fusion = f32[32,4096]{1,0:T(8,128)} fusion(bf16[4,32,4096]{2,1,0:T(8,128)(2,1)} %all-to-all-done.4, pred[4]{0:T(512)(128)(4,1)S(1)} %iota_compare_fusion), kind=kLoop, calls=%fused_computation.1 | loop fusion | flops 1441792 | bytes 1572868 | tf_op jit(solution)/shard_map/reduce_sum | solution.py:175
  142.1 1.3 reduce_sum.21
  144.5 3.4 %all-to-all-start.5 = ((bf16[8,4,4096]{2,1,0:T(4,128)(2,1)}), bf16[8,4,4096]{2,1,0:T(4,128)(2,1)S(1)}, u32[]{:S(2)}, u32[]{:S(2)}) async-start(bf16[8,4,4096]{2,1,0:T(4,128)(2,1)} %get-tuple-element.49), calls=%async_computation.5 | async-start | bytes 524288 | tf_op jit(solution)/shard_map/all_to_all | solution.py:172
  147.9 11.9 %collective-permute-done.9 = bf16[128,4096]{1,0:T(8,128)(2,1)} collective-permute-done((bf16[128,4096]{1,0:T(8,128)(2,1)}, bf16[128,4096]{1,0:T(8,128)(2,1)}, u32[]{:S(2)}, u32[]{:S(2)}) %collective-permute-start.9) | collective-permute-done | bytes 1048608 | tf_op jit(solution)/shard_map/ppermute | solution.py:25
  159.8 3.2 %convert_add_fusion = f32[128,4096]{1,0:T(8,128)} fusion(bf16[128,4096]{1,0:T(8,128)(2,1)} %collective-permute-done.9, f32[128,4096]{1,0:T(8,128)S(1)} %copy-done.6, bf16[128,4096]{1,0:T(8,128)(2,1)} %collective-permute-done.8), kind=kLoop, calls=%fused_computation | loop fusion | flops 2097152 | bytes 6291456 | tf_op jit(solution)/shard_map/add | solution.py:266
  163.2 1.5 bitcast_add_fusion
  (81 shorter events, 22.6 us)
Async XLA Ops:
  0.6 24.7 %collective-permute-start = (bf16[128,4096]{1,0:T(8,128)(2,1)}, bf16[128,4096]{1,0:T(8,128)(2,1)S(1)}, u32[]{:S(2)}, u32[]{:S(2)}) collective-permute-start(bf16[128,4096]{1,0:T(8,128)(2,1)} %here.3), channel_id=1, source_target_pairs={{0,64},{64,128},{128,192},{192,0},{1,65},{65,129},{129,193},{193,1... | collective-permute-start | bytes 3145736 | tf_op jit(solution)/shard_map/ppermute | solution.py:25
  2.8 23.7 %collective-permute-start.1 = (bf16[128,4096]{1,0:T(8,128)(2,1)}, bf16[128,4096]{1,0:T(8,128)(2,1)S(1)}, u32[]{:S(2)}, u32[]{:S(2)}) collective-permute-start(bf16[128,4096]{1,0:T(8,128)(2,1)} %here.3), channel_id=1, source_target_pairs={{0,192},{64,0},{128,64},{192,128},{1,193},{65,1},{129,65},{193,129... | collective-permute-start | bytes 3145736 | tf_op jit(solution)/shard_map/ppermute | solution.py:25
  26.5 7.1 %copy-start = (bf16[128,4096]{1,0:T(8,128)(2,1)}, bf16[128,4096]{1,0:T(8,128)(2,1)S(1)}, u32[]{:S(2)}) copy-start(bf16[128,4096]{1,0:T(8,128)(2,1)S(1)} %collective-permute-done.1.ahead) | copy-start | bytes 3145732
  27.8 22.1 %copy-start.19 = (s32[256,7]{0,1:T(8,128)S(1)}, s32[256,7]{0,1:T(8,128)}, u32[]{:S(2)}) copy-start(s32[256,7]{0,1:T(8,128)} %param.9) | copy-start | bytes 21508
  27.8 23.1 %copy-start.20 = (s32[256]{0:T(256)S(1)}, s32[256]{0:T(256)}, u32[]{:S(2)}) copy-start(s32[256]{0:T(256)} %param.8) | copy-start | bytes 3076
  27.8 19.4 %all-to-all-start.1 = ((bf16[4,32,4096]{2,1,0:T(8,128)(2,1)}), bf16[4,32,4096]{2,1,0:T(8,128)(2,1)S(1)}, u32[]{:S(2)}, u32[]{:S(2)}) async-start(bf16[4,32,4096]{2,1,0:T(8,128)(2,1)} %broadcast_in_dim.39), calls=%async_computation.1 | async-start | bytes 2097152 | tf_op jit(solution)/shard_map/all_to_all | solution.py:30
  32.6 20.2 %copy-start.22 = (s32[4]{0:T(128)S(1)}, s32[4]{0:T(128)}, u32[]{:S(2)}) copy-start(s32[4]{0:T(128)} %constant.56) | copy-start | bytes 52
  32.6 12.9 %collective-permute-start.2 = (bf16[64,4096]{1,0:T(8,128)(2,1)S(1)}, bf16[64,4096]{1,0:T(8,128)(2,1)S(1)}, u32[]{:S(2)}, u32[]{:S(2)}) collective-permute-start(bf16[64,4096]{1,0:T(8,128)(2,1)S(1)} %slice.9), channel_id=1, source_target_pairs={{0,64},{64,128},{128,192},{192,0},{1,65},{65,129},{129,193},{193,1... | collective-permute-start | bytes 1572872 | tf_op jit(solution)/shard_map/ppermute | solution.py:25
  33.7 12.7 %collective-permute-start.3 = (bf16[64,4096]{1,0:T(8,128)(2,1)S(1)}, bf16[64,4096]{1,0:T(8,128)(2,1)S(1)}, u32[]{:S(2)}, u32[]{:S(2)}) collective-permute-start(bf16[64,4096]{1,0:T(8,128)(2,1)S(1)} %slice.10), channel_id=1, source_target_pairs={{0,192},{64,0},{128,64},{192,128},{1,193},{65,1},{129,65},{193,129... | collective-permute-start | bytes 1572872 | tf_op jit(solution)/shard_map/ppermute | solution.py:25
  47.2 5.7 %collective-permute-start.4 = (bf16[128,4096]{1,0:T(8,128)(2,1)S(1)}, bf16[128,4096]{1,0:T(8,128)(2,1)S(1)}, u32[]{:S(2)}, u32[]{:S(2)}) collective-permute-start(bf16[128,4096]{1,0:T(8,128)(2,1)S(1)} %bitcast.17), channel_id=1, source_target_pairs={{0,1},{1,0},{2,3},{3,2},{4,5},{5,4},{6,7},{7,6},{8,9},{9,8},{10,11... | collective-permute-start | bytes 3145736 | tf_op jit(solution)/shard_map/ppermute | solution.py:25
  52.9 1.2 copy-start.1
  54.1 1.2 copy-start.3
  55.3 3.0 %copy-start.10 = (bf16[64,4096]{1,0:T(8,128)(2,1)S(1)}, bf16[64,4096]{1,0:T(8,128)(2,1)}, u32[]{:S(2)}) copy-start(bf16[64,4096]{1,0:T(8,128)(2,1)} %copy-done.9) | copy-start | bytes 1572868
  55.3 3.0 %copy-start.13 = (bf16[64,4096]{1,0:T(8,128)(2,1)S(1)}, bf16[64,4096]{1,0:T(8,128)(2,1)}, u32[]{:S(2)}) copy-start(bf16[64,4096]{1,0:T(8,128)(2,1)} %copy-done.12) | copy-start | bytes 1572868
  58.3 17.5 %copy-start.21 = (f32[256]{0:T(256)S(1)}, f32[256]{0:T(256)}, u32[]{:S(2)}) copy-start(f32[256]{0:T(256)} %param.10) | copy-start | bytes 3076
  63.7 23.0 %all-to-all-start.2 = ((f32[64,2,256]{2,1,0:T(2,128)}), f32[64,2,256]{2,1,0:T(2,128)}, u32[]{:S(2)}, u32[]{:S(2)}) async-start(f32[64,2,256]{2,1,0:T(2,128)} %copy-done.17), calls=%async_computation.2 | async-start | bytes 262144 | tf_op jit(solution)/shard_map/all_to_all | solution.py:223
  86.8 1.0 copy-start.8
  87.8 0.9 copy-start.16
  88.7 19.9 %copy-start.2 = (bf16[128,4096]{1,0:T(8,128)(2,1)S(1)}, bf16[128,4096]{1,0:T(8,128)(2,1)}, u32[]{:S(2)}) copy-start(bf16[128,4096]{1,0:T(8,128)(2,1)} %copy-done) | copy-start | bytes 3145732
  88.7 19.9 %copy-start.4 = (bf16[128,4096]{1,0:T(8,128)(2,1)S(1)}, bf16[128,4096]{1,0:T(8,128)(2,1)}, u32[]{:S(2)}) copy-start(bf16[128,4096]{1,0:T(8,128)(2,1)} %here.3) | copy-start | bytes 3145732
  88.7 19.9 %copy-start.11 = (bf16[64,4096]{1,0:T(8,128)(2,1)S(1)}, bf16[64,4096]{1,0:T(8,128)(2,1)}, u32[]{:S(2)}) copy-start(bf16[64,4096]{1,0:T(8,128)(2,1)} %copy-done.9) | copy-start | bytes 1572868
  88.7 19.9 %copy-start.14 = (bf16[64,4096]{1,0:T(8,128)(2,1)S(1)}, bf16[64,4096]{1,0:T(8,128)(2,1)}, u32[]{:S(2)}) copy-start(bf16[64,4096]{1,0:T(8,128)(2,1)} %copy-done.12) | copy-start | bytes 1572868
  111.8 4.3 %collective-permute-start.5 = (f32[128,4096]{1,0:T(8,128)S(1)}, f32[128,4096]{1,0:T(8,128)S(1)}, u32[]{:S(2)}, u32[]{:S(2)}) collective-permute-start(f32[128,4096]{1,0:T(8,128)S(1)} %get-tuple-element.41), channel_id=1, source_target_pairs={{0,1},{1,0},{2,3},{3,2},{4,5},{5,4},{6,7},{7,6},{8,9},{9,8},{10,11... | collective-permute-start | bytes 6291464 | tf_op jit(solution)/shard_map/ppermute | solution.py:25
  112.3 13.7 %collective-permute-start.6 = (bf16[64,4096]{1,0:T(8,128)(2,1)}, bf16[64,4096]{1,0:T(8,128)(2,1)S(1)}, u32[]{:S(2)}, u32[]{:S(2)}) collective-permute-start(bf16[64,4096]{1,0:T(8,128)(2,1)} %get-tuple-element.44), channel_id=1, source_target_pairs={{0,192},{64,0},{128,64},{192,128},{1,193},{65,1},{129,65},{193,129... | collective-permute-start | bytes 1572872 | tf_op jit(solution)/shard_map/ppermute | solution.py:25
  114.3 14.6 %collective-permute-start.7 = (bf16[64,4096]{1,0:T(8,128)(2,1)}, bf16[64,4096]{1,0:T(8,128)(2,1)S(1)}, u32[]{:S(2)}, u32[]{:S(2)}) collective-permute-start(bf16[64,4096]{1,0:T(8,128)(2,1)} %get-tuple-element.45), channel_id=1, source_target_pairs={{0,64},{64,128},{128,192},{192,0},{1,65},{65,129},{129,193},{193,1... | collective-permute-start | bytes 1572872 | tf_op jit(solution)/shard_map/ppermute | solution.py:25
  119.2 1.3 copy-start.18
  120.6 19.2 %all-to-all-start.4 = ((bf16[4,32,4096]{2,1,0:T(8,128)(2,1)}), bf16[4,32,4096]{2,1,0:T(8,128)(2,1)}, u32[]{:S(2)}, u32[]{:S(2)}) async-start(bf16[4,32,4096]{2,1,0:T(8,128)(2,1)} %bitcast.11), calls=%async_computation.4 | async-start | bytes 2097152 | tf_op jit(solution)/shard_map/all_to_all | solution.py:172
  133.5 1.4 copy-start.5
  134.8 25.0 %collective-permute-start.9 = (bf16[128,4096]{1,0:T(8,128)(2,1)}, bf16[128,4096]{1,0:T(8,128)(2,1)}, u32[]{:S(2)}, u32[]{:S(2)}) collective-permute-start(bf16[128,4096]{1,0:T(8,128)(2,1)} %get-tuple-element.48), channel_id=1, source_target_pairs={{0,64},{64,128},{128,192},{192,0},{1,65},{65,129},{129,193},{193,1... | collective-permute-start | bytes 3145736 | tf_op jit(solution)/shard_map/ppermute | solution.py:25
  134.8 25.0 %collective-permute-start.8 = (bf16[128,4096]{1,0:T(8,128)(2,1)}, bf16[128,4096]{1,0:T(8,128)(2,1)}, u32[]{:S(2)}, u32[]{:S(2)}) collective-permute-start(bf16[128,4096]{1,0:T(8,128)(2,1)} %get-tuple-element.47), channel_id=1, source_target_pairs={{0,192},{64,0},{128,64},{192,128},{1,193},{65,1},{129,65},{193,129... | collective-permute-start | bytes 3145736 | tf_op jit(solution)/shard_map/ppermute | solution.py:25
  142.1 17.8 %copy-start.6 = (f32[128,4096]{1,0:T(8,128)S(1)}, f32[128,4096]{1,0:T(8,128)}, u32[]{:S(2)}) copy-start(f32[128,4096]{1,0:T(8,128)} %copy-done.5) | copy-start | bytes 6291460
  144.5 18.5 %all-to-all-start.5 = ((bf16[8,4,4096]{2,1,0:T(4,128)(2,1)}), bf16[8,4,4096]{2,1,0:T(4,128)(2,1)S(1)}, u32[]{:S(2)}, u32[]{:S(2)}) async-start(bf16[8,4,4096]{2,1,0:T(4,128)(2,1)} %get-tuple-element.49), calls=%async_computation.5 | async-start | bytes 524288 | tf_op jit(solution)/shard_map/all_to_all | solution.py:172
  (5 other events, 3.7 us)

commit v3 on v2

v3 whole, which is shorter than its diff:
```python
import functools

import jax
import jax.numpy as jnp
from jax import lax
from jax.experimental import pallas as pl
from jax.experimental.pallas import tpu as pltpu
from jax.sharding import Mesh
from jax.sharding import PartitionSpec as P

Y, Z, X, CORE = "row", "col_0", "col_1", "col_2"
COL = (Z, X, CORE)
ROW_COL = (Y, Z, X, CORE)
COL_ROW = (Z, X, CORE, Y)

inv_temp = 50.0
sharpness = 4.0
LOWEST = -3.0e38
F32, BF16 = jnp.float32, jnp.bfloat16
TILE = 1024


def shifted(value, axis, step):
    n = lax.axis_size(axis)
    return lax.ppermute(value, axis, [(i, (i + step) % n) for i in range(n)])


def copies(value, axis):
    n = lax.axis_size(axis)
    return lax.all_to_all(jnp.broadcast_to(value, (n, *value.shape)), axis, 0, 0, tiled=True)


def shape(dims, dtype):
    return jax.ShapeDtypeStruct(dims, dtype)


def call(body, outs, args, flops=0, scalars=0, tiled=(), scratch=()):
    size = sum(a.size * a.dtype.itemsize for a in (*args, *outs))
    specs = []
    for k, a in enumerate((*args, *outs)):
        if k < scalars:
            specs.append(pl.BlockSpec(memory_space=pltpu.SMEM))
        elif k in tiled:
            specs.append(pl.BlockSpec((a.shape[0], TILE), lambda i: (0, i)))
        else:
            specs.append(pl.BlockSpec(a.shape, lambda i, n=len(a.shape): (0,) * n))
    steps = (*args, *outs)[tiled[0]].shape[1] // TILE if tiled else 1
    return pl.pallas_call(
        body,
        grid=(steps,),
        out_shape=outs,
        in_specs=specs[: len(args)],
        out_specs=specs[len(args) :],
        scratch_shapes=scratch,
        cost_estimate=pl.CostEstimate(flops=flops, bytes_accessed=size, transcendentals=0),
        compiler_params=pltpu.CompilerParams(vmem_limit_bytes=24 << 20),
    )(*args)


def swapped(core, row):
    half = row.shape[1] // 2
    return jnp.where(core == 0, row, jnp.concatenate([row[:, half:], row[:, :half]], axis=1))


def on_step(k):
    return pl.when(pl.program_id(0) == k)


def marks(place, ids, k, lines):
    column = place[1 + k] + lax.broadcasted_iota(jnp.int32, (128, ids.shape[1]), 0)
    found = [column == ids[slot : slot + 1, :] for slot in range(lines)]
    return found[0], functools.reduce(jnp.logical_or, found)


def score_body(place, own, other, *refs):
    pool, ids, scores, table = refs[:7], *refs[7:]

    @on_step(0)
    def _():
        scores[...] = jnp.zeros_like(scores)

    rows = jnp.concatenate([p[...] for p in pool], axis=0)
    columns = jnp.concatenate([own[...], other[...]], axis=0)
    scores[...] += lax.dot_general(
        rows, columns, (((1,), (1,)), ((), ())), preferred_element_type=F32
    )

    @pl.when(pl.program_id(0) == pl.num_programs(0) - 1)
    def _():
        tops = [[], []]
        for k in range(4):
            rows = slice(128 * k, 128 * k + 128)
            block = scores[rows, :] * inv_temp
            scores[rows, :] = block
            for top, mark in zip(tops, marks(place, ids, k, 8)):
                top.append(jnp.max(jnp.where(mark, block, LOWEST), axis=0, keepdims=True))
        lines = [swapped(place[0], functools.reduce(jnp.maximum, top)) for top in tops]
        table[...] = jnp.broadcast_to(jnp.concatenate(lines, axis=0)[None], table.shape)


def soft_body(place, table, margin_ref, ids, scores, weights, totals, stats):
    merged = swapped(place[0], jnp.max(table[...], axis=0))
    picked, kept = merged[0:1], merged[1:2]
    margin = margin_ref[0:1, :]
    ceiling = jnp.maximum(kept, picked + margin)
    sums = []
    for k in range(4):
        rows = slice(128 * k, 128 * k + 128)
        block = scores[rows, :]
        over = sharpness * (block - picked - margin)
        penalty = jnp.maximum(over, 0.0) + jnp.log(1.0 + jnp.exp(-jnp.abs(over)))
        logits = jnp.where(marks(place, ids, k, 8)[1], block, block - penalty)
        weight = jnp.exp(logits - ceiling)
        weights[rows, :] = weight
        sums.append(jnp.sum(weight, axis=0, keepdims=True))
    total = swapped(place[0], functools.reduce(jnp.add, sums))
    totals[...] = jnp.broadcast_to(total[None], totals.shape)
    stats[...] = jnp.broadcast_to(ceiling - picked, stats.shape)


def grad_body(place, table, stats, ids, weights, own, other, *refs):
    pool, outs, (grads, turned) = refs[:7], refs[7:17], refs[17:]
    losses, low, high, back_low, back_high, ahead_low, ahead_high, here, mine, theirs = outs

    @on_step(0)
    def _():
        total = swapped(place[0], jnp.sum(table[...], axis=0))
        losses[...] = stats[...] + jnp.log(total)
        for k in range(4):
            rows = slice(128 * k, 128 * k + 128)
            positive = jnp.where(marks(place, ids, k, 1)[0], 1.0, 0.0)
            grads[rows, :] = ((weights[rows, :] / total - positive) * inv_temp).astype(BF16)
        turned[...] = grads[...].T

    columns = jnp.concatenate([own[...], other[...]], axis=0)
    out = jnp.dot(grads[...], columns, preferred_element_type=F32)
    here[...] = out[0:128]
    halves = (back_low, back_high, ahead_low, ahead_high, low, high)
    for k, half in enumerate(halves):
        half[...] = out[128 + 64 * k : 192 + 64 * k].astype(half.dtype)
    rows = jnp.concatenate([p[...] for p in pool], axis=0)
    out = jnp.dot(turned[...], rows, preferred_element_type=F32)
    mine[...] = out[:128]
    theirs[...] = out[128:]


def total_body(here, back_low, back_high, ahead_low, ahead_high, total):
    half = back_low.shape[0]
    for rows, parts in (
        (slice(0, half), (back_low, ahead_low)),
        (slice(half, 2 * half), (back_high, ahead_high)),
    ):
        total[rows, :] = here[rows, :] + parts[0][...].astype(F32) + parts[1][...].astype(F32)


def on_device(queries, passages, positives, hard_negatives, thresholds):
    rows, width = queries.shape
    count = passages.shape[0]
    depth, breadth, ring = lax.axis_size(Z), lax.axis_size(X), lax.axis_size(Y)
    core, far, across, along = (lax.axis_index(a) for a in (CORE, Z, X, Y))
    half = count // 2
    plane = depth * breadth * rows
    total, pool, members = 2 * plane, ring * count, 2 * depth * breadth

    low, high = passages[:half], passages[half:]
    back_low, ahead_high = shifted(low, Y, 1), shifted(high, Y, -1)
    back_high, ahead_low = shifted(high, Y, 1), shifted(low, Y, -1)
    line = copies(queries, Z)
    line, back_low, ahead_high = lax.optimization_barrier((line, back_low, ahead_high))
    far_low, far_high = shifted(back_low, Y, 1), shifted(ahead_high, Y, -1)
    own = copies(line.reshape(depth * rows, width), X)

    def ordered(table):
        table = table.reshape(-1, depth, breadth, 2, rows)
        table = jnp.transpose(table, (0, 3, 2, 1, 4)).reshape(-1, 2, plane)
        return jnp.where(core == 0, table, jnp.flip(table, 1)).reshape(-1, total)

    ids = ordered(jnp.concatenate([positives[None, :], hard_negatives.T], axis=0))
    margin = ordered(jnp.broadcast_to(thresholds, (8, total)))
    steps = jnp.array([0, 1, 3, 2], jnp.int32)
    base = (((far * breadth + across) * 2 + core) * ring + (along - steps) % ring) * count
    place = jnp.concatenate([core.reshape(1), base]).astype(jnp.int32)
    own, far_low, far_high, back_high, ahead_low, ids, margin, place = lax.optimization_barrier(
        (own, far_low, far_high, back_high, ahead_low, ids, margin, place)
    )
    own = own.reshape(plane, width)
    other = shifted(own, CORE, 1)
    blocks = [passages, back_low, back_high, ahead_low, ahead_high, far_low, far_high]

    scores, table = call(
        score_body,
        [shape((pool, total), F32), shape((members, 2, total), F32)],
        [place, own, other, *blocks, ids],
        flops=2 * total * pool * width,
        scalars=1,
        tiled=range(1, 10),
    )
    table = lax.all_to_all(table, COL, 0, 0, tiled=True)
    weights, table, stats = call(
        soft_body,
        [shape((pool, total), F32), shape((members, 1, total), F32), shape((8, total), F32)],
        [place, table, margin, ids, scores],
        scalars=1,
    )
    table = lax.all_to_all(table, COL, 0, 0, tiled=True)
    piece, exact = shape((half, width), BF16), shape((half, width), F32)
    sums = [piece, piece, exact, piece, piece, exact] + [shape((count, width), F32)]
    losses, low, high, back_low, back_high, ahead_low, ahead_high, here, mine, theirs = call(
        grad_body,
        [shape((8, total), F32)] + sums + [shape((plane, width), F32)] * 2,
        [place, table, stats, ids, weights, own, other, *blocks],
        flops=4 * total * pool * width,
        scalars=1,
        tiled=(*range(5, 14), *range(15, 24)),
        scratch=[pltpu.VMEM((pool, total), BF16), pltpu.VMEM((total, pool), BF16)],
    )

    low, high = shifted(low, Y, -1), shifted(high, Y, 1)
    back_high, ahead_low = shifted(back_high, Y, -1), shifted(ahead_low, Y, 1)
    theirs = shifted(theirs, CORE, 1)
    back_low = shifted((back_low + low.astype(F32)).astype(BF16), Y, -1)
    ahead_high = shifted((ahead_high + high.astype(F32)).astype(BF16), Y, 1)
    grad_passages = call(
        total_body,
        [shape((count, width), F32)],
        [here, back_low, back_high, ahead_low, ahead_high],
        tiled=range(6),
    )[0]

    place_of = across * depth + far
    at = place_of * rows
    exact = lax.dynamic_slice_in_dim(mine, at, rows, 0) + lax.dynamic_slice_in_dim(theirs, at, rows, 0)
    sent = (mine + theirs).astype(BF16).reshape(breadth * depth, rows, width)
    parts = lax.all_to_all(sent, (X, Z), 0, 0, tiled=True)
    others = (lax.iota(jnp.int32, breadth * depth) != place_of)[:, None, None]
    grad_queries = exact + jnp.sum(jnp.where(others, parts.astype(F32), 0.0), axis=0)

    row_losses = lax.dynamic_slice_in_dim(losses[0], at, rows, 0)
    return row_losses, grad_queries, grad_passages


def solution(mesh):
    torus = Mesh(mesh.devices.reshape(mesh.shape[Y], 8, 4, 2), ROW_COL)
    in_specs = (P(ROW_COL, None), P(COL_ROW, None), P(Y), P(Y, None), P(Y))
    out_specs = (P(ROW_COL), P(ROW_COL, None), P(COL_ROW, None))
    return jax.shard_map(
        on_device, mesh=torus, in_specs=in_specs, out_specs=out_specs, check_vma=False
    )
```

time: 166 us -> 143 us (0.86)
  local copies, waits for them, and re-layouts: 20.5 us -> 11.8 us
  Pallas kernels: 23.1 us -> 15.6 us
  waiting for transfers between devices: 39.2 us -> 35.3 us
  starting transfers between devices: 38.9 us -> 37 us
    all_to_all x1 -> x2, blocking collectives: 13.9 us -> 32 us  [on_device(): table = lax.all_to_all(table, COL, 0, 0, tiled=True)]
    all_to_all x1 -> x0, blocking collectives: 18.1 us -> none  [copies(): lax.all_to_all(jnp.broadcast_to(value, (n, *value.shape)), axis, 0, 0, ti...]
    all_to_all x3 -> x1, starting transfers between devices: 19.7 us -> 4.66 us  [on_device(): parts = lax.all_to_all(sent, (X, Z), 0, 0, tiled=True)]
    all_to_all x3 -> x1, waiting for transfers between devices: 8.73 us -> 0.01 us  [on_device(): parts = lax.all_to_all(sent, (X, Z), 0, 0, tiled=True)]
    pallas_call x7 -> x4, Pallas kernels: 23.1 us -> 15.6 us  [call(): pl.pallas_call(body, grid=(steps,), out_shape=outs, in_specs=specs[:len(a...]
    all_to_all x1 -> x2, starting transfers between devices: 4.79 us -> 12.2 us  [copies(): lax.all_to_all(jnp.broadcast_to(value, (n, *value.shape)), axis, 0, 0, ti...]
    unnamed x46 -> x28, local copies, waits for them, and re-layouts: 10.8 us -> 4.4 us
    all_to_all x1 -> x2, waiting for transfers between devices: 0.01 us -> 6.29 us  [copies(): lax.all_to_all(jnp.broadcast_to(value, (n, *value.shape)), axis, 0, 0, ti...]
  transfers between devices with their start and end apart: 14 -> 17, of which waited for: 9 -> 7; matrix products, arithmetic and copies ran while one was open for 10% -> 8% of each run, Pallas kernels for 5% -> 3%
where the time goes in v3:
time: 143 us; the launch traced here: 142 us
  starting transfers between devices  37 us (26%)
  waiting for transfers between devices  35.3 us (25%)
  blocking collectives  32 us (22%)
  Pallas kernels  15.6 us (11%)
  local copies, waits for them, and re-layouts  11.8 us (8%)
  other arithmetic  9.99 us (7%)
    all_to_all x2, blocking collectives, on_device(): table = lax.all_to_all(table, COL, 0, 0, tiled=True)  32 us
    ppermute x14, waiting for transfers between devices, shifted(): return lax.ppermute(value, axis, [(i, (i + step) % n) for i in range(n)])  29 us
    ppermute x14, starting transfers between devices, shifted(): return lax.ppermute(value, axis, [(i, (i + step) % n) for i in range(n)])  20.2 us
    pallas_call x4, Pallas kernels, call(): pl.pallas_call(body, grid=(steps,), out_shape=outs, in_specs=specs[:len(a...  15.6 us
    all_to_all x2, starting transfers between devices, copies(): lax.all_to_all(jnp.broadcast_to(value, (n, *value.shape)), axis, 0, 0, ti...  12.2 us
    all_to_all x2, waiting for transfers between devices, copies(): lax.all_to_all(jnp.broadcast_to(value, (n, *value.shape)), axis, 0, 0, ti...  6.29 us
    all_to_all x1, starting transfers between devices, on_device(): parts = lax.all_to_all(sent, (X, Z), 0, 0, tiled=True)  4.66 us
    unnamed x28, local copies, waits for them, and re-layouts  4.4 us
  transfers between devices with their start and end apart: 17, of which 7 were waited for; matrix products, arithmetic and copies ran while one was open for 8% of the time, Pallas kernels for 3%

profile of v3, /device:TPU:1, one launch (start us, length us, event | category | flops | bytes accessed | tf_op | source)
XLA Modules:
  0.0 142.5 jit_solution(4033704395132728631)
XLA Ops:
  0.7 2.3 %fusion.4 = (bf16[64,4096]{1,0:T(8,128)(2,1)}, bf16[64,4096]{1,0:T(8,128)(2,1)}) fusion(bf16[128,4096]{1,0:T(8,128)(2,1)} %refs_0_.3), kind=kLoop, calls=%fused_computation.18 | loop fusion | bytes 2097152 | tf_op jit(solution)/shard_map/slice | solution.py:165
  3.0 2.1 %collective-permute-start = (bf16[64,4096]{1,0:T(8,128)(2,1)}, bf16[64,4096]{1,0:T(8,128)(2,1)S(1)}, u32[]{:S(2)}, u32[]{:S(2)}) collective-permute-start(bf16[64,4096]{1,0:T(8,128)(2,1)} %get-tuple-element.56), channel_id=1, source_target_pairs={{0,64},{64,128},{128,192},{192,0},{1,65},{65,129},{129,193},{193,1... | collective-permute-start | bytes 1572872 | tf_op jit(solution)/shard_map/ppermute | solution.py:25
  5.1 1.4 %collective-permute-start.1 = (bf16[64,4096]{1,0:T(8,128)(2,1)}, bf16[64,4096]{1,0:T(8,128)(2,1)S(1)}, u32[]{:S(2)}, u32[]{:S(2)}) collective-permute-start(bf16[64,4096]{1,0:T(8,128)(2,1)} %get-tuple-element.55), channel_id=1, source_target_pairs={{0,192},{64,0},{128,64},{192,128},{1,193},{65,1},{129,65},{193,129... | collective-permute-start | bytes 1572872 | tf_op jit(solution)/shard_map/ppermute | solution.py:25
  7.3 8.2 %all-to-all-start = ((bf16[8,4,4096]{2,1,0:T(4,128)(2,1)}), bf16[8,4,4096]{2,1,0:T(4,128)(2,1)S(1)}, u32[]{:S(2)}, u32[]{:S(2)}) async-start(bf16[8,4,4096]{2,1,0:T(4,128)(2,1)} %broadcast_in_dim.25), calls=%async_computation | async-start | bytes 524288 | tf_op jit(solution)/shard_map/all_to_all | solution.py:30
  15.5 2.7 %collective-permute-start.5 = (bf16[64,4096]{1,0:T(8,128)(2,1)}, bf16[64,4096]{1,0:T(8,128)(2,1)}, u32[]{:S(2)}, u32[]{:S(2)}) collective-permute-start(bf16[64,4096]{1,0:T(8,128)(2,1)} %get-tuple-element.56), channel_id=1, source_target_pairs={{0,192},{64,0},{128,64},{192,128},{1,193},{65,1},{129,65},{193,129... | collective-permute-start | bytes 1572872 | tf_op jit(solution)/shard_map/ppermute | solution.py:25
  19.4 6.3 %all-to-all-done = bf16[8,4,4096]{2,1,0:T(4,128)(2,1)S(1)} async-done(((bf16[8,4,4096]{2,1,0:T(4,128)(2,1)}), bf16[8,4,4096]{2,1,0:T(4,128)(2,1)S(1)}, u32[]{:S(2)}, u32[]{:S(2)}) %all-to-all-start) | async-done | bytes 262176 | tf_op jit(solution)/shard_map/all_to_all | solution.py:30
  25.8 1.1 broadcast_in_dim.26
  26.8 4.0 %all-to-all-start.1 = ((bf16[4,32,4096]{2,1,0:T(8,128)(2,1)}), bf16[4,32,4096]{2,1,0:T(8,128)(2,1)S(1)}, u32[]{:S(2)}, u32[]{:S(2)}) async-start(bf16[4,32,4096]{2,1,0:T(8,128)(2,1)} %broadcast_in_dim.26), calls=%async_computation.1 | async-start | bytes 2097152 | tf_op jit(solution)/shard_map/all_to_all | solution.py:30
  31.2 2.7 %collective-permute-start.3 = (bf16[64,4096]{1,0:T(8,128)(2,1)S(1)}, bf16[64,4096]{1,0:T(8,128)(2,1)}, u32[]{:S(2)}, u32[]{:S(2)}) collective-permute-start(bf16[64,4096]{1,0:T(8,128)(2,1)S(1)} %collective-permute-done.1.refs_4_), channel_id=1, source_target_pairs={{0,192},{64,0},{128,64},{192,128},{1,193},{65,1},{129,65},{193,129... | collective-permute-start | bytes 1572872 | tf_op jit(solution)/shard_map/ppermute | solution.py:25
  34.2 8.8 %collective-permute-done.2.refs_5_ = bf16[64,4096]{1,0:T(8,128)(2,1)} collective-permute-done((bf16[64,4096]{1,0:T(8,128)(2,1)S(1)}, bf16[64,4096]{1,0:T(8,128)(2,1)}, u32[]{:S(2)}, u32[]{:S(2)}) %collective-permute-start.2) | collective-permute-done | bytes 524320 | tf_op jit(solution)/shard_map/ppermute | solution.py:25
  42.9 4.0 %collective-permute-start.6 = (bf16[128,4096]{1,0:T(8,128)(2,1)S(1)}, bf16[128,4096]{1,0:T(8,128)(2,1)S(1)}, u32[]{:S(2)}, u32[]{:S(2)}) collective-permute-start(bf16[128,4096]{1,0:T(8,128)(2,1)S(1)} %bitcast.13), channel_id=1, source_target_pairs={{0,1},{1,0},{2,3},{3,2},{4,5},{5,4},{6,7},{7,6},{8,9},{9,8},{10,11... | collective-permute-start | bytes 3145736 | tf_op jit(solution)/shard_map/ppermute | solution.py:25
  46.9 2.3 %collective-permute-done.6.other = bf16[128,4096]{1,0:T(8,128)(2,1)S(1)} collective-permute-done((bf16[128,4096]{1,0:T(8,128)(2,1)S(1)}, bf16[128,4096]{1,0:T(8,128)(2,1)S(1)}, u32[]{:S(2)}, u32[]{:S(2)}) %collective-permute-start.6) | collective-permute-done | bytes 1048608 | tf_op jit(solution)/shard_map/ppermute | solution.py:25
  49.2 4.6 %shard_map.85 = (f32[512,256]{1,0:T(8,128)S(1)}, f32[64,2,256]{2,1,0:T(2,128)S(1)}) custom-call(s32[5]{0:T(128)S(1)} %pad_add_fusion.place, bf16[128,4096]{1,0:T(8,128)(2,1)S(1)} %bitcast.14, bf16[128,4096]{1,0:T(8,128)(2,1)S(1)} %collective-permute-done.6.other, bf16[128,4096]{1,0:T(8,128)(2,1)S(1)} %copy-done, ...), custom_call_target="tpu_custom_call" | custom-call | flops 1073741824 | bytes 6955028 | tf_op jit(solution)/shard_map/pallas_call | solution.py:48
  53.8 18.1 %all_to_all.25.table = f32[64,2,256]{2,1,0:T(2,128)S(1)} all-to-all(f32[64,2,256]{2,1,0:T(2,128)S(1)} %get-tuple-element.39), channel_id=1, replica_groups=mesh['row'=4,'col_0'=8,'col_1'=4,'col_2'=2] {'col_0','col_1','col_2'}, dimensions={0} | all-to-all | bytes 262144 | tf_op jit(solution)/shard_map/all_to_all | solution.py:198
  73.0 13.9 %all_to_all.26.table = f32[64,1,256]{2,1,0:T(1,128)S(1)} all-to-all(f32[64,1,256]{2,1,0:T(1,128)S(1)} %get-tuple-element.42), channel_id=1, replica_groups=mesh['row'=4,'col_0'=8,'col_1'=4,'col_2'=2] {'col_0','col_1','col_2'}, dimensions={0} | all-to-all | bytes 131072 | tf_op jit(solution)/shard_map/all_to_all | solution.py:205
  88.9 6.0 %shard_map.87 = (f32[8,256]{1,0:T(8,128)S(1)}, bf16[64,4096]{1,0:T(8,128)(2,1)}, bf16[64,4096]{1,0:T(8,128)(2,1)}, f32[64,4096]{1,0:T(8,128)S(1)}, bf16[64,4096]...) custom-call(s32[5]{0:T(128)S(1)} %pad_add_fusion.place, ...), custom_call_target="tpu_custom_call" | custom-call | flops 2147483648 | bytes 17391636 | tf_op jit(solution)/shard_map/pallas_call | solution.py:48
  94.9 1.3 copy-done.2
  97.6 1.3 collective-permute-start.12
  98.9 1.4 collective-permute-start.8
  100.3 1.4 %collective-permute-start.10 = (bf16[64,4096]{1,0:T(8,128)(2,1)}, bf16[64,4096]{1,0:T(8,128)(2,1)}, u32[]{:S(2)}, u32[]{:S(2)}) collective-permute-start(bf16[64,4096]{1,0:T(8,128)(2,1)} %get-tuple-element.51), channel_id=1, source_target_pairs={{0,192},{64,0},{128,64},{192,128},{1,193},{65,1},{129,65},{193,129... | collective-permute-start | bytes 1572872 | tf_op jit(solution)/shard_map/ppermute | solution.py:25
  101.8 1.8 %add_convert_fusion = bf16[128,4096]{1,0:T(8,128)(2,1)S(1)} fusion(f32[128,4096]{1,0:T(8,128)S(1)} %get-tuple-element.46, f32[128,4096]{1,0:T(8,128)} %collective-permute-done.7), kind=kLoop, calls=%fused_computation.1 | loop fusion | flops 1048576 | bytes 5242880 | tf_op jit(solution)/shard_map/convert_element_type | solution.py:233
  103.6 1.2 reshape.51
  104.8 4.7 %all-to-all-start.4 = ((bf16[32,4,4096]{2,1,0:T(4,128)(2,1)}), bf16[32,4,4096]{2,1,0:T(4,128)(2,1)}, u32[]{:S(2)}, u32[]{:S(2)}) async-start(bf16[32,4,4096]{2,1,0:T(4,128)(2,1)} %reshape.51), calls=%async_computation.4 | async-start | bytes 2097152 | tf_op jit(solution)/shard_map/all_to_all | solution.py:234
  109.4 3.1 %collective-permute-done.12 = bf16[64,4096]{1,0:T(8,128)(2,1)} collective-permute-done((bf16[64,4096]{1,0:T(8,128)(2,1)}, bf16[64,4096]{1,0:T(8,128)(2,1)}, u32[]{:S(2)}, u32[]{:S(2)}) %collective-permute-start.12) | collective-permute-done | bytes 524320 | tf_op jit(solution)/shard_map/ppermute | solution.py:25
  112.5 2.4 %add_convert_fusion.1 = bf16[64,4096]{1,0:T(8,128)(2,1)} fusion(f32[64,4096]{1,0:T(8,128)} %copy-done.4, bf16[64,4096]{1,0:T(8,128)(2,1)} %collective-permute-done.12), kind=kLoop, calls=%fused_computation.2 | loop fusion | flops 786432 | bytes 2097152 | tf_op jit(solution)/shard_map/convert_element_type | solution.py:222
  115.0 2.0 %add_convert_fusion.2 = bf16[64,4096]{1,0:T(8,128)(2,1)} fusion(f32[64,4096]{1,0:T(8,128)S(1)} %get-tuple-element.49, bf16[64,4096]{1,0:T(8,128)(2,1)} %collective-permute-done.8), kind=kLoop, calls=%fused_computation.3 | loop fusion | flops 786432 | bytes 2097152 | tf_op jit(solution)/shard_map/convert_element_type | solution.py:221
  117.0 2.6 %collective-permute-start.9 = (bf16[64,4096]{1,0:T(8,128)(2,1)}, bf16[64,4096]{1,0:T(8,128)(2,1)S(1)}, u32[]{:S(2)}, u32[]{:S(2)}) collective-permute-start(bf16[64,4096]{1,0:T(8,128)(2,1)} %add_convert_fusion.2), channel_id=1, source_target_pairs={{0,192},{64,0},{128,64},{192,128},{1,193},{65,1},{129,65},{193,129... | collective-permute-start | bytes 1572872 | tf_op jit(solution)/shard_map/ppermute | solution.py:25
  120.2 3.4 %collective-permute-done.10.back_high = bf16[64,4096]{1,0:T(8,128)(2,1)} collective-permute-done((bf16[64,4096]{1,0:T(8,128)(2,1)}, bf16[64,4096]{1,0:T(8,128)(2,1)}, u32[]{:S(2)}, u32[]{:S(2)}) %collective-permute-start.10) | collective-permute-done | bytes 524320 | tf_op jit(solution)/shard_map/ppermute | solution.py:25
  123.8 11.2 %collective-permute-done.13.ahead_high = bf16[64,4096]{1,0:T(8,128)(2,1)} collective-permute-done((bf16[64,4096]{1,0:T(8,128)(2,1)}, bf16[64,4096]{1,0:T(8,128)(2,1)}, u32[]{:S(2)}, u32[]{:S(2)}) %collective-permute-start.13) | collective-permute-done | bytes 524320 | tf_op jit(solution)/shard_map/ppermute | solution.py:25
  135.0 3.9 %shard_map.88 = f32[128,4096]{1,0:T(8,128)} custom-call(f32[128,4096]{1,0:T(8,128)S(1)} %copy-done.3, bf16[64,4096]{1,0:T(8,128)(2,1)S(1)} %collective-permute-done.9.back_low, bf16[64,4096]{1,0:T(8,128)(2,1)} %collective-permute-done.10.back_high, bf16[64,4096]{1,0:T(8,128)(2,1)} %collective-permute-done.11.ahead_low, ...), custom_call_target="tpu_custom_call" | custom-call | bytes 6291456 | tf_op jit(solution)/shard_map/pallas_call | solution.py:48
  138.9 1.9 %select_reduce_fusion = f32[4,4096]{1,0:T(4,128)S(1)} fusion(bf16[32,4,4096]{2,1,0:T(4,128)(2,1)} %all-to-all-done.4, pred[32]{0:T(512)(128)(4,1)S(1)} %iota_compare_fusion), kind=kLoop, calls=%fused_computation | loop fusion | flops 1556480 | bytes 1114144 | tf_op jit(solution)/shard_map/reduce_sum | solution.py:236
  140.9 1.6 %add_add_fusion = f32[4,4096]{1,0:T(4,128)} fusion(f32[4,4096]{1,0:T(4,128)S(1)} %select_reduce_fusion, f32[128,4096]{1,0:T(8,128)} %collective-permute-done.7, s32[]{:T(128)S(6)} %select_n.37, f32[128,4096]{1,0:T(8,128)} %copy-done.1), kind=kLoop, calls=%fused_computation.7 | loop fusion | flops 32768 | bytes 262148 | tf_op jit(solution)/shard_map/add | solution.py:236
  (62 shorter events, 8.1 us)
Async XLA Ops:
  0.6 5.9 %copy-start.9 = (bf16[4,4096]{1,0:T(4,128)(2,1)S(1)}, bf16[4,4096]{1,0:T(4,128)(2,1)}, u32[]{:S(2)}) copy-start(bf16[4,4096]{1,0:T(4,128)(2,1)} %param.6) | copy-start | bytes 98308
  0.6 17.5 %copy-start.10 = (s32[256,7]{0,1:T(8,128)S(1)}, s32[256,7]{0,1:T(8,128)}, u32[]{:S(2)}) copy-start(s32[256,7]{0,1:T(8,128)} %param.9) | copy-start | bytes 21508
  0.7 17.9 %copy-start.11 = (s32[256]{0:T(256)S(1)}, s32[256]{0:T(256)}, u32[]{:S(2)}) copy-start(s32[256]{0:T(256)} %param.8) | copy-start | bytes 3076
  3.0 22.7 %collective-permute-start = (bf16[64,4096]{1,0:T(8,128)(2,1)}, bf16[64,4096]{1,0:T(8,128)(2,1)S(1)}, u32[]{:S(2)}, u32[]{:S(2)}) collective-permute-start(bf16[64,4096]{1,0:T(8,128)(2,1)} %get-tuple-element.56), channel_id=1, source_target_pairs={{0,64},{64,128},{128,192},{192,0},{1,65},{65,129},{129,193},{193,1... | collective-permute-start | bytes 1572872 | tf_op jit(solution)/shard_map/ppermute | solution.py:25
  5.1 20.6 %collective-permute-start.1 = (bf16[64,4096]{1,0:T(8,128)(2,1)}, bf16[64,4096]{1,0:T(8,128)(2,1)S(1)}, u32[]{:S(2)}, u32[]{:S(2)}) collective-permute-start(bf16[64,4096]{1,0:T(8,128)(2,1)} %get-tuple-element.55), channel_id=1, source_target_pairs={{0,192},{64,0},{128,64},{192,128},{1,193},{65,1},{129,65},{193,129... | collective-permute-start | bytes 1572872 | tf_op jit(solution)/shard_map/ppermute | solution.py:25
  7.3 18.3 %all-to-all-start = ((bf16[8,4,4096]{2,1,0:T(4,128)(2,1)}), bf16[8,4,4096]{2,1,0:T(4,128)(2,1)S(1)}, u32[]{:S(2)}, u32[]{:S(2)}) async-start(bf16[8,4,4096]{2,1,0:T(4,128)(2,1)} %broadcast_in_dim.25), calls=%async_computation | async-start | bytes 524288 | tf_op jit(solution)/shard_map/all_to_all | solution.py:30
  15.5 18.7 %collective-permute-start.4 = (bf16[64,4096]{1,0:T(8,128)(2,1)}, bf16[64,4096]{1,0:T(8,128)(2,1)}, u32[]{:S(2)}, u32[]{:S(2)}) collective-permute-start(bf16[64,4096]{1,0:T(8,128)(2,1)} %get-tuple-element.55), channel_id=1, source_target_pairs={{0,64},{64,128},{128,192},{192,0},{1,65},{65,129},{129,193},{193,1... | collective-permute-start | bytes 1572872 | tf_op jit(solution)/shard_map/ppermute | solution.py:25
  15.5 18.6 %collective-permute-start.5 = (bf16[64,4096]{1,0:T(8,128)(2,1)}, bf16[64,4096]{1,0:T(8,128)(2,1)}, u32[]{:S(2)}, u32[]{:S(2)}) collective-permute-start(bf16[64,4096]{1,0:T(8,128)(2,1)} %get-tuple-element.56), channel_id=1, source_target_pairs={{0,192},{64,0},{128,64},{192,128},{1,193},{65,1},{129,65},{193,129... | collective-permute-start | bytes 1572872 | tf_op jit(solution)/shard_map/ppermute | solution.py:25
  19.4 11.6 %copy-start.12 = (f32[256]{0:T(256)S(1)}, f32[256]{0:T(256)}, u32[]{:S(2)}) copy-start(f32[256]{0:T(256)} %param.10) | copy-start | bytes 3076
  25.6 23.5 %copy-start.5 = (bf16[64,4096]{1,0:T(8,128)(2,1)}, bf16[64,4096]{1,0:T(8,128)(2,1)S(1)}, u32[]{:S(2)}) copy-start(bf16[64,4096]{1,0:T(8,128)(2,1)S(1)} %collective-permute-done.refs_1_) | copy-start | bytes 1572868
  25.7 23.5 %copy-start.7 = (bf16[64,4096]{1,0:T(8,128)(2,1)}, bf16[64,4096]{1,0:T(8,128)(2,1)S(1)}, u32[]{:S(2)}) copy-start(bf16[64,4096]{1,0:T(8,128)(2,1)S(1)} %collective-permute-done.1.refs_4_) | copy-start | bytes 1572868
  25.7 8.3 %copy-start.13 = (s32[4]{0:T(128)S(1)}, s32[4]{0:T(128)}, u32[]{:S(2)}) copy-start(s32[4]{0:T(128)} %constant.49) | copy-start | bytes 52
  25.7 23.4 %copy-start = (bf16[128,4096]{1,0:T(8,128)(2,1)S(1)}, bf16[128,4096]{1,0:T(8,128)(2,1)}, u32[]{:S(2)}) copy-start(bf16[128,4096]{1,0:T(8,128)(2,1)} %refs_0_.3) | copy-start | bytes 3145732
  26.8 16.1 %all-to-all-start.1 = ((bf16[4,32,4096]{2,1,0:T(8,128)(2,1)}), bf16[4,32,4096]{2,1,0:T(8,128)(2,1)S(1)}, u32[]{:S(2)}, u32[]{:S(2)}) async-start(bf16[4,32,4096]{2,1,0:T(8,128)(2,1)} %broadcast_in_dim.26), calls=%async_computation.1 | async-start | bytes 2097152 | tf_op jit(solution)/shard_map/all_to_all | solution.py:30
  31.1 11.9 %collective-permute-start.2 = (bf16[64,4096]{1,0:T(8,128)(2,1)S(1)}, bf16[64,4096]{1,0:T(8,128)(2,1)}, u32[]{:S(2)}, u32[]{:S(2)}) collective-permute-start(bf16[64,4096]{1,0:T(8,128)(2,1)S(1)} %collective-permute-done.refs_1_), channel_id=1, source_target_pairs={{0,64},{64,128},{128,192},{192,0},{1,65},{65,129},{129,193},{193,1... | collective-permute-start | bytes 1572872 | tf_op jit(solution)/shard_map/ppermute | solution.py:25
  31.2 11.8 %collective-permute-start.3 = (bf16[64,4096]{1,0:T(8,128)(2,1)S(1)}, bf16[64,4096]{1,0:T(8,128)(2,1)}, u32[]{:S(2)}, u32[]{:S(2)}) collective-permute-start(bf16[64,4096]{1,0:T(8,128)(2,1)S(1)} %collective-permute-done.1.refs_4_), channel_id=1, source_target_pairs={{0,192},{64,0},{128,64},{192,128},{1,193},{65,1},{129,65},{193,129... | collective-permute-start | bytes 1572872 | tf_op jit(solution)/shard_map/ppermute | solution.py:25
  42.9 6.2 %collective-permute-start.6 = (bf16[128,4096]{1,0:T(8,128)(2,1)S(1)}, bf16[128,4096]{1,0:T(8,128)(2,1)S(1)}, u32[]{:S(2)}, u32[]{:S(2)}) collective-permute-start(bf16[128,4096]{1,0:T(8,128)(2,1)S(1)} %bitcast.13), channel_id=1, source_target_pairs={{0,1},{1,0},{2,3},{3,2},{4,5},{5,4},{6,7},{7,6},{8,9},{9,8},{10,11... | collective-permute-start | bytes 3145736 | tf_op jit(solution)/shard_map/ppermute | solution.py:25
  86.8 1.0 copy-start.6
  87.9 1.0 copy-start.8
  94.9 1.3 copy-start.2
  96.2 1.0 copy-start.4
  97.2 4.5 %copy-start.1 = (f32[128,4096]{1,0:T(8,128)}, f32[128,4096]{1,0:T(8,128)S(1)}, u32[]{:S(2)}) copy-start(f32[128,4096]{1,0:T(8,128)S(1)} %get-tuple-element.46) | copy-start | bytes 6291460
  97.2 4.5 %collective-permute-start.7 = (f32[128,4096]{1,0:T(8,128)S(1)}, f32[128,4096]{1,0:T(8,128)}, u32[]{:S(2)}, u32[]{:S(2)}) collective-permute-start(f32[128,4096]{1,0:T(8,128)S(1)} %get-tuple-element.47), channel_id=1, source_target_pairs={{0,1},{1,0},{2,3},{3,2},{4,5},{5,4},{6,7},{7,6},{8,9},{9,8},{10,11... | collective-permute-start | bytes 6291464 | tf_op jit(solution)/shard_map/ppermute | solution.py:25
  97.6 14.9 %collective-permute-start.12 = (bf16[64,4096]{1,0:T(8,128)(2,1)}, bf16[64,4096]{1,0:T(8,128)(2,1)}, u32[]{:S(2)}, u32[]{:S(2)}) collective-permute-start(bf16[64,4096]{1,0:T(8,128)(2,1)} %get-tuple-element.54), channel_id=1, source_target_pairs={{0,64},{64,128},{128,192},{192,0},{1,65},{65,129},{129,193},{193,1... | collective-permute-start | bytes 1572872 | tf_op jit(solution)/shard_map/ppermute | solution.py:25
  98.9 16.1 %collective-permute-start.8 = (bf16[64,4096]{1,0:T(8,128)(2,1)}, bf16[64,4096]{1,0:T(8,128)(2,1)}, u32[]{:S(2)}, u32[]{:S(2)}) collective-permute-start(bf16[64,4096]{1,0:T(8,128)(2,1)} %get-tuple-element.50), channel_id=1, source_target_pairs={{0,192},{64,0},{128,64},{192,128},{1,193},{65,1},{129,65},{193,129... | collective-permute-start | bytes 1572872 | tf_op jit(solution)/shard_map/ppermute | solution.py:25
  100.3 23.2 %collective-permute-start.10 = (bf16[64,4096]{1,0:T(8,128)(2,1)}, bf16[64,4096]{1,0:T(8,128)(2,1)}, u32[]{:S(2)}, u32[]{:S(2)}) collective-permute-start(bf16[64,4096]{1,0:T(8,128)(2,1)} %get-tuple-element.51), channel_id=1, source_target_pairs={{0,192},{64,0},{128,64},{192,128},{1,193},{65,1},{129,65},{193,129... | collective-permute-start | bytes 1572872 | tf_op jit(solution)/shard_map/ppermute | solution.py:25
  101.7 22.0 %collective-permute-start.11 = (bf16[64,4096]{1,0:T(8,128)(2,1)}, bf16[64,4096]{1,0:T(8,128)(2,1)}, u32[]{:S(2)}, u32[]{:S(2)}) collective-permute-start(bf16[64,4096]{1,0:T(8,128)(2,1)} %get-tuple-element.52), channel_id=1, source_target_pairs={{0,64},{64,128},{128,192},{192,0},{1,65},{65,129},{129,193},{193,1... | collective-permute-start | bytes 1572872 | tf_op jit(solution)/shard_map/ppermute | solution.py:25
  104.8 34.1 %all-to-all-start.4 = ((bf16[32,4,4096]{2,1,0:T(4,128)(2,1)}), bf16[32,4,4096]{2,1,0:T(4,128)(2,1)}, u32[]{:S(2)}, u32[]{:S(2)}) async-start(bf16[32,4,4096]{2,1,0:T(4,128)(2,1)} %reshape.51), calls=%async_computation.4 | async-start | bytes 2097152 | tf_op jit(solution)/shard_map/all_to_all | solution.py:234
  112.5 22.5 %copy-start.3 = (f32[128,4096]{1,0:T(8,128)S(1)}, f32[128,4096]{1,0:T(8,128)}, u32[]{:S(2)}) copy-start(f32[128,4096]{1,0:T(8,128)} %copy-done.2) | copy-start | bytes 6291460
  114.9 20.1 %collective-permute-start.13 = (bf16[64,4096]{1,0:T(8,128)(2,1)}, bf16[64,4096]{1,0:T(8,128)(2,1)}, u32[]{:S(2)}, u32[]{:S(2)}) collective-permute-start(bf16[64,4096]{1,0:T(8,128)(2,1)} %add_convert_fusion.1), channel_id=1, source_target_pairs={{0,64},{64,128},{128,192},{192,0},{1,65},{65,129},{129,193},{193,1... | collective-permute-start | bytes 1572872 | tf_op jit(solution)/shard_map/ppermute | solution.py:25
  117.0 18.0 %collective-permute-start.9 = (bf16[64,4096]{1,0:T(8,128)(2,1)}, bf16[64,4096]{1,0:T(8,128)(2,1)S(1)}, u32[]{:S(2)}, u32[]{:S(2)}) collective-permute-start(bf16[64,4096]{1,0:T(8,128)(2,1)} %add_convert_fusion.2), channel_id=1, source_target_pairs={{0,192},{64,0},{128,64},{192,128},{1,193},{65,1},{129,65},{193,129... | collective-permute-start | bytes 1572872 | tf_op jit(solution)/shard_map/ppermute | solution.py:25

commit v4 on v3

--- a/solution.py
+++ b/solution.py
@@ -34,7 +34,7 @@
     return jax.ShapeDtypeStruct(dims, dtype)
 
 
-def call(body, outs, args, flops=0, scalars=0, tiled=(), scratch=()):
+def call(body, outs, args, flops=0, scalars=0, tiled=(), scratch=(), outside=()):
     size = sum(a.size * a.dtype.itemsize for a in (*args, *outs))
     specs = []
     for k, a in enumerate((*args, *outs)):
@@ -44,6 +44,15 @@
             specs.append(pl.BlockSpec((a.shape[0], TILE), lambda i: (0, i)))
         else:
             specs.append(pl.BlockSpec(a.shape, lambda i, n=len(a.shape): (0,) * n))
+    kinds = [pltpu.HBM if k in outside else None for k in range(len(specs))]
+    args = [
+        a if kind is None else pltpu.with_memory_space_constraint(a, kind)
+        for a, kind in zip(args, kinds)
+    ]
+    outs = [
+        o if kind is None else pltpu.HBM(o.shape, o.dtype)
+        for o, kind in zip(outs, kinds[len(args) :])
+    ]
     steps = (*args, *outs)[tiled[0]].shape[1] // TILE if tiled else 1
     return pl.pallas_call(
         body,
@@ -213,6 +222,7 @@
         scalars=1,
         tiled=(*range(5, 14), *range(15, 24)),
         scratch=[pltpu.VMEM((pool, total), BF16), pltpu.VMEM((total, pool), BF16)],
+        outside=(15, 16, 17, 18, 19, 20, 21, 22, 23),
     )
 
     low, high = shifted(low, Y, -1), shifted(high, Y, 1)
@@ -220,12 +230,6 @@
     theirs = shifted(theirs, CORE, 1)
     back_low = shifted((back_low + low.astype(F32)).astype(BF16), Y, -1)
     ahead_high = shifted((ahead_high + high.astype(F32)).astype(BF16), Y, 1)
-    grad_passages = call(
-        total_body,
-        [shape((count, width), F32)],
-        [here, back_low, back_high, ahead_low, ahead_high],
-        tiled=range(6),
-    )[0]
 
     place_of = across * depth + far
     at = place_of * rows
@@ -235,6 +239,13 @@
     others = (lax.iota(jnp.int32, breadth * depth) != place_of)[:, None, None]
     grad_queries = exact + jnp.sum(jnp.where(others, parts.astype(F32), 0.0), axis=0)
 
+    grad_passages = call(
+        total_body,
+        [shape((count, width), F32)],
+        [here, back_low, back_high, ahead_low, ahead_high],
+        tiled=range(6),
+    )[0]
+
     row_losses = lax.dynamic_slice_in_dim(losses[0], at, rows, 0)
     return row_losses, grad_queries, grad_passages
 

time: 143 us -> 140 us (0.979)
  local copies, waits for them, and re-layouts: 11.8 us -> 8.25 us
  waiting for transfers between devices: 35.3 us -> 33.6 us
    unnamed x28 -> x18, local copies, waits for them, and re-layouts: 4.4 us -> 0.83 us
    ppermute x14, waiting for transfers between devices: 29 us -> 27.4 us  [shifted(): return lax.ppermute(value, axis, [(i, (i + step) % n) for i in range(n)])]
  transfers between devices with their start and end apart: 17 -> 17, of which waited for: 7 -> 7; matrix products, arithmetic and copies ran while one was open for 8% -> 9% of each run, Pallas kernels for 3% -> 3%
where the time goes in v4:
time: 140 us; the launch traced here: 139 us
  starting transfers between devices  37.1 us (26%)
  waiting for transfers between devices  33.6 us (24%)
  blocking collectives  32 us (23%)
  Pallas kernels  16.4 us (12%)
  other arithmetic  10.7 us (8%)
  local copies, waits for them, and re-layouts  8.25 us (6%)
    all_to_all x2, blocking collectives, on_device(): table = lax.all_to_all(table, COL, 0, 0, tiled=True)  32 us
    ppermute x14, waiting for transfers between devices, shifted(): return lax.ppermute(value, axis, [(i, (i + step) % n) for i in range(n)])  27.4 us
    ppermute x14, starting transfers between devices, shifted(): return lax.ppermute(value, axis, [(i, (i + step) % n) for i in range(n)])  20.2 us
    pallas_call x4, Pallas kernels, call(): pl.pallas_call(body, grid=(steps,), out_shape=outs, in_specs=specs[:len(a...  16.4 us
    all_to_all x2, starting transfers between devices, copies(): lax.all_to_all(jnp.broadcast_to(value, (n, *value.shape)), axis, 0, 0, ti...  12.2 us
    all_to_all x2, waiting for transfers between devices, copies(): lax.all_to_all(jnp.broadcast_to(value, (n, *value.shape)), axis, 0, 0, ti...  6.29 us
    all_to_all x1, starting transfers between devices, on_device(): parts = lax.all_to_all(sent, (X, Z), 0, 0, tiled=True)  4.67 us
  transfers between devices with their start and end apart: 17, of which 7 were waited for; matrix products, arithmetic and copies ran while one was open for 9% of the time, Pallas kernels for 3%

profile of v4, /device:TPU:1, one launch (start us, length us, event | category | flops | bytes accessed | tf_op | source)
XLA Modules:
  0.0 138.9 jit_solution(9154783350684534930)
XLA Ops:
  0.7 2.3 %fusion.4 = (bf16[64,4096]{1,0:T(8,128)(2,1)}, bf16[64,4096]{1,0:T(8,128)(2,1)}) fusion(bf16[128,4096]{1,0:T(8,128)(2,1)} %refs_0_.3), kind=kLoop, calls=%fused_computation.18 | loop fusion | bytes 2097152 | tf_op jit(solution)/shard_map/slice | solution.py:174
  3.0 2.1 %collective-permute-start = (bf16[64,4096]{1,0:T(8,128)(2,1)}, bf16[64,4096]{1,0:T(8,128)(2,1)S(1)}, u32[]{:S(2)}, u32[]{:S(2)}) collective-permute-start(bf16[64,4096]{1,0:T(8,128)(2,1)} %get-tuple-element.56), channel_id=1, source_target_pairs={{0,64},{64,128},{128,192},{192,0},{1,65},{65,129},{129,193},{193,1... | collective-permute-start | bytes 1572872 | tf_op jit(solution)/shard_map/ppermute | solution.py:25
  5.1 1.4 %collective-permute-start.1 = (bf16[64,4096]{1,0:T(8,128)(2,1)}, bf16[64,4096]{1,0:T(8,128)(2,1)S(1)}, u32[]{:S(2)}, u32[]{:S(2)}) collective-permute-start(bf16[64,4096]{1,0:T(8,128)(2,1)} %get-tuple-element.55), channel_id=1, source_target_pairs={{0,192},{64,0},{128,64},{192,128},{1,193},{65,1},{129,65},{193,129... | collective-permute-start | bytes 1572872 | tf_op jit(solution)/shard_map/ppermute | solution.py:25
  7.3 8.2 %all-to-all-start = ((bf16[8,4,4096]{2,1,0:T(4,128)(2,1)}), bf16[8,4,4096]{2,1,0:T(4,128)(2,1)S(1)}, u32[]{:S(2)}, u32[]{:S(2)}) async-start(bf16[8,4,4096]{2,1,0:T(4,128)(2,1)} %broadcast_in_dim.25), calls=%async_computation | async-start | bytes 524288 | tf_op jit(solution)/shard_map/all_to_all | solution.py:30
  15.5 2.7 %collective-permute-start.5 = (bf16[64,4096]{1,0:T(8,128)(2,1)}, bf16[64,4096]{1,0:T(8,128)(2,1)}, u32[]{:S(2)}, u32[]{:S(2)}) collective-permute-start(bf16[64,4096]{1,0:T(8,128)(2,1)} %get-tuple-element.56), channel_id=1, source_target_pairs={{0,192},{64,0},{128,64},{192,128},{1,193},{65,1},{129,65},{193,129... | collective-permute-start | bytes 1572872 | tf_op jit(solution)/shard_map/ppermute | solution.py:25
  19.4 6.3 %all-to-all-done = bf16[8,4,4096]{2,1,0:T(4,128)(2,1)S(1)} async-done(((bf16[8,4,4096]{2,1,0:T(4,128)(2,1)}), bf16[8,4,4096]{2,1,0:T(4,128)(2,1)S(1)}, u32[]{:S(2)}, u32[]{:S(2)}) %all-to-all-start) | async-done | bytes 262176 | tf_op jit(solution)/shard_map/all_to_all | solution.py:30
  25.7 1.1 broadcast_in_dim.26
  26.8 4.0 %all-to-all-start.1 = ((bf16[4,32,4096]{2,1,0:T(8,128)(2,1)}), bf16[4,32,4096]{2,1,0:T(8,128)(2,1)S(1)}, u32[]{:S(2)}, u32[]{:S(2)}) async-start(bf16[4,32,4096]{2,1,0:T(8,128)(2,1)} %broadcast_in_dim.26), calls=%async_computation.1 | async-start | bytes 2097152 | tf_op jit(solution)/shard_map/all_to_all | solution.py:30
  31.2 2.7 %collective-permute-start.3 = (bf16[64,4096]{1,0:T(8,128)(2,1)S(1)}, bf16[64,4096]{1,0:T(8,128)(2,1)}, u32[]{:S(2)}, u32[]{:S(2)}) collective-permute-start(bf16[64,4096]{1,0:T(8,128)(2,1)S(1)} %collective-permute-done.1.refs_4_), channel_id=1, source_target_pairs={{0,192},{64,0},{128,64},{192,128},{1,193},{65,1},{129,65},{193,129... | collective-permute-start | bytes 1572872 | tf_op jit(solution)/shard_map/ppermute | solution.py:25
  34.1 8.8 %collective-permute-done.2.refs_5_ = bf16[64,4096]{1,0:T(8,128)(2,1)} collective-permute-done((bf16[64,4096]{1,0:T(8,128)(2,1)S(1)}, bf16[64,4096]{1,0:T(8,128)(2,1)}, u32[]{:S(2)}, u32[]{:S(2)}) %collective-permute-start.2) | collective-permute-done | bytes 524320 | tf_op jit(solution)/shard_map/ppermute | solution.py:25
  42.9 4.0 %collective-permute-start.6 = (bf16[128,4096]{1,0:T(8,128)(2,1)S(1)}, bf16[128,4096]{1,0:T(8,128)(2,1)S(1)}, u32[]{:S(2)}, u32[]{:S(2)}) collective-permute-start(bf16[128,4096]{1,0:T(8,128)(2,1)S(1)} %bitcast.13), channel_id=1, source_target_pairs={{0,1},{1,0},{2,3},{3,2},{4,5},{5,4},{6,7},{7,6},{8,9},{9,8},{10,11... | collective-permute-start | bytes 3145736 | tf_op jit(solution)/shard_map/ppermute | solution.py:25
  46.9 2.3 %collective-permute-done.6.other = bf16[128,4096]{1,0:T(8,128)(2,1)S(1)} collective-permute-done((bf16[128,4096]{1,0:T(8,128)(2,1)S(1)}, bf16[128,4096]{1,0:T(8,128)(2,1)S(1)}, u32[]{:S(2)}, u32[]{:S(2)}) %collective-permute-start.6) | collective-permute-done | bytes 1048608 | tf_op jit(solution)/shard_map/ppermute | solution.py:25
  49.2 4.6 %shard_map.85 = (f32[512,256]{1,0:T(8,128)S(1)}, f32[64,2,256]{2,1,0:T(2,128)S(1)}) custom-call(s32[5]{0:T(128)S(1)} %pad_add_fusion.place, bf16[128,4096]{1,0:T(8,128)(2,1)S(1)} %bitcast.14, bf16[128,4096]{1,0:T(8,128)(2,1)S(1)} %collective-permute-done.6.other, bf16[128,4096]{1,0:T(8,128)(2,1)S(1)} %copy-done, ...), custom_call_target="tpu_custom_call" | custom-call | flops 1073741824 | bytes 6955028 | tf_op jit(solution)/shard_map/pallas_call | solution.py:57
  53.7 18.1 %all_to_all.25.table = f32[64,2,256]{2,1,0:T(2,128)S(1)} all-to-all(f32[64,2,256]{2,1,0:T(2,128)S(1)} %get-tuple-element.39), channel_id=1, replica_groups=mesh['row'=4,'col_0'=8,'col_1'=4,'col_2'=2] {'col_0','col_1','col_2'}, dimensions={0} | all-to-all | bytes 262144 | tf_op jit(solution)/shard_map/all_to_all | solution.py:207
  71.8 1.1 shard_map.86
  72.9 13.9 %all_to_all.26.table = f32[64,1,256]{2,1,0:T(1,128)S(1)} all-to-all(f32[64,1,256]{2,1,0:T(1,128)S(1)} %get-tuple-element.42), channel_id=1, replica_groups=mesh['row'=4,'col_0'=8,'col_1'=4,'col_2'=2] {'col_0','col_1','col_2'}, dimensions={0} | all-to-all | bytes 131072 | tf_op jit(solution)/shard_map/all_to_all | solution.py:214
  86.8 7.0 %shard_map.87 = (f32[8,256]{1,0:T(8,128)S(1)}, bf16[64,4096]{1,0:T(8,128)(2,1)}, bf16[64,4096]{1,0:T(8,128)(2,1)}, f32[64,4096]{1,0:T(8,128)}, bf16[64,4096]{1,0...) custom-call(s32[5]{0:T(128)S(1)} %pad_add_fusion.place, ...), custom_call_target="tpu_custom_call" | custom-call | flops 2147483648 | bytes 17391636 | tf_op jit(solution)/shard_map/pallas_call | solution.py:57
  94.3 1.3 collective-permute-start.12
  95.6 1.4 collective-permute-start.8
  97.0 1.4 %collective-permute-start.10 = (bf16[64,4096]{1,0:T(8,128)(2,1)}, bf16[64,4096]{1,0:T(8,128)(2,1)S(1)}, u32[]{:S(2)}, u32[]{:S(2)}) collective-permute-start(bf16[64,4096]{1,0:T(8,128)(2,1)} %get-tuple-element.51), channel_id=1, source_target_pairs={{0,192},{64,0},{128,64},{192,128},{1,193},{65,1},{129,65},{193,129... | collective-permute-start | bytes 1572872 | tf_op jit(solution)/shard_map/ppermute | solution.py:25
  98.5 2.4 %add_convert_fusion = bf16[128,4096]{1,0:T(8,128)(2,1)S(1)} fusion(f32[128,4096]{1,0:T(8,128)} %get-tuple-element.46, f32[128,4096]{1,0:T(8,128)} %collective-permute-done.7), kind=kLoop, calls=%fused_computation.1 | loop fusion | flops 1048576 | bytes 5242880 | tf_op jit(solution)/shard_map/convert_element_type | solution.py:237
  100.9 1.2 reshape.51
  102.2 4.7 %all-to-all-start.4 = ((bf16[32,4,4096]{2,1,0:T(4,128)(2,1)}), bf16[32,4,4096]{2,1,0:T(4,128)(2,1)}, u32[]{:S(2)}, u32[]{:S(2)}) async-start(bf16[32,4,4096]{2,1,0:T(4,128)(2,1)} %reshape.51), calls=%async_computation.4 | async-start | bytes 2097152 | tf_op jit(solution)/shard_map/all_to_all | solution.py:238
  106.8 2.2 %collective-permute-done.12 = bf16[64,4096]{1,0:T(8,128)(2,1)S(1)} collective-permute-done((bf16[64,4096]{1,0:T(8,128)(2,1)}, bf16[64,4096]{1,0:T(8,128)(2,1)S(1)}, u32[]{:S(2)}, u32[]{:S(2)}) %collective-permute-start.12) | collective-permute-done | bytes 524320 | tf_op jit(solution)/shard_map/ppermute | solution.py:25
  109.8 2.4 %add_convert_fusion.1 = bf16[64,4096]{1,0:T(8,128)(2,1)} fusion(f32[64,4096]{1,0:T(8,128)} %get-tuple-element.53, bf16[64,4096]{1,0:T(8,128)(2,1)} %copy-done.3), kind=kLoop, calls=%fused_computation.2 | loop fusion | flops 786432 | bytes 2097152 | tf_op jit(solution)/shard_map/convert_element_type | solution.py:232
  112.4 2.0 %add_convert_fusion.2 = bf16[64,4096]{1,0:T(8,128)(2,1)} fusion(f32[64,4096]{1,0:T(8,128)S(1)} %copy-done.2, bf16[64,4096]{1,0:T(8,128)(2,1)} %collective-permute-done.8), kind=kLoop, calls=%fused_computation.3 | loop fusion | flops 786432 | bytes 2097152 | tf_op jit(solution)/shard_map/convert_element_type | solution.py:231
  114.4 2.5 %collective-permute-start.9 = (bf16[64,4096]{1,0:T(8,128)(2,1)}, bf16[64,4096]{1,0:T(8,128)(2,1)}, u32[]{:S(2)}, u32[]{:S(2)}) collective-permute-start(bf16[64,4096]{1,0:T(8,128)(2,1)} %add_convert_fusion.2), channel_id=1, source_target_pairs={{0,192},{64,0},{128,64},{192,128},{1,193},{65,1},{129,65},{193,129... | collective-permute-start | bytes 1572872 | tf_op jit(solution)/shard_map/ppermute | solution.py:25
  117.5 2.6 %collective-permute-done.10.back_high = bf16[64,4096]{1,0:T(8,128)(2,1)S(1)} collective-permute-done((bf16[64,4096]{1,0:T(8,128)(2,1)}, bf16[64,4096]{1,0:T(8,128)(2,1)S(1)}, u32[]{:S(2)}, u32[]{:S(2)}) %collective-permute-start.10) | collective-permute-done | bytes 524320 | tf_op jit(solution)/shard_map/ppermute | solution.py:25
  120.3 11.2 %collective-permute-done.13.ahead_high = bf16[64,4096]{1,0:T(8,128)(2,1)} collective-permute-done((bf16[64,4096]{1,0:T(8,128)(2,1)}, bf16[64,4096]{1,0:T(8,128)(2,1)}, u32[]{:S(2)}, u32[]{:S(2)}) %collective-permute-start.13) | collective-permute-done | bytes 524320 | tf_op jit(solution)/shard_map/ppermute | solution.py:25
  131.6 3.8 %shard_map.88 = f32[128,4096]{1,0:T(8,128)} custom-call(f32[128,4096]{1,0:T(8,128)S(1)} %copy-done.1, bf16[64,4096]{1,0:T(8,128)(2,1)} %collective-permute-done.9.back_low, bf16[64,4096]{1,0:T(8,128)(2,1)S(1)} %collective-permute-done.10.back_high, bf16[64,4096]{1,0:T(8,128)(2,1)S(1)} %collective-permute-done.11.ahead_low, ...), custom_call_target="tpu_custom_call" | custom-call | bytes 6291456 | tf_op jit(solution)/shard_map/pallas_call | solution.py:57
  135.4 1.9 %select_reduce_fusion = f32[4,4096]{1,0:T(4,128)S(1)} fusion(bf16[32,4,4096]{2,1,0:T(4,128)(2,1)} %all-to-all-done.4, pred[32]{0:T(512)(128)(4,1)S(1)} %iota_compare_fusion), kind=kLoop, calls=%fused_computation | loop fusion | flops 1556480 | bytes 1114144 | tf_op jit(solution)/shard_map/reduce_sum | solution.py:240
  137.3 1.6 %add_add_fusion = f32[4,4096]{1,0:T(4,128)} fusion(f32[4,4096]{1,0:T(4,128)S(1)} %select_reduce_fusion, f32[128,4096]{1,0:T(8,128)} %collective-permute-done.7, s32[]{:T(128)S(6)} %select_n.37, f32[128,4096]{1,0:T(8,128)} %get-tuple-element.46), kind=kLoop, calls=%fused_computation.7 | loop fusion | flops 32768 | bytes 262148 | tf_op jit(solution)/shard_map/add | solution.py:240
  (52 shorter events, 5.0 us)
Async XLA Ops:
  0.6 5.9 %copy-start.4 = (bf16[4,4096]{1,0:T(4,128)(2,1)S(1)}, bf16[4,4096]{1,0:T(4,128)(2,1)}, u32[]{:S(2)}) copy-start(bf16[4,4096]{1,0:T(4,128)(2,1)} %param.6) | copy-start | bytes 98308
  0.6 17.5 %copy-start.5 = (s32[256,7]{0,1:T(8,128)S(1)}, s32[256,7]{0,1:T(8,128)}, u32[]{:S(2)}) copy-start(s32[256,7]{0,1:T(8,128)} %param.9) | copy-start | bytes 21508
  0.7 17.9 %copy-start.6 = (s32[256]{0:T(256)S(1)}, s32[256]{0:T(256)}, u32[]{:S(2)}) copy-start(s32[256]{0:T(256)} %param.8) | copy-start | bytes 3076
  3.0 22.7 %collective-permute-start = (bf16[64,4096]{1,0:T(8,128)(2,1)}, bf16[64,4096]{1,0:T(8,128)(2,1)S(1)}, u32[]{:S(2)}, u32[]{:S(2)}) collective-permute-start(bf16[64,4096]{1,0:T(8,128)(2,1)} %get-tuple-element.56), channel_id=1, source_target_pairs={{0,64},{64,128},{128,192},{192,0},{1,65},{65,129},{129,193},{193,1... | collective-permute-start | bytes 1572872 | tf_op jit(solution)/shard_map/ppermute | solution.py:25
  5.1 20.6 %collective-permute-start.1 = (bf16[64,4096]{1,0:T(8,128)(2,1)}, bf16[64,4096]{1,0:T(8,128)(2,1)S(1)}, u32[]{:S(2)}, u32[]{:S(2)}) collective-permute-start(bf16[64,4096]{1,0:T(8,128)(2,1)} %get-tuple-element.55), channel_id=1, source_target_pairs={{0,192},{64,0},{128,64},{192,128},{1,193},{65,1},{129,65},{193,129... | collective-permute-start | bytes 1572872 | tf_op jit(solution)/shard_map/ppermute | solution.py:25
  7.3 18.3 %all-to-all-start = ((bf16[8,4,4096]{2,1,0:T(4,128)(2,1)}), bf16[8,4,4096]{2,1,0:T(4,128)(2,1)S(1)}, u32[]{:S(2)}, u32[]{:S(2)}) async-start(bf16[8,4,4096]{2,1,0:T(4,128)(2,1)} %broadcast_in_dim.25), calls=%async_computation | async-start | bytes 524288 | tf_op jit(solution)/shard_map/all_to_all | solution.py:30
  15.5 18.6 %collective-permute-start.4 = (bf16[64,4096]{1,0:T(8,128)(2,1)}, bf16[64,4096]{1,0:T(8,128)(2,1)}, u32[]{:S(2)}, u32[]{:S(2)}) collective-permute-start(bf16[64,4096]{1,0:T(8,128)(2,1)} %get-tuple-element.55), channel_id=1, source_target_pairs={{0,64},{64,128},{128,192},{192,0},{1,65},{65,129},{129,193},{193,1... | collective-permute-start | bytes 1572872 | tf_op jit(solution)/shard_map/ppermute | solution.py:25
  15.5 18.6 %collective-permute-start.5 = (bf16[64,4096]{1,0:T(8,128)(2,1)}, bf16[64,4096]{1,0:T(8,128)(2,1)}, u32[]{:S(2)}, u32[]{:S(2)}) collective-permute-start(bf16[64,4096]{1,0:T(8,128)(2,1)} %get-tuple-element.56), channel_id=1, source_target_pairs={{0,192},{64,0},{128,64},{192,128},{1,193},{65,1},{129,65},{193,129... | collective-permute-start | bytes 1572872 | tf_op jit(solution)/shard_map/ppermute | solution.py:25
  19.4 11.6 %copy-start.7 = (f32[256]{0:T(256)S(1)}, f32[256]{0:T(256)}, u32[]{:S(2)}) copy-start(f32[256]{0:T(256)} %param.10) | copy-start | bytes 3076
  25.7 8.3 %copy-start.8 = (s32[4]{0:T(128)S(1)}, s32[4]{0:T(128)}, u32[]{:S(2)}) copy-start(s32[4]{0:T(128)} %constant.49) | copy-start | bytes 52
  25.7 23.4 %copy-start = (bf16[128,4096]{1,0:T(8,128)(2,1)S(1)}, bf16[128,4096]{1,0:T(8,128)(2,1)}, u32[]{:S(2)}) copy-start(bf16[128,4096]{1,0:T(8,128)(2,1)} %refs_0_.3) | copy-start | bytes 3145732
  26.8 16.1 %all-to-all-start.1 = ((bf16[4,32,4096]{2,1,0:T(8,128)(2,1)}), bf16[4,32,4096]{2,1,0:T(8,128)(2,1)S(1)}, u32[]{:S(2)}, u32[]{:S(2)}) async-start(bf16[4,32,4096]{2,1,0:T(8,128)(2,1)} %broadcast_in_dim.26), calls=%async_computation.1 | async-start | bytes 2097152 | tf_op jit(solution)/shard_map/all_to_all | solution.py:30
  31.1 11.9 %collective-permute-start.2 = (bf16[64,4096]{1,0:T(8,128)(2,1)S(1)}, bf16[64,4096]{1,0:T(8,128)(2,1)}, u32[]{:S(2)}, u32[]{:S(2)}) collective-permute-start(bf16[64,4096]{1,0:T(8,128)(2,1)S(1)} %collective-permute-done.refs_1_), channel_id=1, source_target_pairs={{0,64},{64,128},{128,192},{192,0},{1,65},{65,129},{129,193},{193,1... | collective-permute-start | bytes 1572872 | tf_op jit(solution)/shard_map/ppermute | solution.py:25
  31.2 11.8 %collective-permute-start.3 = (bf16[64,4096]{1,0:T(8,128)(2,1)S(1)}, bf16[64,4096]{1,0:T(8,128)(2,1)}, u32[]{:S(2)}, u32[]{:S(2)}) collective-permute-start(bf16[64,4096]{1,0:T(8,128)(2,1)S(1)} %collective-permute-done.1.refs_4_), channel_id=1, source_target_pairs={{0,192},{64,0},{128,64},{192,128},{1,193},{65,1},{129,65},{193,129... | collective-permute-start | bytes 1572872 | tf_op jit(solution)/shard_map/ppermute | solution.py:25
  42.9 6.2 %collective-permute-start.6 = (bf16[128,4096]{1,0:T(8,128)(2,1)S(1)}, bf16[128,4096]{1,0:T(8,128)(2,1)S(1)}, u32[]{:S(2)}, u32[]{:S(2)}) collective-permute-start(bf16[128,4096]{1,0:T(8,128)(2,1)S(1)} %bitcast.13), channel_id=1, source_target_pairs={{0,1},{1,0},{2,3},{3,2},{4,5},{5,4},{6,7},{7,6},{8,9},{9,8},{10,11... | collective-permute-start | bytes 3145736 | tf_op jit(solution)/shard_map/ppermute | solution.py:25
  93.9 4.6 %collective-permute-start.7 = (f32[128,4096]{1,0:T(8,128)}, f32[128,4096]{1,0:T(8,128)}, u32[]{:S(2)}, u32[]{:S(2)}) collective-permute-start(f32[128,4096]{1,0:T(8,128)} %get-tuple-element.47), channel_id=1, source_target_pairs={{0,1},{1,0},{2,3},{3,2},{4,5},{5,4},{6,7},{7,6},{8,9},{9,8},{10,11... | collective-permute-start | bytes 6291464 | tf_op jit(solution)/shard_map/ppermute | solution.py:25
  94.3 14.7 %collective-permute-start.12 = (bf16[64,4096]{1,0:T(8,128)(2,1)}, bf16[64,4096]{1,0:T(8,128)(2,1)S(1)}, u32[]{:S(2)}, u32[]{:S(2)}) collective-permute-start(bf16[64,4096]{1,0:T(8,128)(2,1)} %get-tuple-element.54), channel_id=1, source_target_pairs={{0,64},{64,128},{128,192},{192,0},{1,65},{65,129},{129,193},{193,1... | collective-permute-start | bytes 1572872 | tf_op jit(solution)/shard_map/ppermute | solution.py:25
  95.6 16.8 %collective-permute-start.8 = (bf16[64,4096]{1,0:T(8,128)(2,1)}, bf16[64,4096]{1,0:T(8,128)(2,1)}, u32[]{:S(2)}, u32[]{:S(2)}) collective-permute-start(bf16[64,4096]{1,0:T(8,128)(2,1)} %get-tuple-element.50), channel_id=1, source_target_pairs={{0,192},{64,0},{128,64},{192,128},{1,193},{65,1},{129,65},{193,129... | collective-permute-start | bytes 1572872 | tf_op jit(solution)/shard_map/ppermute | solution.py:25
  97.0 23.1 %collective-permute-start.10 = (bf16[64,4096]{1,0:T(8,128)(2,1)}, bf16[64,4096]{1,0:T(8,128)(2,1)S(1)}, u32[]{:S(2)}, u32[]{:S(2)}) collective-permute-start(bf16[64,4096]{1,0:T(8,128)(2,1)} %get-tuple-element.51), channel_id=1, source_target_pairs={{0,192},{64,0},{128,64},{192,128},{1,193},{65,1},{129,65},{193,129... | collective-permute-start | bytes 1572872 | tf_op jit(solution)/shard_map/ppermute | solution.py:25
  98.5 21.9 %collective-permute-start.11 = (bf16[64,4096]{1,0:T(8,128)(2,1)}, bf16[64,4096]{1,0:T(8,128)(2,1)S(1)}, u32[]{:S(2)}, u32[]{:S(2)}) collective-permute-start(bf16[64,4096]{1,0:T(8,128)(2,1)} %get-tuple-element.52), channel_id=1, source_target_pairs={{0,64},{64,128},{128,192},{192,0},{1,65},{65,129},{129,193},{193,1... | collective-permute-start | bytes 1572872 | tf_op jit(solution)/shard_map/ppermute | solution.py:25
  102.2 33.2 %all-to-all-start.4 = ((bf16[32,4,4096]{2,1,0:T(4,128)(2,1)}), bf16[32,4,4096]{2,1,0:T(4,128)(2,1)}, u32[]{:S(2)}, u32[]{:S(2)}) async-start(bf16[32,4,4096]{2,1,0:T(4,128)(2,1)} %reshape.51), calls=%async_computation.4 | async-start | bytes 2097152 | tf_op jit(solution)/shard_map/all_to_all | solution.py:238
  106.8 5.6 %copy-start.2 = (f32[64,4096]{1,0:T(8,128)S(1)}, f32[64,4096]{1,0:T(8,128)}, u32[]{:S(2)}) copy-start(f32[64,4096]{1,0:T(8,128)} %get-tuple-element.49) | copy-start | bytes 3145732
  109.0 0.8 copy-start.3
  109.8 21.8 %copy-start.1 = (f32[128,4096]{1,0:T(8,128)S(1)}, f32[128,4096]{1,0:T(8,128)}, u32[]{:S(2)}) copy-start(f32[128,4096]{1,0:T(8,128)} %get-tuple-element.48.here) | copy-start | bytes 6291460
  112.2 19.4 %collective-permute-start.13 = (bf16[64,4096]{1,0:T(8,128)(2,1)}, bf16[64,4096]{1,0:T(8,128)(2,1)}, u32[]{:S(2)}, u32[]{:S(2)}) collective-permute-start(bf16[64,4096]{1,0:T(8,128)(2,1)} %add_convert_fusion.1), channel_id=1, source_target_pairs={{0,64},{64,128},{128,192},{192,0},{1,65},{65,129},{129,193},{193,1... | collective-permute-start | bytes 1572872 | tf_op jit(solution)/shard_map/ppermute | solution.py:25
  114.4 17.2 %collective-permute-start.9 = (bf16[64,4096]{1,0:T(8,128)(2,1)}, bf16[64,4096]{1,0:T(8,128)(2,1)}, u32[]{:S(2)}, u32[]{:S(2)}) collective-permute-start(bf16[64,4096]{1,0:T(8,128)(2,1)} %add_convert_fusion.2), channel_id=1, source_target_pairs={{0,192},{64,0},{128,64},{192,128},{1,193},{65,1},{129,65},{193,129... | collective-permute-start | bytes 1572872 | tf_op jit(solution)/shard_map/ppermute | solution.py:25

commit v5 on v4

v5 whole, which is shorter than its diff:
```python
import functools

import jax
import jax.numpy as jnp
from jax import lax
from jax.experimental import pallas as pl
from jax.experimental.pallas import tpu as pltpu
from jax.sharding import Mesh
from jax.sharding import PartitionSpec as P

Y, Z, X, CORE = "row", "col_0", "col_1", "col_2"
COL = (Z, X, CORE)
ROW_COL = (Y, Z, X, CORE)
COL_ROW = (Z, X, CORE, Y)

inv_temp = 50.0
sharpness = 4.0
LOWEST = -3.0e38
F32, BF16 = jnp.float32, jnp.bfloat16
TILE = 1024


def shifted(value, axis, step):
    n = lax.axis_size(axis)
    return lax.ppermute(value, axis, [(i, (i + step) % n) for i in range(n)])


def copies(value, axis):
    n = lax.axis_size(axis)
    return lax.all_to_all(jnp.broadcast_to(value, (n, *value.shape)), axis, 0, 0, tiled=True)


def shape(dims, dtype):
    return jax.ShapeDtypeStruct(dims, dtype)


def call(body, outs, args, flops=0, scalars=0, tiled=(), scratch=(), outside=(), brief=False):
    size = sum(a.size * a.dtype.itemsize for a in (*args, *outs))
    specs = []
    for k, a in enumerate((*args, *outs)):
        if k < scalars:
            specs.append(pl.BlockSpec(memory_space=pltpu.SMEM))
        elif k in tiled:
            lead = (0,) * (len(a.shape) - 1)
            specs.append(pl.BlockSpec((*a.shape[:-1], TILE), lambda i, lead=lead: (*lead, i)))
        else:
            specs.append(pl.BlockSpec(a.shape, lambda i, n=len(a.shape): (0,) * n))
    kinds = [pltpu.HBM if k in outside else None for k in range(len(specs))]
    args = [
        a if kind is None else pltpu.with_memory_space_constraint(a, kind)
        for a, kind in zip(args, kinds)
    ]
    outs = [
        o if kind is None else pltpu.HBM(o.shape, o.dtype)
        for o, kind in zip(outs, kinds[len(args) :])
    ]
    steps = (*args, *outs)[tiled[0]].shape[-1] // TILE if tiled else 1
    return pl.pallas_call(
        body,
        grid=(steps,),
        out_shape=outs,
        in_specs=specs[: len(args)],
        out_specs=specs[len(args) :],
        scratch_shapes=scratch,
        cost_estimate=pl.CostEstimate(flops=flops, bytes_accessed=1024 if brief else size, transcendentals=0),
        compiler_params=pltpu.CompilerParams(vmem_limit_bytes=24 << 20),
    )(*args)


def on_step(k):
    return pl.when(pl.program_id(0) == k)


def marks(place, ids, block, lines):
    column = place[block] + lax.broadcasted_iota(jnp.int32, (128, ids.shape[1]), 0)
    found = [column == ids[slot : slot + 1, :] for slot in range(lines)]
    return found[0], functools.reduce(jnp.logical_or, found)


BLOCKS = [
    (4 * m + k, slice(384 * m + 128 * k, 384 * m + 128 * k + 128) if k < 3 else None, slice(128 * m, 128 * m + 128))
    for m in range(2)
    for k in range(4)
]


def products(own, pool, scores):
    @on_step(0)
    def _():
        scores[...] = jnp.zeros_like(scores)

    rows = jnp.concatenate([p[...] for p in pool], axis=0)
    scores[...] += lax.dot_general(
        rows, own[...], (((1,), (1,)), ((), ())), preferred_element_type=F32
    )


def near_body(own, *refs):
    products(own, refs[:-1], refs[-1])


def far_body(place, own, *refs):
    pool, near, ids, far, table = refs[:4], *refs[4:]
    products(own, pool, far)

    @pl.when(pl.program_id(0) == pl.num_programs(0) - 1)
    def _():
        tops = [[], []]
        for block, at, other in BLOCKS:
            value = (far[other, :] if at is None else near[at, :]) * inv_temp
            for top, mark in zip(tops, marks(place, ids, block, 8)):
                top.append(jnp.max(jnp.where(mark, value, LOWEST), axis=0, keepdims=True))
        lines = [functools.reduce(jnp.maximum, top) for top in tops]
        table[...] = jnp.broadcast_to(jnp.concatenate(lines, axis=0)[None], table.shape)


def soft_body(place, table, margin_ref, ids, near, far, weights, totals, stats):
    merged = jnp.max(table[...], axis=0)
    picked, kept = merged[0:1], merged[1:2]
    margin = margin_ref[0:1, :]
    ceiling = jnp.maximum(kept, picked + margin)
    sums = []
    for block, at, other in BLOCKS:
        value = (far[other, :] if at is None else near[at, :]) * inv_temp
        over = sharpness * (value - picked - margin)
        penalty = jnp.maximum(over, 0.0) + jnp.log(1.0 + jnp.exp(-jnp.abs(over)))
        logits = jnp.where(marks(place, ids, block, 8)[1], value, value - penalty)
        weight = jnp.exp(logits - ceiling)
        weights[128 * block : 128 * block + 128, :] = weight
        sums.append(jnp.sum(weight, axis=0, keepdims=True))
    totals[...] = jnp.broadcast_to(functools.reduce(jnp.add, sums)[None], totals.shape)
    stats[...] = jnp.broadcast_to(ceiling - picked, stats.shape)


def grad_body(place, table, stats, ids, weights, losses, mine, theirs):
    total = jnp.sum(table[...], axis=0)
    losses[...] = stats[...] + jnp.log(total)
    for block in range(8):
        positive = jnp.where(marks(place, ids, block, 1)[0], 1.0, 0.0)
        rows = slice(128 * block, 128 * block + 128)
        value = ((weights[rows, :] / total - positive) * inv_temp).astype(BF16)
        rows = slice(128 * (block % 4), 128 * (block % 4) + 128)
        (mine if block < 4 else theirs)[rows, :] = value


def query_body(place, mine, theirs, *refs):
    pool, sent, exact, turned, sums = refs[:14], *refs[14:]

    @on_step(0)
    def _():
        turned[...] = jnp.concatenate([mine[...], theirs[...]], axis=0).T

    rows = jnp.concatenate([p[...] for p in pool], axis=0)
    sums[...] = jnp.dot(turned[...], rows, preferred_element_type=F32)
    sent[...] = sums[...].reshape(sent.shape).astype(BF16)
    exact[...] = sums[pl.ds(pl.multiple_of(place[8], 8), 8), :]


def passage_body(mine, arrived, own, other, down, up, low, high, here):
    weights = jnp.concatenate([mine[...], arrived[...]], axis=1)
    columns = jnp.concatenate([own[...], other[...]], axis=0)
    out = jnp.dot(weights, columns, preferred_element_type=F32)
    here[...] = out[0:128]
    low[...] = out[128:192]
    high[...] = out[320:384]
    down[0:64, :] = out[384:448].astype(BF16)
    down[64:128, :] = out[192:256].astype(BF16)
    up[0:64, :] = out[256:320].astype(BF16)
    up[64:128, :] = out[448:512].astype(BF16)


def total_body(here, down, up, low, high, total):
    total[0:64, :] = here[0:64, :] + up[0:64, :].astype(F32) + low[...].astype(F32)
    total[64:128, :] = here[64:128, :] + down[64:128, :].astype(F32) + high[...].astype(F32)


def on_device(queries, passages, positives, hard_negatives, thresholds):
    rows, width = queries.shape
    count = passages.shape[0]
    depth, breadth, ring = lax.axis_size(Z), lax.axis_size(X), lax.axis_size(Y)
    core, far, across, along = (lax.axis_index(a) for a in (CORE, Z, X, Y))
    half, members = count // 2, depth * breadth
    plane, pool = members * rows, ring * count

    low, high = passages[:half], passages[half:]
    back_low, ahead_high = shifted(low, Y, 1), shifted(high, Y, -1)
    back_high, ahead_low = shifted(high, Y, 1), shifted(low, Y, -1)
    line = copies(queries, Z)
    line, back_low, ahead_high = lax.optimization_barrier((line, back_low, ahead_high))
    far_low, far_high = shifted(back_low, Y, 1), shifted(ahead_high, Y, -1)
    own = copies(line.reshape(depth * rows, width), X)

    def ordered(table):
        table = table.reshape(-1, depth, breadth, 2, rows)
        table = lax.dynamic_index_in_dim(table, core, 3, keepdims=False)
        return jnp.swapaxes(table, 1, 2).reshape(-1, plane)

    ids = ordered(jnp.concatenate([positives[None, :], hard_negatives.T], axis=0))
    margin = ordered(jnp.broadcast_to(thresholds, (8, thresholds.shape[0])))
    steps = jnp.array([0, 1, 3, 2], jnp.int32)
    cores = jnp.stack([core, 1 - core])[:, None]
    base = (((far * breadth + across) * 2 + cores) * ring + (along - steps) % ring) * count
    place_of = across * depth + far
    at = place_of * rows
    place = jnp.concatenate([base.reshape(-1), (at // 8 * 8).reshape(1)]).astype(jnp.int32)

    near = [passages, back_low, back_high, ahead_low, ahead_high]
    near_pair = [shifted(p, CORE, 1) for p in near]
    own, near, near_pair, ids, margin, place = lax.optimization_barrier(
        (own, near, near_pair, ids, margin, place)
    )
    own = own.reshape(plane, width)
    other = shifted(own, CORE, 1)
    far_pair = [shifted(far_low, CORE, 1), shifted(far_high, CORE, 1)]

    near_scores = call(
        near_body,
        [shape((6 * count, plane), F32)],
        [own, *near, *near_pair],
        flops=2 * plane * 6 * count * width,
        tiled=range(11),
    )[0]
    far_scores, table = call(
        far_body,
        [shape((2 * count, plane), F32), shape((members, 2, plane), F32)],
        [place, own, far_low, far_high, *far_pair, near_scores, ids],
        flops=2 * plane * 2 * count * width,
        scalars=1,
        tiled=range(1, 6),
        outside=(8, 9),
    )
    table = lax.all_to_all(table, (Z, X), 0, 0, tiled=True)
    weights, table, stats = call(
        soft_body,
        [shape((2 * pool, plane), F32), shape((members, 1, plane), F32), shape((8, plane), F32)],
        [place, table, margin, ids, near_scores, far_scores],
        scalars=1,
    )
    table = lax.all_to_all(table, (Z, X), 0, 0, tiled=True)
    losses, mine, theirs = call(
        grad_body,
        [shape((8, plane), F32)] + [shape((pool, plane), BF16)] * 2,
        [place, table, stats, ids, weights],
        scalars=1,
    )
    arrived = shifted(theirs, CORE, 1)

    sent, exact = call(
        query_body,
        [shape((members, rows, width), BF16), shape((8, width), F32)],
        [place, mine, theirs, *near, far_low, far_high, *near_pair, *far_pair],
        scalars=1,
        tiled=range(3, 19),
        scratch=[pltpu.VMEM((plane, 2 * pool), BF16), pltpu.VMEM((plane, TILE), F32)],
        outside=(17, 18),
        brief=True,
    )
    parts = lax.all_to_all(sent, (X, Z), 0, 0, tiled=True)
    exact = lax.dynamic_slice_in_dim(exact, at % 8, rows, 0)
    others = (lax.iota(jnp.int32, members) != place_of)[:, None, None]
    grad_queries = exact + jnp.sum(jnp.where(others, parts.astype(F32), 0.0), axis=0)

    block = [shape((count, width), BF16)] * 2 + [shape((half, width), F32)] * 2
    down, up, low, high, here = call(
        passage_body,
        block + [shape((count, width), F32)],
        [mine, arrived, own, other],
        flops=4 * plane * pool * width,
        tiled=range(2, 9),
        outside=range(4, 9),
    )
    down, up = shifted(down, Y, -1), shifted(up, Y, 1)
    down, up = lax.optimization_barrier((down, up))
    low = shifted((low + down[:half].astype(F32)).astype(BF16), Y, -1)
    high = shifted((high + up[half:].astype(F32)).astype(BF16), Y, 1)
    grad_passages = call(
        total_body, [shape((count, width), F32)], [here, down, up, low, high], tiled=range(6), outside=(0, 3, 4)
    )[0]

    row_losses = lax.dynamic_slice_in_dim(losses[0], at, rows, 0)
    return row_losses, grad_queries, grad_passages


def solution(mesh):
    torus = Mesh(mesh.devices.reshape(mesh.shape[Y], 8, 4, 2), ROW_COL)
    in_specs = (P(ROW_COL, None), P(COL_ROW, None), P(Y), P(Y, None), P(Y))
    out_specs = (P(ROW_COL), P(ROW_COL, None), P(COL_ROW, None))
    return jax.shard_map(
        on_device, mesh=torus, in_specs=in_specs, out_specs=out_specs, check_vma=False
    )
```

time: 140 us -> 153 us (1.093)
  waiting for transfers between devices: 33.6 us -> 54.9 us
  blocking collectives: 32 us -> 11.5 us
  Pallas kernels: 16.4 us -> 25.8 us
  starting transfers between devices: 37.1 us -> 42 us
  other arithmetic: 10.7 us -> 5.83 us
  local copies, waits for them, and re-layouts: 8.25 us -> 10.4 us
    all_to_all x2 -> x1, blocking collectives: 32 us -> 11.5 us  [on_device(): table = lax.all_to_all(table, (Z, X), 0, 0, tiled=True)]
    all_to_all x2, waiting for transfers between devices: 6.29 us -> 20 us  [copies(): lax.all_to_all(jnp.broadcast_to(value, (n, *value.shape)), axis, 0, 0, ti...]
    pallas_call x4 -> x7, Pallas kernels: 16.4 us -> 25.8 us  [call(): pl.pallas_call(body, grid=(steps,), out_shape=outs, in_specs=specs[:len(a...]
    all_to_all x0 -> x1, waiting for transfers between devices: none -> 7.73 us  [on_device(): table = lax.all_to_all(table, (Z, X), 0, 0, tiled=True)]
    all_to_all x0 -> x1, starting transfers between devices: none -> 5.63 us  [on_device(): table = lax.all_to_all(table, (Z, X), 0, 0, tiled=True)]
    ppermute x14 -> x19, waiting for transfers between devices: 27.4 us -> 23.5 us  [shifted(): return lax.ppermute(value, axis, [(i, (i + step) % n) for i in range(n)])]
    all_to_all x1, waiting for transfers between devices: 0.01 us -> 3.66 us  [on_device(): parts = lax.all_to_all(sent, (X, Z), 0, 0, tiled=True)]
    convert_element_type x3 -> x2, other arithmetic: 6.83 us -> 4.06 us  [the longest x1 2.1 us: on_device(): low = shifted((low + down[:half].astype(F32)).astype(BF16), Y, -1)]
  transfers between devices with their start and end apart: 17 -> 23, of which waited for: 7 -> 9; matrix products, arithmetic and copies ran while one was open for 9% -> 7% of each run, Pallas kernels for 3% -> 11%
where the time goes in v5:
time: 153 us; the launch traced here: 151 us
  waiting for transfers between devices  54.9 us (36%)
  starting transfers between devices  42 us (27%)
  Pallas kernels  25.8 us (17%)
  blocking collectives  11.5 us (8%)
  local copies, waits for them, and re-layouts  10.4 us (7%)
  other arithmetic  5.83 us (4%)
    pallas_call x7, Pallas kernels, call(): pl.pallas_call(body, grid=(steps,), out_shape=outs, in_specs=specs[:len(a...  25.8 us
    ppermute x19, waiting for transfers between devices, shifted(): return lax.ppermute(value, axis, [(i, (i + step) % n) for i in range(n)])  23.5 us
    ppermute x19, starting transfers between devices, shifted(): return lax.ppermute(value, axis, [(i, (i + step) % n) for i in range(n)])  21.9 us
    all_to_all x2, waiting for transfers between devices, copies(): lax.all_to_all(jnp.broadcast_to(value, (n, *value.shape)), axis, 0, 0, ti...  20 us
    all_to_all x1, blocking collectives, on_device(): table = lax.all_to_all(table, (Z, X), 0, 0, tiled=True)  11.5 us
    all_to_all x2, starting transfers between devices, copies(): lax.all_to_all(jnp.broadcast_to(value, (n, *value.shape)), axis, 0, 0, ti...  10.5 us
    all_to_all x1, waiting for transfers between devices, on_device(): table = lax.all_to_all(table, (Z, X), 0, 0, tiled=True)  7.73 us
    all_to_all x1, starting transfers between devices, on_device(): table = lax.all_to_all(table, (Z, X), 0, 0, tiled=True)  5.63 us
  transfers between devices with their start and end apart: 23, of which 9 were waited for; matrix products, arithmetic and copies ran while one was open for 7% of the time, Pallas kernels for 11%

profile of v5, /device:TPU:1, one launch (start us, length us, event | category | flops | bytes accessed | tf_op | source)
XLA Modules:
  0.0 151.4 jit_solution(13192477878973651619)
XLA Ops:
  0.7 2.4 %fusion.4 = (bf16[64,4096]{1,0:T(8,128)(2,1)}, bf16[64,4096]{1,0:T(8,128)(2,1)}) fusion(bf16[128,4096]{1,0:T(8,128)(2,1)} %refs_0_.1), kind=kLoop, calls=%fused_computation.19 | loop fusion | bytes 2097152 | tf_op jit(solution)/shard_map/slice | solution.py:185
  3.0 2.1 %collective-permute-start = (bf16[64,4096]{1,0:T(8,128)(2,1)}, bf16[64,4096]{1,0:T(8,128)(2,1)}, u32[]{:S(2)}, u32[]{:S(2)}) collective-permute-start(bf16[64,4096]{1,0:T(8,128)(2,1)} %get-tuple-element.72), channel_id=1, source_target_pairs={{0,64},{64,128},{128,192},{192,0},{1,65},{65,129},{129,193},{193,1... | collective-permute-start | bytes 1572872 | tf_op jit(solution)/shard_map/ppermute | solution.py:25
  5.2 1.4 collective-permute-start.1
  6.6 2.9 %collective-permute-start.4 = (bf16[128,4096]{1,0:T(8,128)(2,1)S(1)}, bf16[128,4096]{1,0:T(8,128)(2,1)S(1)}, u32[]{:S(2)}, u32[]{:S(2)}) collective-permute-start(bf16[128,4096]{1,0:T(8,128)(2,1)S(1)} %copy-done), channel_id=1, source_target_pairs={{0,1},{1,0},{2,3},{3,2},{4,5},{5,4},{6,7},{7,6},{8,9},{9,8},{10,11... | collective-permute-start | bytes 3145736 | tf_op jit(solution)/shard_map/ppermute | solution.py:25
  10.3 6.4 %all-to-all-start = ((bf16[8,4,4096]{2,1,0:T(4,128)(2,1)}), bf16[8,4,4096]{2,1,0:T(4,128)(2,1)S(1)}, u32[]{:S(2)}, u32[]{:S(2)}) async-start(bf16[8,4,4096]{2,1,0:T(4,128)(2,1)} %broadcast_in_dim.25), calls=%async_computation | async-start | bytes 524288 | tf_op jit(solution)/shard_map/all_to_all | solution.py:30
  16.8 2.6 %collective-permute-start.3 = (bf16[64,4096]{1,0:T(8,128)(2,1)}, bf16[64,4096]{1,0:T(8,128)(2,1)}, u32[]{:S(2)}, u32[]{:S(2)}) collective-permute-start(bf16[64,4096]{1,0:T(8,128)(2,1)} %get-tuple-element.72), channel_id=1, source_target_pairs={{0,192},{64,0},{128,64},{192,128},{1,193},{65,1},{129,65},{193,129... | collective-permute-start | bytes 1572872 | tf_op jit(solution)/shard_map/ppermute | solution.py:25
  19.9 9.2 %all-to-all-done = bf16[8,4,4096]{2,1,0:T(4,128)(2,1)S(1)} async-done(((bf16[8,4,4096]{2,1,0:T(4,128)(2,1)}), bf16[8,4,4096]{2,1,0:T(4,128)(2,1)S(1)}, u32[]{:S(2)}, u32[]{:S(2)}) %all-to-all-start) | async-done | bytes 262176 | tf_op jit(solution)/shard_map/all_to_all | solution.py:30
  30.4 1.1 broadcast_in_dim.26
  31.5 4.0 %all-to-all-start.1 = ((bf16[4,32,4096]{2,1,0:T(8,128)(2,1)}), bf16[4,32,4096]{2,1,0:T(8,128)(2,1)S(1)}, u32[]{:S(2)}, u32[]{:S(2)}) async-start(bf16[4,32,4096]{2,1,0:T(8,128)(2,1)} %broadcast_in_dim.26), calls=%async_computation.1 | async-start | bytes 2097152 | tf_op jit(solution)/shard_map/all_to_all | solution.py:30
  36.7 2.6 %collective-permute-start.10 = (bf16[64,4096]{1,0:T(8,128)(2,1)}, bf16[64,4096]{1,0:T(8,128)(2,1)}, u32[]{:S(2)}, u32[]{:S(2)}) collective-permute-start(bf16[64,4096]{1,0:T(8,128)(2,1)} %copy-done.1), channel_id=1, source_target_pairs={{0,192},{64,0},{128,64},{192,128},{1,193},{65,1},{129,65},{193,129... | collective-permute-start | bytes 1572872 | tf_op jit(solution)/shard_map/ppermute | solution.py:25
  39.6 10.9 %all-to-all-done.1 = bf16[4,32,4096]{2,1,0:T(8,128)(2,1)S(1)} async-done(((bf16[4,32,4096]{2,1,0:T(8,128)(2,1)}), bf16[4,32,4096]{2,1,0:T(8,128)(2,1)S(1)}, u32[]{:S(2)}, u32[]{:S(2)}) %all-to-all-start.1) | async-done | bytes 1048608 | tf_op jit(solution)/shard_map/all_to_all | solution.py:30
  51.2 1.1 collective-permute-start.14
  53.9 4.5 %shard_map.85.refs_4_.near = f32[768,128]{1,0:T(8,128)S(1)} custom-call(bf16[128,4096]{1,0:T(8,128)(2,1)S(1)} %bitcast.16, bf16[128,4096]{1,0:T(8,128)(2,1)S(1)} %copy-done, bf16[64,4096]{1,0:T(8,128)(2,1)} %collective-permute-done.refs_1_, bf16[64,4096]{1,0:T(8,128)(2,1)} %collective-permute-done.2.refs_2_, ...), custom_call_target="tpu_custom_call" | custom-call | flops 805306368 | bytes 7733248 | tf_op jit(solution)/shard_map/pallas_call | solution.py:58
  58.4 4.5 %shard_map.86 = (f32[256,128]{1,0:T(8,128)}, f32[32,2,128]{2,1,0:T(2,128)}) custom-call(s32[9]{0:T(128)S(1)} %pad_add_fusion.place, bf16[128,4096]{1,0:T(8,128)(2,1)S(1)} %bitcast.17, bf16[64,4096]{1,0:T(8,128)(2,1)} %collective-permute-done.9.refs_0_.refs_5_, bf16[64,4096]{1,0:T(8,128)(2,1)} %collective-permute-done.10.refs_1_.refs_6_, ...), custom_call_target="tpu_custom_call" | custom-call | flops 268435456 | bytes 3706916 | tf_op jit(solution)/shard_map/pallas_call | solution.py:58
  63.0 5.6 %all-to-all-start.2 = ((f32[32,2,128]{2,1,0:T(2,128)}), f32[32,2,128]{2,1,0:T(2,128)}, u32[]{:S(2)}, u32[]{:S(2)}) async-start(f32[32,2,128]{2,1,0:T(2,128)} %get-tuple-element.53), calls=%async_computation.2 | async-start | bytes 65536 | tf_op jit(solution)/shard_map/all_to_all | solution.py:232
  69.5 7.7 %all-to-all-done.2.table = f32[32,2,128]{2,1,0:T(2,128)} async-done(((f32[32,2,128]{2,1,0:T(2,128)}), f32[32,2,128]{2,1,0:T(2,128)}, u32[]{:S(2)}, u32[]{:S(2)}) %all-to-all-start.2) | async-done | bytes 32800 | tf_op jit(solution)/shard_map/all_to_all | solution.py:232
  78.2 1.3 shard_map.87
  79.5 11.5 %all_to_all.25.table = f32[32,1,128]{2,1,0:T(1,128)S(1)} all-to-all(f32[32,1,128]{2,1,0:T(1,128)S(1)} %get-tuple-element.56), channel_id=1, replica_groups=mesh['row'=4,'col_0'=8,'col_1'=4,'col_2'=2] {'col_0','col_1'}, dimensions={0} | all-to-all | bytes 32768 | tf_op jit(solution)/shard_map/all_to_all | solution.py:239
  91.7 3.2 %collective-permute-start.13 = (bf16[512,128]{1,0:T(8,128)(2,1)S(1)}, bf16[512,128]{1,0:T(8,128)(2,1)S(1)}, u32[]{:S(2)}, u32[]{:S(2)}) collective-permute-start(bf16[512,128]{1,0:T(8,128)(2,1)S(1)} %get-tuple-element.61.theirs), channel_id=1, source_target_pairs={{0,1},{1,0},{2,3},{3,2},{4,5},{5,4},{6,7},{7,6},{8,9},{9,8},{10,11... | collective-permute-start | bytes 393224 | tf_op jit(solution)/shard_map/ppermute | solution.py:25
  95.9 5.2 %shard_map.90 = (bf16[128,4096]{1,0:T(8,128)(2,1)}, bf16[128,4096]{1,0:T(8,128)(2,1)}, f32[64,4096]{1,0:T(8,128)}, f32[64,4096]{1,0:T(8,128)}, f32[128,4096]{1,0:T(8,128)}) custom-call(bf16[512,128]{1,0:T(8,128)(2,1)S(1)} %get-tuple-element.60.mine, bf16[512,128]{1,0:T(8,128)(2,1)S(1)} %collective-permute-done.13.arrived, bf16[128,4096]{1,0:T(8,128)(2,1)S(1)} %bitcast.18, ...), custom_call_target="tpu_custom_call" | custom-call | flops 1073741824 | bytes 8650752 | tf_op jit(solution)/shard_map/pallas_call | solution.py:58
  101.0 2.2 %collective-permute-start.15 = (bf16[128,4096]{1,0:T(8,128)(2,1)}, bf16[128,4096]{1,0:T(8,128)(2,1)S(1)}, u32[]{:S(2)}, u32[]{:S(2)}) collective-permute-start(bf16[128,4096]{1,0:T(8,128)(2,1)} %get-tuple-element.65), channel_id=1, source_target_pairs={{0,192},{64,0},{128,64},{192,128},{1,193},{65,1},{129,65},{193,129... | collective-permute-start | bytes 3145736 | tf_op jit(solution)/shard_map/ppermute | solution.py:25
  103.3 5.5 %shard_map.89 = (bf16[32,4,4096]{2,1,0:T(4,128)(2,1)}, f32[8,4096]{1,0:T(8,128)}) custom-call(s32[9]{0:T(128)S(1)} %pad_add_fusion.place, bf16[512,128]{1,0:T(8,128)(2,1)S(1)} %get-tuple-element.60.mine, bf16[512,128]{1,0:T(8,128)(2,1)S(1)} %get-tuple-element.61.theirs, bf16[128,4096]{1,0:T(8,128)(2,1)S(1)} %copy-done, ...), custom_call_target="tpu_custom_call" | custom-call | bytes 1024 | tf_op jit(solution)/shard_map/pallas_call | solution.py:58
  108.8 4.1 %all-to-all-start.4 = ((bf16[32,4,4096]{2,1,0:T(4,128)(2,1)}), bf16[32,4,4096]{2,1,0:T(4,128)(2,1)S(1)}, u32[]{:S(2)}, u32[]{:S(2)}) async-start(bf16[32,4,4096]{2,1,0:T(4,128)(2,1)} %get-tuple-element.63), calls=%async_computation.4 | async-start | bytes 2097152 | tf_op jit(solution)/shard_map/all_to_all | solution.py:258
  113.5 12.3 %collective-permute-done.15.down = bf16[128,4096]{1,0:T(8,128)(2,1)S(1)} collective-permute-done((bf16[128,4096]{1,0:T(8,128)(2,1)}, bf16[128,4096]{1,0:T(8,128)(2,1)S(1)}, u32[]{:S(2)}, u32[]{:S(2)}) %collective-permute-start.15) | collective-permute-done | bytes 1048608 | tf_op jit(solution)/shard_map/ppermute | solution.py:25
  125.7 3.1 %collective-permute-done.16.up = bf16[128,4096]{1,0:T(8,128)(2,1)} collective-permute-done((bf16[128,4096]{1,0:T(8,128)(2,1)}, bf16[128,4096]{1,0:T(8,128)(2,1)}, u32[]{:S(2)}, u32[]{:S(2)}) %collective-permute-start.16) | collective-permute-done | bytes 1048608 | tf_op jit(solution)/shard_map/ppermute | solution.py:25
  128.8 2.1 %add_convert_fusion.1 = bf16[64,4096]{1,0:T(8,128)(2,1)} fusion(f32[64,4096]{1,0:T(8,128)} %get-tuple-element.69, bf16[128,4096]{1,0:T(8,128)(2,1)S(1)} %collective-permute-done.15.down), kind=kLoop, calls=%fused_computation.2 | loop fusion | flops 786432 | bytes 2097152 | tf_op jit(solution)/shard_map/convert_element_type | solution.py:274
  131.2 2.0 %add_convert_fusion = bf16[64,4096]{1,0:T(8,128)(2,1)} fusion(f32[64,4096]{1,0:T(8,128)S(1)} %copy-done.5, bf16[128,4096]{1,0:T(8,128)(2,1)} %collective-permute-done.16.up), kind=kLoop, calls=%fused_computation.1 | loop fusion | flops 786432 | bytes 2097152 | tf_op jit(solution)/shard_map/convert_element_type | solution.py:275
  133.1 1.2 collective-permute-start.18
  134.4 3.7 %all-to-all-done.4 = bf16[32,4,4096]{2,1,0:T(4,128)(2,1)S(1)} async-done(((bf16[32,4,4096]{2,1,0:T(4,128)(2,1)}), bf16[32,4,4096]{2,1,0:T(4,128)(2,1)S(1)}, u32[]{:S(2)}, u32[]{:S(2)}) %all-to-all-start.4) | async-done | bytes 1048608 | tf_op jit(solution)/shard_map/all_to_all | solution.py:258
  139.4 3.8 %collective-permute-done.17.low = bf16[64,4096]{1,0:T(8,128)(2,1)} collective-permute-done((bf16[64,4096]{1,0:T(8,128)(2,1)}, bf16[64,4096]{1,0:T(8,128)(2,1)}, u32[]{:S(2)}, u32[]{:S(2)}) %collective-permute-start.17) | collective-permute-done | bytes 524320 | tf_op jit(solution)/shard_map/ppermute | solution.py:25
  143.1 3.3 %collective-permute-done.18.high = bf16[64,4096]{1,0:T(8,128)(2,1)S(1)} collective-permute-done((bf16[64,4096]{1,0:T(8,128)(2,1)}, bf16[64,4096]{1,0:T(8,128)(2,1)S(1)}, u32[]{:S(2)}, u32[]{:S(2)}) %collective-permute-start.18) | collective-permute-done | bytes 524320 | tf_op jit(solution)/shard_map/ppermute | solution.py:25
  147.3 4.2 %shard_map.91 = f32[128,4096]{1,0:T(8,128)} custom-call(f32[128,4096]{1,0:T(8,128)} %get-tuple-element.64.here, bf16[128,4096]{1,0:T(8,128)(2,1)S(1)} %collective-permute-done.15.down, bf16[128,4096]{1,0:T(8,128)(2,1)} %collective-permute-done.16.up, bf16[64,4096]{1,0:T(8,128)(2,1)} %collective-permute-done.17.low, bf16[64,4096]{1,0:T(8,128)(2,1)} %copy-done.6), custom_call_target="tpu_custom_call" | custom-call | bytes 7340032 | tf_op jit(solution)/shard_map/pallas_call | solution.py:58
  (75 shorter events, 12.8 us)
Async XLA Ops:
  0.6 6.0 %copy-start = (bf16[128,4096]{1,0:T(8,128)(2,1)S(1)}, bf16[128,4096]{1,0:T(8,128)(2,1)}, u32[]{:S(2)}) copy-start(bf16[128,4096]{1,0:T(8,128)(2,1)} %refs_0_.1) | copy-start | bytes 3145732
  0.6 8.9 %copy-start.8 = (bf16[4,4096]{1,0:T(4,128)(2,1)S(1)}, bf16[4,4096]{1,0:T(4,128)(2,1)}, u32[]{:S(2)}) copy-start(bf16[4,4096]{1,0:T(4,128)(2,1)} %param.6) | copy-start | bytes 98308
  0.7 18.8 %copy-start.10 = (s32[256]{0:T(256)S(1)}, s32[256]{0:T(256)}, u32[]{:S(2)}) copy-start(s32[256]{0:T(256)} %param.8) | copy-start | bytes 3076
  0.7 18.9 %copy-start.9 = (s32[256,7]{0,1:T(8,128)S(1)}, s32[256,7]{0,1:T(8,128)}, u32[]{:S(2)}) copy-start(s32[256,7]{0,1:T(8,128)} %param.9) | copy-start | bytes 21508
  0.7 29.6 %copy-start.11 = (f32[256]{0:T(256)S(1)}, f32[256]{0:T(256)}, u32[]{:S(2)}) copy-start(f32[256]{0:T(256)} %param.10) | copy-start | bytes 3076
  3.0 26.1 %collective-permute-start = (bf16[64,4096]{1,0:T(8,128)(2,1)}, bf16[64,4096]{1,0:T(8,128)(2,1)}, u32[]{:S(2)}, u32[]{:S(2)}) collective-permute-start(bf16[64,4096]{1,0:T(8,128)(2,1)} %get-tuple-element.72), channel_id=1, source_target_pairs={{0,64},{64,128},{128,192},{192,0},{1,65},{65,129},{129,193},{193,1... | collective-permute-start | bytes 1572872 | tf_op jit(solution)/shard_map/ppermute | solution.py:25
  5.2 24.0 %collective-permute-start.1 = (bf16[64,4096]{1,0:T(8,128)(2,1)}, bf16[64,4096]{1,0:T(8,128)(2,1)S(1)}, u32[]{:S(2)}, u32[]{:S(2)}) collective-permute-start(bf16[64,4096]{1,0:T(8,128)(2,1)} %get-tuple-element.71), channel_id=1, source_target_pairs={{0,192},{64,0},{128,64},{192,128},{1,193},{65,1},{129,65},{193,129... | collective-permute-start | bytes 1572872 | tf_op jit(solution)/shard_map/ppermute | solution.py:25
  6.6 29.9 %collective-permute-start.4 = (bf16[128,4096]{1,0:T(8,128)(2,1)S(1)}, bf16[128,4096]{1,0:T(8,128)(2,1)S(1)}, u32[]{:S(2)}, u32[]{:S(2)}) collective-permute-start(bf16[128,4096]{1,0:T(8,128)(2,1)S(1)} %copy-done), channel_id=1, source_target_pairs={{0,1},{1,0},{2,3},{3,2},{4,5},{5,4},{6,7},{7,6},{8,9},{9,8},{10,11... | collective-permute-start | bytes 3145736 | tf_op jit(solution)/shard_map/ppermute | solution.py:25
  10.3 18.8 %all-to-all-start = ((bf16[8,4,4096]{2,1,0:T(4,128)(2,1)}), bf16[8,4,4096]{2,1,0:T(4,128)(2,1)S(1)}, u32[]{:S(2)}, u32[]{:S(2)}) async-start(bf16[8,4,4096]{2,1,0:T(4,128)(2,1)} %broadcast_in_dim.25), calls=%async_computation | async-start | bytes 524288 | tf_op jit(solution)/shard_map/all_to_all | solution.py:30
  16.7 19.3 %collective-permute-start.2 = (bf16[64,4096]{1,0:T(8,128)(2,1)}, bf16[64,4096]{1,0:T(8,128)(2,1)}, u32[]{:S(2)}, u32[]{:S(2)}) collective-permute-start(bf16[64,4096]{1,0:T(8,128)(2,1)} %get-tuple-element.71), channel_id=1, source_target_pairs={{0,64},{64,128},{128,192},{192,0},{1,65},{65,129},{129,193},{193,1... | collective-permute-start | bytes 1572872 | tf_op jit(solution)/shard_map/ppermute | solution.py:25
  16.8 19.4 %collective-permute-start.3 = (bf16[64,4096]{1,0:T(8,128)(2,1)}, bf16[64,4096]{1,0:T(8,128)(2,1)}, u32[]{:S(2)}, u32[]{:S(2)}) collective-permute-start(bf16[64,4096]{1,0:T(8,128)(2,1)} %get-tuple-element.72), channel_id=1, source_target_pairs={{0,192},{64,0},{128,64},{192,128},{1,193},{65,1},{129,65},{193,129... | collective-permute-start | bytes 1572872 | tf_op jit(solution)/shard_map/ppermute | solution.py:25
  29.1 7.6 %collective-permute-start.5 = (bf16[64,4096]{1,0:T(8,128)(2,1)}, bf16[64,4096]{1,0:T(8,128)(2,1)}, u32[]{:S(2)}, u32[]{:S(2)}) collective-permute-start(bf16[64,4096]{1,0:T(8,128)(2,1)} %collective-permute-done.refs_1_), channel_id=1, source_target_pairs={{0,1},{1,0},{2,3},{3,2},{4,5},{5,4},{6,7},{7,6},{8,9},{9,8},{10,11... | collective-permute-start | bytes 1572872 | tf_op jit(solution)/shard_map/ppermute | solution.py:25
  30.1 6.4 %copy-start.12 = (s32[4]{0:T(128)S(1)}, s32[4]{0:T(128)}, u32[]{:S(2)}) copy-start(s32[4]{0:T(128)} %constant.79) | copy-start | bytes 52
  31.5 18.9 %all-to-all-start.1 = ((bf16[4,32,4096]{2,1,0:T(8,128)(2,1)}), bf16[4,32,4096]{2,1,0:T(8,128)(2,1)S(1)}, u32[]{:S(2)}, u32[]{:S(2)}) async-start(bf16[4,32,4096]{2,1,0:T(8,128)(2,1)} %broadcast_in_dim.26), calls=%async_computation.1 | async-start | bytes 2097152 | tf_op jit(solution)/shard_map/all_to_all | solution.py:30
  35.7 3.9 %collective-permute-start.8 = (bf16[64,4096]{1,0:T(8,128)(2,1)}, bf16[64,4096]{1,0:T(8,128)(2,1)}, u32[]{:S(2)}, u32[]{:S(2)}) collective-permute-start(bf16[64,4096]{1,0:T(8,128)(2,1)} %copy-done.1), channel_id=1, source_target_pairs={{0,1},{1,0},{2,3},{3,2},{4,5},{5,4},{6,7},{7,6},{8,9},{9,8},{10,11... | collective-permute-start | bytes 1572872 | tf_op jit(solution)/shard_map/ppermute | solution.py:25
  36.0 3.5 %collective-permute-start.6 = (bf16[64,4096]{1,0:T(8,128)(2,1)}, bf16[64,4096]{1,0:T(8,128)(2,1)}, u32[]{:S(2)}, u32[]{:S(2)}) collective-permute-start(bf16[64,4096]{1,0:T(8,128)(2,1)} %collective-permute-done.2.refs_2_), channel_id=1, source_target_pairs={{0,1},{1,0},{2,3},{3,2},{4,5},{5,4},{6,7},{7,6},{8,9},{9,8},{10,11... | collective-permute-start | bytes 1572872 | tf_op jit(solution)/shard_map/ppermute | solution.py:25
  36.2 3.3 %collective-permute-start.7 = (bf16[64,4096]{1,0:T(8,128)(2,1)}, bf16[64,4096]{1,0:T(8,128)(2,1)}, u32[]{:S(2)}, u32[]{:S(2)}) collective-permute-start(bf16[64,4096]{1,0:T(8,128)(2,1)} %collective-permute-done.3.refs_3_), channel_id=1, source_target_pairs={{0,1},{1,0},{2,3},{3,2},{4,5},{5,4},{6,7},{7,6},{8,9},{9,8},{10,11... | collective-permute-start | bytes 1572872 | tf_op jit(solution)/shard_map/ppermute | solution.py:25
  36.6 15.8 %collective-permute-start.9 = (bf16[64,4096]{1,0:T(8,128)(2,1)}, bf16[64,4096]{1,0:T(8,128)(2,1)}, u32[]{:S(2)}, u32[]{:S(2)}) collective-permute-start(bf16[64,4096]{1,0:T(8,128)(2,1)} %collective-permute-done.refs_1_), channel_id=1, source_target_pairs={{0,64},{64,128},{128,192},{192,0},{1,65},{65,129},{129,193},{193,1... | collective-permute-start | bytes 1572872 | tf_op jit(solution)/shard_map/ppermute | solution.py:25
  36.7 15.8 %collective-permute-start.10 = (bf16[64,4096]{1,0:T(8,128)(2,1)}, bf16[64,4096]{1,0:T(8,128)(2,1)}, u32[]{:S(2)}, u32[]{:S(2)}) collective-permute-start(bf16[64,4096]{1,0:T(8,128)(2,1)} %copy-done.1), channel_id=1, source_target_pairs={{0,192},{64,0},{128,64},{192,128},{1,193},{65,1},{129,65},{193,129... | collective-permute-start | bytes 1572872 | tf_op jit(solution)/shard_map/ppermute | solution.py:25
  51.2 44.7 %collective-permute-start.14 = (bf16[128,4096]{1,0:T(8,128)(2,1)S(1)}, bf16[128,4096]{1,0:T(8,128)(2,1)}, u32[]{:S(2)}, u32[]{:S(2)}) collective-permute-start(bf16[128,4096]{1,0:T(8,128)(2,1)S(1)} %bitcast.15), channel_id=1, source_target_pairs={{0,1},{1,0},{2,3},{3,2},{4,5},{5,4},{6,7},{7,6},{8,9},{9,8},{10,11... | collective-permute-start | bytes 3145736 | tf_op jit(solution)/shard_map/ppermute | solution.py:25
  52.3 6.1 %collective-permute-start.11 = (bf16[64,4096]{1,0:T(8,128)(2,1)}, bf16[64,4096]{1,0:T(8,128)(2,1)}, u32[]{:S(2)}, u32[]{:S(2)}) collective-permute-start(bf16[64,4096]{1,0:T(8,128)(2,1)} %collective-permute-done.9.refs_0_.refs_5_), channel_id=1, source_target_pairs={{0,1},{1,0},{2,3},{3,2},{4,5},{5,4},{6,7},{7,6},{8,9},{9,8},{10,11... | collective-permute-start | bytes 1572872 | tf_op jit(solution)/shard_map/ppermute | solution.py:25
  52.5 5.9 %collective-permute-start.12 = (bf16[64,4096]{1,0:T(8,128)(2,1)}, bf16[64,4096]{1,0:T(8,128)(2,1)}, u32[]{:S(2)}, u32[]{:S(2)}) collective-permute-start(bf16[64,4096]{1,0:T(8,128)(2,1)} %collective-permute-done.10.refs_1_.refs_6_), channel_id=1, source_target_pairs={{0,1},{1,0},{2,3},{3,2},{4,5},{5,4},{6,7},{7,6},{8,9},{9,8},{10,11... | collective-permute-start | bytes 1572872 | tf_op jit(solution)/shard_map/ppermute | solution.py:25
  63.0 14.3 %all-to-all-start.2 = ((f32[32,2,128]{2,1,0:T(2,128)}), f32[32,2,128]{2,1,0:T(2,128)}, u32[]{:S(2)}, u32[]{:S(2)}) async-start(f32[32,2,128]{2,1,0:T(2,128)} %get-tuple-element.53), calls=%async_computation.2 | async-start | bytes 65536 | tf_op jit(solution)/shard_map/all_to_all | solution.py:232
  91.7 11.6 %copy-start.3 = (bf16[64,4096]{1,0:T(8,128)(2,1)S(1)}, bf16[64,4096]{1,0:T(8,128)(2,1)}, u32[]{:S(2)}) copy-start(bf16[64,4096]{1,0:T(8,128)(2,1)} %copy-done.1) | copy-start | bytes 1572868
  91.7 4.2 %collective-permute-start.13 = (bf16[512,128]{1,0:T(8,128)(2,1)S(1)}, bf16[512,128]{1,0:T(8,128)(2,1)S(1)}, u32[]{:S(2)}, u32[]{:S(2)}) collective-permute-start(bf16[512,128]{1,0:T(8,128)(2,1)S(1)} %get-tuple-element.61.theirs), channel_id=1, source_target_pairs={{0,1},{1,0},{2,3},{3,2},{4,5},{5,4},{6,7},{7,6},{8,9},{9,8},{10,11... | collective-permute-start | bytes 393224 | tf_op jit(solution)/shard_map/ppermute | solution.py:25
  101.0 24.7 %collective-permute-start.15 = (bf16[128,4096]{1,0:T(8,128)(2,1)}, bf16[128,4096]{1,0:T(8,128)(2,1)S(1)}, u32[]{:S(2)}, u32[]{:S(2)}) collective-permute-start(bf16[128,4096]{1,0:T(8,128)(2,1)} %get-tuple-element.65), channel_id=1, source_target_pairs={{0,192},{64,0},{128,64},{192,128},{1,193},{65,1},{129,65},{193,129... | collective-permute-start | bytes 3145736 | tf_op jit(solution)/shard_map/ppermute | solution.py:25
  103.3 25.6 %collective-permute-start.16 = (bf16[128,4096]{1,0:T(8,128)(2,1)}, bf16[128,4096]{1,0:T(8,128)(2,1)}, u32[]{:S(2)}, u32[]{:S(2)}) collective-permute-start(bf16[128,4096]{1,0:T(8,128)(2,1)} %get-tuple-element.66), channel_id=1, source_target_pairs={{0,64},{64,128},{128,192},{192,0},{1,65},{65,129},{129,193},{193,1... | collective-permute-start | bytes 3145736 | tf_op jit(solution)/shard_map/ppermute | solution.py:25
  108.7 22.4 %copy-start.5 = (f32[64,4096]{1,0:T(8,128)S(1)}, f32[64,4096]{1,0:T(8,128)}, u32[]{:S(2)}) copy-start(f32[64,4096]{1,0:T(8,128)} %get-tuple-element.70) | copy-start | bytes 3145732
  108.8 29.3 %all-to-all-start.4 = ((bf16[32,4,4096]{2,1,0:T(4,128)(2,1)}), bf16[32,4,4096]{2,1,0:T(4,128)(2,1)S(1)}, u32[]{:S(2)}, u32[]{:S(2)}) async-start(bf16[32,4,4096]{2,1,0:T(4,128)(2,1)} %get-tuple-element.63), calls=%async_computation.4 | async-start | bytes 2097152 | tf_op jit(solution)/shard_map/all_to_all | solution.py:258
  130.9 7.8 %copy-start.7 = (f32[8,4096]{1,0:T(8,128)S(1)}, f32[8,4096]{1,0:T(8,128)}, u32[]{:S(2)}) copy-start(f32[8,4096]{1,0:T(8,128)} %get-tuple-element.62) | copy-start | bytes 393220
  130.9 12.2 %collective-permute-start.17 = (bf16[64,4096]{1,0:T(8,128)(2,1)}, bf16[64,4096]{1,0:T(8,128)(2,1)}, u32[]{:S(2)}, u32[]{:S(2)}) collective-permute-start(bf16[64,4096]{1,0:T(8,128)(2,1)} %add_convert_fusion.1), channel_id=1, source_target_pairs={{0,192},{64,0},{128,64},{192,128},{1,193},{65,1},{129,65},{193,129... | collective-permute-start | bytes 1572872 | tf_op jit(solution)/shard_map/ppermute | solution.py:25
  133.1 13.4 %collective-permute-start.18 = (bf16[64,4096]{1,0:T(8,128)(2,1)}, bf16[64,4096]{1,0:T(8,128)(2,1)S(1)}, u32[]{:S(2)}, u32[]{:S(2)}) collective-permute-start(bf16[64,4096]{1,0:T(8,128)(2,1)} %add_convert_fusion), channel_id=1, source_target_pairs={{0,64},{64,128},{128,192},{192,0},{1,65},{65,129},{129,193},{193,1... | collective-permute-start | bytes 1572872 | tf_op jit(solution)/shard_map/ppermute | solution.py:25
  (4 other events, 5.2 us)

commit v6 on v4

--- a/solution.py
+++ b/solution.py
@@ -41,7 +41,8 @@
         if k < scalars:
             specs.append(pl.BlockSpec(memory_space=pltpu.SMEM))
         elif k in tiled:
-            specs.append(pl.BlockSpec((a.shape[0], TILE), lambda i: (0, i)))
+            lead = (0,) * (len(a.shape) - 1)
+            specs.append(pl.BlockSpec((*a.shape[:-1], TILE), lambda i, lead=lead: (*lead, i)))
         else:
             specs.append(pl.BlockSpec(a.shape, lambda i, n=len(a.shape): (0,) * n))
     kinds = [pltpu.HBM if k in outside else None for k in range(len(specs))]
@@ -53,7 +54,7 @@
         o if kind is None else pltpu.HBM(o.shape, o.dtype)
         for o, kind in zip(outs, kinds[len(args) :])
     ]
-    steps = (*args, *outs)[tiled[0]].shape[1] // TILE if tiled else 1
+    steps = (*args, *outs)[tiled[0]].shape[-1] // TILE if tiled else 1
     return pl.pallas_call(
         body,
         grid=(steps,),
@@ -153,6 +154,12 @@
     theirs[...] = out[128:]
 
 
+def join_body(place, mine, theirs, sent, exact, sums):
+    sums[...] = mine[...] + theirs[...]
+    sent[...] = sums[...].reshape(sent.shape).astype(BF16)
+    exact[...] = sums[pl.ds(pl.multiple_of(place[5], 8), 8), :]
+
+
 def total_body(here, back_low, back_high, ahead_low, ahead_high, total):
     half = back_low.shape[0]
     for rows, parts in (
@@ -188,7 +195,9 @@
     margin = ordered(jnp.broadcast_to(thresholds, (8, total)))
     steps = jnp.array([0, 1, 3, 2], jnp.int32)
     base = (((far * breadth + across) * 2 + core) * ring + (along - steps) % ring) * count
-    place = jnp.concatenate([core.reshape(1), base]).astype(jnp.int32)
+    place_of = across * depth + far
+    at = place_of * rows
+    place = jnp.concatenate([core.reshape(1), base, (at // 8 * 8).reshape(1)]).astype(jnp.int32)
     own, far_low, far_high, back_high, ahead_low, ids, margin, place = lax.optimization_barrier(
         (own, far_low, far_high, back_high, ahead_low, ids, margin, place)
     )
@@ -231,10 +240,30 @@
     back_low = shifted((back_low + low.astype(F32)).astype(BF16), Y, -1)
     ahead_high = shifted((ahead_high + high.astype(F32)).astype(BF16), Y, 1)
 
-    place_of = across * depth + far
-    at = place_of * rows
-    exact = lax.dynamic_slice_in_dim(mine, at, rows, 0) + lax.dynamic_slice_in_dim(theirs, at, rows, 0)
-    sent = (mine + theirs).astype(BF16).reshape(breadth * depth, rows, width)
+    sent, exact = call(
+        join_body,
+        [shape((breadth * depth, rows, width), BF16), shape((8, width), F32)],
+        [place, mine, theirs],
+        scalars=1,
+        tiled=(1, 2, 3, 4),
+        scratch=[pltpu.VMEM((plane, TILE), F32)],
+        outside=(1, 3, 4),
+    )
+    exact = lax.dynamic_slice_in_dim(exact, at % 8, rows, 0)
+    parts = lax.all_to_all(sent, (X, Z), 0, 0, tiled=True)
+    others = (lax.iota(jnp.int32, breadth * depth) != place_of)[:, None, None]
+    grad_queries = exact + jnp.sum(jnp.where(others, parts.astype(F32), 0.0), axis=0)
+
+    sent, exact = call(
+        join_body,
+        [shape((breadth * depth, rows, width), BF16), shape((8, width), F32)],
+        [place, mine, theirs],
+        scalars=1,
+        tiled=(1, 2, 3, 4),
+        scratch=[pltpu.VMEM((plane, TILE), F32)],
+        outside=(1, 3, 4),
+    )
+    exact = lax.dynamic_slice_in_dim(exact, at % 8, rows, 0)
     parts = lax.all_to_all(sent, (X, Z), 0, 0, tiled=True)
     others = (lax.iota(jnp.int32, breadth * depth) != place_of)[:, None, None]
     grad_queries = exact + jnp.sum(jnp.where(others, parts.astype(F32), 0.0), axis=0)

time: 140 us -> 147 us (1.050)
  waiting for transfers between devices: 33.6 us -> 40.2 us
  Pallas kernels: 16.4 us -> 20.4 us
  other arithmetic: 10.7 us -> 8.15 us
    ppermute x14, waiting for transfers between devices: 27.4 us -> 33 us  [shifted(): return lax.ppermute(value, axis, [(i, (i + step) % n) for i in range(n)])]
    pallas_call x4 -> x5, Pallas kernels: 16.4 us -> 20.4 us  [call(): pl.pallas_call(body, grid=(steps,), out_shape=outs, in_specs=specs[:len(a...]
    convert_element_type x1 -> x0, other arithmetic: 2.43 us -> none  [on_device(): sent = (mine + theirs).astype(BF16).reshape(breadth * depth, rows, width)]
  transfers between devices with their start and end apart: 17 -> 17, of which waited for: 7 -> 7; matrix products, arithmetic and copies ran while one was open for 9% -> 7% of each run, Pallas kernels for 3% -> 5%
where the time goes in v6:
time: 147 us
  waiting for transfers between devices  40.2 us (27%)
  starting transfers between devices  38.2 us (26%)
  blocking collectives  31.8 us (22%)
  Pallas kernels  20.4 us (14%)
  other arithmetic  8.15 us (6%)
  local copies, waits for them, and re-layouts  6.94 us (5%)
    ppermute x14, waiting for transfers between devices, shifted(): return lax.ppermute(value, axis, [(i, (i + step) % n) for i in range(n)])  33 us
    all_to_all x2, blocking collectives, on_device(): table = lax.all_to_all(table, COL, 0, 0, tiled=True)  31.8 us
    ppermute x14, starting transfers between devices, shifted(): return lax.ppermute(value, axis, [(i, (i + step) % n) for i in range(n)])  21.2 us
    pallas_call x5, Pallas kernels, call(): pl.pallas_call(body, grid=(steps,), out_shape=outs, in_specs=specs[:len(a...  20.4 us
    all_to_all x2, starting transfers between devices, copies(): lax.all_to_all(jnp.broadcast_to(value, (n, *value.shape)), axis, 0, 0, ti...  12.3 us
    all_to_all x2, waiting for transfers between devices, copies(): lax.all_to_all(jnp.broadcast_to(value, (n, *value.shape)), axis, 0, 0, ti...  7.17 us
    all_to_all x1, starting transfers between devices, on_device(): parts = lax.all_to_all(sent, (X, Z), 0, 0, tiled=True)  4.66 us
  transfers between devices with their start and end apart: 17, of which 7 were waited for; matrix products, arithmetic and copies ran while one was open for 7% of the time, Pallas kernels for 5%

profile of v6, /device:TPU:1, one launch (start us, length us, event | category | flops | bytes accessed | tf_op | source)
XLA Modules:
  0.0 146.5 jit_solution(8050901916439709773)
XLA Ops:
  0.6 2.3 %fusion.3 = (bf16[64,4096]{1,0:T(8,128)(2,1)}, bf16[64,4096]{1,0:T(8,128)(2,1)}) fusion(bf16[128,4096]{1,0:T(8,128)(2,1)} %refs_0_.3), kind=kLoop, calls=%fused_computation.16 | loop fusion | bytes 2097152 | tf_op jit(solution)/shard_map/slice | solution.py:181
  2.9 3.6 %collective-permute-start.1 = (bf16[64,4096]{1,0:T(8,128)(2,1)}, bf16[64,4096]{1,0:T(8,128)(2,1)S(1)}, u32[]{:S(2)}, u32[]{:S(2)}) collective-permute-start(bf16[64,4096]{1,0:T(8,128)(2,1)} %get-tuple-element.59), channel_id=1, source_target_pairs={{0,192},{64,0},{128,64},{192,128},{1,193},{65,1},{129,65},{193,129... | collective-permute-start | bytes 1572872 | tf_op jit(solution)/shard_map/ppermute | solution.py:25
  6.5 0.8 broadcast_in_dim.25
  7.3 8.2 %all-to-all-start = ((bf16[8,4,4096]{2,1,0:T(4,128)(2,1)}), bf16[8,4,4096]{2,1,0:T(4,128)(2,1)S(1)}, u32[]{:S(2)}, u32[]{:S(2)}) async-start(bf16[8,4,4096]{2,1,0:T(4,128)(2,1)} %broadcast_in_dim.25), calls=%async_computation | async-start | bytes 524288 | tf_op jit(solution)/shard_map/all_to_all | solution.py:30
  15.5 2.7 %collective-permute-start.5 = (bf16[64,4096]{1,0:T(8,128)(2,1)}, bf16[64,4096]{1,0:T(8,128)(2,1)}, u32[]{:S(2)}, u32[]{:S(2)}) collective-permute-start(bf16[64,4096]{1,0:T(8,128)(2,1)} %get-tuple-element.60), channel_id=1, source_target_pairs={{0,192},{64,0},{128,64},{192,128},{1,193},{65,1},{129,65},{193,129... | collective-permute-start | bytes 1572872 | tf_op jit(solution)/shard_map/ppermute | solution.py:25
  18.4 7.2 %all-to-all-done = bf16[8,4,4096]{2,1,0:T(4,128)(2,1)S(1)} async-done(((bf16[8,4,4096]{2,1,0:T(4,128)(2,1)}), bf16[8,4,4096]{2,1,0:T(4,128)(2,1)S(1)}, u32[]{:S(2)}, u32[]{:S(2)}) %all-to-all-start) | async-done | bytes 262176 | tf_op jit(solution)/shard_map/all_to_all | solution.py:30
  25.6 1.1 broadcast_in_dim.26
  26.7 4.1 %all-to-all-start.1 = ((bf16[4,32,4096]{2,1,0:T(8,128)(2,1)}), bf16[4,32,4096]{2,1,0:T(8,128)(2,1)S(1)}, u32[]{:S(2)}, u32[]{:S(2)}) async-start(bf16[4,32,4096]{2,1,0:T(8,128)(2,1)} %broadcast_in_dim.26), calls=%async_computation.1 | async-start | bytes 2097152 | tf_op jit(solution)/shard_map/all_to_all | solution.py:30
  31.2 1.1 concatenate.12
  32.3 1.1 add_bitcast_fusion
  34.1 2.7 %collective-permute-start.3 = (bf16[64,4096]{1,0:T(8,128)(2,1)S(1)}, bf16[64,4096]{1,0:T(8,128)(2,1)}, u32[]{:S(2)}, u32[]{:S(2)}) collective-permute-start(bf16[64,4096]{1,0:T(8,128)(2,1)S(1)} %collective-permute-done.1.refs_4_), channel_id=1, source_target_pairs={{0,192},{64,0},{128,64},{192,128},{1,193},{65,1},{129,65},{193,129... | collective-permute-start | bytes 1572872 | tf_op jit(solution)/shard_map/ppermute | solution.py:25
  37.0 8.8 %collective-permute-done.2.refs_5_ = bf16[64,4096]{1,0:T(8,128)(2,1)} collective-permute-done((bf16[64,4096]{1,0:T(8,128)(2,1)S(1)}, bf16[64,4096]{1,0:T(8,128)(2,1)}, u32[]{:S(2)}, u32[]{:S(2)}) %collective-permute-start.2) | collective-permute-done | bytes 524320 | tf_op jit(solution)/shard_map/ppermute | solution.py:25
  45.8 3.9 %collective-permute-start.6 = (bf16[128,4096]{1,0:T(8,128)(2,1)S(1)}, bf16[128,4096]{1,0:T(8,128)(2,1)S(1)}, u32[]{:S(2)}, u32[]{:S(2)}) collective-permute-start(bf16[128,4096]{1,0:T(8,128)(2,1)S(1)} %bitcast.14), channel_id=1, source_target_pairs={{0,1},{1,0},{2,3},{3,2},{4,5},{5,4},{6,7},{7,6},{8,9},{9,8},{10,11... | collective-permute-start | bytes 3145736 | tf_op jit(solution)/shard_map/ppermute | solution.py:25
  49.7 2.3 %collective-permute-done.6.other = bf16[128,4096]{1,0:T(8,128)(2,1)S(1)} collective-permute-done((bf16[128,4096]{1,0:T(8,128)(2,1)S(1)}, bf16[128,4096]{1,0:T(8,128)(2,1)S(1)}, u32[]{:S(2)}, u32[]{:S(2)}) %collective-permute-start.6) | collective-permute-done | bytes 1048608 | tf_op jit(solution)/shard_map/ppermute | solution.py:25
  52.0 4.6 %shard_map.85 = (f32[512,256]{1,0:T(8,128)S(1)}, f32[64,2,256]{2,1,0:T(2,128)S(1)}) custom-call(s32[6]{0:T(128)S(1)} %pad_add_fusion.place, bf16[128,4096]{1,0:T(8,128)(2,1)S(1)} %bitcast.15, bf16[128,4096]{1,0:T(8,128)(2,1)S(1)} %collective-permute-done.6.other, bf16[128,4096]{1,0:T(8,128)(2,1)S(1)} %copy-done, ...), custom_call_target="tpu_custom_call" | custom-call | flops 1073741824 | bytes 6955032 | tf_op jit(solution)/shard_map/pallas_call | solution.py:58
  56.6 17.9 %all_to_all.25.table = f32[64,2,256]{2,1,0:T(2,128)S(1)} all-to-all(f32[64,2,256]{2,1,0:T(2,128)S(1)} %get-tuple-element.41), channel_id=1, replica_groups=mesh['row'=4,'col_0'=8,'col_1'=4,'col_2'=2] {'col_0','col_1','col_2'}, dimensions={0} | all-to-all | bytes 262144 | tf_op jit(solution)/shard_map/all_to_all | solution.py:216
  74.5 1.1 shard_map.86
  75.5 13.9 %all_to_all.26.table = f32[64,1,256]{2,1,0:T(1,128)S(1)} all-to-all(f32[64,1,256]{2,1,0:T(1,128)S(1)} %get-tuple-element.44), channel_id=1, replica_groups=mesh['row'=4,'col_0'=8,'col_1'=4,'col_2'=2] {'col_0','col_1','col_2'}, dimensions={0} | all-to-all | bytes 131072 | tf_op jit(solution)/shard_map/all_to_all | solution.py:223
  89.4 7.0 %shard_map.87 = (f32[8,256]{1,0:T(8,128)S(1)}, bf16[64,4096]{1,0:T(8,128)(2,1)}, bf16[64,4096]{1,0:T(8,128)(2,1)}, f32[64,4096]{1,0:T(8,128)}, bf16[64,4096]{1,0...) custom-call(s32[6]{0:T(128)S(1)} %pad_add_fusion.place, ...), custom_call_target="tpu_custom_call" | custom-call | flops 2147483648 | bytes 17391640 | tf_op jit(solution)/shard_map/pallas_call | solution.py:58
  96.9 2.6 %collective-permute-start.8 = (bf16[64,4096]{1,0:T(8,128)(2,1)}, bf16[64,4096]{1,0:T(8,128)(2,1)}, u32[]{:S(2)}, u32[]{:S(2)}) collective-permute-start(bf16[64,4096]{1,0:T(8,128)(2,1)} %get-tuple-element.54), channel_id=1, source_target_pairs={{0,192},{64,0},{128,64},{192,128},{1,193},{65,1},{129,65},{193,129... | collective-permute-start | bytes 1572872 | tf_op jit(solution)/shard_map/ppermute | solution.py:25
  99.5 1.4 collective-permute-start.11
  101.0 3.9 %shard_map.88 = (bf16[32,4,4096]{2,1,0:T(4,128)(2,1)}, f32[8,4096]{1,0:T(8,128)}) custom-call(s32[6]{0:T(128)S(1)} %pad_add_fusion.place, f32[128,4096]{1,0:T(8,128)} %get-tuple-element.48.mine, f32[128,4096]{1,0:T(8,128)S(1)} %collective-permute-done.7.theirs), custom_call_target="tpu_custom_call" | custom-call | bytes 5373976 | tf_op jit(solution)/shard_map/pallas_call | solution.py:58
  105.0 4.7 %all-to-all-start.4 = ((bf16[32,4,4096]{2,1,0:T(4,128)(2,1)}), bf16[32,4,4096]{2,1,0:T(4,128)(2,1)}, u32[]{:S(2)}, u32[]{:S(2)}) async-start(bf16[32,4,4096]{2,1,0:T(4,128)(2,1)} %get-tuple-element.51), calls=%async_computation.4 | async-start | bytes 2097152 | tf_op jit(solution)/shard_map/all_to_all | solution.py:267
  109.6 1.2 collective-permute-done.8
  110.9 2.4 %add_convert_fusion.1 = bf16[64,4096]{1,0:T(8,128)(2,1)} fusion(f32[64,4096]{1,0:T(8,128)} %get-tuple-element.53, bf16[64,4096]{1,0:T(8,128)(2,1)} %collective-permute-done.8), kind=kLoop, calls=%fused_computation.2 | loop fusion | flops 786432 | bytes 2097152 | tf_op jit(solution)/shard_map/convert_element_type | solution.py:240
  113.3 3.4 %collective-permute-start.9 = (bf16[64,4096]{1,0:T(8,128)(2,1)}, bf16[64,4096]{1,0:T(8,128)(2,1)}, u32[]{:S(2)}, u32[]{:S(2)}) collective-permute-start(bf16[64,4096]{1,0:T(8,128)(2,1)} %add_convert_fusion.1), channel_id=1, source_target_pairs={{0,192},{64,0},{128,64},{192,128},{1,193},{65,1},{129,65},{193,129... | collective-permute-start | bytes 1572872 | tf_op jit(solution)/shard_map/ppermute | solution.py:25
  116.7 8.2 %collective-permute-done.12 = bf16[64,4096]{1,0:T(8,128)(2,1)} collective-permute-done((bf16[64,4096]{1,0:T(8,128)(2,1)}, bf16[64,4096]{1,0:T(8,128)(2,1)}, u32[]{:S(2)}, u32[]{:S(2)}) %collective-permute-start.12) | collective-permute-done | bytes 524320 | tf_op jit(solution)/shard_map/ppermute | solution.py:25
  124.9 1.9 %add_convert_fusion = bf16[64,4096]{1,0:T(8,128)(2,1)} fusion(f32[64,4096]{1,0:T(8,128)S(1)} %copy-done.2, bf16[64,4096]{1,0:T(8,128)(2,1)} %collective-permute-done.12), kind=kLoop, calls=%fused_computation.1 | loop fusion | flops 786432 | bytes 2097152 | tf_op jit(solution)/shard_map/convert_element_type | solution.py:241
  127.7 5.7 %collective-permute-done.9.back_low = bf16[64,4096]{1,0:T(8,128)(2,1)} collective-permute-done((bf16[64,4096]{1,0:T(8,128)(2,1)}, bf16[64,4096]{1,0:T(8,128)(2,1)}, u32[]{:S(2)}, u32[]{:S(2)}) %collective-permute-start.9) | collective-permute-done | bytes 524320 | tf_op jit(solution)/shard_map/ppermute | solution.py:25
  133.3 6.8 %collective-permute-done.13.ahead_high = bf16[64,4096]{1,0:T(8,128)(2,1)} collective-permute-done((bf16[64,4096]{1,0:T(8,128)(2,1)}, bf16[64,4096]{1,0:T(8,128)(2,1)}, u32[]{:S(2)}, u32[]{:S(2)}) %collective-permute-start.13) | collective-permute-done | bytes 524320 | tf_op jit(solution)/shard_map/ppermute | solution.py:25
  140.1 3.8 %shard_map.89 = f32[128,4096]{1,0:T(8,128)} custom-call(f32[128,4096]{1,0:T(8,128)S(1)} %copy-done.1, bf16[64,4096]{1,0:T(8,128)(2,1)} %collective-permute-done.9.back_low, bf16[64,4096]{1,0:T(8,128)(2,1)S(1)} %collective-permute-done.10.back_high, bf16[64,4096]{1,0:T(8,128)(2,1)S(1)} %collective-permute-done.11.ahead_low, ...), custom_call_target="tpu_custom_call" | custom-call | bytes 6291456 | tf_op jit(solution)/shard_map/pallas_call | solution.py:58
  143.9 1.9 %select_reduce_fusion = f32[4,4096]{1,0:T(4,128)S(1)} fusion(bf16[32,4,4096]{2,1,0:T(4,128)(2,1)} %all-to-all-done.4, pred[32]{0:T(512)(128)(4,1)S(1)} %iota_compare_fusion), kind=kLoop, calls=%fused_computation | loop fusion | flops 1556480 | bytes 1114144 | tf_op jit(solution)/shard_map/reduce_sum | solution.py:269
  (51 shorter events, 3.4 us)
Async XLA Ops:
  0.6 5.9 %copy-start.4 = (bf16[4,4096]{1,0:T(4,128)(2,1)S(1)}, bf16[4,4096]{1,0:T(4,128)(2,1)}, u32[]{:S(2)}) copy-start(bf16[4,4096]{1,0:T(4,128)(2,1)} %param.6) | copy-start | bytes 98308
  0.6 17.6 %copy-start.6 = (f32[256]{0:T(256)S(1)}, f32[256]{0:T(256)}, u32[]{:S(2)}) copy-start(f32[256]{0:T(256)} %param.10) | copy-start | bytes 3076
  2.9 22.6 %collective-permute-start.1 = (bf16[64,4096]{1,0:T(8,128)(2,1)}, bf16[64,4096]{1,0:T(8,128)(2,1)S(1)}, u32[]{:S(2)}, u32[]{:S(2)}) collective-permute-start(bf16[64,4096]{1,0:T(8,128)(2,1)} %get-tuple-element.59), channel_id=1, source_target_pairs={{0,192},{64,0},{128,64},{192,128},{1,193},{65,1},{129,65},{193,129... | collective-permute-start | bytes 1572872 | tf_op jit(solution)/shard_map/ppermute | solution.py:25
  6.5 19.1 %collective-permute-start = (bf16[64,4096]{1,0:T(8,128)(2,1)}, bf16[64,4096]{1,0:T(8,128)(2,1)S(1)}, u32[]{:S(2)}, u32[]{:S(2)}) collective-permute-start(bf16[64,4096]{1,0:T(8,128)(2,1)} %get-tuple-element.60), channel_id=1, source_target_pairs={{0,64},{64,128},{128,192},{192,0},{1,65},{65,129},{129,193},{193,1... | collective-permute-start | bytes 1572872 | tf_op jit(solution)/shard_map/ppermute | solution.py:25
  7.3 18.3 %all-to-all-start = ((bf16[8,4,4096]{2,1,0:T(4,128)(2,1)}), bf16[8,4,4096]{2,1,0:T(4,128)(2,1)S(1)}, u32[]{:S(2)}, u32[]{:S(2)}) async-start(bf16[8,4,4096]{2,1,0:T(4,128)(2,1)} %broadcast_in_dim.25), calls=%async_computation | async-start | bytes 524288 | tf_op jit(solution)/shard_map/all_to_all | solution.py:30
  15.5 21.5 %collective-permute-start.4 = (bf16[64,4096]{1,0:T(8,128)(2,1)}, bf16[64,4096]{1,0:T(8,128)(2,1)}, u32[]{:S(2)}, u32[]{:S(2)}) collective-permute-start(bf16[64,4096]{1,0:T(8,128)(2,1)} %get-tuple-element.59), channel_id=1, source_target_pairs={{0,64},{64,128},{128,192},{192,0},{1,65},{65,129},{129,193},{193,1... | collective-permute-start | bytes 1572872 | tf_op jit(solution)/shard_map/ppermute | solution.py:25
  15.5 21.5 %collective-permute-start.5 = (bf16[64,4096]{1,0:T(8,128)(2,1)}, bf16[64,4096]{1,0:T(8,128)(2,1)}, u32[]{:S(2)}, u32[]{:S(2)}) collective-permute-start(bf16[64,4096]{1,0:T(8,128)(2,1)} %get-tuple-element.60), channel_id=1, source_target_pairs={{0,192},{64,0},{128,64},{192,128},{1,193},{65,1},{129,65},{193,129... | collective-permute-start | bytes 1572872 | tf_op jit(solution)/shard_map/ppermute | solution.py:25
  18.4 12.7 %copy-start.7 = (s32[256]{0:T(256)S(1)}, s32[256]{0:T(256)}, u32[]{:S(2)}) copy-start(s32[256]{0:T(256)} %param.8) | copy-start | bytes 3076
  25.6 5.6 %copy-start.5 = (s32[256,7]{0,1:T(8,128)S(1)}, s32[256,7]{0,1:T(8,128)}, u32[]{:S(2)}) copy-start(s32[256,7]{0,1:T(8,128)} %param.9) | copy-start | bytes 21508
  26.7 10.2 %copy-start.8 = (s32[4]{0:T(128)S(1)}, s32[4]{0:T(128)}, u32[]{:S(2)}) copy-start(s32[4]{0:T(128)} %constant.70) | copy-start | bytes 52
  26.7 25.3 %copy-start = (bf16[128,4096]{1,0:T(8,128)(2,1)S(1)}, bf16[128,4096]{1,0:T(8,128)(2,1)}, u32[]{:S(2)}) copy-start(bf16[128,4096]{1,0:T(8,128)(2,1)} %refs_0_.3) | copy-start | bytes 3145732
  26.7 19.1 %all-to-all-start.1 = ((bf16[4,32,4096]{2,1,0:T(8,128)(2,1)}), bf16[4,32,4096]{2,1,0:T(8,128)(2,1)S(1)}, u32[]{:S(2)}, u32[]{:S(2)}) async-start(bf16[4,32,4096]{2,1,0:T(8,128)(2,1)} %broadcast_in_dim.26), calls=%async_computation.1 | async-start | bytes 2097152 | tf_op jit(solution)/shard_map/all_to_all | solution.py:30
  33.9 11.9 %collective-permute-start.2 = (bf16[64,4096]{1,0:T(8,128)(2,1)S(1)}, bf16[64,4096]{1,0:T(8,128)(2,1)}, u32[]{:S(2)}, u32[]{:S(2)}) collective-permute-start(bf16[64,4096]{1,0:T(8,128)(2,1)S(1)} %collective-permute-done.refs_1_), channel_id=1, source_target_pairs={{0,64},{64,128},{128,192},{192,0},{1,65},{65,129},{129,193},{193,1... | collective-permute-start | bytes 1572872 | tf_op jit(solution)/shard_map/ppermute | solution.py:25
  34.1 11.7 %collective-permute-start.3 = (bf16[64,4096]{1,0:T(8,128)(2,1)S(1)}, bf16[64,4096]{1,0:T(8,128)(2,1)}, u32[]{:S(2)}, u32[]{:S(2)}) collective-permute-start(bf16[64,4096]{1,0:T(8,128)(2,1)S(1)} %collective-permute-done.1.refs_4_), channel_id=1, source_target_pairs={{0,192},{64,0},{128,64},{192,128},{1,193},{65,1},{129,65},{193,129... | collective-permute-start | bytes 1572872 | tf_op jit(solution)/shard_map/ppermute | solution.py:25
  45.8 6.2 %collective-permute-start.6 = (bf16[128,4096]{1,0:T(8,128)(2,1)S(1)}, bf16[128,4096]{1,0:T(8,128)(2,1)S(1)}, u32[]{:S(2)}, u32[]{:S(2)}) collective-permute-start(bf16[128,4096]{1,0:T(8,128)(2,1)S(1)} %bitcast.14), channel_id=1, source_target_pairs={{0,1},{1,0},{2,3},{3,2},{4,5},{5,4},{6,7},{7,6},{8,9},{9,8},{10,11... | collective-permute-start | bytes 3145736 | tf_op jit(solution)/shard_map/ppermute | solution.py:25
  96.5 4.5 %collective-permute-start.7 = (f32[128,4096]{1,0:T(8,128)}, f32[128,4096]{1,0:T(8,128)S(1)}, u32[]{:S(2)}, u32[]{:S(2)}) collective-permute-start(f32[128,4096]{1,0:T(8,128)} %get-tuple-element.49), channel_id=1, source_target_pairs={{0,1},{1,0},{2,3},{3,2},{4,5},{5,4},{6,7},{7,6},{8,9},{9,8},{10,11... | collective-permute-start | bytes 6291464 | tf_op jit(solution)/shard_map/ppermute | solution.py:25
  96.9 13.9 %collective-permute-start.8 = (bf16[64,4096]{1,0:T(8,128)(2,1)}, bf16[64,4096]{1,0:T(8,128)(2,1)}, u32[]{:S(2)}, u32[]{:S(2)}) collective-permute-start(bf16[64,4096]{1,0:T(8,128)(2,1)} %get-tuple-element.54), channel_id=1, source_target_pairs={{0,192},{64,0},{128,64},{192,128},{1,193},{65,1},{129,65},{193,129... | collective-permute-start | bytes 1572872 | tf_op jit(solution)/shard_map/ppermute | solution.py:25
  99.5 28.2 %collective-permute-start.10 = (bf16[64,4096]{1,0:T(8,128)(2,1)}, bf16[64,4096]{1,0:T(8,128)(2,1)S(1)}, u32[]{:S(2)}, u32[]{:S(2)}) collective-permute-start(bf16[64,4096]{1,0:T(8,128)(2,1)} %get-tuple-element.55), channel_id=1, source_target_pairs={{0,192},{64,0},{128,64},{192,128},{1,193},{65,1},{129,65},{193,129... | collective-permute-start | bytes 1572872 | tf_op jit(solution)/shard_map/ppermute | solution.py:25
  99.5 28.1 %collective-permute-start.11 = (bf16[64,4096]{1,0:T(8,128)(2,1)}, bf16[64,4096]{1,0:T(8,128)(2,1)S(1)}, u32[]{:S(2)}, u32[]{:S(2)}) collective-permute-start(bf16[64,4096]{1,0:T(8,128)(2,1)} %get-tuple-element.56), channel_id=1, source_target_pairs={{0,64},{64,128},{128,192},{192,0},{1,65},{65,129},{129,193},{193,1... | collective-permute-start | bytes 1572872 | tf_op jit(solution)/shard_map/ppermute | solution.py:25
  101.0 24.0 %collective-permute-start.12 = (bf16[64,4096]{1,0:T(8,128)(2,1)}, bf16[64,4096]{1,0:T(8,128)(2,1)}, u32[]{:S(2)}, u32[]{:S(2)}) collective-permute-start(bf16[64,4096]{1,0:T(8,128)(2,1)} %get-tuple-element.58), channel_id=1, source_target_pairs={{0,64},{64,128},{128,192},{192,0},{1,65},{65,129},{129,193},{193,1... | collective-permute-start | bytes 1572872 | tf_op jit(solution)/shard_map/ppermute | solution.py:25
  105.0 39.0 %all-to-all-start.4 = ((bf16[32,4,4096]{2,1,0:T(4,128)(2,1)}), bf16[32,4,4096]{2,1,0:T(4,128)(2,1)}, u32[]{:S(2)}, u32[]{:S(2)}) async-start(bf16[32,4,4096]{2,1,0:T(4,128)(2,1)} %get-tuple-element.51), calls=%async_computation.4 | async-start | bytes 2097152 | tf_op jit(solution)/shard_map/all_to_all | solution.py:267
  109.6 15.3 %copy-start.2 = (f32[64,4096]{1,0:T(8,128)S(1)}, f32[64,4096]{1,0:T(8,128)}, u32[]{:S(2)}) copy-start(f32[64,4096]{1,0:T(8,128)} %get-tuple-element.57) | copy-start | bytes 3145732
  110.9 29.2 %copy-start.1 = (f32[128,4096]{1,0:T(8,128)S(1)}, f32[128,4096]{1,0:T(8,128)}, u32[]{:S(2)}) copy-start(f32[128,4096]{1,0:T(8,128)} %get-tuple-element.52.here) | copy-start | bytes 6291460
  113.3 20.0 %collective-permute-start.9 = (bf16[64,4096]{1,0:T(8,128)(2,1)}, bf16[64,4096]{1,0:T(8,128)(2,1)}, u32[]{:S(2)}, u32[]{:S(2)}) collective-permute-start(bf16[64,4096]{1,0:T(8,128)(2,1)} %add_convert_fusion.1), channel_id=1, source_target_pairs={{0,192},{64,0},{128,64},{192,128},{1,193},{65,1},{129,65},{193,129... | collective-permute-start | bytes 1572872 | tf_op jit(solution)/shard_map/ppermute | solution.py:25
  126.9 13.2 %collective-permute-start.13 = (bf16[64,4096]{1,0:T(8,128)(2,1)}, bf16[64,4096]{1,0:T(8,128)(2,1)}, u32[]{:S(2)}, u32[]{:S(2)}) collective-permute-start(bf16[64,4096]{1,0:T(8,128)(2,1)} %add_convert_fusion), channel_id=1, source_target_pairs={{0,64},{64,128},{128,192},{192,0},{1,65},{65,129},{129,193},{193,1... | collective-permute-start | bytes 1572872 | tf_op jit(solution)/shard_map/ppermute | solution.py:25
  140.1 5.7 %copy-start.3 = (f32[8,4096]{1,0:T(8,128)S(1)}, f32[8,4096]{1,0:T(8,128)}, u32[]{:S(2)}) copy-start(f32[8,4096]{1,0:T(8,128)} %get-tuple-element.50) | copy-start | bytes 393220

commit v7 on v4

--- a/solution.py
+++ b/solution.py
@@ -62,7 +62,7 @@
         out_specs=specs[len(args) :],
         scratch_shapes=scratch,
         cost_estimate=pl.CostEstimate(flops=flops, bytes_accessed=size, transcendentals=0),
-        compiler_params=pltpu.CompilerParams(vmem_limit_bytes=24 << 20),
+        compiler_params=pltpu.CompilerParams(vmem_limit_bytes=(24 if flops else 8) << 20),
     )(*args)
 
 
@@ -212,8 +212,7 @@
         scalars=1,
     )
     table = lax.all_to_all(table, COL, 0, 0, tiled=True)
-    piece, exact = shape((half, width), BF16), shape((half, width), F32)
-    sums = [piece, piece, exact, piece, piece, exact] + [shape((count, width), F32)]
+    sums = [shape((half, width), BF16)] * 6 + [shape((count, width), F32)]
     losses, low, high, back_low, back_high, ahead_low, ahead_high, here, mine, theirs = call(
         grad_body,
         [shape((8, total), F32)] + sums + [shape((plane, width), F32)] * 2,
@@ -228,13 +227,14 @@
     low, high = shifted(low, Y, -1), shifted(high, Y, 1)
     back_high, ahead_low = shifted(back_high, Y, -1), shifted(ahead_low, Y, 1)
     theirs = shifted(theirs, CORE, 1)
-    back_low = shifted((back_low + low.astype(F32)).astype(BF16), Y, -1)
-    ahead_high = shifted((ahead_high + high.astype(F32)).astype(BF16), Y, 1)
+    back_low = shifted((back_low.astype(F32) + low.astype(F32)).astype(BF16), Y, -1)
+    ahead_high = shifted((ahead_high.astype(F32) + high.astype(F32)).astype(BF16), Y, 1)
 
     place_of = across * depth + far
     at = place_of * rows
     exact = lax.dynamic_slice_in_dim(mine, at, rows, 0) + lax.dynamic_slice_in_dim(theirs, at, rows, 0)
     sent = (mine + theirs).astype(BF16).reshape(breadth * depth, rows, width)
+    exact, sent = lax.optimization_barrier((exact, sent))
     parts = lax.all_to_all(sent, (X, Z), 0, 0, tiled=True)
     others = (lax.iota(jnp.int32, breadth * depth) != place_of)[:, None, None]
     grad_queries = exact + jnp.sum(jnp.where(others, parts.astype(F32), 0.0), axis=0)

time: 140 us -> 139 us (level)
  transfers between devices with their start and end apart: 17 -> 17, of which waited for: 7 -> 7; matrix products, arithmetic and copies ran while one was open for 9% -> 10% of each run, Pallas kernels for 3% -> 3%
where the time goes in v7:
time: 139 us; the launch traced here: 138 us
  starting transfers between devices  37.1 us (27%)
  waiting for transfers between devices  33.5 us (24%)
  blocking collectives  32 us (23%)
  Pallas kernels  16.2 us (12%)
  other arithmetic  10.6 us (8%)
  local copies, waits for them, and re-layouts  7.48 us (5%)
    all_to_all x2, blocking collectives, on_device(): table = lax.all_to_all(table, COL, 0, 0, tiled=True)  32 us
    ppermute x14, waiting for transfers between devices, shifted(): return lax.ppermute(value, axis, [(i, (i + step) % n) for i in range(n)])  27.3 us
    ppermute x14, starting transfers between devices, shifted(): return lax.ppermute(value, axis, [(i, (i + step) % n) for i in range(n)])  20.2 us
    pallas_call x4, Pallas kernels, call(): pl.pallas_call(body, grid=(steps,), out_shape=outs, in_specs=specs[:len(a...  16.2 us
    all_to_all x2, starting transfers between devices, copies(): lax.all_to_all(jnp.broadcast_to(value, (n, *value.shape)), axis, 0, 0, ti...  12.2 us
    all_to_all x2, waiting for transfers between devices, copies(): lax.all_to_all(jnp.broadcast_to(value, (n, *value.shape)), axis, 0, 0, ti...  6.29 us
    all_to_all x1, starting transfers between devices, on_device(): parts = lax.all_to_all(sent, (X, Z), 0, 0, tiled=True)  4.67 us
  transfers between devices with their start and end apart: 17, of which 7 were waited for; matrix products, arithmetic and copies ran while one was open for 10% of the time, Pallas kernels for 3%

profile of v7, /device:TPU:1, one launch (start us, length us, event | category | flops | bytes accessed | tf_op | source)
XLA Modules:
  0.0 137.7 jit_solution(3500696455245180343)
XLA Ops:
  0.7 2.3 %fusion.4 = (bf16[64,4096]{1,0:T(8,128)(2,1)}, bf16[64,4096]{1,0:T(8,128)(2,1)}) fusion(bf16[128,4096]{1,0:T(8,128)(2,1)} %refs_0_.3), kind=kLoop, calls=%fused_computation.18 | loop fusion | bytes 2097152 | tf_op jit(solution)/shard_map/slice | solution.py:174
  3.0 2.1 %collective-permute-start = (bf16[64,4096]{1,0:T(8,128)(2,1)}, bf16[64,4096]{1,0:T(8,128)(2,1)S(1)}, u32[]{:S(2)}, u32[]{:S(2)}) collective-permute-start(bf16[64,4096]{1,0:T(8,128)(2,1)} %get-tuple-element.60), channel_id=1, source_target_pairs={{0,64},{64,128},{128,192},{192,0},{1,65},{65,129},{129,193},{193,1... | collective-permute-start | bytes 1572872 | tf_op jit(solution)/shard_map/ppermute | solution.py:25
  5.1 1.4 %collective-permute-start.1 = (bf16[64,4096]{1,0:T(8,128)(2,1)}, bf16[64,4096]{1,0:T(8,128)(2,1)S(1)}, u32[]{:S(2)}, u32[]{:S(2)}) collective-permute-start(bf16[64,4096]{1,0:T(8,128)(2,1)} %get-tuple-element.59), channel_id=1, source_target_pairs={{0,192},{64,0},{128,64},{192,128},{1,193},{65,1},{129,65},{193,129... | collective-permute-start | bytes 1572872 | tf_op jit(solution)/shard_map/ppermute | solution.py:25
  7.3 8.2 %all-to-all-start = ((bf16[8,4,4096]{2,1,0:T(4,128)(2,1)}), bf16[8,4,4096]{2,1,0:T(4,128)(2,1)S(1)}, u32[]{:S(2)}, u32[]{:S(2)}) async-start(bf16[8,4,4096]{2,1,0:T(4,128)(2,1)} %broadcast_in_dim.25), calls=%async_computation | async-start | bytes 524288 | tf_op jit(solution)/shard_map/all_to_all | solution.py:30
  15.5 2.7 %collective-permute-start.5 = (bf16[64,4096]{1,0:T(8,128)(2,1)}, bf16[64,4096]{1,0:T(8,128)(2,1)}, u32[]{:S(2)}, u32[]{:S(2)}) collective-permute-start(bf16[64,4096]{1,0:T(8,128)(2,1)} %get-tuple-element.60), channel_id=1, source_target_pairs={{0,192},{64,0},{128,64},{192,128},{1,193},{65,1},{129,65},{193,129... | collective-permute-start | bytes 1572872 | tf_op jit(solution)/shard_map/ppermute | solution.py:25
  19.4 6.3 %all-to-all-done = bf16[8,4,4096]{2,1,0:T(4,128)(2,1)S(1)} async-done(((bf16[8,4,4096]{2,1,0:T(4,128)(2,1)}), bf16[8,4,4096]{2,1,0:T(4,128)(2,1)S(1)}, u32[]{:S(2)}, u32[]{:S(2)}) %all-to-all-start) | async-done | bytes 262176 | tf_op jit(solution)/shard_map/all_to_all | solution.py:30
  25.8 1.1 broadcast_in_dim.26
  26.8 4.0 %all-to-all-start.1 = ((bf16[4,32,4096]{2,1,0:T(8,128)(2,1)}), bf16[4,32,4096]{2,1,0:T(8,128)(2,1)S(1)}, u32[]{:S(2)}, u32[]{:S(2)}) async-start(bf16[4,32,4096]{2,1,0:T(8,128)(2,1)} %broadcast_in_dim.26), calls=%async_computation.1 | async-start | bytes 2097152 | tf_op jit(solution)/shard_map/all_to_all | solution.py:30
  31.2 2.7 %collective-permute-start.3 = (bf16[64,4096]{1,0:T(8,128)(2,1)S(1)}, bf16[64,4096]{1,0:T(8,128)(2,1)}, u32[]{:S(2)}, u32[]{:S(2)}) collective-permute-start(bf16[64,4096]{1,0:T(8,128)(2,1)S(1)} %collective-permute-done.1.refs_4_), channel_id=1, source_target_pairs={{0,192},{64,0},{128,64},{192,128},{1,193},{65,1},{129,65},{193,129... | collective-permute-start | bytes 1572872 | tf_op jit(solution)/shard_map/ppermute | solution.py:25
  34.2 8.8 %collective-permute-done.2.refs_5_ = bf16[64,4096]{1,0:T(8,128)(2,1)} collective-permute-done((bf16[64,4096]{1,0:T(8,128)(2,1)S(1)}, bf16[64,4096]{1,0:T(8,128)(2,1)}, u32[]{:S(2)}, u32[]{:S(2)}) %collective-permute-start.2) | collective-permute-done | bytes 524320 | tf_op jit(solution)/shard_map/ppermute | solution.py:25
  42.9 4.0 %collective-permute-start.6 = (bf16[128,4096]{1,0:T(8,128)(2,1)S(1)}, bf16[128,4096]{1,0:T(8,128)(2,1)S(1)}, u32[]{:S(2)}, u32[]{:S(2)}) collective-permute-start(bf16[128,4096]{1,0:T(8,128)(2,1)S(1)} %bitcast.13), channel_id=1, source_target_pairs={{0,1},{1,0},{2,3},{3,2},{4,5},{5,4},{6,7},{7,6},{8,9},{9,8},{10,11... | collective-permute-start | bytes 3145736 | tf_op jit(solution)/shard_map/ppermute | solution.py:25
  46.9 2.3 %collective-permute-done.6.other = bf16[128,4096]{1,0:T(8,128)(2,1)S(1)} collective-permute-done((bf16[128,4096]{1,0:T(8,128)(2,1)S(1)}, bf16[128,4096]{1,0:T(8,128)(2,1)S(1)}, u32[]{:S(2)}, u32[]{:S(2)}) %collective-permute-start.6) | collective-permute-done | bytes 1048608 | tf_op jit(solution)/shard_map/ppermute | solution.py:25
  49.2 4.6 %shard_map.85 = (f32[512,256]{1,0:T(8,128)S(1)}, f32[64,2,256]{2,1,0:T(2,128)S(1)}) custom-call(s32[5]{0:T(128)S(1)} %pad_add_fusion.place, bf16[128,4096]{1,0:T(8,128)(2,1)S(1)} %bitcast.14, bf16[128,4096]{1,0:T(8,128)(2,1)S(1)} %collective-permute-done.6.other, bf16[128,4096]{1,0:T(8,128)(2,1)S(1)} %copy-done, ...), custom_call_target="tpu_custom_call" | custom-call | flops 1073741824 | bytes 6955028 | tf_op jit(solution)/shard_map/pallas_call | solution.py:57
  53.8 18.1 %all_to_all.25.table = f32[64,2,256]{2,1,0:T(2,128)S(1)} all-to-all(f32[64,2,256]{2,1,0:T(2,128)S(1)} %get-tuple-element.41), channel_id=1, replica_groups=mesh['row'=4,'col_0'=8,'col_1'=4,'col_2'=2] {'col_0','col_1','col_2'}, dimensions={0} | all-to-all | bytes 262144 | tf_op jit(solution)/shard_map/all_to_all | solution.py:207
  71.9 1.1 shard_map.86
  72.9 13.9 %all_to_all.26.table = f32[64,1,256]{2,1,0:T(1,128)S(1)} all-to-all(f32[64,1,256]{2,1,0:T(1,128)S(1)} %get-tuple-element.44), channel_id=1, replica_groups=mesh['row'=4,'col_0'=8,'col_1'=4,'col_2'=2] {'col_0','col_1','col_2'}, dimensions={0} | all-to-all | bytes 131072 | tf_op jit(solution)/shard_map/all_to_all | solution.py:214
  86.8 6.7 %shard_map.87 = (f32[8,256]{1,0:T(8,128)S(1)}, bf16[64,4096]{1,0:T(8,128)(2,1)}, bf16[64,4096]{1,0:T(8,128)(2,1)}, bf16[64,4096]{1,0:T(8,128)(2,1)}, bf16[64,409...) custom-call(s32[5]{0:T(128)S(1)} %pad_add_fusion.place, ...), custom_call_target="tpu_custom_call" | custom-call | flops 2147483648 | bytes 16343060 | tf_op jit(solution)/shard_map/pallas_call | solution.py:57
  94.1 1.3 collective-permute-start.12
  95.4 1.4 collective-permute-start.8
  96.7 1.4 %collective-permute-start.10 = (bf16[64,4096]{1,0:T(8,128)(2,1)}, bf16[64,4096]{1,0:T(8,128)(2,1)S(1)}, u32[]{:S(2)}, u32[]{:S(2)}) collective-permute-start(bf16[64,4096]{1,0:T(8,128)(2,1)} %get-tuple-element.55), channel_id=1, source_target_pairs={{0,192},{64,0},{128,64},{192,128},{1,193},{65,1},{129,65},{193,129... | collective-permute-start | bytes 1572872 | tf_op jit(solution)/shard_map/ppermute | solution.py:25
  98.2 2.4 %add_convert_fusion = bf16[128,4096]{1,0:T(8,128)(2,1)S(1)} fusion(f32[128,4096]{1,0:T(8,128)} %get-tuple-element.48, f32[128,4096]{1,0:T(8,128)} %collective-permute-done.7), kind=kLoop, calls=%fused_computation.1 | loop fusion | flops 1048576 | bytes 5242880 | tf_op jit(solution)/shard_map/convert_element_type | solution.py:236
  100.7 1.2 reshape.51
  101.9 1.0 dynamic-slice_add_fusion
  102.9 4.7 %all-to-all-start.4 = ((bf16[32,4,4096]{2,1,0:T(4,128)(2,1)}), bf16[32,4,4096]{2,1,0:T(4,128)(2,1)}, u32[]{:S(2)}, u32[]{:S(2)}) async-start(bf16[32,4,4096]{2,1,0:T(4,128)(2,1)} %reshape.51), calls=%async_computation.4 | async-start | bytes 2097152 | tf_op jit(solution)/shard_map/all_to_all | solution.py:238
  107.6 1.3 collective-permute-done.12
  108.8 2.1 %add_convert_fusion.1 = bf16[64,4096]{1,0:T(8,128)(2,1)} fusion(bf16[64,4096]{1,0:T(8,128)(2,1)} %collective-permute-done.12, bf16[64,4096]{1,0:T(8,128)(2,1)} %get-tuple-element.57), kind=kLoop, calls=%fused_computation.2 | loop fusion | flops 1048576 | bytes 1572864 | tf_op jit(solution)/shard_map/convert_element_type | solution.py:231
  111.2 2.2 %add_convert_fusion.2 = bf16[64,4096]{1,0:T(8,128)(2,1)} fusion(bf16[64,4096]{1,0:T(8,128)(2,1)} %collective-permute-done.8, bf16[64,4096]{1,0:T(8,128)(2,1)} %get-tuple-element.53), kind=kLoop, calls=%fused_computation.3 | loop fusion | flops 1048576 | bytes 1572864 | tf_op jit(solution)/shard_map/convert_element_type | solution.py:230
  113.4 2.5 %collective-permute-start.9 = (bf16[64,4096]{1,0:T(8,128)(2,1)}, bf16[64,4096]{1,0:T(8,128)(2,1)}, u32[]{:S(2)}, u32[]{:S(2)}) collective-permute-start(bf16[64,4096]{1,0:T(8,128)(2,1)} %add_convert_fusion.2), channel_id=1, source_target_pairs={{0,192},{64,0},{128,64},{192,128},{1,193},{65,1},{129,65},{193,129... | collective-permute-start | bytes 1572872 | tf_op jit(solution)/shard_map/ppermute | solution.py:25
  116.4 3.4 %collective-permute-done.10.back_high = bf16[64,4096]{1,0:T(8,128)(2,1)S(1)} collective-permute-done((bf16[64,4096]{1,0:T(8,128)(2,1)}, bf16[64,4096]{1,0:T(8,128)(2,1)S(1)}, u32[]{:S(2)}, u32[]{:S(2)}) %collective-permute-start.10) | collective-permute-done | bytes 524320 | tf_op jit(solution)/shard_map/ppermute | solution.py:25
  120.1 11.2 %collective-permute-done.13.ahead_high = bf16[64,4096]{1,0:T(8,128)(2,1)} collective-permute-done((bf16[64,4096]{1,0:T(8,128)(2,1)}, bf16[64,4096]{1,0:T(8,128)(2,1)}, u32[]{:S(2)}, u32[]{:S(2)}) %collective-permute-start.13) | collective-permute-done | bytes 524320 | tf_op jit(solution)/shard_map/ppermute | solution.py:25
  131.3 3.8 %shard_map.88 = f32[128,4096]{1,0:T(8,128)} custom-call(f32[128,4096]{1,0:T(8,128)S(1)} %copy-done.1, bf16[64,4096]{1,0:T(8,128)(2,1)} %collective-permute-done.9.back_low, bf16[64,4096]{1,0:T(8,128)(2,1)S(1)} %collective-permute-done.10.back_high, bf16[64,4096]{1,0:T(8,128)(2,1)S(1)} %collective-permute-done.11.ahead_low, ...), custom_call_target="tpu_custom_call" | custom-call | bytes 6291456 | tf_op jit(solution)/shard_map/pallas_call | solution.py:57
  135.1 1.9 %select_reduce_fusion = f32[4,4096]{1,0:T(4,128)S(1)} fusion(bf16[32,4,4096]{2,1,0:T(4,128)(2,1)} %all-to-all-done.4, pred[32]{0:T(512)(128)(4,1)S(1)} %iota_compare_fusion), kind=kLoop, calls=%fused_computation | loop fusion | flops 1556480 | bytes 1114144 | tf_op jit(solution)/shard_map/reduce_sum | solution.py:240
  (49 shorter events, 4.8 us)
Async XLA Ops:
  0.6 5.9 %copy-start.2 = (bf16[4,4096]{1,0:T(4,128)(2,1)S(1)}, bf16[4,4096]{1,0:T(4,128)(2,1)}, u32[]{:S(2)}) copy-start(bf16[4,4096]{1,0:T(4,128)(2,1)} %param.6) | copy-start | bytes 98308
  0.6 17.5 %copy-start.3 = (s32[256,7]{0,1:T(8,128)S(1)}, s32[256,7]{0,1:T(8,128)}, u32[]{:S(2)}) copy-start(s32[256,7]{0,1:T(8,128)} %param.9) | copy-start | bytes 21508
  0.7 17.9 %copy-start.4 = (s32[256]{0:T(256)S(1)}, s32[256]{0:T(256)}, u32[]{:S(2)}) copy-start(s32[256]{0:T(256)} %param.8) | copy-start | bytes 3076
  3.0 22.7 %collective-permute-start = (bf16[64,4096]{1,0:T(8,128)(2,1)}, bf16[64,4096]{1,0:T(8,128)(2,1)S(1)}, u32[]{:S(2)}, u32[]{:S(2)}) collective-permute-start(bf16[64,4096]{1,0:T(8,128)(2,1)} %get-tuple-element.60), channel_id=1, source_target_pairs={{0,64},{64,128},{128,192},{192,0},{1,65},{65,129},{129,193},{193,1... | collective-permute-start | bytes 1572872 | tf_op jit(solution)/shard_map/ppermute | solution.py:25
  5.1 20.6 %collective-permute-start.1 = (bf16[64,4096]{1,0:T(8,128)(2,1)}, bf16[64,4096]{1,0:T(8,128)(2,1)S(1)}, u32[]{:S(2)}, u32[]{:S(2)}) collective-permute-start(bf16[64,4096]{1,0:T(8,128)(2,1)} %get-tuple-element.59), channel_id=1, source_target_pairs={{0,192},{64,0},{128,64},{192,128},{1,193},{65,1},{129,65},{193,129... | collective-permute-start | bytes 1572872 | tf_op jit(solution)/shard_map/ppermute | solution.py:25
  7.3 18.3 %all-to-all-start = ((bf16[8,4,4096]{2,1,0:T(4,128)(2,1)}), bf16[8,4,4096]{2,1,0:T(4,128)(2,1)S(1)}, u32[]{:S(2)}, u32[]{:S(2)}) async-start(bf16[8,4,4096]{2,1,0:T(4,128)(2,1)} %broadcast_in_dim.25), calls=%async_computation | async-start | bytes 524288 | tf_op jit(solution)/shard_map/all_to_all | solution.py:30
  15.5 18.6 %collective-permute-start.4 = (bf16[64,4096]{1,0:T(8,128)(2,1)}, bf16[64,4096]{1,0:T(8,128)(2,1)}, u32[]{:S(2)}, u32[]{:S(2)}) collective-permute-start(bf16[64,4096]{1,0:T(8,128)(2,1)} %get-tuple-element.59), channel_id=1, source_target_pairs={{0,64},{64,128},{128,192},{192,0},{1,65},{65,129},{129,193},{193,1... | collective-permute-start | bytes 1572872 | tf_op jit(solution)/shard_map/ppermute | solution.py:25
  15.5 18.6 %collective-permute-start.5 = (bf16[64,4096]{1,0:T(8,128)(2,1)}, bf16[64,4096]{1,0:T(8,128)(2,1)}, u32[]{:S(2)}, u32[]{:S(2)}) collective-permute-start(bf16[64,4096]{1,0:T(8,128)(2,1)} %get-tuple-element.60), channel_id=1, source_target_pairs={{0,192},{64,0},{128,64},{192,128},{1,193},{65,1},{129,65},{193,129... | collective-permute-start | bytes 1572872 | tf_op jit(solution)/shard_map/ppermute | solution.py:25
  19.4 11.6 %copy-start.5 = (f32[256]{0:T(256)S(1)}, f32[256]{0:T(256)}, u32[]{:S(2)}) copy-start(f32[256]{0:T(256)} %param.10) | copy-start | bytes 3076
  25.7 8.3 %copy-start.6 = (s32[4]{0:T(128)S(1)}, s32[4]{0:T(128)}, u32[]{:S(2)}) copy-start(s32[4]{0:T(128)} %constant.49) | copy-start | bytes 52
  25.8 23.4 %copy-start = (bf16[128,4096]{1,0:T(8,128)(2,1)S(1)}, bf16[128,4096]{1,0:T(8,128)(2,1)}, u32[]{:S(2)}) copy-start(bf16[128,4096]{1,0:T(8,128)(2,1)} %refs_0_.3) | copy-start | bytes 3145732
  26.8 16.1 %all-to-all-start.1 = ((bf16[4,32,4096]{2,1,0:T(8,128)(2,1)}), bf16[4,32,4096]{2,1,0:T(8,128)(2,1)S(1)}, u32[]{:S(2)}, u32[]{:S(2)}) async-start(bf16[4,32,4096]{2,1,0:T(8,128)(2,1)} %broadcast_in_dim.26), calls=%async_computation.1 | async-start | bytes 2097152 | tf_op jit(solution)/shard_map/all_to_all | solution.py:30
  31.1 11.9 %collective-permute-start.2 = (bf16[64,4096]{1,0:T(8,128)(2,1)S(1)}, bf16[64,4096]{1,0:T(8,128)(2,1)}, u32[]{:S(2)}, u32[]{:S(2)}) collective-permute-start(bf16[64,4096]{1,0:T(8,128)(2,1)S(1)} %collective-permute-done.refs_1_), channel_id=1, source_target_pairs={{0,64},{64,128},{128,192},{192,0},{1,65},{65,129},{129,193},{193,1... | collective-permute-start | bytes 1572872 | tf_op jit(solution)/shard_map/ppermute | solution.py:25
  31.2 11.8 %collective-permute-start.3 = (bf16[64,4096]{1,0:T(8,128)(2,1)S(1)}, bf16[64,4096]{1,0:T(8,128)(2,1)}, u32[]{:S(2)}, u32[]{:S(2)}) collective-permute-start(bf16[64,4096]{1,0:T(8,128)(2,1)S(1)} %collective-permute-done.1.refs_4_), channel_id=1, source_target_pairs={{0,192},{64,0},{128,64},{192,128},{1,193},{65,1},{129,65},{193,129... | collective-permute-start | bytes 1572872 | tf_op jit(solution)/shard_map/ppermute | solution.py:25
  42.9 6.2 %collective-permute-start.6 = (bf16[128,4096]{1,0:T(8,128)(2,1)S(1)}, bf16[128,4096]{1,0:T(8,128)(2,1)S(1)}, u32[]{:S(2)}, u32[]{:S(2)}) collective-permute-start(bf16[128,4096]{1,0:T(8,128)(2,1)S(1)} %bitcast.13), channel_id=1, source_target_pairs={{0,1},{1,0},{2,3},{3,2},{4,5},{5,4},{6,7},{7,6},{8,9},{9,8},{10,11... | collective-permute-start | bytes 3145736 | tf_op jit(solution)/shard_map/ppermute | solution.py:25
  93.6 4.6 %collective-permute-start.7 = (f32[128,4096]{1,0:T(8,128)}, f32[128,4096]{1,0:T(8,128)}, u32[]{:S(2)}, u32[]{:S(2)}) collective-permute-start(f32[128,4096]{1,0:T(8,128)} %get-tuple-element.49), channel_id=1, source_target_pairs={{0,1},{1,0},{2,3},{3,2},{4,5},{5,4},{6,7},{7,6},{8,9},{9,8},{10,11... | collective-permute-start | bytes 6291464 | tf_op jit(solution)/shard_map/ppermute | solution.py:25
  94.1 14.8 %collective-permute-start.12 = (bf16[64,4096]{1,0:T(8,128)(2,1)}, bf16[64,4096]{1,0:T(8,128)(2,1)}, u32[]{:S(2)}, u32[]{:S(2)}) collective-permute-start(bf16[64,4096]{1,0:T(8,128)(2,1)} %get-tuple-element.58), channel_id=1, source_target_pairs={{0,64},{64,128},{128,192},{192,0},{1,65},{65,129},{129,193},{193,1... | collective-permute-start | bytes 1572872 | tf_op jit(solution)/shard_map/ppermute | solution.py:25
  95.4 15.8 %collective-permute-start.8 = (bf16[64,4096]{1,0:T(8,128)(2,1)}, bf16[64,4096]{1,0:T(8,128)(2,1)}, u32[]{:S(2)}, u32[]{:S(2)}) collective-permute-start(bf16[64,4096]{1,0:T(8,128)(2,1)} %get-tuple-element.54), channel_id=1, source_target_pairs={{0,192},{64,0},{128,64},{192,128},{1,193},{65,1},{129,65},{193,129... | collective-permute-start | bytes 1572872 | tf_op jit(solution)/shard_map/ppermute | solution.py:25
  96.7 23.1 %collective-permute-start.10 = (bf16[64,4096]{1,0:T(8,128)(2,1)}, bf16[64,4096]{1,0:T(8,128)(2,1)S(1)}, u32[]{:S(2)}, u32[]{:S(2)}) collective-permute-start(bf16[64,4096]{1,0:T(8,128)(2,1)} %get-tuple-element.55), channel_id=1, source_target_pairs={{0,192},{64,0},{128,64},{192,128},{1,193},{65,1},{129,65},{193,129... | collective-permute-start | bytes 1572872 | tf_op jit(solution)/shard_map/ppermute | solution.py:25
  98.2 21.9 %collective-permute-start.11 = (bf16[64,4096]{1,0:T(8,128)(2,1)}, bf16[64,4096]{1,0:T(8,128)(2,1)S(1)}, u32[]{:S(2)}, u32[]{:S(2)}) collective-permute-start(bf16[64,4096]{1,0:T(8,128)(2,1)} %get-tuple-element.56), channel_id=1, source_target_pairs={{0,64},{64,128},{128,192},{192,0},{1,65},{65,129},{129,193},{193,1... | collective-permute-start | bytes 1572872 | tf_op jit(solution)/shard_map/ppermute | solution.py:25
  102.9 32.2 %all-to-all-start.4 = ((bf16[32,4,4096]{2,1,0:T(4,128)(2,1)}), bf16[32,4,4096]{2,1,0:T(4,128)(2,1)}, u32[]{:S(2)}, u32[]{:S(2)}) async-start(bf16[32,4,4096]{2,1,0:T(4,128)(2,1)} %reshape.51), calls=%async_computation.4 | async-start | bytes 2097152 | tf_op jit(solution)/shard_map/all_to_all | solution.py:238
  107.6 23.8 %copy-start.1 = (f32[128,4096]{1,0:T(8,128)S(1)}, f32[128,4096]{1,0:T(8,128)}, u32[]{:S(2)}) copy-start(f32[128,4096]{1,0:T(8,128)} %get-tuple-element.52.here) | copy-start | bytes 6291460
  111.0 20.4 %collective-permute-start.13 = (bf16[64,4096]{1,0:T(8,128)(2,1)}, bf16[64,4096]{1,0:T(8,128)(2,1)}, u32[]{:S(2)}, u32[]{:S(2)}) collective-permute-start(bf16[64,4096]{1,0:T(8,128)(2,1)} %add_convert_fusion.1), channel_id=1, source_target_pairs={{0,64},{64,128},{128,192},{192,0},{1,65},{65,129},{129,193},{193,1... | collective-permute-start | bytes 1572872 | tf_op jit(solution)/shard_map/ppermute | solution.py:25
  113.4 17.9 %collective-permute-start.9 = (bf16[64,4096]{1,0:T(8,128)(2,1)}, bf16[64,4096]{1,0:T(8,128)(2,1)}, u32[]{:S(2)}, u32[]{:S(2)}) collective-permute-start(bf16[64,4096]{1,0:T(8,128)(2,1)} %add_convert_fusion.2), channel_id=1, source_target_pairs={{0,192},{64,0},{128,64},{192,128},{1,193},{65,1},{129,65},{193,129... | collective-permute-start | bytes 1572872 | tf_op jit(solution)/shard_map/ppermute | solution.py:25

commit v8 on v7

--- a/solution.py
+++ b/solution.py
@@ -34,14 +34,14 @@
     return jax.ShapeDtypeStruct(dims, dtype)
 
 
-def call(body, outs, args, flops=0, scalars=0, tiled=(), scratch=(), outside=()):
+def call(body, outs, args, flops=0, scalars=0, tiled=(), scratch=(), outside=(), tile=TILE):
     size = sum(a.size * a.dtype.itemsize for a in (*args, *outs))
     specs = []
     for k, a in enumerate((*args, *outs)):
         if k < scalars:
             specs.append(pl.BlockSpec(memory_space=pltpu.SMEM))
         elif k in tiled:
-            specs.append(pl.BlockSpec((a.shape[0], TILE), lambda i: (0, i)))
+            specs.append(pl.BlockSpec((*a.shape[:-1], tile), lambda i, n=len(a.shape): (0,) * (n - 1) + (i,)))
         else:
             specs.append(pl.BlockSpec(a.shape, lambda i, n=len(a.shape): (0,) * n))
     kinds = [pltpu.HBM if k in outside else None for k in range(len(specs))]
@@ -53,7 +53,7 @@
         o if kind is None else pltpu.HBM(o.shape, o.dtype)
         for o, kind in zip(outs, kinds[len(args) :])
     ]
-    steps = (*args, *outs)[tiled[0]].shape[1] // TILE if tiled else 1
+    steps = (*args, *outs)[tiled[0]].shape[-1] // tile if tiled else 1
     return pl.pallas_call(
         body,
         grid=(steps,),
@@ -81,25 +81,31 @@
     return found[0], functools.reduce(jnp.logical_or, found)
 
 
-def score_body(place, own, other, *refs):
-    pool, ids, scores, table = refs[:7], *refs[7:]
-
+def products(queries, pool, scores):
     @on_step(0)
     def _():
         scores[...] = jnp.zeros_like(scores)
 
     rows = jnp.concatenate([p[...] for p in pool], axis=0)
-    columns = jnp.concatenate([own[...], other[...]], axis=0)
     scores[...] += lax.dot_general(
-        rows, columns, (((1,), (1,)), ((), ())), preferred_element_type=F32
-    )
+        rows, queries[...], (((1,), (1,)), ((), ())), preferred_element_type=F32
+    )
+
+
+def own_body(own, *refs):
+    products(own, refs[:7], refs[7])
+
+
+def score_body(place, other, *refs):
+    pool, own_scores, ids, scores, table, sums = refs[:7], *refs[7:]
+    products(other, pool, sums)
 
     @pl.when(pl.program_id(0) == pl.num_programs(0) - 1)
     def _():
         tops = [[], []]
         for k in range(4):
             rows = slice(128 * k, 128 * k + 128)
-            block = scores[rows, :] * inv_temp
+            block = jnp.concatenate([own_scores[rows, :], sums[rows, :]], axis=1) * inv_temp
             scores[rows, :] = block
             for top, mark in zip(tops, marks(place, ids, k, 8)):
                 top.append(jnp.max(jnp.where(mark, block, LOWEST), axis=0, keepdims=True))
@@ -153,6 +159,11 @@
     theirs[...] = out[128:]
 
 
+def gathered_body(place, parts, exact, total):
+    one = lax.broadcasted_iota(jnp.int32, parts.shape, 0) != place[0]
+    total[...] = exact[...] + jnp.sum(jnp.where(one, parts[...].astype(F32), 0.0), axis=0)
+
+
 def total_body(here, back_low, back_high, ahead_low, ahead_high, total):
     half = back_low.shape[0]
     for rows, parts in (
@@ -196,13 +207,21 @@
     other = shifted(own, CORE, 1)
     blocks = [passages, back_low, back_high, ahead_low, ahead_high, far_low, far_high]
 
+    own_scores = call(
+        own_body,
+        [shape((pool, plane), F32)],
+        [own, *blocks],
+        flops=2 * plane * pool * width,
+        tiled=range(8),
+    )[0]
     scores, table = call(
         score_body,
         [shape((pool, total), F32), shape((members, 2, total), F32)],
-        [place, own, other, *blocks, ids],
-        flops=2 * total * pool * width,
-        scalars=1,
-        tiled=range(1, 10),
+        [place, other, *blocks, own_scores, ids],
+        flops=2 * plane * pool * width,
+        scalars=1,
+        tiled=range(1, 9),
+        scratch=[pltpu.VMEM((pool, plane), F32)],
     )
     table = lax.all_to_all(table, COL, 0, 0, tiled=True)
     weights, table, stats = call(
@@ -236,14 +255,20 @@
     sent = (mine + theirs).astype(BF16).reshape(breadth * depth, rows, width)
     exact, sent = lax.optimization_barrier((exact, sent))
     parts = lax.all_to_all(sent, (X, Z), 0, 0, tiled=True)
-    others = (lax.iota(jnp.int32, breadth * depth) != place_of)[:, None, None]
-    grad_queries = exact + jnp.sum(jnp.where(others, parts.astype(F32), 0.0), axis=0)
+    grad_queries = call(
+        gathered_body,
+        [shape((rows, width), F32)],
+        [place_of.reshape(1).astype(jnp.int32), parts, exact],
+        scalars=1,
+        tiled=(1, 2, 3),
+    )[0]
 
     grad_passages = call(
         total_body,
         [shape((count, width), F32)],
         [here, back_low, back_high, ahead_low, ahead_high],
         tiled=range(6),
+        tile=2048,
     )[0]
 
     row_losses = lax.dynamic_slice_in_dim(losses[0], at, rows, 0)

time: 139 us -> 138 us (level)
  Pallas kernels: 16.2 us -> 20.4 us
  other arithmetic: 10.6 us -> 7.27 us
    pallas_call x4 -> x6, Pallas kernels: 16.2 us -> 20.4 us  [call(): pl.pallas_call(body, grid=(steps,), out_shape=outs, in_specs=specs[:len(a...]
    reduce_sum x1 -> x0, other arithmetic: 1.93 us -> none  [on_device(): jnp.sum(jnp.where(others, parts.astype(F32), 0.0), axis=0)]
  transfers between devices with their start and end apart: 17 -> 17, of which waited for: 7 -> 6; matrix products, arithmetic and copies ran while one was open for 10% -> 9% of each run, Pallas kernels for 3% -> 5%
where the time goes in v8:
time: 138 us; the launch traced here: 137 us
  starting transfers between devices  36.6 us (27%)
  waiting for transfers between devices  32.8 us (24%)
  blocking collectives  31.7 us (23%)
  Pallas kernels  20.4 us (15%)
  local copies, waits for them, and re-layouts  7.45 us (5%)
  other arithmetic  7.27 us (5%)
    all_to_all x2, blocking collectives, on_device(): table = lax.all_to_all(table, COL, 0, 0, tiled=True)  31.7 us
    ppermute x14, waiting for transfers between devices, shifted(): return lax.ppermute(value, axis, [(i, (i + step) % n) for i in range(n)])  26.6 us
    ppermute x14, starting transfers between devices, shifted(): return lax.ppermute(value, axis, [(i, (i + step) % n) for i in range(n)])  20.5 us
    pallas_call x6, Pallas kernels, call(): pl.pallas_call(body, grid=(steps,), out_shape=outs, in_specs=specs[:len(a...  20.4 us
    all_to_all x2, starting transfers between devices, copies(): lax.all_to_all(jnp.broadcast_to(value, (n, *value.shape)), axis, 0, 0, ti...  12.2 us
    all_to_all x2, waiting for transfers between devices, copies(): lax.all_to_all(jnp.broadcast_to(value, (n, *value.shape)), axis, 0, 0, ti...  6.29 us
    all_to_all x1, starting transfers between devices, on_device(): parts = lax.all_to_all(sent, (X, Z), 0, 0, tiled=True)  3.94 us
  transfers between devices with their start and end apart: 17, of which 6 were waited for; matrix products, arithmetic and copies ran while one was open for 9% of the time, Pallas kernels for 5%

profile of v8, /device:TPU:1, one launch (start us, length us, event | category | flops | bytes accessed | tf_op | source)
XLA Modules:
  0.0 137.1 jit_solution(16028386780911268702)
XLA Ops:
  0.7 2.3 %fusion.4 = (bf16[64,4096]{1,0:T(8,128)(2,1)}, bf16[64,4096]{1,0:T(8,128)(2,1)}) fusion(bf16[128,4096]{1,0:T(8,128)(2,1)} %refs_0_.5), kind=kLoop, calls=%fused_computation.16 | loop fusion | bytes 2097152 | tf_op jit(solution)/shard_map/slice | solution.py:185
  3.0 2.1 %collective-permute-start = (bf16[64,4096]{1,0:T(8,128)(2,1)}, bf16[64,4096]{1,0:T(8,128)(2,1)S(1)}, u32[]{:S(2)}, u32[]{:S(2)}) collective-permute-start(bf16[64,4096]{1,0:T(8,128)(2,1)} %get-tuple-element.60), channel_id=1, source_target_pairs={{0,64},{64,128},{128,192},{192,0},{1,65},{65,129},{129,193},{193,1... | collective-permute-start | bytes 1572872 | tf_op jit(solution)/shard_map/ppermute | solution.py:25
  5.1 1.4 %collective-permute-start.1 = (bf16[64,4096]{1,0:T(8,128)(2,1)}, bf16[64,4096]{1,0:T(8,128)(2,1)S(1)}, u32[]{:S(2)}, u32[]{:S(2)}) collective-permute-start(bf16[64,4096]{1,0:T(8,128)(2,1)} %get-tuple-element.59), channel_id=1, source_target_pairs={{0,192},{64,0},{128,64},{192,128},{1,193},{65,1},{129,65},{193,129... | collective-permute-start | bytes 1572872 | tf_op jit(solution)/shard_map/ppermute | solution.py:25
  7.3 8.2 %all-to-all-start = ((bf16[8,4,4096]{2,1,0:T(4,128)(2,1)}), bf16[8,4,4096]{2,1,0:T(4,128)(2,1)S(1)}, u32[]{:S(2)}, u32[]{:S(2)}) async-start(bf16[8,4,4096]{2,1,0:T(4,128)(2,1)} %broadcast_in_dim.12), calls=%async_computation | async-start | bytes 524288 | tf_op jit(solution)/shard_map/all_to_all | solution.py:30
  15.5 2.7 %collective-permute-start.5 = (bf16[64,4096]{1,0:T(8,128)(2,1)}, bf16[64,4096]{1,0:T(8,128)(2,1)}, u32[]{:S(2)}, u32[]{:S(2)}) collective-permute-start(bf16[64,4096]{1,0:T(8,128)(2,1)} %get-tuple-element.60), channel_id=1, source_target_pairs={{0,192},{64,0},{128,64},{192,128},{1,193},{65,1},{129,65},{193,129... | collective-permute-start | bytes 1572872 | tf_op jit(solution)/shard_map/ppermute | solution.py:25
  19.4 6.3 %all-to-all-done = bf16[8,4,4096]{2,1,0:T(4,128)(2,1)S(1)} async-done(((bf16[8,4,4096]{2,1,0:T(4,128)(2,1)}), bf16[8,4,4096]{2,1,0:T(4,128)(2,1)S(1)}, u32[]{:S(2)}, u32[]{:S(2)}) %all-to-all-start) | async-done | bytes 262176 | tf_op jit(solution)/shard_map/all_to_all | solution.py:30
  25.8 1.1 broadcast_in_dim.13
  26.8 4.0 %all-to-all-start.1 = ((bf16[4,32,4096]{2,1,0:T(8,128)(2,1)}), bf16[4,32,4096]{2,1,0:T(8,128)(2,1)S(1)}, u32[]{:S(2)}, u32[]{:S(2)}) async-start(bf16[4,32,4096]{2,1,0:T(8,128)(2,1)} %broadcast_in_dim.13), calls=%async_computation.1 | async-start | bytes 2097152 | tf_op jit(solution)/shard_map/all_to_all | solution.py:30
  31.2 2.7 %collective-permute-start.3 = (bf16[64,4096]{1,0:T(8,128)(2,1)S(1)}, bf16[64,4096]{1,0:T(8,128)(2,1)}, u32[]{:S(2)}, u32[]{:S(2)}) collective-permute-start(bf16[64,4096]{1,0:T(8,128)(2,1)S(1)} %collective-permute-done.1.refs_4_), channel_id=1, source_target_pairs={{0,192},{64,0},{128,64},{192,128},{1,193},{65,1},{129,65},{193,129... | collective-permute-start | bytes 1572872 | tf_op jit(solution)/shard_map/ppermute | solution.py:25
  34.1 8.8 %collective-permute-done.2.refs_5_ = bf16[64,4096]{1,0:T(8,128)(2,1)} collective-permute-done((bf16[64,4096]{1,0:T(8,128)(2,1)S(1)}, bf16[64,4096]{1,0:T(8,128)(2,1)}, u32[]{:S(2)}, u32[]{:S(2)}) %collective-permute-start.2) | collective-permute-done | bytes 524320 | tf_op jit(solution)/shard_map/ppermute | solution.py:25
  42.9 4.0 %collective-permute-start.6 = (bf16[128,4096]{1,0:T(8,128)(2,1)S(1)}, bf16[128,4096]{1,0:T(8,128)(2,1)S(1)}, u32[]{:S(2)}, u32[]{:S(2)}) collective-permute-start(bf16[128,4096]{1,0:T(8,128)(2,1)S(1)} %bitcast.14), channel_id=1, source_target_pairs={{0,1},{1,0},{2,3},{3,2},{4,5},{5,4},{6,7},{7,6},{8,9},{9,8},{10,11... | collective-permute-start | bytes 3145736 | tf_op jit(solution)/shard_map/ppermute | solution.py:25
  46.9 3.7 %shard_map.85.refs_7_ = f32[512,128]{1,0:T(8,128)S(1)} custom-call(bf16[128,4096]{1,0:T(8,128)(2,1)S(1)} %bitcast.15, bf16[128,4096]{1,0:T(8,128)(2,1)S(1)} %copy-done, bf16[64,4096]{1,0:T(8,128)(2,1)S(1)} %collective-permute-done.refs_1_, bf16[64,4096]{1,0:T(8,128)(2,1)} %collective-permute-done.4.refs_2_, bf16[64,4096]{1,0:T(8,128)(2,1)} %collective-permute-done.5.refs_3_, ...), custom_call_target="tpu_custom_call" | custom-call | flops 536870912 | bytes 5505024 | tf_op jit(solution)/shard_map/pallas_call | solution.py:57
  50.7 4.4 %shard_map.86 = (f32[512,256]{1,0:T(8,128)S(1)}, f32[64,2,256]{2,1,0:T(2,128)S(1)}) custom-call(s32[5]{0:T(128)S(1)} %pad_add_fusion.place, bf16[128,4096]{1,0:T(8,128)(2,1)S(1)} %collective-permute-done.6.other, bf16[128,4096]{1,0:T(8,128)(2,1)S(1)} %copy-done, bf16[64,4096]{1,0:T(8,128)(2,1)S(1)} %collective-permute-done.refs_1_, ...), custom_call_target="tpu_custom_call" | custom-call | flops 536870912 | bytes 6168596 | tf_op jit(solution)/shard_map/pallas_call | solution.py:57
  55.0 17.8 %all_to_all.25.table = f32[64,2,256]{2,1,0:T(2,128)S(1)} all-to-all(f32[64,2,256]{2,1,0:T(2,128)S(1)} %get-tuple-element.41), channel_id=1, replica_groups=mesh['row'=4,'col_0'=8,'col_1'=4,'col_2'=2] {'col_0','col_1','col_2'}, dimensions={0} | all-to-all | bytes 262144 | tf_op jit(solution)/shard_map/all_to_all | solution.py:226
  72.9 1.1 shard_map.87
  73.9 13.9 %all_to_all.26.table = f32[64,1,256]{2,1,0:T(1,128)S(1)} all-to-all(f32[64,1,256]{2,1,0:T(1,128)S(1)} %get-tuple-element.44), channel_id=1, replica_groups=mesh['row'=4,'col_0'=8,'col_1'=4,'col_2'=2] {'col_0','col_1','col_2'}, dimensions={0} | all-to-all | bytes 131072 | tf_op jit(solution)/shard_map/all_to_all | solution.py:233
  87.8 6.8 %shard_map.88 = (f32[8,256]{1,0:T(8,128)S(1)}, bf16[64,4096]{1,0:T(8,128)(2,1)}, bf16[64,4096]{1,0:T(8,128)(2,1)}, bf16[64,4096]{1,0:T(8,128)(2,1)}, bf16[64,409...) custom-call(s32[5]{0:T(128)S(1)} %pad_add_fusion.place, ...), custom_call_target="tpu_custom_call" | custom-call | flops 2147483648 | bytes 16343060 | tf_op jit(solution)/shard_map/pallas_call | solution.py:57
  95.3 1.3 collective-permute-start.12
  96.6 1.3 collective-permute-start.8
  98.0 1.5 %collective-permute-start.10 = (bf16[64,4096]{1,0:T(8,128)(2,1)}, bf16[64,4096]{1,0:T(8,128)(2,1)}, u32[]{:S(2)}, u32[]{:S(2)}) collective-permute-start(bf16[64,4096]{1,0:T(8,128)(2,1)} %get-tuple-element.55), channel_id=1, source_target_pairs={{0,192},{64,0},{128,64},{192,128},{1,193},{65,1},{129,65},{193,129... | collective-permute-start | bytes 1572872 | tf_op jit(solution)/shard_map/ppermute | solution.py:25
  99.5 1.8 %add_convert_fusion = bf16[128,4096]{1,0:T(8,128)(2,1)S(1)} fusion(f32[128,4096]{1,0:T(8,128)} %get-tuple-element.48, f32[128,4096]{1,0:T(8,128)S(1)} %collective-permute-done.7), kind=kLoop, calls=%fused_computation | loop fusion | flops 1048576 | bytes 5242880 | tf_op jit(solution)/shard_map/convert_element_type | solution.py:255
  101.3 1.2 reshape.51
  102.5 0.9 dynamic-slice_add_fusion.exact
  103.4 3.9 %all-to-all-start.4 = ((bf16[32,4,4096]{2,1,0:T(4,128)(2,1)}), bf16[32,4,4096]{2,1,0:T(4,128)(2,1)S(1)}, u32[]{:S(2)}, u32[]{:S(2)}) async-start(bf16[32,4,4096]{2,1,0:T(4,128)(2,1)} %reshape.51), calls=%async_computation.4 | async-start | bytes 2097152 | tf_op jit(solution)/shard_map/all_to_all | solution.py:257
  107.4 2.8 %collective-permute-done.12 = bf16[64,4096]{1,0:T(8,128)(2,1)} collective-permute-done((bf16[64,4096]{1,0:T(8,128)(2,1)}, bf16[64,4096]{1,0:T(8,128)(2,1)}, u32[]{:S(2)}, u32[]{:S(2)}) %collective-permute-start.12) | collective-permute-done | bytes 524320 | tf_op jit(solution)/shard_map/ppermute | solution.py:25
  110.2 2.2 %add_convert_fusion.1 = bf16[64,4096]{1,0:T(8,128)(2,1)} fusion(bf16[64,4096]{1,0:T(8,128)(2,1)} %collective-permute-done.12, bf16[64,4096]{1,0:T(8,128)(2,1)} %get-tuple-element.57), kind=kLoop, calls=%fused_computation.1 | loop fusion | flops 1048576 | bytes 1572864 | tf_op jit(solution)/shard_map/convert_element_type | solution.py:250
  112.6 2.1 %add_convert_fusion.2 = bf16[64,4096]{1,0:T(8,128)(2,1)} fusion(bf16[64,4096]{1,0:T(8,128)(2,1)} %collective-permute-done.8, bf16[64,4096]{1,0:T(8,128)(2,1)} %get-tuple-element.53), kind=kLoop, calls=%fused_computation.2 | loop fusion | flops 1048576 | bytes 1572864 | tf_op jit(solution)/shard_map/convert_element_type | solution.py:249
  114.7 2.5 %collective-permute-start.9 = (bf16[64,4096]{1,0:T(8,128)(2,1)}, bf16[64,4096]{1,0:T(8,128)(2,1)}, u32[]{:S(2)}, u32[]{:S(2)}) collective-permute-start(bf16[64,4096]{1,0:T(8,128)(2,1)} %add_convert_fusion.2), channel_id=1, source_target_pairs={{0,192},{64,0},{128,64},{192,128},{1,193},{65,1},{129,65},{193,129... | collective-permute-start | bytes 1572872 | tf_op jit(solution)/shard_map/ppermute | solution.py:25
  117.8 3.6 %collective-permute-done.10.back_high = bf16[64,4096]{1,0:T(8,128)(2,1)} collective-permute-done((bf16[64,4096]{1,0:T(8,128)(2,1)}, bf16[64,4096]{1,0:T(8,128)(2,1)}, u32[]{:S(2)}, u32[]{:S(2)}) %collective-permute-start.10) | collective-permute-done | bytes 524320 | tf_op jit(solution)/shard_map/ppermute | solution.py:25
  121.4 11.2 %collective-permute-done.13.ahead_high = bf16[64,4096]{1,0:T(8,128)(2,1)} collective-permute-done((bf16[64,4096]{1,0:T(8,128)(2,1)}, bf16[64,4096]{1,0:T(8,128)(2,1)}, u32[]{:S(2)}, u32[]{:S(2)}) %collective-permute-start.13) | collective-permute-done | bytes 524320 | tf_op jit(solution)/shard_map/ppermute | solution.py:25
  132.7 2.7 %shard_map.90 = f32[128,4096]{1,0:T(8,128)} custom-call(f32[128,4096]{1,0:T(8,128)S(1)} %copy-done.1, bf16[64,4096]{1,0:T(8,128)(2,1)} %collective-permute-done.9.back_low, bf16[64,4096]{1,0:T(8,128)(2,1)} %collective-permute-done.10.back_high, bf16[64,4096]{1,0:T(8,128)(2,1)} %collective-permute-done.11.ahead_low, ...), custom_call_target="tpu_custom_call" | custom-call | bytes 6291456 | tf_op jit(solution)/shard_map/pallas_call | solution.py:57
  135.4 1.7 %shard_map.89 = f32[4,4096]{1,0:T(4,128)} custom-call(s32[1]{0:T(128)} %bitcast.11.place, bf16[32,4,4096]{2,1,0:T(4,128)(2,1)S(1)} %all-to-all-done.4.parts, f32[4,4096]{1,0:T(4,128)S(1)} %dynamic-slice_add_fusion.exact), custom_call_target="tpu_custom_call" | custom-call | bytes 1179652 | tf_op jit(solution)/shard_map/pallas_call | solution.py:57
  (48 shorter events, 4.2 us)
Async XLA Ops:
  0.6 5.9 %copy-start.2 = (bf16[4,4096]{1,0:T(4,128)(2,1)S(1)}, bf16[4,4096]{1,0:T(4,128)(2,1)}, u32[]{:S(2)}) copy-start(bf16[4,4096]{1,0:T(4,128)(2,1)} %param.6) | copy-start | bytes 98308
  0.6 17.5 %copy-start.3 = (s32[256,7]{0,1:T(8,128)S(1)}, s32[256,7]{0,1:T(8,128)}, u32[]{:S(2)}) copy-start(s32[256,7]{0,1:T(8,128)} %param.9) | copy-start | bytes 21508
  0.7 17.9 %copy-start.4 = (s32[256]{0:T(256)S(1)}, s32[256]{0:T(256)}, u32[]{:S(2)}) copy-start(s32[256]{0:T(256)} %param.8) | copy-start | bytes 3076
  3.0 22.7 %collective-permute-start = (bf16[64,4096]{1,0:T(8,128)(2,1)}, bf16[64,4096]{1,0:T(8,128)(2,1)S(1)}, u32[]{:S(2)}, u32[]{:S(2)}) collective-permute-start(bf16[64,4096]{1,0:T(8,128)(2,1)} %get-tuple-element.60), channel_id=1, source_target_pairs={{0,64},{64,128},{128,192},{192,0},{1,65},{65,129},{129,193},{193,1... | collective-permute-start | bytes 1572872 | tf_op jit(solution)/shard_map/ppermute | solution.py:25
  5.1 20.6 %collective-permute-start.1 = (bf16[64,4096]{1,0:T(8,128)(2,1)}, bf16[64,4096]{1,0:T(8,128)(2,1)S(1)}, u32[]{:S(2)}, u32[]{:S(2)}) collective-permute-start(bf16[64,4096]{1,0:T(8,128)(2,1)} %get-tuple-element.59), channel_id=1, source_target_pairs={{0,192},{64,0},{128,64},{192,128},{1,193},{65,1},{129,65},{193,129... | collective-permute-start | bytes 1572872 | tf_op jit(solution)/shard_map/ppermute | solution.py:25
  7.3 18.3 %all-to-all-start = ((bf16[8,4,4096]{2,1,0:T(4,128)(2,1)}), bf16[8,4,4096]{2,1,0:T(4,128)(2,1)S(1)}, u32[]{:S(2)}, u32[]{:S(2)}) async-start(bf16[8,4,4096]{2,1,0:T(4,128)(2,1)} %broadcast_in_dim.12), calls=%async_computation | async-start | bytes 524288 | tf_op jit(solution)/shard_map/all_to_all | solution.py:30
  15.5 18.6 %collective-permute-start.4 = (bf16[64,4096]{1,0:T(8,128)(2,1)}, bf16[64,4096]{1,0:T(8,128)(2,1)}, u32[]{:S(2)}, u32[]{:S(2)}) collective-permute-start(bf16[64,4096]{1,0:T(8,128)(2,1)} %get-tuple-element.59), channel_id=1, source_target_pairs={{0,64},{64,128},{128,192},{192,0},{1,65},{65,129},{129,193},{193,1... | collective-permute-start | bytes 1572872 | tf_op jit(solution)/shard_map/ppermute | solution.py:25
  15.5 18.6 %collective-permute-start.5 = (bf16[64,4096]{1,0:T(8,128)(2,1)}, bf16[64,4096]{1,0:T(8,128)(2,1)}, u32[]{:S(2)}, u32[]{:S(2)}) collective-permute-start(bf16[64,4096]{1,0:T(8,128)(2,1)} %get-tuple-element.60), channel_id=1, source_target_pairs={{0,192},{64,0},{128,64},{192,128},{1,193},{65,1},{129,65},{193,129... | collective-permute-start | bytes 1572872 | tf_op jit(solution)/shard_map/ppermute | solution.py:25
  19.4 11.6 %copy-start.5 = (f32[256]{0:T(256)S(1)}, f32[256]{0:T(256)}, u32[]{:S(2)}) copy-start(f32[256]{0:T(256)} %param.10) | copy-start | bytes 3076
  25.7 8.3 %copy-start.6 = (s32[4]{0:T(128)S(1)}, s32[4]{0:T(128)}, u32[]{:S(2)}) copy-start(s32[4]{0:T(128)} %constant.47) | copy-start | bytes 52
  25.7 21.2 %copy-start = (bf16[128,4096]{1,0:T(8,128)(2,1)S(1)}, bf16[128,4096]{1,0:T(8,128)(2,1)}, u32[]{:S(2)}) copy-start(bf16[128,4096]{1,0:T(8,128)(2,1)} %refs_0_.5) | copy-start | bytes 3145732
  26.8 16.1 %all-to-all-start.1 = ((bf16[4,32,4096]{2,1,0:T(8,128)(2,1)}), bf16[4,32,4096]{2,1,0:T(8,128)(2,1)S(1)}, u32[]{:S(2)}, u32[]{:S(2)}) async-start(bf16[4,32,4096]{2,1,0:T(8,128)(2,1)} %broadcast_in_dim.13), calls=%async_computation.1 | async-start | bytes 2097152 | tf_op jit(solution)/shard_map/all_to_all | solution.py:30
  31.1 11.9 %collective-permute-start.2 = (bf16[64,4096]{1,0:T(8,128)(2,1)S(1)}, bf16[64,4096]{1,0:T(8,128)(2,1)}, u32[]{:S(2)}, u32[]{:S(2)}) collective-permute-start(bf16[64,4096]{1,0:T(8,128)(2,1)S(1)} %collective-permute-done.refs_1_), channel_id=1, source_target_pairs={{0,64},{64,128},{128,192},{192,0},{1,65},{65,129},{129,193},{193,1... | collective-permute-start | bytes 1572872 | tf_op jit(solution)/shard_map/ppermute | solution.py:25
  31.2 11.8 %collective-permute-start.3 = (bf16[64,4096]{1,0:T(8,128)(2,1)S(1)}, bf16[64,4096]{1,0:T(8,128)(2,1)}, u32[]{:S(2)}, u32[]{:S(2)}) collective-permute-start(bf16[64,4096]{1,0:T(8,128)(2,1)S(1)} %collective-permute-done.1.refs_4_), channel_id=1, source_target_pairs={{0,192},{64,0},{128,64},{192,128},{1,193},{65,1},{129,65},{193,129... | collective-permute-start | bytes 1572872 | tf_op jit(solution)/shard_map/ppermute | solution.py:25
  42.9 7.7 %collective-permute-start.6 = (bf16[128,4096]{1,0:T(8,128)(2,1)S(1)}, bf16[128,4096]{1,0:T(8,128)(2,1)S(1)}, u32[]{:S(2)}, u32[]{:S(2)}) collective-permute-start(bf16[128,4096]{1,0:T(8,128)(2,1)S(1)} %bitcast.14), channel_id=1, source_target_pairs={{0,1},{1,0},{2,3},{3,2},{4,5},{5,4},{6,7},{7,6},{8,9},{9,8},{10,11... | collective-permute-start | bytes 3145736 | tf_op jit(solution)/shard_map/ppermute | solution.py:25
  94.6 4.8 %collective-permute-start.7 = (f32[128,4096]{1,0:T(8,128)}, f32[128,4096]{1,0:T(8,128)S(1)}, u32[]{:S(2)}, u32[]{:S(2)}) collective-permute-start(f32[128,4096]{1,0:T(8,128)} %get-tuple-element.49), channel_id=1, source_target_pairs={{0,1},{1,0},{2,3},{3,2},{4,5},{5,4},{6,7},{7,6},{8,9},{9,8},{10,11... | collective-permute-start | bytes 6291464 | tf_op jit(solution)/shard_map/ppermute | solution.py:25
  95.3 14.9 %collective-permute-start.12 = (bf16[64,4096]{1,0:T(8,128)(2,1)}, bf16[64,4096]{1,0:T(8,128)(2,1)}, u32[]{:S(2)}, u32[]{:S(2)}) collective-permute-start(bf16[64,4096]{1,0:T(8,128)(2,1)} %get-tuple-element.58), channel_id=1, source_target_pairs={{0,64},{64,128},{128,192},{192,0},{1,65},{65,129},{129,193},{193,1... | collective-permute-start | bytes 1572872 | tf_op jit(solution)/shard_map/ppermute | solution.py:25
  96.6 16.0 %collective-permute-start.8 = (bf16[64,4096]{1,0:T(8,128)(2,1)}, bf16[64,4096]{1,0:T(8,128)(2,1)}, u32[]{:S(2)}, u32[]{:S(2)}) collective-permute-start(bf16[64,4096]{1,0:T(8,128)(2,1)} %get-tuple-element.54), channel_id=1, source_target_pairs={{0,192},{64,0},{128,64},{192,128},{1,193},{65,1},{129,65},{193,129... | collective-permute-start | bytes 1572872 | tf_op jit(solution)/shard_map/ppermute | solution.py:25
  98.0 23.4 %collective-permute-start.10 = (bf16[64,4096]{1,0:T(8,128)(2,1)}, bf16[64,4096]{1,0:T(8,128)(2,1)}, u32[]{:S(2)}, u32[]{:S(2)}) collective-permute-start(bf16[64,4096]{1,0:T(8,128)(2,1)} %get-tuple-element.55), channel_id=1, source_target_pairs={{0,192},{64,0},{128,64},{192,128},{1,193},{65,1},{129,65},{193,129... | collective-permute-start | bytes 1572872 | tf_op jit(solution)/shard_map/ppermute | solution.py:25
  99.5 22.0 %collective-permute-start.11 = (bf16[64,4096]{1,0:T(8,128)(2,1)}, bf16[64,4096]{1,0:T(8,128)(2,1)}, u32[]{:S(2)}, u32[]{:S(2)}) collective-permute-start(bf16[64,4096]{1,0:T(8,128)(2,1)} %get-tuple-element.56), channel_id=1, source_target_pairs={{0,64},{64,128},{128,192},{192,0},{1,65},{65,129},{129,193},{193,1... | collective-permute-start | bytes 1572872 | tf_op jit(solution)/shard_map/ppermute | solution.py:25
  103.4 32.0 %all-to-all-start.4 = ((bf16[32,4,4096]{2,1,0:T(4,128)(2,1)}), bf16[32,4,4096]{2,1,0:T(4,128)(2,1)S(1)}, u32[]{:S(2)}, u32[]{:S(2)}) async-start(bf16[32,4,4096]{2,1,0:T(4,128)(2,1)} %reshape.51), calls=%async_computation.4 | async-start | bytes 2097152 | tf_op jit(solution)/shard_map/all_to_all | solution.py:257
  107.3 25.3 %copy-start.1 = (f32[128,4096]{1,0:T(8,128)S(1)}, f32[128,4096]{1,0:T(8,128)}, u32[]{:S(2)}) copy-start(f32[128,4096]{1,0:T(8,128)} %get-tuple-element.52.here) | copy-start | bytes 6291460
  112.4 20.3 %collective-permute-start.13 = (bf16[64,4096]{1,0:T(8,128)(2,1)}, bf16[64,4096]{1,0:T(8,128)(2,1)}, u32[]{:S(2)}, u32[]{:S(2)}) collective-permute-start(bf16[64,4096]{1,0:T(8,128)(2,1)} %add_convert_fusion.1), channel_id=1, source_target_pairs={{0,64},{64,128},{128,192},{192,0},{1,65},{65,129},{129,193},{193,1... | collective-permute-start | bytes 1572872 | tf_op jit(solution)/shard_map/ppermute | solution.py:25
  114.7 18.0 %collective-permute-start.9 = (bf16[64,4096]{1,0:T(8,128)(2,1)}, bf16[64,4096]{1,0:T(8,128)(2,1)}, u32[]{:S(2)}, u32[]{:S(2)}) collective-permute-start(bf16[64,4096]{1,0:T(8,128)(2,1)} %add_convert_fusion.2), channel_id=1, source_target_pairs={{0,192},{64,0},{128,64},{192,128},{1,193},{65,1},{129,65},{193,129... | collective-permute-start | bytes 1572872 | tf_op jit(solution)/shard_map/ppermute | solution.py:25

commit v9 on v7

--- a/solution.py
+++ b/solution.py
@@ -34,14 +34,14 @@
     return jax.ShapeDtypeStruct(dims, dtype)
 
 
-def call(body, outs, args, flops=0, scalars=0, tiled=(), scratch=(), outside=()):
+def call(body, outs, args, flops=0, scalars=0, tiled=(), scratch=(), outside=(), tile=TILE):
     size = sum(a.size * a.dtype.itemsize for a in (*args, *outs))
     specs = []
     for k, a in enumerate((*args, *outs)):
         if k < scalars:
             specs.append(pl.BlockSpec(memory_space=pltpu.SMEM))
         elif k in tiled:
-            specs.append(pl.BlockSpec((a.shape[0], TILE), lambda i: (0, i)))
+            specs.append(pl.BlockSpec((*a.shape[:-1], tile), lambda i, n=len(a.shape): (0,) * (n - 1) + (i,)))
         else:
             specs.append(pl.BlockSpec(a.shape, lambda i, n=len(a.shape): (0,) * n))
     kinds = [pltpu.HBM if k in outside else None for k in range(len(specs))]
@@ -53,7 +53,7 @@
         o if kind is None else pltpu.HBM(o.shape, o.dtype)
         for o, kind in zip(outs, kinds[len(args) :])
     ]
-    steps = (*args, *outs)[tiled[0]].shape[1] // TILE if tiled else 1
+    steps = (*args, *outs)[tiled[0]].shape[-1] // tile if tiled else 1
     return pl.pallas_call(
         body,
         grid=(steps,),
@@ -153,6 +153,11 @@
     theirs[...] = out[128:]
 
 
+def gathered_body(place, parts, exact, total):
+    one = lax.broadcasted_iota(jnp.int32, parts.shape, 0) != place[0]
+    total[...] = exact[...] + jnp.sum(jnp.where(one, parts[...].astype(F32), 0.0), axis=0)
+
+
 def total_body(here, back_low, back_high, ahead_low, ahead_high, total):
     half = back_low.shape[0]
     for rows, parts in (
@@ -203,6 +208,7 @@
         flops=2 * total * pool * width,
         scalars=1,
         tiled=range(1, 10),
+        tile=2048,
     )
     table = lax.all_to_all(table, COL, 0, 0, tiled=True)
     weights, table, stats = call(
@@ -220,6 +226,7 @@
         flops=4 * total * pool * width,
         scalars=1,
         tiled=(*range(5, 14), *range(15, 24)),
+        tile=2048,
         scratch=[pltpu.VMEM((pool, total), BF16), pltpu.VMEM((total, pool), BF16)],
         outside=(15, 16, 17, 18, 19, 20, 21, 22, 23),
     )
@@ -236,14 +243,20 @@
     sent = (mine + theirs).astype(BF16).reshape(breadth * depth, rows, width)
     exact, sent = lax.optimization_barrier((exact, sent))
     parts = lax.all_to_all(sent, (X, Z), 0, 0, tiled=True)
-    others = (lax.iota(jnp.int32, breadth * depth) != place_of)[:, None, None]
-    grad_queries = exact + jnp.sum(jnp.where(others, parts.astype(F32), 0.0), axis=0)
+    grad_queries = call(
+        gathered_body,
+        [shape((rows, width), F32)],
+        [place_of.reshape(1).astype(jnp.int32), parts, exact],
+        scalars=1,
+        tiled=(1, 2, 3),
+    )[0]
 
     grad_passages = call(
         total_body,
         [shape((count, width), F32)],
         [here, back_low, back_high, ahead_low, ahead_high],
         tiled=range(6),
+        tile=2048,
     )[0]
 
     row_losses = lax.dynamic_slice_in_dim(losses[0], at, rows, 0)

time: 139 us -> 135 us (0.971)
  other arithmetic: 10.6 us -> 7.27 us
  waiting for transfers between devices: 33.5 us -> 35.2 us
    reduce_sum x1 -> x0, other arithmetic: 1.93 us -> none  [on_device(): jnp.sum(jnp.where(others, parts.astype(F32), 0.0), axis=0)]
    ppermute x14, waiting for transfers between devices: 27.3 us -> 28.9 us  [shifted(): return lax.ppermute(value, axis, [(i, (i + step) % n) for i in range(n)])]
    pallas_call x4 -> x5, Pallas kernels: 16.2 us -> 15.3 us  [call(): pl.pallas_call(body, grid=(steps,), out_shape=outs, in_specs=specs[:len(a...]
  transfers between devices with their start and end apart: 17 -> 17, of which waited for: 7 -> 7; matrix products, arithmetic and copies ran while one was open for 10% -> 9% of each run, Pallas kernels for 3% -> 2%
where the time goes in v9:
time: 135 us; the launch traced here: 134 us
  starting transfers between devices  36.4 us (27%)
  waiting for transfers between devices  35.2 us (26%)
  blocking collectives  32 us (24%)
  Pallas kernels  15.3 us (11%)
  local copies, waits for them, and re-layouts  7.45 us (6%)
  other arithmetic  7.27 us (5%)
    all_to_all x2, blocking collectives, on_device(): table = lax.all_to_all(table, COL, 0, 0, tiled=True)  32 us
    ppermute x14, waiting for transfers between devices, shifted(): return lax.ppermute(value, axis, [(i, (i + step) % n) for i in range(n)])  28.9 us
    ppermute x14, starting transfers between devices, shifted(): return lax.ppermute(value, axis, [(i, (i + step) % n) for i in range(n)])  20.2 us
    pallas_call x5, Pallas kernels, call(): pl.pallas_call(body, grid=(steps,), out_shape=outs, in_specs=specs[:len(a...  15.3 us
    all_to_all x2, starting transfers between devices, copies(): lax.all_to_all(jnp.broadcast_to(value, (n, *value.shape)), axis, 0, 0, ti...  12.2 us
    all_to_all x2, waiting for transfers between devices, copies(): lax.all_to_all(jnp.broadcast_to(value, (n, *value.shape)), axis, 0, 0, ti...  6.29 us
    all_to_all x1, starting transfers between devices, on_device(): parts = lax.all_to_all(sent, (X, Z), 0, 0, tiled=True)  3.94 us
  transfers between devices with their start and end apart: 17, of which 7 were waited for; matrix products, arithmetic and copies ran while one was open for 9% of the time, Pallas kernels for 2%

profile of v9, /device:TPU:1, one launch (start us, length us, event | category | flops | bytes accessed | tf_op | source)
XLA Modules:
  0.0 134.3 jit_solution(5644768214089585073)
XLA Ops:
  0.7 2.3 %fusion.4 = (bf16[64,4096]{1,0:T(8,128)(2,1)}, bf16[64,4096]{1,0:T(8,128)(2,1)}) fusion(bf16[128,4096]{1,0:T(8,128)(2,1)} %refs_0_.3), kind=kLoop, calls=%fused_computation.16 | loop fusion | bytes 2097152 | tf_op jit(solution)/shard_map/slice | solution.py:179
  3.0 2.1 %collective-permute-start = (bf16[64,4096]{1,0:T(8,128)(2,1)}, bf16[64,4096]{1,0:T(8,128)(2,1)S(1)}, u32[]{:S(2)}, u32[]{:S(2)}) collective-permute-start(bf16[64,4096]{1,0:T(8,128)(2,1)} %get-tuple-element.60), channel_id=1, source_target_pairs={{0,64},{64,128},{128,192},{192,0},{1,65},{65,129},{129,193},{193,1... | collective-permute-start | bytes 1572872 | tf_op jit(solution)/shard_map/ppermute | solution.py:25
  5.1 1.4 %collective-permute-start.1 = (bf16[64,4096]{1,0:T(8,128)(2,1)}, bf16[64,4096]{1,0:T(8,128)(2,1)S(1)}, u32[]{:S(2)}, u32[]{:S(2)}) collective-permute-start(bf16[64,4096]{1,0:T(8,128)(2,1)} %get-tuple-element.59), channel_id=1, source_target_pairs={{0,192},{64,0},{128,64},{192,128},{1,193},{65,1},{129,65},{193,129... | collective-permute-start | bytes 1572872 | tf_op jit(solution)/shard_map/ppermute | solution.py:25
  7.3 8.2 %all-to-all-start = ((bf16[8,4,4096]{2,1,0:T(4,128)(2,1)}), bf16[8,4,4096]{2,1,0:T(4,128)(2,1)S(1)}, u32[]{:S(2)}, u32[]{:S(2)}) async-start(bf16[8,4,4096]{2,1,0:T(4,128)(2,1)} %broadcast_in_dim.12), calls=%async_computation | async-start | bytes 524288 | tf_op jit(solution)/shard_map/all_to_all | solution.py:30
  15.5 2.7 %collective-permute-start.5 = (bf16[64,4096]{1,0:T(8,128)(2,1)}, bf16[64,4096]{1,0:T(8,128)(2,1)}, u32[]{:S(2)}, u32[]{:S(2)}) collective-permute-start(bf16[64,4096]{1,0:T(8,128)(2,1)} %get-tuple-element.60), channel_id=1, source_target_pairs={{0,192},{64,0},{128,64},{192,128},{1,193},{65,1},{129,65},{193,129... | collective-permute-start | bytes 1572872 | tf_op jit(solution)/shard_map/ppermute | solution.py:25
  19.4 6.3 %all-to-all-done = bf16[8,4,4096]{2,1,0:T(4,128)(2,1)S(1)} async-done(((bf16[8,4,4096]{2,1,0:T(4,128)(2,1)}), bf16[8,4,4096]{2,1,0:T(4,128)(2,1)S(1)}, u32[]{:S(2)}, u32[]{:S(2)}) %all-to-all-start) | async-done | bytes 262176 | tf_op jit(solution)/shard_map/all_to_all | solution.py:30
  25.8 1.1 broadcast_in_dim.13
  26.8 4.0 %all-to-all-start.1 = ((bf16[4,32,4096]{2,1,0:T(8,128)(2,1)}), bf16[4,32,4096]{2,1,0:T(8,128)(2,1)S(1)}, u32[]{:S(2)}, u32[]{:S(2)}) async-start(bf16[4,32,4096]{2,1,0:T(8,128)(2,1)} %broadcast_in_dim.13), calls=%async_computation.1 | async-start | bytes 2097152 | tf_op jit(solution)/shard_map/all_to_all | solution.py:30
  31.2 2.7 %collective-permute-start.3 = (bf16[64,4096]{1,0:T(8,128)(2,1)S(1)}, bf16[64,4096]{1,0:T(8,128)(2,1)}, u32[]{:S(2)}, u32[]{:S(2)}) collective-permute-start(bf16[64,4096]{1,0:T(8,128)(2,1)S(1)} %collective-permute-done.1.refs_4_), channel_id=1, source_target_pairs={{0,192},{64,0},{128,64},{192,128},{1,193},{65,1},{129,65},{193,129... | collective-permute-start | bytes 1572872 | tf_op jit(solution)/shard_map/ppermute | solution.py:25
  34.1 8.8 %collective-permute-done.2.refs_5_ = bf16[64,4096]{1,0:T(8,128)(2,1)} collective-permute-done((bf16[64,4096]{1,0:T(8,128)(2,1)S(1)}, bf16[64,4096]{1,0:T(8,128)(2,1)}, u32[]{:S(2)}, u32[]{:S(2)}) %collective-permute-start.2) | collective-permute-done | bytes 524320 | tf_op jit(solution)/shard_map/ppermute | solution.py:25
  42.9 4.0 %collective-permute-start.6 = (bf16[128,4096]{1,0:T(8,128)(2,1)S(1)}, bf16[128,4096]{1,0:T(8,128)(2,1)S(1)}, u32[]{:S(2)}, u32[]{:S(2)}) collective-permute-start(bf16[128,4096]{1,0:T(8,128)(2,1)S(1)} %bitcast.14), channel_id=1, source_target_pairs={{0,1},{1,0},{2,3},{3,2},{4,5},{5,4},{6,7},{7,6},{8,9},{9,8},{10,11... | collective-permute-start | bytes 3145736 | tf_op jit(solution)/shard_map/ppermute | solution.py:25
  46.9 2.3 %collective-permute-done.6.other = bf16[128,4096]{1,0:T(8,128)(2,1)S(1)} collective-permute-done((bf16[128,4096]{1,0:T(8,128)(2,1)S(1)}, bf16[128,4096]{1,0:T(8,128)(2,1)S(1)}, u32[]{:S(2)}, u32[]{:S(2)}) %collective-permute-start.6) | collective-permute-done | bytes 1048608 | tf_op jit(solution)/shard_map/ppermute | solution.py:25
  49.2 3.5 %shard_map.85 = (f32[512,256]{1,0:T(8,128)S(1)}, f32[64,2,256]{2,1,0:T(2,128)S(1)}) custom-call(s32[5]{0:T(128)S(1)} %pad_add_fusion.place, bf16[128,4096]{1,0:T(8,128)(2,1)S(1)} %bitcast.15, bf16[128,4096]{1,0:T(8,128)(2,1)S(1)} %collective-permute-done.6.other, bf16[128,4096]{1,0:T(8,128)(2,1)S(1)} %copy-done, ...), custom_call_target="tpu_custom_call" | custom-call | flops 1073741824 | bytes 6955028 | tf_op jit(solution)/shard_map/pallas_call | solution.py:57
  52.7 18.1 %all_to_all.25.table = f32[64,2,256]{2,1,0:T(2,128)S(1)} all-to-all(f32[64,2,256]{2,1,0:T(2,128)S(1)} %get-tuple-element.41), channel_id=1, replica_groups=mesh['row'=4,'col_0'=8,'col_1'=4,'col_2'=2] {'col_0','col_1','col_2'}, dimensions={0} | all-to-all | bytes 262144 | tf_op jit(solution)/shard_map/all_to_all | solution.py:213
  70.8 1.1 shard_map.86
  71.9 13.9 %all_to_all.26.table = f32[64,1,256]{2,1,0:T(1,128)S(1)} all-to-all(f32[64,1,256]{2,1,0:T(1,128)S(1)} %get-tuple-element.44), channel_id=1, replica_groups=mesh['row'=4,'col_0'=8,'col_1'=4,'col_2'=2] {'col_0','col_1','col_2'}, dimensions={0} | all-to-all | bytes 131072 | tf_op jit(solution)/shard_map/all_to_all | solution.py:220
  85.8 6.2 %shard_map.87 = (f32[8,256]{1,0:T(8,128)S(1)}, bf16[64,4096]{1,0:T(8,128)(2,1)}, bf16[64,4096]{1,0:T(8,128)(2,1)}, bf16[64,4096]{1,0:T(8,128)(2,1)}, bf16[64,409...) custom-call(s32[5]{0:T(128)S(1)} %pad_add_fusion.place, ...), custom_call_target="tpu_custom_call" | custom-call | flops 2147483648 | bytes 16343060 | tf_op jit(solution)/shard_map/pallas_call | solution.py:57
  92.5 1.3 collective-permute-start.12
  93.8 1.4 %collective-permute-start.8 = (bf16[64,4096]{1,0:T(8,128)(2,1)}, bf16[64,4096]{1,0:T(8,128)(2,1)}, u32[]{:S(2)}, u32[]{:S(2)}) collective-permute-start(bf16[64,4096]{1,0:T(8,128)(2,1)} %get-tuple-element.54), channel_id=1, source_target_pairs={{0,192},{64,0},{128,64},{192,128},{1,193},{65,1},{129,65},{193,129... | collective-permute-start | bytes 1572872 | tf_op jit(solution)/shard_map/ppermute | solution.py:25
  95.2 1.4 %collective-permute-start.10 = (bf16[64,4096]{1,0:T(8,128)(2,1)}, bf16[64,4096]{1,0:T(8,128)(2,1)}, u32[]{:S(2)}, u32[]{:S(2)}) collective-permute-start(bf16[64,4096]{1,0:T(8,128)(2,1)} %get-tuple-element.55), channel_id=1, source_target_pairs={{0,192},{64,0},{128,64},{192,128},{1,193},{65,1},{129,65},{193,129... | collective-permute-start | bytes 1572872 | tf_op jit(solution)/shard_map/ppermute | solution.py:25
  96.6 1.8 %add_convert_fusion = bf16[128,4096]{1,0:T(8,128)(2,1)S(1)} fusion(f32[128,4096]{1,0:T(8,128)} %get-tuple-element.48, f32[128,4096]{1,0:T(8,128)S(1)} %collective-permute-done.7), kind=kLoop, calls=%fused_computation | loop fusion | flops 1048576 | bytes 5242880 | tf_op jit(solution)/shard_map/convert_element_type | solution.py:243
  98.4 1.2 reshape.51
  99.6 0.9 dynamic-slice_add_fusion.exact
  100.6 3.9 %all-to-all-start.4 = ((bf16[32,4,4096]{2,1,0:T(4,128)(2,1)}), bf16[32,4,4096]{2,1,0:T(4,128)(2,1)S(1)}, u32[]{:S(2)}, u32[]{:S(2)}) async-start(bf16[32,4,4096]{2,1,0:T(4,128)(2,1)} %reshape.51), calls=%async_computation.4 | async-start | bytes 2097152 | tf_op jit(solution)/shard_map/all_to_all | solution.py:245
  104.5 2.9 %collective-permute-done.12 = bf16[64,4096]{1,0:T(8,128)(2,1)} collective-permute-done((bf16[64,4096]{1,0:T(8,128)(2,1)}, bf16[64,4096]{1,0:T(8,128)(2,1)}, u32[]{:S(2)}, u32[]{:S(2)}) %collective-permute-start.12) | collective-permute-done | bytes 524320 | tf_op jit(solution)/shard_map/ppermute | solution.py:25
  107.4 2.2 %add_convert_fusion.1 = bf16[64,4096]{1,0:T(8,128)(2,1)} fusion(bf16[64,4096]{1,0:T(8,128)(2,1)} %collective-permute-done.12, bf16[64,4096]{1,0:T(8,128)(2,1)} %get-tuple-element.57), kind=kLoop, calls=%fused_computation.1 | loop fusion | flops 1048576 | bytes 1572864 | tf_op jit(solution)/shard_map/convert_element_type | solution.py:238
  109.7 2.1 %add_convert_fusion.2 = bf16[64,4096]{1,0:T(8,128)(2,1)} fusion(bf16[64,4096]{1,0:T(8,128)(2,1)} %collective-permute-done.8, bf16[64,4096]{1,0:T(8,128)(2,1)} %get-tuple-element.53), kind=kLoop, calls=%fused_computation.2 | loop fusion | flops 1048576 | bytes 1572864 | tf_op jit(solution)/shard_map/convert_element_type | solution.py:237
  111.8 2.6 %collective-permute-start.9 = (bf16[64,4096]{1,0:T(8,128)(2,1)}, bf16[64,4096]{1,0:T(8,128)(2,1)}, u32[]{:S(2)}, u32[]{:S(2)}) collective-permute-start(bf16[64,4096]{1,0:T(8,128)(2,1)} %add_convert_fusion.2), channel_id=1, source_target_pairs={{0,192},{64,0},{128,64},{192,128},{1,193},{65,1},{129,65},{193,129... | collective-permute-start | bytes 1572872 | tf_op jit(solution)/shard_map/ppermute | solution.py:25
  115.0 3.4 %collective-permute-done.10.back_high = bf16[64,4096]{1,0:T(8,128)(2,1)} collective-permute-done((bf16[64,4096]{1,0:T(8,128)(2,1)}, bf16[64,4096]{1,0:T(8,128)(2,1)}, u32[]{:S(2)}, u32[]{:S(2)}) %collective-permute-start.10) | collective-permute-done | bytes 524320 | tf_op jit(solution)/shard_map/ppermute | solution.py:25
  118.6 11.2 %collective-permute-done.13.ahead_high = bf16[64,4096]{1,0:T(8,128)(2,1)} collective-permute-done((bf16[64,4096]{1,0:T(8,128)(2,1)}, bf16[64,4096]{1,0:T(8,128)(2,1)}, u32[]{:S(2)}, u32[]{:S(2)}) %collective-permute-start.13) | collective-permute-done | bytes 524320 | tf_op jit(solution)/shard_map/ppermute | solution.py:25
  129.9 2.7 %shard_map.89 = f32[128,4096]{1,0:T(8,128)} custom-call(f32[128,4096]{1,0:T(8,128)S(1)} %copy-done.1, bf16[64,4096]{1,0:T(8,128)(2,1)} %collective-permute-done.9.back_low, bf16[64,4096]{1,0:T(8,128)(2,1)} %collective-permute-done.10.back_high, bf16[64,4096]{1,0:T(8,128)(2,1)} %collective-permute-done.11.ahead_low, ...), custom_call_target="tpu_custom_call" | custom-call | bytes 6291456 | tf_op jit(solution)/shard_map/pallas_call | solution.py:57
  132.6 1.7 %shard_map.88 = f32[4,4096]{1,0:T(4,128)} custom-call(s32[1]{0:T(128)} %bitcast.11.place, bf16[32,4,4096]{2,1,0:T(4,128)(2,1)S(1)} %all-to-all-done.4.parts, f32[4,4096]{1,0:T(4,128)S(1)} %dynamic-slice_add_fusion.exact), custom_call_target="tpu_custom_call" | custom-call | bytes 1179652 | tf_op jit(solution)/shard_map/pallas_call | solution.py:57
  (47 shorter events, 4.1 us)
Async XLA Ops:
  0.6 5.9 %copy-start.2 = (bf16[4,4096]{1,0:T(4,128)(2,1)S(1)}, bf16[4,4096]{1,0:T(4,128)(2,1)}, u32[]{:S(2)}) copy-start(bf16[4,4096]{1,0:T(4,128)(2,1)} %param.6) | copy-start | bytes 98308
  0.6 17.5 %copy-start.3 = (s32[256,7]{0,1:T(8,128)S(1)}, s32[256,7]{0,1:T(8,128)}, u32[]{:S(2)}) copy-start(s32[256,7]{0,1:T(8,128)} %param.9) | copy-start | bytes 21508
  0.7 17.9 %copy-start.4 = (s32[256]{0:T(256)S(1)}, s32[256]{0:T(256)}, u32[]{:S(2)}) copy-start(s32[256]{0:T(256)} %param.8) | copy-start | bytes 3076
  3.0 22.7 %collective-permute-start = (bf16[64,4096]{1,0:T(8,128)(2,1)}, bf16[64,4096]{1,0:T(8,128)(2,1)S(1)}, u32[]{:S(2)}, u32[]{:S(2)}) collective-permute-start(bf16[64,4096]{1,0:T(8,128)(2,1)} %get-tuple-element.60), channel_id=1, source_target_pairs={{0,64},{64,128},{128,192},{192,0},{1,65},{65,129},{129,193},{193,1... | collective-permute-start | bytes 1572872 | tf_op jit(solution)/shard_map/ppermute | solution.py:25
  5.1 20.6 %collective-permute-start.1 = (bf16[64,4096]{1,0:T(8,128)(2,1)}, bf16[64,4096]{1,0:T(8,128)(2,1)S(1)}, u32[]{:S(2)}, u32[]{:S(2)}) collective-permute-start(bf16[64,4096]{1,0:T(8,128)(2,1)} %get-tuple-element.59), channel_id=1, source_target_pairs={{0,192},{64,0},{128,64},{192,128},{1,193},{65,1},{129,65},{193,129... | collective-permute-start | bytes 1572872 | tf_op jit(solution)/shard_map/ppermute | solution.py:25
  7.3 18.3 %all-to-all-start = ((bf16[8,4,4096]{2,1,0:T(4,128)(2,1)}), bf16[8,4,4096]{2,1,0:T(4,128)(2,1)S(1)}, u32[]{:S(2)}, u32[]{:S(2)}) async-start(bf16[8,4,4096]{2,1,0:T(4,128)(2,1)} %broadcast_in_dim.12), calls=%async_computation | async-start | bytes 524288 | tf_op jit(solution)/shard_map/all_to_all | solution.py:30
  15.5 18.6 %collective-permute-start.4 = (bf16[64,4096]{1,0:T(8,128)(2,1)}, bf16[64,4096]{1,0:T(8,128)(2,1)}, u32[]{:S(2)}, u32[]{:S(2)}) collective-permute-start(bf16[64,4096]{1,0:T(8,128)(2,1)} %get-tuple-element.59), channel_id=1, source_target_pairs={{0,64},{64,128},{128,192},{192,0},{1,65},{65,129},{129,193},{193,1... | collective-permute-start | bytes 1572872 | tf_op jit(solution)/shard_map/ppermute | solution.py:25
  15.5 18.6 %collective-permute-start.5 = (bf16[64,4096]{1,0:T(8,128)(2,1)}, bf16[64,4096]{1,0:T(8,128)(2,1)}, u32[]{:S(2)}, u32[]{:S(2)}) collective-permute-start(bf16[64,4096]{1,0:T(8,128)(2,1)} %get-tuple-element.60), channel_id=1, source_target_pairs={{0,192},{64,0},{128,64},{192,128},{1,193},{65,1},{129,65},{193,129... | collective-permute-start | bytes 1572872 | tf_op jit(solution)/shard_map/ppermute | solution.py:25
  19.4 11.6 %copy-start.5 = (f32[256]{0:T(256)S(1)}, f32[256]{0:T(256)}, u32[]{:S(2)}) copy-start(f32[256]{0:T(256)} %param.10) | copy-start | bytes 3076
  25.7 8.3 %copy-start.6 = (s32[4]{0:T(128)S(1)}, s32[4]{0:T(128)}, u32[]{:S(2)}) copy-start(s32[4]{0:T(128)} %constant.47) | copy-start | bytes 52
  25.7 23.4 %copy-start = (bf16[128,4096]{1,0:T(8,128)(2,1)S(1)}, bf16[128,4096]{1,0:T(8,128)(2,1)}, u32[]{:S(2)}) copy-start(bf16[128,4096]{1,0:T(8,128)(2,1)} %refs_0_.3) | copy-start | bytes 3145732
  26.8 16.1 %all-to-all-start.1 = ((bf16[4,32,4096]{2,1,0:T(8,128)(2,1)}), bf16[4,32,4096]{2,1,0:T(8,128)(2,1)S(1)}, u32[]{:S(2)}, u32[]{:S(2)}) async-start(bf16[4,32,4096]{2,1,0:T(8,128)(2,1)} %broadcast_in_dim.13), calls=%async_computation.1 | async-start | bytes 2097152 | tf_op jit(solution)/shard_map/all_to_all | solution.py:30
  31.1 11.9 %collective-permute-start.2 = (bf16[64,4096]{1,0:T(8,128)(2,1)S(1)}, bf16[64,4096]{1,0:T(8,128)(2,1)}, u32[]{:S(2)}, u32[]{:S(2)}) collective-permute-start(bf16[64,4096]{1,0:T(8,128)(2,1)S(1)} %collective-permute-done.refs_1_), channel_id=1, source_target_pairs={{0,64},{64,128},{128,192},{192,0},{1,65},{65,129},{129,193},{193,1... | collective-permute-start | bytes 1572872 | tf_op jit(solution)/shard_map/ppermute | solution.py:25
  31.2 11.8 %collective-permute-start.3 = (bf16[64,4096]{1,0:T(8,128)(2,1)S(1)}, bf16[64,4096]{1,0:T(8,128)(2,1)}, u32[]{:S(2)}, u32[]{:S(2)}) collective-permute-start(bf16[64,4096]{1,0:T(8,128)(2,1)S(1)} %collective-permute-done.1.refs_4_), channel_id=1, source_target_pairs={{0,192},{64,0},{128,64},{192,128},{1,193},{65,1},{129,65},{193,129... | collective-permute-start | bytes 1572872 | tf_op jit(solution)/shard_map/ppermute | solution.py:25
  42.9 6.2 %collective-permute-start.6 = (bf16[128,4096]{1,0:T(8,128)(2,1)S(1)}, bf16[128,4096]{1,0:T(8,128)(2,1)S(1)}, u32[]{:S(2)}, u32[]{:S(2)}) collective-permute-start(bf16[128,4096]{1,0:T(8,128)(2,1)S(1)} %bitcast.14), channel_id=1, source_target_pairs={{0,1},{1,0},{2,3},{3,2},{4,5},{5,4},{6,7},{7,6},{8,9},{9,8},{10,11... | collective-permute-start | bytes 3145736 | tf_op jit(solution)/shard_map/ppermute | solution.py:25
  92.0 4.6 %collective-permute-start.7 = (f32[128,4096]{1,0:T(8,128)}, f32[128,4096]{1,0:T(8,128)S(1)}, u32[]{:S(2)}, u32[]{:S(2)}) collective-permute-start(f32[128,4096]{1,0:T(8,128)} %get-tuple-element.49), channel_id=1, source_target_pairs={{0,1},{1,0},{2,3},{3,2},{4,5},{5,4},{6,7},{7,6},{8,9},{9,8},{10,11... | collective-permute-start | bytes 6291464 | tf_op jit(solution)/shard_map/ppermute | solution.py:25
  92.5 14.9 %collective-permute-start.12 = (bf16[64,4096]{1,0:T(8,128)(2,1)}, bf16[64,4096]{1,0:T(8,128)(2,1)}, u32[]{:S(2)}, u32[]{:S(2)}) collective-permute-start(bf16[64,4096]{1,0:T(8,128)(2,1)} %get-tuple-element.58), channel_id=1, source_target_pairs={{0,64},{64,128},{128,192},{192,0},{1,65},{65,129},{129,193},{193,1... | collective-permute-start | bytes 1572872 | tf_op jit(solution)/shard_map/ppermute | solution.py:25
  93.8 15.9 %collective-permute-start.8 = (bf16[64,4096]{1,0:T(8,128)(2,1)}, bf16[64,4096]{1,0:T(8,128)(2,1)}, u32[]{:S(2)}, u32[]{:S(2)}) collective-permute-start(bf16[64,4096]{1,0:T(8,128)(2,1)} %get-tuple-element.54), channel_id=1, source_target_pairs={{0,192},{64,0},{128,64},{192,128},{1,193},{65,1},{129,65},{193,129... | collective-permute-start | bytes 1572872 | tf_op jit(solution)/shard_map/ppermute | solution.py:25
  95.2 23.2 %collective-permute-start.10 = (bf16[64,4096]{1,0:T(8,128)(2,1)}, bf16[64,4096]{1,0:T(8,128)(2,1)}, u32[]{:S(2)}, u32[]{:S(2)}) collective-permute-start(bf16[64,4096]{1,0:T(8,128)(2,1)} %get-tuple-element.55), channel_id=1, source_target_pairs={{0,192},{64,0},{128,64},{192,128},{1,193},{65,1},{129,65},{193,129... | collective-permute-start | bytes 1572872 | tf_op jit(solution)/shard_map/ppermute | solution.py:25
  96.6 22.0 %collective-permute-start.11 = (bf16[64,4096]{1,0:T(8,128)(2,1)}, bf16[64,4096]{1,0:T(8,128)(2,1)}, u32[]{:S(2)}, u32[]{:S(2)}) collective-permute-start(bf16[64,4096]{1,0:T(8,128)(2,1)} %get-tuple-element.56), channel_id=1, source_target_pairs={{0,64},{64,128},{128,192},{192,0},{1,65},{65,129},{129,193},{193,1... | collective-permute-start | bytes 1572872 | tf_op jit(solution)/shard_map/ppermute | solution.py:25
  100.6 32.0 %all-to-all-start.4 = ((bf16[32,4,4096]{2,1,0:T(4,128)(2,1)}), bf16[32,4,4096]{2,1,0:T(4,128)(2,1)S(1)}, u32[]{:S(2)}, u32[]{:S(2)}) async-start(bf16[32,4,4096]{2,1,0:T(4,128)(2,1)} %reshape.51), calls=%async_computation.4 | async-start | bytes 2097152 | tf_op jit(solution)/shard_map/all_to_all | solution.py:245
  104.5 25.4 %copy-start.1 = (f32[128,4096]{1,0:T(8,128)S(1)}, f32[128,4096]{1,0:T(8,128)}, u32[]{:S(2)}) copy-start(f32[128,4096]{1,0:T(8,128)} %get-tuple-element.52.here) | copy-start | bytes 6291460
  109.6 20.3 %collective-permute-start.13 = (bf16[64,4096]{1,0:T(8,128)(2,1)}, bf16[64,4096]{1,0:T(8,128)(2,1)}, u32[]{:S(2)}, u32[]{:S(2)}) collective-permute-start(bf16[64,4096]{1,0:T(8,128)(2,1)} %add_convert_fusion.1), channel_id=1, source_target_pairs={{0,64},{64,128},{128,192},{192,0},{1,65},{65,129},{129,193},{193,1... | collective-permute-start | bytes 1572872 | tf_op jit(solution)/shard_map/ppermute | solution.py:25
  111.8 18.1 %collective-permute-start.9 = (bf16[64,4096]{1,0:T(8,128)(2,1)}, bf16[64,4096]{1,0:T(8,128)(2,1)}, u32[]{:S(2)}, u32[]{:S(2)}) collective-permute-start(bf16[64,4096]{1,0:T(8,128)(2,1)} %add_convert_fusion.2), channel_id=1, source_target_pairs={{0,192},{64,0},{128,64},{192,128},{1,193},{65,1},{129,65},{193,129... | collective-permute-start | bytes 1572872 | tf_op jit(solution)/shard_map/ppermute | solution.py:25

commit v10 on v9

--- a/solution.py
+++ b/solution.py
@@ -208,7 +208,7 @@
         flops=2 * total * pool * width,
         scalars=1,
         tiled=range(1, 10),
-        tile=2048,
+        tile=4096,
     )
     table = lax.all_to_all(table, COL, 0, 0, tiled=True)
     weights, table, stats = call(
@@ -249,6 +249,7 @@
         [place_of.reshape(1).astype(jnp.int32), parts, exact],
         scalars=1,
         tiled=(1, 2, 3),
+        tile=2048,
     )[0]
 
     grad_passages = call(
@@ -256,7 +257,7 @@
         [shape((count, width), F32)],
         [here, back_low, back_high, ahead_low, ahead_high],
         tiled=range(6),
-        tile=2048,
+        tile=4096,
     )[0]
 
     row_losses = lax.dynamic_slice_in_dim(losses[0], at, rows, 0)

time: 135 us -> 135 us (level)
  no operation moved by 1% of the time
where the time goes in v10:
time: 135 us; the launch traced here: 134 us
  starting transfers between devices  36.4 us (27%)
  waiting for transfers between devices  35.2 us (26%)
  blocking collectives  32 us (24%)
  Pallas kernels  14.9 us (11%)
  local copies, waits for them, and re-layouts  7.45 us (6%)
  other arithmetic  7.27 us (5%)
    all_to_all x2, blocking collectives, on_device(): table = lax.all_to_all(table, COL, 0, 0, tiled=True)  32 us
    ppermute x14, waiting for transfers between devices, shifted(): return lax.ppermute(value, axis, [(i, (i + step) % n) for i in range(n)])  28.9 us
    ppermute x14, starting transfers between devices, shifted(): return lax.ppermute(value, axis, [(i, (i + step) % n) for i in range(n)])  20.2 us
    pallas_call x5, Pallas kernels, call(): pl.pallas_call(body, grid=(steps,), out_shape=outs, in_specs=specs[:len(a...  14.9 us
    all_to_all x2, starting transfers between devices, copies(): lax.all_to_all(jnp.broadcast_to(value, (n, *value.shape)), axis, 0, 0, ti...  12.2 us
    all_to_all x2, waiting for transfers between devices, copies(): lax.all_to_all(jnp.broadcast_to(value, (n, *value.shape)), axis, 0, 0, ti...  6.29 us
    all_to_all x1, starting transfers between devices, on_device(): parts = lax.all_to_all(sent, (X, Z), 0, 0, tiled=True)  3.94 us
  transfers between devices with their start and end apart: 17, of which 7 were waited for; matrix products, arithmetic and copies ran while one was open for 9% of the time, Pallas kernels for 2%

profile of v10, /device:TPU:1, one launch (start us, length us, event | category | flops | bytes accessed | tf_op | source)
XLA Modules:
  0.0 134.0 jit_solution(11109608613369187262)
XLA Ops:
  0.7 2.3 %fusion.4 = (bf16[64,4096]{1,0:T(8,128)(2,1)}, bf16[64,4096]{1,0:T(8,128)(2,1)}) fusion(bf16[128,4096]{1,0:T(8,128)(2,1)} %refs_0_.3), kind=kLoop, calls=%fused_computation.16 | loop fusion | bytes 2097152 | tf_op jit(solution)/shard_map/slice | solution.py:179
  3.0 2.1 %collective-permute-start = (bf16[64,4096]{1,0:T(8,128)(2,1)}, bf16[64,4096]{1,0:T(8,128)(2,1)S(1)}, u32[]{:S(2)}, u32[]{:S(2)}) collective-permute-start(bf16[64,4096]{1,0:T(8,128)(2,1)} %get-tuple-element.60), channel_id=1, source_target_pairs={{0,64},{64,128},{128,192},{192,0},{1,65},{65,129},{129,193},{193,1... | collective-permute-start | bytes 1572872 | tf_op jit(solution)/shard_map/ppermute | solution.py:25
  5.1 1.4 %collective-permute-start.1 = (bf16[64,4096]{1,0:T(8,128)(2,1)}, bf16[64,4096]{1,0:T(8,128)(2,1)S(1)}, u32[]{:S(2)}, u32[]{:S(2)}) collective-permute-start(bf16[64,4096]{1,0:T(8,128)(2,1)} %get-tuple-element.59), channel_id=1, source_target_pairs={{0,192},{64,0},{128,64},{192,128},{1,193},{65,1},{129,65},{193,129... | collective-permute-start | bytes 1572872 | tf_op jit(solution)/shard_map/ppermute | solution.py:25
  7.3 8.2 %all-to-all-start = ((bf16[8,4,4096]{2,1,0:T(4,128)(2,1)}), bf16[8,4,4096]{2,1,0:T(4,128)(2,1)S(1)}, u32[]{:S(2)}, u32[]{:S(2)}) async-start(bf16[8,4,4096]{2,1,0:T(4,128)(2,1)} %broadcast_in_dim.12), calls=%async_computation | async-start | bytes 524288 | tf_op jit(solution)/shard_map/all_to_all | solution.py:30
  15.5 2.7 %collective-permute-start.5 = (bf16[64,4096]{1,0:T(8,128)(2,1)}, bf16[64,4096]{1,0:T(8,128)(2,1)}, u32[]{:S(2)}, u32[]{:S(2)}) collective-permute-start(bf16[64,4096]{1,0:T(8,128)(2,1)} %get-tuple-element.60), channel_id=1, source_target_pairs={{0,192},{64,0},{128,64},{192,128},{1,193},{65,1},{129,65},{193,129... | collective-permute-start | bytes 1572872 | tf_op jit(solution)/shard_map/ppermute | solution.py:25
  19.4 6.3 %all-to-all-done = bf16[8,4,4096]{2,1,0:T(4,128)(2,1)S(1)} async-done(((bf16[8,4,4096]{2,1,0:T(4,128)(2,1)}), bf16[8,4,4096]{2,1,0:T(4,128)(2,1)S(1)}, u32[]{:S(2)}, u32[]{:S(2)}) %all-to-all-start) | async-done | bytes 262176 | tf_op jit(solution)/shard_map/all_to_all | solution.py:30
  25.8 1.1 broadcast_in_dim.13
  26.8 4.0 %all-to-all-start.1 = ((bf16[4,32,4096]{2,1,0:T(8,128)(2,1)}), bf16[4,32,4096]{2,1,0:T(8,128)(2,1)S(1)}, u32[]{:S(2)}, u32[]{:S(2)}) async-start(bf16[4,32,4096]{2,1,0:T(8,128)(2,1)} %broadcast_in_dim.13), calls=%async_computation.1 | async-start | bytes 2097152 | tf_op jit(solution)/shard_map/all_to_all | solution.py:30
  31.2 2.7 %collective-permute-start.3 = (bf16[64,4096]{1,0:T(8,128)(2,1)S(1)}, bf16[64,4096]{1,0:T(8,128)(2,1)}, u32[]{:S(2)}, u32[]{:S(2)}) collective-permute-start(bf16[64,4096]{1,0:T(8,128)(2,1)S(1)} %collective-permute-done.1.refs_4_), channel_id=1, source_target_pairs={{0,192},{64,0},{128,64},{192,128},{1,193},{65,1},{129,65},{193,129... | collective-permute-start | bytes 1572872 | tf_op jit(solution)/shard_map/ppermute | solution.py:25
  34.1 8.8 %collective-permute-done.2.refs_5_ = bf16[64,4096]{1,0:T(8,128)(2,1)} collective-permute-done((bf16[64,4096]{1,0:T(8,128)(2,1)S(1)}, bf16[64,4096]{1,0:T(8,128)(2,1)}, u32[]{:S(2)}, u32[]{:S(2)}) %collective-permute-start.2) | collective-permute-done | bytes 524320 | tf_op jit(solution)/shard_map/ppermute | solution.py:25
  42.9 4.0 %collective-permute-start.6 = (bf16[128,4096]{1,0:T(8,128)(2,1)S(1)}, bf16[128,4096]{1,0:T(8,128)(2,1)S(1)}, u32[]{:S(2)}, u32[]{:S(2)}) collective-permute-start(bf16[128,4096]{1,0:T(8,128)(2,1)S(1)} %bitcast.14), channel_id=1, source_target_pairs={{0,1},{1,0},{2,3},{3,2},{4,5},{5,4},{6,7},{7,6},{8,9},{9,8},{10,11... | collective-permute-start | bytes 3145736 | tf_op jit(solution)/shard_map/ppermute | solution.py:25
  46.9 2.3 %collective-permute-done.6.other = bf16[128,4096]{1,0:T(8,128)(2,1)S(1)} collective-permute-done((bf16[128,4096]{1,0:T(8,128)(2,1)S(1)}, bf16[128,4096]{1,0:T(8,128)(2,1)S(1)}, u32[]{:S(2)}, u32[]{:S(2)}) %collective-permute-start.6) | collective-permute-done | bytes 1048608 | tf_op jit(solution)/shard_map/ppermute | solution.py:25
  49.2 3.2 %shard_map.85 = (f32[512,256]{1,0:T(8,128)S(1)}, f32[64,2,256]{2,1,0:T(2,128)S(1)}) custom-call(s32[5]{0:T(128)S(1)} %pad_add_fusion.place, bf16[128,4096]{1,0:T(8,128)(2,1)S(1)} %bitcast.15, bf16[128,4096]{1,0:T(8,128)(2,1)S(1)} %collective-permute-done.6.other, bf16[128,4096]{1,0:T(8,128)(2,1)S(1)} %copy-done, ...), custom_call_target="tpu_custom_call" | custom-call | flops 1073741824 | bytes 6955028 | tf_op jit(solution)/shard_map/pallas_call | solution.py:57
  52.4 18.1 %all_to_all.25.table = f32[64,2,256]{2,1,0:T(2,128)S(1)} all-to-all(f32[64,2,256]{2,1,0:T(2,128)S(1)} %get-tuple-element.41), channel_id=1, replica_groups=mesh['row'=4,'col_0'=8,'col_1'=4,'col_2'=2] {'col_0','col_1','col_2'}, dimensions={0} | all-to-all | bytes 262144 | tf_op jit(solution)/shard_map/all_to_all | solution.py:213
  70.5 1.1 shard_map.86
  71.6 13.9 %all_to_all.26.table = f32[64,1,256]{2,1,0:T(1,128)S(1)} all-to-all(f32[64,1,256]{2,1,0:T(1,128)S(1)} %get-tuple-element.44), channel_id=1, replica_groups=mesh['row'=4,'col_0'=8,'col_1'=4,'col_2'=2] {'col_0','col_1','col_2'}, dimensions={0} | all-to-all | bytes 131072 | tf_op jit(solution)/shard_map/all_to_all | solution.py:220
  85.5 6.2 %shard_map.87 = (f32[8,256]{1,0:T(8,128)S(1)}, bf16[64,4096]{1,0:T(8,128)(2,1)}, bf16[64,4096]{1,0:T(8,128)(2,1)}, bf16[64,4096]{1,0:T(8,128)(2,1)}, bf16[64,409...) custom-call(s32[5]{0:T(128)S(1)} %pad_add_fusion.place, ...), custom_call_target="tpu_custom_call" | custom-call | flops 2147483648 | bytes 16343060 | tf_op jit(solution)/shard_map/pallas_call | solution.py:57
  92.2 1.3 collective-permute-start.12
  93.5 1.4 %collective-permute-start.8 = (bf16[64,4096]{1,0:T(8,128)(2,1)}, bf16[64,4096]{1,0:T(8,128)(2,1)}, u32[]{:S(2)}, u32[]{:S(2)}) collective-permute-start(bf16[64,4096]{1,0:T(8,128)(2,1)} %get-tuple-element.54), channel_id=1, source_target_pairs={{0,192},{64,0},{128,64},{192,128},{1,193},{65,1},{129,65},{193,129... | collective-permute-start | bytes 1572872 | tf_op jit(solution)/shard_map/ppermute | solution.py:25
  94.9 1.4 %collective-permute-start.10 = (bf16[64,4096]{1,0:T(8,128)(2,1)}, bf16[64,4096]{1,0:T(8,128)(2,1)}, u32[]{:S(2)}, u32[]{:S(2)}) collective-permute-start(bf16[64,4096]{1,0:T(8,128)(2,1)} %get-tuple-element.55), channel_id=1, source_target_pairs={{0,192},{64,0},{128,64},{192,128},{1,193},{65,1},{129,65},{193,129... | collective-permute-start | bytes 1572872 | tf_op jit(solution)/shard_map/ppermute | solution.py:25
  96.4 1.8 %add_convert_fusion = bf16[128,4096]{1,0:T(8,128)(2,1)S(1)} fusion(f32[128,4096]{1,0:T(8,128)} %get-tuple-element.48, f32[128,4096]{1,0:T(8,128)S(1)} %collective-permute-done.7), kind=kLoop, calls=%fused_computation | loop fusion | flops 1048576 | bytes 5242880 | tf_op jit(solution)/shard_map/convert_element_type | solution.py:243
  98.2 1.2 reshape.51
  99.4 0.9 dynamic-slice_add_fusion.exact
  100.3 3.9 %all-to-all-start.4 = ((bf16[32,4,4096]{2,1,0:T(4,128)(2,1)}), bf16[32,4,4096]{2,1,0:T(4,128)(2,1)S(1)}, u32[]{:S(2)}, u32[]{:S(2)}) async-start(bf16[32,4,4096]{2,1,0:T(4,128)(2,1)} %reshape.51), calls=%async_computation.4 | async-start | bytes 2097152 | tf_op jit(solution)/shard_map/all_to_all | solution.py:245
  104.3 2.9 %collective-permute-done.12 = bf16[64,4096]{1,0:T(8,128)(2,1)} collective-permute-done((bf16[64,4096]{1,0:T(8,128)(2,1)}, bf16[64,4096]{1,0:T(8,128)(2,1)}, u32[]{:S(2)}, u32[]{:S(2)}) %collective-permute-start.12) | collective-permute-done | bytes 524320 | tf_op jit(solution)/shard_map/ppermute | solution.py:25
  107.2 2.2 %add_convert_fusion.1 = bf16[64,4096]{1,0:T(8,128)(2,1)} fusion(bf16[64,4096]{1,0:T(8,128)(2,1)} %collective-permute-done.12, bf16[64,4096]{1,0:T(8,128)(2,1)} %get-tuple-element.57), kind=kLoop, calls=%fused_computation.1 | loop fusion | flops 1048576 | bytes 1572864 | tf_op jit(solution)/shard_map/convert_element_type | solution.py:238
  109.4 2.1 %add_convert_fusion.2 = bf16[64,4096]{1,0:T(8,128)(2,1)} fusion(bf16[64,4096]{1,0:T(8,128)(2,1)} %collective-permute-done.8, bf16[64,4096]{1,0:T(8,128)(2,1)} %get-tuple-element.53), kind=kLoop, calls=%fused_computation.2 | loop fusion | flops 1048576 | bytes 1572864 | tf_op jit(solution)/shard_map/convert_element_type | solution.py:237
  111.5 2.6 %collective-permute-start.9 = (bf16[64,4096]{1,0:T(8,128)(2,1)}, bf16[64,4096]{1,0:T(8,128)(2,1)}, u32[]{:S(2)}, u32[]{:S(2)}) collective-permute-start(bf16[64,4096]{1,0:T(8,128)(2,1)} %add_convert_fusion.2), channel_id=1, source_target_pairs={{0,192},{64,0},{128,64},{192,128},{1,193},{65,1},{129,65},{193,129... | collective-permute-start | bytes 1572872 | tf_op jit(solution)/shard_map/ppermute | solution.py:25
  114.7 3.4 %collective-permute-done.10.back_high = bf16[64,4096]{1,0:T(8,128)(2,1)} collective-permute-done((bf16[64,4096]{1,0:T(8,128)(2,1)}, bf16[64,4096]{1,0:T(8,128)(2,1)}, u32[]{:S(2)}, u32[]{:S(2)}) %collective-permute-start.10) | collective-permute-done | bytes 524320 | tf_op jit(solution)/shard_map/ppermute | solution.py:25
  118.4 11.2 %collective-permute-done.13.ahead_high = bf16[64,4096]{1,0:T(8,128)(2,1)} collective-permute-done((bf16[64,4096]{1,0:T(8,128)(2,1)}, bf16[64,4096]{1,0:T(8,128)(2,1)}, u32[]{:S(2)}, u32[]{:S(2)}) %collective-permute-start.13) | collective-permute-done | bytes 524320 | tf_op jit(solution)/shard_map/ppermute | solution.py:25
  129.6 3.1 %shard_map.89 = f32[128,4096]{1,0:T(8,128)} custom-call(f32[128,4096]{1,0:T(8,128)S(1)} %copy-done.1, bf16[64,4096]{1,0:T(8,128)(2,1)} %collective-permute-done.9.back_low, bf16[64,4096]{1,0:T(8,128)(2,1)} %collective-permute-done.10.back_high, bf16[64,4096]{1,0:T(8,128)(2,1)} %collective-permute-done.11.ahead_low, ...), custom_call_target="tpu_custom_call" | custom-call | bytes 6291456 | tf_op jit(solution)/shard_map/pallas_call | solution.py:57
  132.8 1.3 shard_map.88
  (47 shorter events, 4.1 us)
Async XLA Ops:
  0.6 5.9 %copy-start.2 = (bf16[4,4096]{1,0:T(4,128)(2,1)S(1)}, bf16[4,4096]{1,0:T(4,128)(2,1)}, u32[]{:S(2)}) copy-start(bf16[4,4096]{1,0:T(4,128)(2,1)} %param.6) | copy-start | bytes 98308
  0.6 17.5 %copy-start.3 = (s32[256,7]{0,1:T(8,128)S(1)}, s32[256,7]{0,1:T(8,128)}, u32[]{:S(2)}) copy-start(s32[256,7]{0,1:T(8,128)} %param.9) | copy-start | bytes 21508
  0.7 17.9 %copy-start.4 = (s32[256]{0:T(256)S(1)}, s32[256]{0:T(256)}, u32[]{:S(2)}) copy-start(s32[256]{0:T(256)} %param.8) | copy-start | bytes 3076
  3.0 22.7 %collective-permute-start = (bf16[64,4096]{1,0:T(8,128)(2,1)}, bf16[64,4096]{1,0:T(8,128)(2,1)S(1)}, u32[]{:S(2)}, u32[]{:S(2)}) collective-permute-start(bf16[64,4096]{1,0:T(8,128)(2,1)} %get-tuple-element.60), channel_id=1, source_target_pairs={{0,64},{64,128},{128,192},{192,0},{1,65},{65,129},{129,193},{193,1... | collective-permute-start | bytes 1572872 | tf_op jit(solution)/shard_map/ppermute | solution.py:25
  5.1 20.6 %collective-permute-start.1 = (bf16[64,4096]{1,0:T(8,128)(2,1)}, bf16[64,4096]{1,0:T(8,128)(2,1)S(1)}, u32[]{:S(2)}, u32[]{:S(2)}) collective-permute-start(bf16[64,4096]{1,0:T(8,128)(2,1)} %get-tuple-element.59), channel_id=1, source_target_pairs={{0,192},{64,0},{128,64},{192,128},{1,193},{65,1},{129,65},{193,129... | collective-permute-start | bytes 1572872 | tf_op jit(solution)/shard_map/ppermute | solution.py:25
  7.3 18.3 %all-to-all-start = ((bf16[8,4,4096]{2,1,0:T(4,128)(2,1)}), bf16[8,4,4096]{2,1,0:T(4,128)(2,1)S(1)}, u32[]{:S(2)}, u32[]{:S(2)}) async-start(bf16[8,4,4096]{2,1,0:T(4,128)(2,1)} %broadcast_in_dim.12), calls=%async_computation | async-start | bytes 524288 | tf_op jit(solution)/shard_map/all_to_all | solution.py:30
  15.5 18.6 %collective-permute-start.4 = (bf16[64,4096]{1,0:T(8,128)(2,1)}, bf16[64,4096]{1,0:T(8,128)(2,1)}, u32[]{:S(2)}, u32[]{:S(2)}) collective-permute-start(bf16[64,4096]{1,0:T(8,128)(2,1)} %get-tuple-element.59), channel_id=1, source_target_pairs={{0,64},{64,128},{128,192},{192,0},{1,65},{65,129},{129,193},{193,1... | collective-permute-start | bytes 1572872 | tf_op jit(solution)/shard_map/ppermute | solution.py:25
  15.5 18.6 %collective-permute-start.5 = (bf16[64,4096]{1,0:T(8,128)(2,1)}, bf16[64,4096]{1,0:T(8,128)(2,1)}, u32[]{:S(2)}, u32[]{:S(2)}) collective-permute-start(bf16[64,4096]{1,0:T(8,128)(2,1)} %get-tuple-element.60), channel_id=1, source_target_pairs={{0,192},{64,0},{128,64},{192,128},{1,193},{65,1},{129,65},{193,129... | collective-permute-start | bytes 1572872 | tf_op jit(solution)/shard_map/ppermute | solution.py:25
  19.4 11.6 %copy-start.5 = (f32[256]{0:T(256)S(1)}, f32[256]{0:T(256)}, u32[]{:S(2)}) copy-start(f32[256]{0:T(256)} %param.10) | copy-start | bytes 3076
  25.7 8.3 %copy-start.6 = (s32[4]{0:T(128)S(1)}, s32[4]{0:T(128)}, u32[]{:S(2)}) copy-start(s32[4]{0:T(128)} %constant.47) | copy-start | bytes 52
  25.7 23.4 %copy-start = (bf16[128,4096]{1,0:T(8,128)(2,1)S(1)}, bf16[128,4096]{1,0:T(8,128)(2,1)}, u32[]{:S(2)}) copy-start(bf16[128,4096]{1,0:T(8,128)(2,1)} %refs_0_.3) | copy-start | bytes 3145732
  26.8 16.1 %all-to-all-start.1 = ((bf16[4,32,4096]{2,1,0:T(8,128)(2,1)}), bf16[4,32,4096]{2,1,0:T(8,128)(2,1)S(1)}, u32[]{:S(2)}, u32[]{:S(2)}) async-start(bf16[4,32,4096]{2,1,0:T(8,128)(2,1)} %broadcast_in_dim.13), calls=%async_computation.1 | async-start | bytes 2097152 | tf_op jit(solution)/shard_map/all_to_all | solution.py:30
  31.1 11.9 %collective-permute-start.2 = (bf16[64,4096]{1,0:T(8,128)(2,1)S(1)}, bf16[64,4096]{1,0:T(8,128)(2,1)}, u32[]{:S(2)}, u32[]{:S(2)}) collective-permute-start(bf16[64,4096]{1,0:T(8,128)(2,1)S(1)} %collective-permute-done.refs_1_), channel_id=1, source_target_pairs={{0,64},{64,128},{128,192},{192,0},{1,65},{65,129},{129,193},{193,1... | collective-permute-start | bytes 1572872 | tf_op jit(solution)/shard_map/ppermute | solution.py:25
  31.2 11.8 %collective-permute-start.3 = (bf16[64,4096]{1,0:T(8,128)(2,1)S(1)}, bf16[64,4096]{1,0:T(8,128)(2,1)}, u32[]{:S(2)}, u32[]{:S(2)}) collective-permute-start(bf16[64,4096]{1,0:T(8,128)(2,1)S(1)} %collective-permute-done.1.refs_4_), channel_id=1, source_target_pairs={{0,192},{64,0},{128,64},{192,128},{1,193},{65,1},{129,65},{193,129... | collective-permute-start | bytes 1572872 | tf_op jit(solution)/shard_map/ppermute | solution.py:25
  42.9 6.2 %collective-permute-start.6 = (bf16[128,4096]{1,0:T(8,128)(2,1)S(1)}, bf16[128,4096]{1,0:T(8,128)(2,1)S(1)}, u32[]{:S(2)}, u32[]{:S(2)}) collective-permute-start(bf16[128,4096]{1,0:T(8,128)(2,1)S(1)} %bitcast.14), channel_id=1, source_target_pairs={{0,1},{1,0},{2,3},{3,2},{4,5},{5,4},{6,7},{7,6},{8,9},{9,8},{10,11... | collective-permute-start | bytes 3145736 | tf_op jit(solution)/shard_map/ppermute | solution.py:25
  91.8 4.6 %collective-permute-start.7 = (f32[128,4096]{1,0:T(8,128)}, f32[128,4096]{1,0:T(8,128)S(1)}, u32[]{:S(2)}, u32[]{:S(2)}) collective-permute-start(f32[128,4096]{1,0:T(8,128)} %get-tuple-element.49), channel_id=1, source_target_pairs={{0,1},{1,0},{2,3},{3,2},{4,5},{5,4},{6,7},{7,6},{8,9},{9,8},{10,11... | collective-permute-start | bytes 6291464 | tf_op jit(solution)/shard_map/ppermute | solution.py:25
  92.2 14.9 %collective-permute-start.12 = (bf16[64,4096]{1,0:T(8,128)(2,1)}, bf16[64,4096]{1,0:T(8,128)(2,1)}, u32[]{:S(2)}, u32[]{:S(2)}) collective-permute-start(bf16[64,4096]{1,0:T(8,128)(2,1)} %get-tuple-element.58), channel_id=1, source_target_pairs={{0,64},{64,128},{128,192},{192,0},{1,65},{65,129},{129,193},{193,1... | collective-permute-start | bytes 1572872 | tf_op jit(solution)/shard_map/ppermute | solution.py:25
  93.5 15.9 %collective-permute-start.8 = (bf16[64,4096]{1,0:T(8,128)(2,1)}, bf16[64,4096]{1,0:T(8,128)(2,1)}, u32[]{:S(2)}, u32[]{:S(2)}) collective-permute-start(bf16[64,4096]{1,0:T(8,128)(2,1)} %get-tuple-element.54), channel_id=1, source_target_pairs={{0,192},{64,0},{128,64},{192,128},{1,193},{65,1},{129,65},{193,129... | collective-permute-start | bytes 1572872 | tf_op jit(solution)/shard_map/ppermute | solution.py:25
  94.9 23.2 %collective-permute-start.10 = (bf16[64,4096]{1,0:T(8,128)(2,1)}, bf16[64,4096]{1,0:T(8,128)(2,1)}, u32[]{:S(2)}, u32[]{:S(2)}) collective-permute-start(bf16[64,4096]{1,0:T(8,128)(2,1)} %get-tuple-element.55), channel_id=1, source_target_pairs={{0,192},{64,0},{128,64},{192,128},{1,193},{65,1},{129,65},{193,129... | collective-permute-start | bytes 1572872 | tf_op jit(solution)/shard_map/ppermute | solution.py:25
  96.4 22.0 %collective-permute-start.11 = (bf16[64,4096]{1,0:T(8,128)(2,1)}, bf16[64,4096]{1,0:T(8,128)(2,1)}, u32[]{:S(2)}, u32[]{:S(2)}) collective-permute-start(bf16[64,4096]{1,0:T(8,128)(2,1)} %get-tuple-element.56), channel_id=1, source_target_pairs={{0,64},{64,128},{128,192},{192,0},{1,65},{65,129},{129,193},{193,1... | collective-permute-start | bytes 1572872 | tf_op jit(solution)/shard_map/ppermute | solution.py:25
  100.3 32.4 %all-to-all-start.4 = ((bf16[32,4,4096]{2,1,0:T(4,128)(2,1)}), bf16[32,4,4096]{2,1,0:T(4,128)(2,1)S(1)}, u32[]{:S(2)}, u32[]{:S(2)}) async-start(bf16[32,4,4096]{2,1,0:T(4,128)(2,1)} %reshape.51), calls=%async_computation.4 | async-start | bytes 2097152 | tf_op jit(solution)/shard_map/all_to_all | solution.py:245
  104.3 25.4 %copy-start.1 = (f32[128,4096]{1,0:T(8,128)S(1)}, f32[128,4096]{1,0:T(8,128)}, u32[]{:S(2)}) copy-start(f32[128,4096]{1,0:T(8,128)} %get-tuple-element.52.here) | copy-start | bytes 6291460
  109.3 20.3 %collective-permute-start.13 = (bf16[64,4096]{1,0:T(8,128)(2,1)}, bf16[64,4096]{1,0:T(8,128)(2,1)}, u32[]{:S(2)}, u32[]{:S(2)}) collective-permute-start(bf16[64,4096]{1,0:T(8,128)(2,1)} %add_convert_fusion.1), channel_id=1, source_target_pairs={{0,64},{64,128},{128,192},{192,0},{1,65},{65,129},{129,193},{193,1... | collective-permute-start | bytes 1572872 | tf_op jit(solution)/shard_map/ppermute | solution.py:25
  111.5 18.1 %collective-permute-start.9 = (bf16[64,4096]{1,0:T(8,128)(2,1)}, bf16[64,4096]{1,0:T(8,128)(2,1)}, u32[]{:S(2)}, u32[]{:S(2)}) collective-permute-start(bf16[64,4096]{1,0:T(8,128)(2,1)} %add_convert_fusion.2), channel_id=1, source_target_pairs={{0,192},{64,0},{128,64},{192,128},{1,193},{65,1},{129,65},{193,129... | collective-permute-start | bytes 1572872 | tf_op jit(solution)/shard_map/ppermute | solution.py:25

commit v11 on v9

--- a/solution.py
+++ b/solution.py
@@ -208,7 +208,7 @@
         flops=2 * total * pool * width,
         scalars=1,
         tiled=range(1, 10),
-        tile=2048,
+        tile=4096,
     )
     table = lax.all_to_all(table, COL, 0, 0, tiled=True)
     weights, table, stats = call(
@@ -249,6 +249,7 @@
         [place_of.reshape(1).astype(jnp.int32), parts, exact],
         scalars=1,
         tiled=(1, 2, 3),
+        tile=4096,
     )[0]
 
     grad_passages = call(

time: 135 us -> 134 us (level)
  no operation moved by 1% of the time
where the time goes in v11:
time: 134 us
  starting transfers between devices  36.4 us (27%)
  waiting for transfers between devices  35.2 us (26%)
  blocking collectives  32 us (24%)
  Pallas kernels  14.4 us (11%)
  local copies, waits for them, and re-layouts  7.45 us (6%)
  other arithmetic  7.27 us (5%)
    all_to_all x2, blocking collectives, on_device(): table = lax.all_to_all(table, COL, 0, 0, tiled=True)  32 us
    ppermute x14, waiting for transfers between devices, shifted(): return lax.ppermute(value, axis, [(i, (i + step) % n) for i in range(n)])  28.9 us
    ppermute x14, starting transfers between devices, shifted(): return lax.ppermute(value, axis, [(i, (i + step) % n) for i in range(n)])  20.2 us
    pallas_call x5, Pallas kernels, call(): pl.pallas_call(body, grid=(steps,), out_shape=outs, in_specs=specs[:len(a...  14.4 us
    all_to_all x2, starting transfers between devices, copies(): lax.all_to_all(jnp.broadcast_to(value, (n, *value.shape)), axis, 0, 0, ti...  12.2 us
    all_to_all x2, waiting for transfers between devices, copies(): lax.all_to_all(jnp.broadcast_to(value, (n, *value.shape)), axis, 0, 0, ti...  6.29 us
    all_to_all x1, starting transfers between devices, on_device(): parts = lax.all_to_all(sent, (X, Z), 0, 0, tiled=True)  3.94 us
  transfers between devices with their start and end apart: 17, of which 7 were waited for; matrix products, arithmetic and copies ran while one was open for 9% of the time, Pallas kernels for 2%

profile of v11, /device:TPU:1, one launch (start us, length us, event | category | flops | bytes accessed | tf_op | source)
XLA Modules:
  0.0 133.5 jit_solution(2524513524452040140)
XLA Ops:
  0.7 2.3 %fusion.4 = (bf16[64,4096]{1,0:T(8,128)(2,1)}, bf16[64,4096]{1,0:T(8,128)(2,1)}) fusion(bf16[128,4096]{1,0:T(8,128)(2,1)} %refs_0_.3), kind=kLoop, calls=%fused_computation.16 | loop fusion | bytes 2097152 | tf_op jit(solution)/shard_map/slice | solution.py:179
  3.0 2.1 %collective-permute-start = (bf16[64,4096]{1,0:T(8,128)(2,1)}, bf16[64,4096]{1,0:T(8,128)(2,1)S(1)}, u32[]{:S(2)}, u32[]{:S(2)}) collective-permute-start(bf16[64,4096]{1,0:T(8,128)(2,1)} %get-tuple-element.60), channel_id=1, source_target_pairs={{0,64},{64,128},{128,192},{192,0},{1,65},{65,129},{129,193},{193,1... | collective-permute-start | bytes 1572872 | tf_op jit(solution)/shard_map/ppermute | solution.py:25
  5.1 1.4 %collective-permute-start.1 = (bf16[64,4096]{1,0:T(8,128)(2,1)}, bf16[64,4096]{1,0:T(8,128)(2,1)S(1)}, u32[]{:S(2)}, u32[]{:S(2)}) collective-permute-start(bf16[64,4096]{1,0:T(8,128)(2,1)} %get-tuple-element.59), channel_id=1, source_target_pairs={{0,192},{64,0},{128,64},{192,128},{1,193},{65,1},{129,65},{193,129... | collective-permute-start | bytes 1572872 | tf_op jit(solution)/shard_map/ppermute | solution.py:25
  7.3 8.2 %all-to-all-start = ((bf16[8,4,4096]{2,1,0:T(4,128)(2,1)}), bf16[8,4,4096]{2,1,0:T(4,128)(2,1)S(1)}, u32[]{:S(2)}, u32[]{:S(2)}) async-start(bf16[8,4,4096]{2,1,0:T(4,128)(2,1)} %broadcast_in_dim.12), calls=%async_computation | async-start | bytes 524288 | tf_op jit(solution)/shard_map/all_to_all | solution.py:30
  15.5 2.7 %collective-permute-start.5 = (bf16[64,4096]{1,0:T(8,128)(2,1)}, bf16[64,4096]{1,0:T(8,128)(2,1)}, u32[]{:S(2)}, u32[]{:S(2)}) collective-permute-start(bf16[64,4096]{1,0:T(8,128)(2,1)} %get-tuple-element.60), channel_id=1, source_target_pairs={{0,192},{64,0},{128,64},{192,128},{1,193},{65,1},{129,65},{193,129... | collective-permute-start | bytes 1572872 | tf_op jit(solution)/shard_map/ppermute | solution.py:25
  19.4 6.3 %all-to-all-done = bf16[8,4,4096]{2,1,0:T(4,128)(2,1)S(1)} async-done(((bf16[8,4,4096]{2,1,0:T(4,128)(2,1)}), bf16[8,4,4096]{2,1,0:T(4,128)(2,1)S(1)}, u32[]{:S(2)}, u32[]{:S(2)}) %all-to-all-start) | async-done | bytes 262176 | tf_op jit(solution)/shard_map/all_to_all | solution.py:30
  25.8 1.1 broadcast_in_dim.13
  26.8 4.0 %all-to-all-start.1 = ((bf16[4,32,4096]{2,1,0:T(8,128)(2,1)}), bf16[4,32,4096]{2,1,0:T(8,128)(2,1)S(1)}, u32[]{:S(2)}, u32[]{:S(2)}) async-start(bf16[4,32,4096]{2,1,0:T(8,128)(2,1)} %broadcast_in_dim.13), calls=%async_computation.1 | async-start | bytes 2097152 | tf_op jit(solution)/shard_map/all_to_all | solution.py:30
  31.2 2.7 %collective-permute-start.3 = (bf16[64,4096]{1,0:T(8,128)(2,1)S(1)}, bf16[64,4096]{1,0:T(8,128)(2,1)}, u32[]{:S(2)}, u32[]{:S(2)}) collective-permute-start(bf16[64,4096]{1,0:T(8,128)(2,1)S(1)} %collective-permute-done.1.refs_4_), channel_id=1, source_target_pairs={{0,192},{64,0},{128,64},{192,128},{1,193},{65,1},{129,65},{193,129... | collective-permute-start | bytes 1572872 | tf_op jit(solution)/shard_map/ppermute | solution.py:25
  34.1 8.8 %collective-permute-done.2.refs_5_ = bf16[64,4096]{1,0:T(8,128)(2,1)} collective-permute-done((bf16[64,4096]{1,0:T(8,128)(2,1)S(1)}, bf16[64,4096]{1,0:T(8,128)(2,1)}, u32[]{:S(2)}, u32[]{:S(2)}) %collective-permute-start.2) | collective-permute-done | bytes 524320 | tf_op jit(solution)/shard_map/ppermute | solution.py:25
  42.9 4.0 %collective-permute-start.6 = (bf16[128,4096]{1,0:T(8,128)(2,1)S(1)}, bf16[128,4096]{1,0:T(8,128)(2,1)S(1)}, u32[]{:S(2)}, u32[]{:S(2)}) collective-permute-start(bf16[128,4096]{1,0:T(8,128)(2,1)S(1)} %bitcast.14), channel_id=1, source_target_pairs={{0,1},{1,0},{2,3},{3,2},{4,5},{5,4},{6,7},{7,6},{8,9},{9,8},{10,11... | collective-permute-start | bytes 3145736 | tf_op jit(solution)/shard_map/ppermute | solution.py:25
  46.9 2.3 %collective-permute-done.6.other = bf16[128,4096]{1,0:T(8,128)(2,1)S(1)} collective-permute-done((bf16[128,4096]{1,0:T(8,128)(2,1)S(1)}, bf16[128,4096]{1,0:T(8,128)(2,1)S(1)}, u32[]{:S(2)}, u32[]{:S(2)}) %collective-permute-start.6) | collective-permute-done | bytes 1048608 | tf_op jit(solution)/shard_map/ppermute | solution.py:25
  49.2 3.2 %shard_map.85 = (f32[512,256]{1,0:T(8,128)S(1)}, f32[64,2,256]{2,1,0:T(2,128)S(1)}) custom-call(s32[5]{0:T(128)S(1)} %pad_add_fusion.place, bf16[128,4096]{1,0:T(8,128)(2,1)S(1)} %bitcast.15, bf16[128,4096]{1,0:T(8,128)(2,1)S(1)} %collective-permute-done.6.other, bf16[128,4096]{1,0:T(8,128)(2,1)S(1)} %copy-done, ...), custom_call_target="tpu_custom_call" | custom-call | flops 1073741824 | bytes 6955028 | tf_op jit(solution)/shard_map/pallas_call | solution.py:57
  52.4 18.1 %all_to_all.25.table = f32[64,2,256]{2,1,0:T(2,128)S(1)} all-to-all(f32[64,2,256]{2,1,0:T(2,128)S(1)} %get-tuple-element.41), channel_id=1, replica_groups=mesh['row'=4,'col_0'=8,'col_1'=4,'col_2'=2] {'col_0','col_1','col_2'}, dimensions={0} | all-to-all | bytes 262144 | tf_op jit(solution)/shard_map/all_to_all | solution.py:213
  70.5 1.1 shard_map.86
  71.6 13.9 %all_to_all.26.table = f32[64,1,256]{2,1,0:T(1,128)S(1)} all-to-all(f32[64,1,256]{2,1,0:T(1,128)S(1)} %get-tuple-element.44), channel_id=1, replica_groups=mesh['row'=4,'col_0'=8,'col_1'=4,'col_2'=2] {'col_0','col_1','col_2'}, dimensions={0} | all-to-all | bytes 131072 | tf_op jit(solution)/shard_map/all_to_all | solution.py:220
  85.5 6.2 %shard_map.87 = (f32[8,256]{1,0:T(8,128)S(1)}, bf16[64,4096]{1,0:T(8,128)(2,1)}, bf16[64,4096]{1,0:T(8,128)(2,1)}, bf16[64,4096]{1,0:T(8,128)(2,1)}, bf16[64,409...) custom-call(s32[5]{0:T(128)S(1)} %pad_add_fusion.place, ...), custom_call_target="tpu_custom_call" | custom-call | flops 2147483648 | bytes 16343060 | tf_op jit(solution)/shard_map/pallas_call | solution.py:57
  92.2 1.3 collective-permute-start.12
  93.5 1.4 %collective-permute-start.8 = (bf16[64,4096]{1,0:T(8,128)(2,1)}, bf16[64,4096]{1,0:T(8,128)(2,1)}, u32[]{:S(2)}, u32[]{:S(2)}) collective-permute-start(bf16[64,4096]{1,0:T(8,128)(2,1)} %get-tuple-element.54), channel_id=1, source_target_pairs={{0,192},{64,0},{128,64},{192,128},{1,193},{65,1},{129,65},{193,129... | collective-permute-start | bytes 1572872 | tf_op jit(solution)/shard_map/ppermute | solution.py:25
  94.9 1.4 %collective-permute-start.10 = (bf16[64,4096]{1,0:T(8,128)(2,1)}, bf16[64,4096]{1,0:T(8,128)(2,1)}, u32[]{:S(2)}, u32[]{:S(2)}) collective-permute-start(bf16[64,4096]{1,0:T(8,128)(2,1)} %get-tuple-element.55), channel_id=1, source_target_pairs={{0,192},{64,0},{128,64},{192,128},{1,193},{65,1},{129,65},{193,129... | collective-permute-start | bytes 1572872 | tf_op jit(solution)/shard_map/ppermute | solution.py:25
  96.4 1.8 %add_convert_fusion = bf16[128,4096]{1,0:T(8,128)(2,1)S(1)} fusion(f32[128,4096]{1,0:T(8,128)} %get-tuple-element.48, f32[128,4096]{1,0:T(8,128)S(1)} %collective-permute-done.7), kind=kLoop, calls=%fused_computation | loop fusion | flops 1048576 | bytes 5242880 | tf_op jit(solution)/shard_map/convert_element_type | solution.py:243
  98.2 1.2 reshape.51
  99.4 0.9 dynamic-slice_add_fusion.exact
  100.3 3.9 %all-to-all-start.4 = ((bf16[32,4,4096]{2,1,0:T(4,128)(2,1)}), bf16[32,4,4096]{2,1,0:T(4,128)(2,1)S(1)}, u32[]{:S(2)}, u32[]{:S(2)}) async-start(bf16[32,4,4096]{2,1,0:T(4,128)(2,1)} %reshape.51), calls=%async_computation.4 | async-start | bytes 2097152 | tf_op jit(solution)/shard_map/all_to_all | solution.py:245
  104.3 2.9 %collective-permute-done.12 = bf16[64,4096]{1,0:T(8,128)(2,1)} collective-permute-done((bf16[64,4096]{1,0:T(8,128)(2,1)}, bf16[64,4096]{1,0:T(8,128)(2,1)}, u32[]{:S(2)}, u32[]{:S(2)}) %collective-permute-start.12) | collective-permute-done | bytes 524320 | tf_op jit(solution)/shard_map/ppermute | solution.py:25
  107.2 2.2 %add_convert_fusion.1 = bf16[64,4096]{1,0:T(8,128)(2,1)} fusion(bf16[64,4096]{1,0:T(8,128)(2,1)} %collective-permute-done.12, bf16[64,4096]{1,0:T(8,128)(2,1)} %get-tuple-element.57), kind=kLoop, calls=%fused_computation.1 | loop fusion | flops 1048576 | bytes 1572864 | tf_op jit(solution)/shard_map/convert_element_type | solution.py:238
  109.4 2.1 %add_convert_fusion.2 = bf16[64,4096]{1,0:T(8,128)(2,1)} fusion(bf16[64,4096]{1,0:T(8,128)(2,1)} %collective-permute-done.8, bf16[64,4096]{1,0:T(8,128)(2,1)} %get-tuple-element.53), kind=kLoop, calls=%fused_computation.2 | loop fusion | flops 1048576 | bytes 1572864 | tf_op jit(solution)/shard_map/convert_element_type | solution.py:237
  111.5 2.6 %collective-permute-start.9 = (bf16[64,4096]{1,0:T(8,128)(2,1)}, bf16[64,4096]{1,0:T(8,128)(2,1)}, u32[]{:S(2)}, u32[]{:S(2)}) collective-permute-start(bf16[64,4096]{1,0:T(8,128)(2,1)} %add_convert_fusion.2), channel_id=1, source_target_pairs={{0,192},{64,0},{128,64},{192,128},{1,193},{65,1},{129,65},{193,129... | collective-permute-start | bytes 1572872 | tf_op jit(solution)/shard_map/ppermute | solution.py:25
  114.7 3.4 %collective-permute-done.10.back_high = bf16[64,4096]{1,0:T(8,128)(2,1)} collective-permute-done((bf16[64,4096]{1,0:T(8,128)(2,1)}, bf16[64,4096]{1,0:T(8,128)(2,1)}, u32[]{:S(2)}, u32[]{:S(2)}) %collective-permute-start.10) | collective-permute-done | bytes 524320 | tf_op jit(solution)/shard_map/ppermute | solution.py:25
  118.4 11.2 %collective-permute-done.13.ahead_high = bf16[64,4096]{1,0:T(8,128)(2,1)} collective-permute-done((bf16[64,4096]{1,0:T(8,128)(2,1)}, bf16[64,4096]{1,0:T(8,128)(2,1)}, u32[]{:S(2)}, u32[]{:S(2)}) %collective-permute-start.13) | collective-permute-done | bytes 524320 | tf_op jit(solution)/shard_map/ppermute | solution.py:25
  129.6 2.7 %shard_map.89 = f32[128,4096]{1,0:T(8,128)} custom-call(f32[128,4096]{1,0:T(8,128)S(1)} %copy-done.1, bf16[64,4096]{1,0:T(8,128)(2,1)} %collective-permute-done.9.back_low, bf16[64,4096]{1,0:T(8,128)(2,1)} %collective-permute-done.10.back_high, bf16[64,4096]{1,0:T(8,128)(2,1)} %collective-permute-done.11.ahead_low, ...), custom_call_target="tpu_custom_call" | custom-call | bytes 6291456 | tf_op jit(solution)/shard_map/pallas_call | solution.py:57
  132.4 1.2 shard_map.88
  (47 shorter events, 4.1 us)
Async XLA Ops:
  0.6 5.9 %copy-start.2 = (bf16[4,4096]{1,0:T(4,128)(2,1)S(1)}, bf16[4,4096]{1,0:T(4,128)(2,1)}, u32[]{:S(2)}) copy-start(bf16[4,4096]{1,0:T(4,128)(2,1)} %param.6) | copy-start | bytes 98308
  0.6 17.5 %copy-start.3 = (s32[256,7]{0,1:T(8,128)S(1)}, s32[256,7]{0,1:T(8,128)}, u32[]{:S(2)}) copy-start(s32[256,7]{0,1:T(8,128)} %param.9) | copy-start | bytes 21508
  0.7 17.9 %copy-start.4 = (s32[256]{0:T(256)S(1)}, s32[256]{0:T(256)}, u32[]{:S(2)}) copy-start(s32[256]{0:T(256)} %param.8) | copy-start | bytes 3076
  3.0 22.7 %collective-permute-start = (bf16[64,4096]{1,0:T(8,128)(2,1)}, bf16[64,4096]{1,0:T(8,128)(2,1)S(1)}, u32[]{:S(2)}, u32[]{:S(2)}) collective-permute-start(bf16[64,4096]{1,0:T(8,128)(2,1)} %get-tuple-element.60), channel_id=1, source_target_pairs={{0,64},{64,128},{128,192},{192,0},{1,65},{65,129},{129,193},{193,1... | collective-permute-start | bytes 1572872 | tf_op jit(solution)/shard_map/ppermute | solution.py:25
  5.1 20.6 %collective-permute-start.1 = (bf16[64,4096]{1,0:T(8,128)(2,1)}, bf16[64,4096]{1,0:T(8,128)(2,1)S(1)}, u32[]{:S(2)}, u32[]{:S(2)}) collective-permute-start(bf16[64,4096]{1,0:T(8,128)(2,1)} %get-tuple-element.59), channel_id=1, source_target_pairs={{0,192},{64,0},{128,64},{192,128},{1,193},{65,1},{129,65},{193,129... | collective-permute-start | bytes 1572872 | tf_op jit(solution)/shard_map/ppermute | solution.py:25
  7.3 18.3 %all-to-all-start = ((bf16[8,4,4096]{2,1,0:T(4,128)(2,1)}), bf16[8,4,4096]{2,1,0:T(4,128)(2,1)S(1)}, u32[]{:S(2)}, u32[]{:S(2)}) async-start(bf16[8,4,4096]{2,1,0:T(4,128)(2,1)} %broadcast_in_dim.12), calls=%async_computation | async-start | bytes 524288 | tf_op jit(solution)/shard_map/all_to_all | solution.py:30
  15.5 18.6 %collective-permute-start.4 = (bf16[64,4096]{1,0:T(8,128)(2,1)}, bf16[64,4096]{1,0:T(8,128)(2,1)}, u32[]{:S(2)}, u32[]{:S(2)}) collective-permute-start(bf16[64,4096]{1,0:T(8,128)(2,1)} %get-tuple-element.59), channel_id=1, source_target_pairs={{0,64},{64,128},{128,192},{192,0},{1,65},{65,129},{129,193},{193,1... | collective-permute-start | bytes 1572872 | tf_op jit(solution)/shard_map/ppermute | solution.py:25
  15.5 18.6 %collective-permute-start.5 = (bf16[64,4096]{1,0:T(8,128)(2,1)}, bf16[64,4096]{1,0:T(8,128)(2,1)}, u32[]{:S(2)}, u32[]{:S(2)}) collective-permute-start(bf16[64,4096]{1,0:T(8,128)(2,1)} %get-tuple-element.60), channel_id=1, source_target_pairs={{0,192},{64,0},{128,64},{192,128},{1,193},{65,1},{129,65},{193,129... | collective-permute-start | bytes 1572872 | tf_op jit(solution)/shard_map/ppermute | solution.py:25
  19.4 11.6 %copy-start.5 = (f32[256]{0:T(256)S(1)}, f32[256]{0:T(256)}, u32[]{:S(2)}) copy-start(f32[256]{0:T(256)} %param.10) | copy-start | bytes 3076
  25.7 8.3 %copy-start.6 = (s32[4]{0:T(128)S(1)}, s32[4]{0:T(128)}, u32[]{:S(2)}) copy-start(s32[4]{0:T(128)} %constant.47) | copy-start | bytes 52
  25.7 23.4 %copy-start = (bf16[128,4096]{1,0:T(8,128)(2,1)S(1)}, bf16[128,4096]{1,0:T(8,128)(2,1)}, u32[]{:S(2)}) copy-start(bf16[128,4096]{1,0:T(8,128)(2,1)} %refs_0_.3) | copy-start | bytes 3145732
  26.8 16.1 %all-to-all-start.1 = ((bf16[4,32,4096]{2,1,0:T(8,128)(2,1)}), bf16[4,32,4096]{2,1,0:T(8,128)(2,1)S(1)}, u32[]{:S(2)}, u32[]{:S(2)}) async-start(bf16[4,32,4096]{2,1,0:T(8,128)(2,1)} %broadcast_in_dim.13), calls=%async_computation.1 | async-start | bytes 2097152 | tf_op jit(solution)/shard_map/all_to_all | solution.py:30
  31.1 11.9 %collective-permute-start.2 = (bf16[64,4096]{1,0:T(8,128)(2,1)S(1)}, bf16[64,4096]{1,0:T(8,128)(2,1)}, u32[]{:S(2)}, u32[]{:S(2)}) collective-permute-start(bf16[64,4096]{1,0:T(8,128)(2,1)S(1)} %collective-permute-done.refs_1_), channel_id=1, source_target_pairs={{0,64},{64,128},{128,192},{192,0},{1,65},{65,129},{129,193},{193,1... | collective-permute-start | bytes 1572872 | tf_op jit(solution)/shard_map/ppermute | solution.py:25
  31.2 11.8 %collective-permute-start.3 = (bf16[64,4096]{1,0:T(8,128)(2,1)S(1)}, bf16[64,4096]{1,0:T(8,128)(2,1)}, u32[]{:S(2)}, u32[]{:S(2)}) collective-permute-start(bf16[64,4096]{1,0:T(8,128)(2,1)S(1)} %collective-permute-done.1.refs_4_), channel_id=1, source_target_pairs={{0,192},{64,0},{128,64},{192,128},{1,193},{65,1},{129,65},{193,129... | collective-permute-start | bytes 1572872 | tf_op jit(solution)/shard_map/ppermute | solution.py:25
  42.9 6.2 %collective-permute-start.6 = (bf16[128,4096]{1,0:T(8,128)(2,1)S(1)}, bf16[128,4096]{1,0:T(8,128)(2,1)S(1)}, u32[]{:S(2)}, u32[]{:S(2)}) collective-permute-start(bf16[128,4096]{1,0:T(8,128)(2,1)S(1)} %bitcast.14), channel_id=1, source_target_pairs={{0,1},{1,0},{2,3},{3,2},{4,5},{5,4},{6,7},{7,6},{8,9},{9,8},{10,11... | collective-permute-start | bytes 3145736 | tf_op jit(solution)/shard_map/ppermute | solution.py:25
  91.8 4.6 %collective-permute-start.7 = (f32[128,4096]{1,0:T(8,128)}, f32[128,4096]{1,0:T(8,128)S(1)}, u32[]{:S(2)}, u32[]{:S(2)}) collective-permute-start(f32[128,4096]{1,0:T(8,128)} %get-tuple-element.49), channel_id=1, source_target_pairs={{0,1},{1,0},{2,3},{3,2},{4,5},{5,4},{6,7},{7,6},{8,9},{9,8},{10,11... | collective-permute-start | bytes 6291464 | tf_op jit(solution)/shard_map/ppermute | solution.py:25
  92.2 14.9 %collective-permute-start.12 = (bf16[64,4096]{1,0:T(8,128)(2,1)}, bf16[64,4096]{1,0:T(8,128)(2,1)}, u32[]{:S(2)}, u32[]{:S(2)}) collective-permute-start(bf16[64,4096]{1,0:T(8,128)(2,1)} %get-tuple-element.58), channel_id=1, source_target_pairs={{0,64},{64,128},{128,192},{192,0},{1,65},{65,129},{129,193},{193,1... | collective-permute-start | bytes 1572872 | tf_op jit(solution)/shard_map/ppermute | solution.py:25
  93.5 15.9 %collective-permute-start.8 = (bf16[64,4096]{1,0:T(8,128)(2,1)}, bf16[64,4096]{1,0:T(8,128)(2,1)}, u32[]{:S(2)}, u32[]{:S(2)}) collective-permute-start(bf16[64,4096]{1,0:T(8,128)(2,1)} %get-tuple-element.54), channel_id=1, source_target_pairs={{0,192},{64,0},{128,64},{192,128},{1,193},{65,1},{129,65},{193,129... | collective-permute-start | bytes 1572872 | tf_op jit(solution)/shard_map/ppermute | solution.py:25
  94.9 23.2 %collective-permute-start.10 = (bf16[64,4096]{1,0:T(8,128)(2,1)}, bf16[64,4096]{1,0:T(8,128)(2,1)}, u32[]{:S(2)}, u32[]{:S(2)}) collective-permute-start(bf16[64,4096]{1,0:T(8,128)(2,1)} %get-tuple-element.55), channel_id=1, source_target_pairs={{0,192},{64,0},{128,64},{192,128},{1,193},{65,1},{129,65},{193,129... | collective-permute-start | bytes 1572872 | tf_op jit(solution)/shard_map/ppermute | solution.py:25
  96.4 22.0 %collective-permute-start.11 = (bf16[64,4096]{1,0:T(8,128)(2,1)}, bf16[64,4096]{1,0:T(8,128)(2,1)}, u32[]{:S(2)}, u32[]{:S(2)}) collective-permute-start(bf16[64,4096]{1,0:T(8,128)(2,1)} %get-tuple-element.56), channel_id=1, source_target_pairs={{0,64},{64,128},{128,192},{192,0},{1,65},{65,129},{129,193},{193,1... | collective-permute-start | bytes 1572872 | tf_op jit(solution)/shard_map/ppermute | solution.py:25
  100.3 32.0 %all-to-all-start.4 = ((bf16[32,4,4096]{2,1,0:T(4,128)(2,1)}), bf16[32,4,4096]{2,1,0:T(4,128)(2,1)S(1)}, u32[]{:S(2)}, u32[]{:S(2)}) async-start(bf16[32,4,4096]{2,1,0:T(4,128)(2,1)} %reshape.51), calls=%async_computation.4 | async-start | bytes 2097152 | tf_op jit(solution)/shard_map/all_to_all | solution.py:245
  104.3 25.4 %copy-start.1 = (f32[128,4096]{1,0:T(8,128)S(1)}, f32[128,4096]{1,0:T(8,128)}, u32[]{:S(2)}) copy-start(f32[128,4096]{1,0:T(8,128)} %get-tuple-element.52.here) | copy-start | bytes 6291460
  109.3 20.3 %collective-permute-start.13 = (bf16[64,4096]{1,0:T(8,128)(2,1)}, bf16[64,4096]{1,0:T(8,128)(2,1)}, u32[]{:S(2)}, u32[]{:S(2)}) collective-permute-start(bf16[64,4096]{1,0:T(8,128)(2,1)} %add_convert_fusion.1), channel_id=1, source_target_pairs={{0,64},{64,128},{128,192},{192,0},{1,65},{65,129},{129,193},{193,1... | collective-permute-start | bytes 1572872 | tf_op jit(solution)/shard_map/ppermute | solution.py:25
  111.5 18.1 %collective-permute-start.9 = (bf16[64,4096]{1,0:T(8,128)(2,1)}, bf16[64,4096]{1,0:T(8,128)(2,1)}, u32[]{:S(2)}, u32[]{:S(2)}) collective-permute-start(bf16[64,4096]{1,0:T(8,128)(2,1)} %add_convert_fusion.2), channel_id=1, source_target_pairs={{0,192},{64,0},{128,64},{192,128},{1,193},{65,1},{129,65},{193,129... | collective-permute-start | bytes 1572872 | tf_op jit(solution)/shard_map/ppermute | solution.py:25
